TPU v7x, 512 devices: a whole 4x8x8 slice. The times are simulated.
512 devices in a mesh: box: 64 (over y, z), angle: 8 (over x, core).
Axes of the slice: x: 4, y: 8, z: 8, core: 2. Of those that a mesh axis runs over, the one named last changes fastest.
Arguments:
- child_field: bfloat16 [4096, 2, 64, 128], P('box', None, 'angle'), may hold values from -6 to 6
- child_list: int32 [4096, 8], P('box'), may hold values from -1 to 4095, as said below
- child_op: int32 [4096, 8], P('box'), may hold values from 0 to 39
- child_home: int32 [4096], replicated, may hold values from 0 to 4095, as said below
- child_ops: bfloat16 [40, 2, 64, 128], P(None, None, 'angle'), may hold values from -2 to 2
- parent_list: int32 [1024, 8], P('box'), may hold values from -1 to 1023, as said below
- parent_op: int32 [1024, 8], P('box'), may hold values from 0 to 39
- parent_home: int32 [1024], replicated, may hold values from 0 to 1023, as said below
- parent_ops: bfloat16 [40, 2, 128, 256], P(None, None, 'angle'), may hold values from -2 to 2
Outputs:
- child_out: bfloat16 [4096, 2, 64, 128], P('box', None, 'angle')
Inputs may be any that keep to these rules, and one draw needn't show every extreme that they name: `child_list`: entries are child box ids, or -1 for an empty slot. Among the list rows held by one index of box, at most 8 entries name boxes whose row child_home lies on one index of box (row // 64); some pair of indices reaches 8 in every draw. Entries may repeat. A permutation: child box i is held in row child_home[i]. `parent_list`: entries are parent box ids, or -1 for an empty slot. Among the list rows held by one index of box, at most 2 entries name boxes whose row parent_home lies on one index of box (row // 16); some pair of indices reaches 2 in every draw. Entries may repeat. A permutation: parent box i is held in row parent_home[i].
All inputs are finite; a program needn't handle non-finite values.
Results may differ from a plain program's by a relative error of at most 0.0017.
The roundings to bfloat16 on the way count: a program that leaves them out, or rounds other values in their place, can miss the bound.
Values may be sent and summed in bfloat16 or wider, within the bound.
No kernel may reach another device: no remote copies, remote signals or barrier semaphores. Data moves between devices by JAX's collectives and lax.ppermute only.
A program may use at most 64 MiB of HBM per device.

v0:
```python
import math

import jax
import jax.numpy as jnp
from jax import lax
from jax.sharding import PartitionSpec as P

CT = 64
SUBBOX_HEADINGS = 128
PT = 128
PP = 256
KIDS = 4


WAVE_NUMBER = 6.0


def fourier_table(fine_count, coarse_count, offset):
    fine_pos = (jnp.arange(fine_count, dtype=jnp.float32) + offset) / fine_count
    coarse_pos = (jnp.arange(coarse_count, dtype=jnp.float32) + offset) / coarse_count
    distance = fine_pos[:, None] - coarse_pos[None, :]
    harmonic = jnp.arange(1, coarse_count // 2, dtype=jnp.float32)
    cosines = jnp.cos(2.0 * math.pi * harmonic[None, None, :] * distance[:, :, None])
    summed = 1.0 + 2.0 * jnp.sum(cosines, axis=2) + jnp.cos(math.pi * coarse_count * distance)
    return summed / coarse_count


def shift_parts(polar_rows):
    polar_angle = math.pi * (polar_rows.astype(jnp.float32) + 0.5) / PT
    heading_radians = 2.0 * math.pi / PP * jnp.arange(PP, dtype=jnp.float32)
    kid_index = jnp.arange(KIDS, dtype=jnp.int32)
    side_x = (2 * (kid_index % 2) - 1).astype(jnp.float32)
    side_y = (2 * (kid_index // 2 % 2) - 1).astype(jnp.float32)
    across = (
        side_x[:, None] * jnp.cos(heading_radians)[None, :]
        + side_y[:, None] * jnp.sin(heading_radians)[None, :]
    )
    phase_arg = WAVE_NUMBER * jnp.sin(polar_angle)[None, :, None] * across[:, None, :]
    return (jnp.cos(phase_arg), jnp.sin(phase_arg))


def lift_sum(widened, cos_part, sin_part):
    real_part = jnp.sum(
        cos_part * widened[..., 0, :, :] - sin_part * widened[..., 1, :, :], axis=-3
    )
    imag_part = jnp.sum(
        cos_part * widened[..., 1, :, :] + sin_part * widened[..., 0, :, :], axis=-3
    )
    return jnp.stack([real_part, imag_part], axis=-3).astype(jnp.bfloat16)


def lower_turn(parents, cos_part, sin_part):
    real_in = jnp.expand_dims(parents[..., 0, :, :].astype(jnp.float32), -3)
    imag_in = jnp.expand_dims(parents[..., 1, :, :].astype(jnp.float32), -3)
    real_out = cos_part * real_in + sin_part * imag_in
    imag_out = cos_part * imag_in - sin_part * real_in
    return jnp.stack([real_out, imag_out], axis=-3).astype(jnp.bfloat16)


def plan_requests(far_lists, home_rows, rows_device, owners):
    flat_ids = far_lists.reshape(-1)
    usable = flat_ids >= 0
    target_row = home_rows[jnp.where(usable, flat_ids, 0)]
    owner_of = target_row // rows_device
    local_row = target_row - owner_of * rows_device
    capacity = flat_ids.shape[0] // owners
    matches = (
        (owner_of[:, None] == jnp.arange(owners, dtype=jnp.int32)[None, :]) & usable[:, None]
    ).astype(jnp.int32)
    earlier = jnp.cumsum(matches, axis=0) - matches
    rank_in = jnp.sum(earlier * matches, axis=1)
    position = jnp.where(usable, owner_of * capacity + rank_in, owners * capacity)
    wanted = jnp.zeros((owners * capacity,), jnp.int32).at[position].set(local_row, mode="drop")
    return (wanted.reshape(owners, capacity), position, usable)


def translate_sum(received, position, usable, op_index, op_table):
    rows_here, slot_count = op_index.shape
    pattern_shape = received.shape[2:]
    flat_in = received.reshape((-1,) + pattern_shape)
    clipped = jnp.minimum(position, flat_in.shape[0] - 1)
    source = flat_in[clipped].reshape((rows_here, slot_count) + pattern_shape)
    translator = op_table[op_index]
    weight = usable.reshape(rows_here, slot_count, 1, 1).astype(jnp.float32)
    src_real = source[:, :, 0].astype(jnp.float32)
    src_imag = source[:, :, 1].astype(jnp.float32)
    op_real = translator[:, :, 0].astype(jnp.float32)
    op_imag = translator[:, :, 1].astype(jnp.float32)
    real_part = jnp.sum(weight * (op_real * src_real - op_imag * src_imag), axis=1)
    imag_part = jnp.sum(weight * (op_real * src_imag + op_imag * src_real), axis=1)
    return jnp.stack([real_part, imag_part], axis=1)


def local(
    child_field,
    child_list,
    child_op,
    child_home,
    child_ops,
    parent_list,
    parent_op,
    parent_home,
    parent_ops,
):
    owners = lax.axis_size("box")
    angle_index = lax.axis_index("angle")
    child_rows = child_field.shape[0]
    parent_rows = parent_list.shape[0]
    child_thin = child_field.shape[2]
    parent_thin = parent_ops.shape[2]
    child_wanted, child_position, child_usable = plan_requests(
        child_list, child_home, child_rows, owners
    )
    parent_wanted, parent_position, parent_usable = plan_requests(
        parent_list, parent_home, parent_rows, owners
    )
    child_asked, parent_asked = (
        lax.all_to_all(child_wanted, "box", split_axis=0, concat_axis=0, tiled=True),
        lax.all_to_all(parent_wanted, "box", split_axis=0, concat_axis=0, tiled=True),
    )
    child_sent = lax.all_to_all(
        child_field[child_asked], "box", split_axis=0, concat_axis=0, tiled=True
    )
    child_far = translate_sum(child_sent, child_position, child_usable, child_op, child_ops)
    theta_up = fourier_table(PT, CT, 0.5).astype(jnp.bfloat16)
    phi_up = fourier_table(PP, SUBBOX_HEADINGS, 0.0).T.astype(jnp.bfloat16)
    theta_down = (fourier_table(PT, CT, 0.5).T * (CT / PT)).astype(jnp.bfloat16)
    phi_down = (fourier_table(PP, SUBBOX_HEADINGS, 0.0) * (SUBBOX_HEADINGS / PP)).astype(
        jnp.bfloat16
    )
    up_rows = lax.dynamic_slice_in_dim(theta_up, angle_index * parent_thin, parent_thin, 0)
    columns = up_rows
    stretched = jnp.einsum(
        "ut,rctp->rcup",
        columns,
        lax.all_gather(child_field, "angle", axis=2, tiled=True),
        preferred_element_type=jnp.float32,
    ).astype(jnp.bfloat16)
    widened = jnp.einsum("rcup,pv->rcuv", stretched, phi_up, preferred_element_type=jnp.float32)
    local_polar = angle_index * parent_thin + jnp.arange(parent_thin, dtype=jnp.int32)
    cos_local, sin_local = shift_parts(local_polar)
    parent_field = lift_sum(
        widened.reshape(parent_rows, KIDS, 2, parent_thin, PP), cos_local, sin_local
    )
    parent_sent = lax.all_to_all(
        parent_field[parent_asked], "box", split_axis=0, concat_axis=0, tiled=True
    )
    parent_far = translate_sum(
        parent_sent, parent_position, parent_usable, parent_op, parent_ops
    ).astype(jnp.bfloat16)
    down_rows = lax.dynamic_slice_in_dim(theta_down, angle_index * child_thin, child_thin, 0)
    block_piece = lax.all_gather(parent_far, "angle", axis=2, tiled=True)
    span_rows = block_piece.shape[2]
    cos_piece, sin_piece = shift_parts(jnp.arange(span_rows, dtype=jnp.int32))
    turned = lower_turn(block_piece, cos_piece, sin_piece)
    narrowed = jnp.einsum(
        "qkcuv,vp->qkcup", turned, phi_down, preferred_element_type=jnp.float32
    ).astype(jnp.bfloat16)
    columns = down_rows
    summed_term = jnp.einsum(
        "tu,qkcup->qkctp", columns, narrowed, preferred_element_type=jnp.float32
    )
    child_term = summed_term.astype(jnp.bfloat16).reshape(
        child_rows, 2, child_thin, SUBBOX_HEADINGS
    )
    child_term = lax.optimization_barrier(child_term)
    return (child_far + child_term.astype(jnp.float32)).astype(jnp.bfloat16)


def solution(mesh):
    return jax.shard_map(
        local,
        mesh=mesh,
        in_specs=(
            P("box", None, "angle", None),
            P("box", None),
            P("box", None),
            P(),
            P(None, None, "angle", None),
            P("box", None),
            P("box", None),
            P(),
            P(None, None, "angle", None),
        ),
        out_specs=P("box", None, "angle", None),
        check_vma=False,
    )
```

profile of v0, /device:TPU:104, one launch (start us, length us, event | category | flops | bytes accessed | tf_op | source)
XLA Modules:
  0.0 249.3 jit_solution(16100128311826740797)
XLA Ops:
  6.5 0.7 all-gather.3.cloned.1.call-update
  7.3 0.8 copy.134
  8.0 0.7 fusion.130
  8.7 0.1 reshape.635
  8.8 1.6 gather_fusion.5
  10.5 0.1 copy.135
  10.5 0.1 ge.64
  10.6 0.1 fusion.66
  10.8 0.2 reduce_window_sum.28
  10.9 0.2 select_reduce_fusion
  11.1 1.0 scatter_custom_fusion.1
  12.1 0.7 all_to_all.26
  12.9 15.4 %all-to-all-start.2 = ((s32[64,1,2]{2,1,0:T(1,128)}), s32[64,1,2]{2,1,0:T(1,128)S(1)}, u32[]{:S(2)}, u32[]{:S(2)}) async-start(s32[64,1,2]{2,1,0:T(1,128)} %bitcast.34), calls=%async_computation.2 | async-start | bytes 65536 | tf_op jit(solution)/shard_map/all_to_all | solution.py:119
  28.3 0.8 copy.118
  29.0 0.7 fusion.131
  29.7 0.1 copy.119
  29.8 0.1 ge.61
  29.9 0.1 ge.60
  30.0 0.1 reshape.630
  30.2 3.1 %gather_fusion.1 = s32[512]{0:T(512)S(1)} fusion(s32[4096]{0:T(1024)S(1)} %copy-done.1, s32[1024]{0:T(1024)S(1)} %pad_clamp_fusion.6), kind=kCustom, calls=%fused_computation.1 | custom fusion | bytes 6144 | tf_op jit(solution)/shard_map/gather | solution.py:63
  33.4 1.2 reduce-window.6
  34.6 0.2 slice_reduce_fusion
  35.0 0.1 fusion.40
  35.1 0.1 broadcast_subtract_fusion.3
  35.2 3.3 %cosine_reduce_fusion.1 = f32[128,64]{0,1:T(8,128)S(1)} fusion(f32[128,64]{0,1:T(8,128)S(1)} %broadcast_subtract_fusion.3, f32[31]{0:T(128)S(1)} %add_multiply_fusion.3), kind=kLoop, calls=%fused_computation.67 | loop fusion | flops 499712 | bytes 65660 | tf_op jit(solution)/shard_map/reduce_sum | solution.py:24
  38.6 0.1 multiply_add_fusion.2
  38.7 0.1 broadcast_subtract_fusion
  38.8 0.3 multiply_cosine_fusion.1
  39.1 27.5 %cosine_reduce_fusion = f32[256,128]{1,0:T(8,128)S(1)} fusion(f32[256,128]{1,0:T(8,128)S(1)} %broadcast_subtract_fusion, f32[63]{0:T(128)S(1)} %add_multiply_fusion), kind=kLoop, calls=%fused_computation.16 | loop fusion | flops 4096000 | bytes 262396 | tf_op jit(solution)/shard_map/reduce_sum | solution.py:24
  66.6 2.4 scatter_custom_fusion
  69.0 0.7 all_to_all.22
  69.7 12.7 %all-to-all-start = ((s32[64,1,8]{2,1,0:T(1,128)}), s32[64,1,8]{2,1,0:T(1,128)S(1)}, u32[]{:S(2)}, u32[]{:S(2)}) async-start(s32[64,1,8]{2,1,0:T(1,128)} %bitcast.7), calls=%async_computation | async-start | bytes 65536 | tf_op jit(solution)/shard_map/all_to_all | solution.py:118
  82.4 0.1 copy.137
  82.5 0.1 copy.138
  82.6 0.1 reshape.691
  82.8 2.8 %fusion.29 = f32[64,2,16,256]{3,2,1,0:T(8,128)S(1)} fusion(bf16[64,2,64,128]{3,2,1,0:T(8,128)(2,1)} %all-gather.3.cloned.1.call-done, f32[256,128]{1,0:T(8,128)S(1)} %cosine_reduce_fusion, f32[128]{0:T(128)S(1)} %get-tuple-element.37, f32[256]{0:T(256)S(1)} %iota_multiply_fusion, f32[128,64]{0,1:T(8,128)S(1)} %broadcast_subtract_fusion.3, ...), kind=kOutput, calls=%fused_computation.51 | convolution fusion | flops 168267776 | bytes 4392452 | tf_op jit(solution)/shard_map/rcup,pv->rcuv/dot_general | solution.py:139
  85.6 0.3 subtract_reduce_fusion
  86.0 2.0 gather_fusion.6
  88.0 1.4 all-to-all-done
  89.4 11.5 %all-to-all-start.3 = ((bf16[64,2,2,16,256]{4,3,2,1,0:T(8,128)(2,1)}), bf16[64,2,2,16,256]{4,3,2,1,0:T(8,128)(2,1)S(1)}, u32[]{:S(2)}, u32[]{:S(2)}) async-start(bf16[64,2,2,16,256]{4,3,2,1,0:T(8,128)(2,1)} %bitcast.257), calls=%async_computation.3 | async-start | bytes 4194304 | tf_op jit(solution)/shard_map/all_to_all | solution.py:145
  100.9 0.1 copy.128
  100.9 0.1 reshape.659
  101.1 2.7 %gather_fusion.2 = bf16[512,2,8,128]{3,2,1,0:T(8,128)(2,1)} fusion(bf16[64,2,8,128]{3,2,1,0:T(8,128)(2,1)S(1)} %copy-done.3, s32[1024]{0:T(1024)S(1)} %pad_clamp_fusion.5), kind=kCustom, calls=%fused_computation.2 | custom fusion | bytes 4196352 | tf_op jit(solution)/shard_map/gather | solution.py:122
  103.8 52.6 %all-to-all-done.3 = bf16[64,2,2,16,256]{4,3,2,1,0:T(8,128)(2,1)S(1)} async-done(((bf16[64,2,2,16,256]{4,3,2,1,0:T(8,128)(2,1)}), bf16[64,2,2,16,256]{4,3,2,1,0:T(8,128)(2,1)S(1)}, u32[]{:S(2)}, u32[]{:S(2)}) %all-to-all-start.3) | async-done | bytes 2097184 | tf_op jit(solution)/shard_map/all_to_all | solution.py:145
  156.4 8.2 %all-to-all-start.1 = ((bf16[64,8,2,8,128]{4,3,2,1,0:T(8,128)(2,1)}), bf16[64,8,2,8,128]{4,3,2,1,0:T(8,128)(2,1)}, u32[]{:S(2)}, u32[]{:S(2)}) async-start(bf16[64,8,2,8,128]{4,3,2,1,0:T(8,128)(2,1)} %bitcast.9), calls=%async_computation.1 | async-start | bytes 4194304 | tf_op jit(solution)/shard_map/all_to_all | solution.py:121
  164.7 0.1 copy.129
  164.8 0.1 reshape.675
  164.9 2.0 gather_fusion.4
  166.9 2.0 gather_fusion.7
  168.9 3.4 %fusion.22 = (bf16[16,16,256]{2,1,0:T(8,128)(2,1)S(1)}, bf16[16,16,256]{2,1,0:T(8,128)(2,1)S(1)}) fusion(f32[16,8]{1,0:T(8,128)S(1)} %copy.128, bf16[16,8,2,16,256]{4,3,2,1,0:T(8,128)(2,1)} %bitcast.258, bf16[16,8,2,16,256]{4,3,2,1,0:T(8,128)(2,1)} %bitcast.260), kind=kLoop, calls=%fused_computation.43 | loop fusion | flops 7208960 | bytes 4456960 | tf_op jit(solution)/shard_map/reduce_sum | solution.py:89
  172.4 0.7 pad_maximum_fusion.1
  173.1 0.1 dynamic-slice
  173.2 0.1 copy.115
  173.3 0.1 copy.116
  173.4 0.1 reshape.643
  173.5 2.0 gather_fusion
  175.6 2.7 %multiply_cosine_fusion = (f32[4,128,256]{2,1,0:T(8,128)S(1)}, f32[4,128,256]{2,1,0:T(8,128)}) fusion(f32[4,256]{1,0:T(4,128)S(1)} %multiply_add_fusion.2, f32[128]{0:T(128)S(1)} %sine_multiply_fusion.1), kind=kLoop, calls=%fused_computation.69 | loop fusion | flops 131072 | bytes 1053184 | tf_op jit(solution)/shard_map/cos | solution.py:39
  178.3 41.8 %all-to-all-done.1 = bf16[64,8,2,8,128]{4,3,2,1,0:T(8,128)(2,1)} async-done(((bf16[64,8,2,8,128]{4,3,2,1,0:T(8,128)(2,1)}), bf16[64,8,2,8,128]{4,3,2,1,0:T(8,128)(2,1)}, u32[]{:S(2)}, u32[]{:S(2)}) %all-to-all-start.1) | async-done | bytes 2097184 | tf_op jit(solution)/shard_map/all_to_all | solution.py:121
  220.1 3.9 %gather_fusion.3 = bf16[512,2,8,128]{3,2,1,0:T(8,128)(2,1)} fusion(bf16[512,2,8,128]{3,2,1,0:T(8,128)(2,1)} %bitcast.10, s32[1024]{0:T(1024)S(1)} %pad_clamp_fusion.4), kind=kCustom, calls=%fused_computation.3 | custom fusion | bytes 4196352 | tf_op jit(solution)/shard_map/gather | solution.py:82
  224.1 3.3 %fusion.13 = (f32[64,8,128]{2,1,0:T(8,128)}, f32[64,8,128]{2,1,0:T(8,128)}) fusion(f32[64,8]{1,0:T(8,128)S(1)} %copy.115, bf16[64,8,2,8,128]{4,3,2,1,0:T(8,128)(2,1)S(1)} %bitcast.255, bf16[64,8,2,8,128]{4,3,2,1,0:T(8,128)(2,1)} %bitcast.261), kind=kLoop, calls=%fused_computation.34 | loop fusion | flops 7208960 | bytes 4720640 | tf_op jit(solution)/shard_map/reduce_sum | solution.py:89
  227.4 2.1 fusion.36
  229.5 4.7 %add_convert_fusion = (bf16[16,4,1,128,256]{4,3,2,1,0:T(8,128)(2,1)}, bf16[16,4,1,128,256]{4,3,2,1,0:T(8,128)(2,1)}) fusion(f32[16,128,256]{2,1,0:T(8,128)S(1)} %get-tuple-element.24, f32[4,128,256]{2,1,0:T(8,128)S(1)} %copy-done.4, f32[16,128,256]{2,1,0:T(8,128)S(1)} %get-tuple-element.23, f32[4,128,256]{2,1,0:T(8,128)S(1)} %get-tuple-element.27), kind=kLoop, calls=%fused_computation.15 | loop fusion | flops 16777216 | bytes 13631488 | tf_op jit(solution)/shard_map/convert.2
  234.3 7.4 %fusion.30 = bf16[16,4,2,128,8]{3,4,2,1,0:T(8,128)(2,1)S(1)} fusion(bf16[16,4,1,128,256]{4,3,2,1,0:T(8,128)(2,1)} %get-tuple-element.22, bf16[16,4,1,128,256]{4,3,2,1,0:T(8,128)(2,1)} %get-tuple-element.21, f32[256,128]{1,0:T(8,128)S(1)} %copy-done.8, f32[128]{0:T(128)S(1)} %get-tuple-element.37, f32[256]{0:T(256)S(1)} %iota_multiply_fusion, ...), kind=kOutput, calls=%fused_computation.52 | convolution fusion | flops 1113953280 | bytes 8788484 | tf_op jit(solution)/shard_map/tu,qkcup->qkctp/dot_general | solution.py:160
  241.7 0.8 fusion.37
  (63 shorter events, 0.6 us)
Async XLA Ops:
  6.5 158.4 %copy-start = (bf16[40,2,16,256]{3,2,1,0:T(8,128)(2,1)S(1)}, bf16[40,2,16,256]{3,2,1,0:T(8,128)(2,1)}, u32[]{:S(2)}) copy-start(bf16[40,2,16,256]{3,2,1,0:T(8,128)(2,1)} %param.17) | copy-start | bytes 1966084
  6.5 23.6 %copy-start.1 = (s32[4096]{0:T(1024)S(1)}, s32[4096]{0:T(1024)}, u32[]{:S(2)}) copy-start(s32[4096]{0:T(1024)} %param.12) | copy-start | bytes 49156
  6.5 76.3 %all-gather.3.cloned.1.call-start = ((), (), s32[]{:S(2)}) async-start(), calls=%async_computation.4 | async-start | bytes 2359296 | tf_op jit(solution)/shard_map/all_gather | solution.py:136
  12.9 56.9 %all-to-all-start.2 = ((s32[64,1,2]{2,1,0:T(1,128)}), s32[64,1,2]{2,1,0:T(1,128)S(1)}, u32[]{:S(2)}, u32[]{:S(2)}) async-start(s32[64,1,2]{2,1,0:T(1,128)} %bitcast.34), calls=%async_computation.2 | async-start | bytes 65536 | tf_op jit(solution)/shard_map/all_to_all | solution.py:119
  66.6 19.1 %copy-start.7 = (f32[256,128]{1,0:T(8,128)}, f32[256,128]{1,0:T(8,128)S(1)}, u32[]{:S(2)}) copy-start(f32[256,128]{1,0:T(8,128)S(1)} %cosine_reduce_fusion) | copy-start | bytes 393220
  69.7 19.6 %all-to-all-start = ((s32[64,1,8]{2,1,0:T(1,128)}), s32[64,1,8]{2,1,0:T(1,128)S(1)}, u32[]{:S(2)}, u32[]{:S(2)}) async-start(s32[64,1,8]{2,1,0:T(1,128)} %bitcast.7), calls=%async_computation | async-start | bytes 65536 | tf_op jit(solution)/shard_map/all_to_all | solution.py:118
  89.4 11.7 %copy-start.3 = (bf16[64,2,8,128]{3,2,1,0:T(8,128)(2,1)S(1)}, bf16[64,2,8,128]{3,2,1,0:T(8,128)(2,1)}, u32[]{:S(2)}) copy-start(bf16[64,2,8,128]{3,2,1,0:T(8,128)(2,1)} %param.9) | copy-start | bytes 786436
  89.4 67.0 %all-to-all-start.3 = ((bf16[64,2,2,16,256]{4,3,2,1,0:T(8,128)(2,1)}), bf16[64,2,2,16,256]{4,3,2,1,0:T(8,128)(2,1)S(1)}, u32[]{:S(2)}, u32[]{:S(2)}) async-start(bf16[64,2,2,16,256]{4,3,2,1,0:T(8,128)(2,1)} %bitcast.257), calls=%async_computation.3 | async-start | bytes 4194304 | tf_op jit(solution)/shard_map/all_to_all | solution.py:145
  156.4 8.3 %copy-start.9 = (s32[16,8]{0,1:T(8,128)S(1)}, s32[16,8]{0,1:T(8,128)}, u32[]{:S(2)}) copy-start(s32[16,8]{0,1:T(8,128)} %param.15) | copy-start | bytes 1540
  156.4 63.8 %all-to-all-start.1 = ((bf16[64,8,2,8,128]{4,3,2,1,0:T(8,128)(2,1)}), bf16[64,8,2,8,128]{4,3,2,1,0:T(8,128)(2,1)}, u32[]{:S(2)}, u32[]{:S(2)}) async-start(bf16[64,8,2,8,128]{4,3,2,1,0:T(8,128)(2,1)} %bitcast.9), calls=%async_computation.1 | async-start | bytes 4194304 | tf_op jit(solution)/shard_map/all_to_all | solution.py:121
  164.6 62.8 %all-gather.5.cloned.1.call-start = ((), (), s32[]{:S(2)}) async-start(), calls=%async_computation.5 | async-start | bytes 2359296 | tf_op jit(solution)/shard_map/all_gather | solution.py:152
  168.9 4.3 %copy-start.10 = (s32[64,8]{0,1:T(8,128)S(1)}, s32[64,8]{0,1:T(8,128)}, u32[]{:S(2)}) copy-start(s32[64,8]{0,1:T(8,128)} %param.11) | copy-start | bytes 6148
  168.9 4.5 %copy-start.2 = (bf16[40,2,8,128]{3,2,1,0:T(8,128)(2,1)S(1)}, bf16[40,2,8,128]{3,2,1,0:T(8,128)(2,1)}, u32[]{:S(2)}) copy-start(bf16[40,2,8,128]{3,2,1,0:T(8,128)(2,1)} %param.13) | copy-start | bytes 491524
  227.4 2.1 copy-start.4
  229.5 4.8 %copy-start.8 = (f32[256,128]{1,0:T(8,128)S(1)}, f32[256,128]{1,0:T(8,128)}, u32[]{:S(2)}) copy-start(f32[256,128]{1,0:T(8,128)} %copy-done.7) | copy-start | bytes 393220
  234.3 7.4 %copy-start.5 = (f32[64,8,128]{2,1,0:T(8,128)S(1)}, f32[64,8,128]{2,1,0:T(8,128)}, u32[]{:S(2)}) copy-start(f32[64,8,128]{2,1,0:T(8,128)} %get-tuple-element.5) | copy-start | bytes 786436
  234.3 7.4 %copy-start.6 = (f32[64,8,128]{2,1,0:T(8,128)S(1)}, f32[64,8,128]{2,1,0:T(8,128)}, u32[]{:S(2)}) copy-start(f32[64,8,128]{2,1,0:T(8,128)} %get-tuple-element.6) | copy-start | bytes 786436
Sparse Core Ops, SparseCore 0:
  9.5 35.6 all-gather.2
  173.2 31.3 all-gather.4
where the time goes:
time: 250 us; the launch traced here: 249 us
  waiting for transfers between devices  96.6 us (39%)
  other arithmetic  53 us (21%)
  starting transfers between devices  47.9 us (19%)
  local copies, waits for them, and re-layouts  27.8 us (11%)
  between operations  13.8 us (6%)
  matrix products  10.2 us (4%)
    all_to_all x1, waiting for transfers between devices, local(): lax.all_to_all(parent_field[parent_asked], 'box', split_axis=0, concat_ax...  52.6 us
    all_to_all x1, waiting for transfers between devices, local(): lax.all_to_all(child_field[child_asked], 'box', split_axis=0, concat_axis...  41.8 us
    reduce_sum x2, other arithmetic, fourier_table(): jnp.sum(cosines, axis=2)  30.8 us
    all_to_all x1, starting transfers between devices, local(): lax.all_to_all(parent_wanted, 'box', split_axis=0, concat_axis=0, tiled=T...  15.4 us
    all_to_all x1, starting transfers between devices, local(): lax.all_to_all(child_wanted, 'box', split_axis=0, concat_axis=0, tiled=True)  12.7 us
    all_to_all x1, starting transfers between devices, local(): lax.all_to_all(parent_field[parent_asked], 'box', split_axis=0, concat_ax...  11.5 us
    all_to_all x1, starting transfers between devices, local(): lax.all_to_all(child_field[child_asked], 'box', split_axis=0, concat_axis...  8.25 us
    dot_general x1, matrix products, local(): jnp.einsum('tu,qkcup->qkctp', columns, narrowed, preferred_element_type=j...  7.41 us
  transfers between devices with their start and end apart: 6, of which 3 were waited for; matrix products, arithmetic and copies ran while one was open for 30% of the time, Pallas kernels for 0%

commit v1 on v0

v1 whole, which is shorter than its diff:
```python
import functools
import math

import jax
import jax.numpy as jnp
import numpy as np
from jax import lax
from jax.experimental import pallas as pl
from jax.experimental.pallas import tpu as pltpu
from jax.sharding import PartitionSpec as P

CT = 64
SUBBOX_HEADINGS = 128
PT = 128
PP = 256
KIDS = 4
WAVE_NUMBER = 6.0
SIDE = 8
BOTH = ("box", "angle")
F32, BF16, I32 = jnp.float32, jnp.bfloat16, jnp.int32
VM = pltpu.VMEM
ANY = pl.ANY


def fourier_table(fine_count, coarse_count, offset):
    f32 = np.float32
    fine = (np.arange(fine_count, dtype=f32) + f32(offset)) / f32(fine_count)
    coarse = (np.arange(coarse_count, dtype=f32) + f32(offset)) / f32(coarse_count)
    x = fine[:, None] - coarse[None, :]
    harmonic = np.arange(1, coarse_count // 2, dtype=f32)
    cosines = np.cos(f32(2.0 * math.pi) * harmonic * x[:, :, None])
    summed = f32(1.0) + f32(2.0) * cosines.sum(2, dtype=np.float64) + np.cos(f32(math.pi * coarse_count) * x)
    return (summed / coarse_count).astype(f32)


def shift_tables():
    f32 = np.float32
    polar = (f32(math.pi) * (np.arange(PT, dtype=f32) + f32(0.5)) / f32(PT)).astype(f32)
    heading = (f32(2.0 * math.pi / PP) * np.arange(PP, dtype=f32)).astype(f32)
    cos_h, sin_h = np.cos(heading), np.sin(heading)
    across = np.stack([-cos_h - sin_h, cos_h - sin_h])
    arg = (f32(WAVE_NUMBER) * np.sin(polar))[None, :, None] * across[:, None, :]
    return np.cos(arg).astype(f32), np.sin(arg).astype(f32)


def bmm(a, b):
    return lax.dot_general(a, b, (((1,), (0,)), ((), ())), preferred_element_type=F32)


def iota(shape, dim):
    return lax.broadcasted_iota(I32, shape, dim)


def plan_level(ids_ref, op_ref, home_ref, core, mine, rows_device, cap, empty_op, code_ref):
    slots, rows = ids_ref.shape
    home = home_ref[...]
    owner = home // rows_device
    table = jnp.concatenate([owner, home - owner * rows_device], axis=0).astype(F32).astype(BF16)
    highs = home.shape[0]
    before = (iota((rows, rows), 0) < iota((rows, rows), 1)).astype(F32).astype(BF16)
    carry = jnp.zeros((SIDE, 1), F32)
    wanted = jnp.zeros((2 * SIDE, cap), F32)
    for j in range(slots):
        ids = ids_ref[pl.ds(j, 1), :]
        usable = ids >= 0
        safe = jnp.maximum(ids, 0)
        high, low = safe >> 7, safe & 127
        low_hot = (iota((128, rows), 0) == low).astype(F32).astype(BF16)
        picked = bmm(table, low_hot)
        high_hot = (iota((highs, rows), 0) == high).astype(F32)
        own = jnp.sum(picked[:highs] * high_hot, axis=0, keepdims=True).astype(I32)
        loc = jnp.sum(picked[highs:] * high_hot, axis=0, keepdims=True)
        along_y, along_z = own >> 3, own & 7
        column = jnp.where(core == 0, along_z, along_y)
        place = (jnp.where(core == 0, along_y, along_z) - mine) & 7
        hot = jnp.where((iota((SIDE, rows), 0) == column) & usable, 1.0, 0.0)
        hot_b = hot.astype(BF16)
        prefix = bmm(hot_b, before) + carry
        carry = carry + jnp.sum(hot, axis=1, keepdims=True)
        rank = jnp.sum(hot * prefix, axis=0, keepdims=True).astype(I32)
        position = column * cap + rank
        code_ref[pl.ds(j, 1), pl.ds(0, rows)] = jnp.where(
            usable, position * 64 + op_ref[pl.ds(j, 1), :], empty_op
        )
        rank_hot = (iota((cap, rows), 0) == rank).astype(F32).astype(BF16)
        both = jnp.concatenate([hot * place.astype(F32), hot * loc], axis=0).astype(BF16)
        wanted = wanted + lax.dot_general(
            both, rank_hot, (((1,), (1,)), ((), ())), preferred_element_type=F32
        )
    return (wanted[:SIDE] * rows_device + wanted[SIDE:]).astype(I32)


def plan_body(where, cl, co, ch, plist, po, ph, want_ref, ccode_ref, pcode_ref):
    core, mine = where[0], where[1]
    want_ref[...] = jnp.zeros(want_ref.shape, I32)
    want_ref[:, pl.ds(0, 64)] = plan_level(cl, co, ch, core, mine, 64, 64, 40, ccode_ref)
    want_ref[:, pl.ds(64, 16)] = plan_level(plist, po, ph, core, mine, 16, 16, 40, pcode_ref)


def plan(where, child_list, child_op, child_home, parent_list, parent_op, parent_home):
    args = (
        where,
        child_list.T,
        child_op.T,
        child_home.reshape(-1, 128),
        parent_list.T,
        parent_op.T,
        parent_home.reshape(-1, 128),
    )
    return pl.pallas_call(
        plan_body,
        out_shape=(
            jax.ShapeDtypeStruct((SIDE, 128), I32),
            jax.ShapeDtypeStruct((8, 64), I32),
            jax.ShapeDtypeStruct((8, 16), I32),
        ),
        in_specs=[pl.BlockSpec(memory_space=pltpu.SMEM)] + [pl.BlockSpec(memory_space=VM)] * 6,
        out_specs=(pl.BlockSpec(memory_space=VM),) * 3,
        name="plan",
    )(*args)


def up_body(field, theta, phi, cos_t, sin_t, out, wide):
    for r in range(8):
        for c in range(2):
            rows = jnp.concatenate([field[s, r, c] for s in range(8)], axis=0)
            stretched = bmm(theta[...], rows).astype(BF16)
            wide[r * 2 + c] = bmm(stretched, phi[...])
    for q in range(2):
        for u in range(PT // 8):
            at = pl.ds(u * 8, 8)
            w = [[wide[(q * 4 + k) * 2 + c, at, :] for c in range(2)] for k in range(4)]
            real = jnp.zeros((8, PP), F32)
            imag = jnp.zeros((8, PP), F32)
            for t, (k, m) in enumerate(((0, 3), (1, 2))):
                cs, sn = cos_t[t, at, :], sin_t[t, at, :]
                real = real + cs * (w[k][0] + w[m][0]) - sn * (w[k][1] - w[m][1])
                imag = imag + cs * (w[k][1] + w[m][1]) + sn * (w[k][0] - w[m][0])
            for c, part in enumerate((real, imag)):
                part = part.astype(BF16)
                for v in range(2):
                    out[u // 2, q, c * 4 + (u % 2) * 2 + v] = part[:, v * 128 : (v + 1) * 128]


def lift(field, theta, phi, cos_t, sin_t):
    return pl.pallas_call(
        up_body,
        out_shape=jax.ShapeDtypeStruct((8, 2, 8, 8, 128), BF16),
        in_specs=[pl.BlockSpec(memory_space=VM)] * 5,
        out_specs=pl.BlockSpec(memory_space=VM),
        scratch_shapes=[pltpu.VMEM((16, PT, PP), F32)],
        name="lift",
    )(field, theta, phi, cos_t, sin_t)


def select_body(first, rows, tiles, asked, *refs):
    blocks, out, pool, sems = refs[:8], refs[8], refs[9], refs[10]
    count = rows * tiles
    copies = [
        pltpu.make_async_copy(b.at[pl.ds(first[1], count)], pool.at[pl.ds(i * count, count)], sems.at[i])
        for i, b in enumerate(blocks)
    ]
    for copy in copies:
        copy.start()
    for copy in copies:
        copy.wait()
    per_peer = out.shape[1]

    def step(h, carry):
        for k in range(per_peer):
            row = asked[h, first[0] + k]
            at = pl.multiple_of(row * tiles, tiles)
            out[h, k] = pool[pl.ds(at, tiles)]
        return carry

    lax.fori_loop(0, SIDE, step, 0)


def select(asked, blocks, first, rows, tiles, per_peer):
    return pl.pallas_call(
        functools.partial(select_body, first, rows, tiles),
        out_shape=jax.ShapeDtypeStruct((SIDE, per_peer, tiles, 8, 128), BF16),
        in_specs=[pl.BlockSpec(memory_space=pltpu.SMEM)] + [pl.BlockSpec(memory_space=ANY)] * 8,
        out_specs=pl.BlockSpec(memory_space=VM),
        scratch_shapes=[pltpu.VMEM((8 * rows * tiles, 8, 128), BF16), pltpu.SemaphoreType.DMA((8,))],
        name="select",
    )(asked, *blocks)


def parent_far_body(code, recv, ops_hbm, out, ops, sem):
    copy = pltpu.make_async_copy(ops_hbm, ops.at[pl.ds(0, 40)], sem)
    copy.start()
    ops[40] = jnp.zeros(ops.shape[1:], BF16)
    copy.wait()

    def row(r, carry):
        real = [jnp.zeros((8, 128), F32) for _ in range(4)]
        imag = [jnp.zeros((8, 128), F32) for _ in range(4)]
        for j in range(8):
            both = code[j, r]
            at, op = both >> 6, both & 63
            for t in range(4):
                u, v = t // 2, t % 2
                a = ops[op, 0, u * 8 : u * 8 + 8, v * 128 : v * 128 + 128].astype(F32)
                b = ops[op, 1, u * 8 : u * 8 + 8, v * 128 : v * 128 + 128].astype(F32)
                c = recv[at, t].astype(F32)
                d = recv[at, 4 + t].astype(F32)
                real[t] = real[t] + (a * c - b * d)
                imag[t] = imag[t] + (a * d + b * c)
        for t in range(4):
            out[r, t] = real[t].astype(BF16)
            out[r, 4 + t] = imag[t].astype(BF16)
        return carry

    lax.fori_loop(0, 16, row, 0)


def far_parents(code, recv, ops):
    return pl.pallas_call(
        parent_far_body,
        out_shape=jax.ShapeDtypeStruct((16, 8, 8, 128), BF16),
        in_specs=[
            pl.BlockSpec(memory_space=pltpu.SMEM),
            pl.BlockSpec(memory_space=VM),
            pl.BlockSpec(memory_space=ANY),
        ],
        out_specs=pl.BlockSpec(memory_space=VM),
        scratch_shapes=[pltpu.VMEM((41, 2, 16, PP), BF16), pltpu.SemaphoreType.DMA],
        name="far_parents",
    )(code, recv, ops)


def child_far_body(code, recv, ops_hbm, term, out, ops, sem):
    copy = pltpu.make_async_copy(ops_hbm, ops.at[pl.ds(0, 40)], sem)
    copy.start()
    ops[40] = jnp.zeros(ops.shape[1:], BF16)
    copy.wait()

    def row(r, carry):
        real = jnp.zeros((8, 128), F32)
        imag = jnp.zeros((8, 128), F32)
        for j in range(8):
            both = code[j, r]
            at, op = both >> 6, both & 63
            a, b = ops[op, 0].astype(F32), ops[op, 1].astype(F32)
            c, d = recv[at, 0].astype(F32), recv[at, 1].astype(F32)
            real = real + (a * c - b * d)
            imag = imag + (a * d + b * c)
        out[r, 0] = (real + term[r, 0].astype(F32)).astype(BF16)
        out[r, 1] = (imag + term[r, 1].astype(F32)).astype(BF16)
        return carry

    lax.fori_loop(0, 64, row, 0, unroll=2)


def far_children(code, recv, ops, term):
    return pl.pallas_call(
        child_far_body,
        out_shape=jax.ShapeDtypeStruct((64, 2, 8, 128), BF16),
        in_specs=[
            pl.BlockSpec(memory_space=pltpu.SMEM),
            pl.BlockSpec(memory_space=VM),
            pl.BlockSpec(memory_space=ANY),
            pl.BlockSpec(memory_space=VM),
        ],
        out_specs=pl.BlockSpec(memory_space=VM),
        scratch_shapes=[pltpu.VMEM((41, 2, 8, 128), BF16), pltpu.SemaphoreType.DMA],
        name="far_children",
    )(code, recv, ops, term)


def down_body(far, theta, phi, cos_t, sin_t, out, turned):
    for q in range(2):
        for u in range(PT // 8):
            at = pl.ds(u * 8, 8)
            re, im = (
                jnp.concatenate(
                    [far[u // 2, q, c * 4 + (u % 2) * 2 + v].astype(F32) for v in range(2)], axis=1
                )
                for c in range(2)
            )
            for t, (k, m) in enumerate(((0, 3), (1, 2))):
                cs, sn = cos_t[t, at, :], sin_t[t, at, :]
                cr, si, ci, sr = cs * re, sn * im, cs * im, sn * re
                turned[(q * 4 + k) * 2, at, :] = (cr + si).astype(BF16)
                turned[(q * 4 + k) * 2 + 1, at, :] = (ci - sr).astype(BF16)
                turned[(q * 4 + m) * 2, at, :] = (cr - si).astype(BF16)
                turned[(q * 4 + m) * 2 + 1, at, :] = (ci + sr).astype(BF16)
    for r in range(8):
        for c in range(2):
            narrowed = bmm(turned[r * 2 + c], phi[...]).astype(BF16)
            term = bmm(theta[...], narrowed).astype(BF16)
            for s in range(8):
                out[s, r, c] = term[s * 8 : s * 8 + 8, :]


def lower(far, theta, phi, cos_t, sin_t):
    return pl.pallas_call(
        down_body,
        out_shape=jax.ShapeDtypeStruct((8, 8, 2, 8, 128), BF16),
        in_specs=[pl.BlockSpec(memory_space=VM)] * 5,
        out_specs=pl.BlockSpec(memory_space=VM),
        scratch_shapes=[pltpu.VMEM((16, PT, PP), BF16)],
        name="lower",
    )(far, theta, phi, cos_t, sin_t)


def groups(straight):
    found = []
    for angle in range(8):
        for o in range(SIDE):
            line = [(o, i) if (angle % 2) == straight else (i, o) for i in range(SIDE)]
            found.append([(y * SIDE + z) * 8 + angle for y, z in line])
    return found


SPREAD, TRADE = groups(1), groups(0)


def hop(x, step):
    pairs = [(g[i], g[(i + step) % SIDE]) for g in SPREAD for i in range(SIDE)]
    return lax.ppermute(x, BOTH, pairs)


def swap(x, axis, **kw):
    return lax.all_to_all(x, axis, split_axis=0, concat_axis=0, tiled=True, **kw)


def local(
    child_field,
    child_list,
    child_op,
    child_home,
    child_ops,
    parent_list,
    parent_op,
    parent_home,
    parent_ops,
):
    theta_up = jnp.asarray(fourier_table(PT, CT, 0.5)).astype(BF16)
    phi_up = jnp.asarray(np.ascontiguousarray(fourier_table(PP, SUBBOX_HEADINGS, 0.0).T)).astype(BF16)
    theta_down = jnp.asarray(np.ascontiguousarray(fourier_table(PT, CT, 0.5).T) * np.float32(CT / PT)).astype(BF16)
    phi_down = jnp.asarray(
        fourier_table(PP, SUBBOX_HEADINGS, 0.0) * np.float32(SUBBOX_HEADINGS / PP)
    ).astype(BF16)
    cos_np, sin_np = shift_tables()
    cos_t, sin_t = jnp.asarray(cos_np), jnp.asarray(sin_np)

    box, angle = lax.axis_index("box"), lax.axis_index("angle")
    core = angle % 2
    mine = jnp.where(core == 0, box // SIDE, box % SIDE)
    where = jnp.stack([core, mine]).astype(I32)

    wanted, child_code, parent_code = plan(
        where, child_list, child_op, child_home, parent_list, parent_op, parent_home
    )
    asked = swap(wanted.reshape(SIDE, 1, 128), BOTH, axis_index_groups=TRADE).reshape(SIDE, 128)

    whole = swap(child_field, "angle").reshape(8, 8, 2, 8, 128)
    parents = swap(lift(whole, theta_up, phi_up, cos_t, sin_t), "angle")
    own = jnp.concatenate([child_field.reshape(128, 8, 128), parents.reshape(128, 8, 128)])
    forth, back = [own], [own]
    for step in range(4):
        forth.append(hop(forth[-1], 1))
        if step < 3:
            back.append(hop(back[-1], -1))
    blocks = back + [forth[8 - p] for p in range(4, 8)]

    parents_out = select(asked, blocks, (64, 128), 16, 8, 16)
    children_out = select(asked, blocks, (0, 0), 64, 2, 64)
    parents_in = swap(parents_out, BOTH, axis_index_groups=TRADE)
    children_in = swap(children_out, BOTH, axis_index_groups=TRADE)
    parent_far = far_parents(parent_code, parents_in.reshape(128, 8, 8, 128), parent_ops)
    turned = swap(parent_far, "angle").reshape(8, 2, 8, 8, 128)
    terms = swap(lower(turned, theta_down, phi_down, cos_t, sin_t), "angle")
    return far_children(
        child_code, children_in.reshape(512, 2, 8, 128), child_ops, terms.reshape(64, 2, 8, 128)
    )


def solution(mesh):
    return jax.shard_map(
        local,
        mesh=mesh,
        in_specs=(
            P("box", None, "angle", None),
            P("box", None),
            P("box", None),
            P(),
            P(None, None, "angle", None),
            P("box", None),
            P("box", None),
            P(),
            P(None, None, "angle", None),
        ),
        out_specs=P("box", None, "angle", None),
        check_vma=False,
    )
```

time: 250 us -> 196 us (0.78)
  the two profiles are of different devices: /device:TPU:104 before, /device:TPU:24 now
where the time goes in v1:
time: 196 us; the launch traced here: 195 us
  blocking collectives  86.9 us (44%)
  waiting for transfers between devices  43 us (22%)
  starting transfers between devices  34.2 us (17%)
  Pallas kernels  30 us (15%)
    all_to_all x5, blocking collectives, swap(): lax.all_to_all(x, axis, split_axis=0, concat_axis=0, tiled=True, **kw)  86.9 us
    all_to_all x2, waiting for transfers between devices, swap(): lax.all_to_all(x, axis, split_axis=0, concat_axis=0, tiled=True, **kw)  28.8 us
    ppermute x7, starting transfers between devices, hop(): return lax.ppermute(x, BOTH, pairs)  27.2 us
    ppermute x7, waiting for transfers between devices, hop(): return lax.ppermute(x, BOTH, pairs)  14.2 us
    pallas_call x2, Pallas kernels, select(): pl.pallas_call(functools.partial(select_body, first, rows, tiles), out_sh...  7.99 us
    all_to_all x2, starting transfers between devices, swap(): lax.all_to_all(x, axis, split_axis=0, concat_axis=0, tiled=True, **kw)  7.03 us
    pallas_call x1, Pallas kernels, plan(): pl.pallas_call(plan_body, out_shape=(jax.ShapeDtypeStruct((SIDE, 128), I3...  4.88 us
    pallas_call x1, Pallas kernels, far_children(): pl.pallas_call(child_far_body, out_shape=jax.ShapeDtypeStruct((64, 2, 8,...  4.8 us
  transfers between devices with their start and end apart: 9, of which 5 were waited for; matrix products, arithmetic and copies ran while one was open for 0% of the time, Pallas kernels for 7%

profile of v1, /device:TPU:24, one launch (start us, length us, event | category | flops | bytes accessed | tf_op | source)
XLA Modules:
  0.0 195.2 jit_solution(8944280130338089288)
XLA Ops:
  0.0 0.0 copy-start.8
  0.0 12.0 %all_to_all.35 = bf16[64,2,8,128]{3,2,1,0:T(8,128)(2,1)} all-to-all(bf16[64,2,8,128]{3,2,1,0:T(8,128)(2,1)} %param.15), channel_id=1, replica_groups=mesh['box'=64,'angle'=8] {'angle'}, dimensions={0} | all-to-all | bytes 524288 | tf_op jit(solution)/shard_map/all_to_all | solution.py:326
  12.0 3.4 %lift.1 = bf16[8,2,8,8,128]{4,3,2,1,0:T(8,128)(2,1)} custom-call(bf16[8,8,2,8,128]{4,3,2,1,0:T(8,128)(2,1)} %bitcast.23, bf16[128,64]{1,0:T(8,128)(2,1)} %constant.65.theta, bf16[128,256]{1,0:T(8,128)(2,1)} %constant.66.phi, f32[2,128,256]{2,1,0:T(8,128)} %constant.61.clone.cos_t, f32[2,128,256]{2,1,0:T(8,128)} %constant.62.clone.sin_t), custom_call_target="tpu_custom_call" | custom-call | tf_op jit(solution)/shard_map/lift/pallas_call | solution.py:146
  15.4 10.8 %all_to_all.36 = bf16[8,2,8,8,128]{4,3,2,1,0:T(8,128)(2,1)S(1)} all-to-all(bf16[8,2,8,8,128]{4,3,2,1,0:T(8,128)(2,1)} %lift.1), channel_id=1, replica_groups=mesh['box'=64,'angle'=8] {'angle'}, dimensions={0} | all-to-all | bytes 524288 | tf_op jit(solution)/shard_map/all_to_all | solution.py:326
  26.2 0.0 copy-done.8
  26.3 0.0 copy-start.1
  26.3 4.7 %collective-permute-start.3 = (bf16[256,8,128]{2,1,0:T(8,128)(2,1)S(1)}, bf16[256,8,128]{2,1,0:T(8,128)(2,1)S(1)}, u32[]{:S(2)}, u32[]{:S(2)}) collective-permute-start(bf16[256,8,128]{2,1,0:T(8,128)(2,1)S(1)} %pad_maximum_fusion.refs_0_), channel_id=1, source_target_pairs={{0,64},{64,128},{128,192},{192,256},{256,320},{320,384},{384,448},... | collective-permute-start | bytes 1572872 | tf_op jit(solution)/shard_map/ppermute | solution.py:322
  31.0 1.9 collective-permute-start
  32.9 4.7 %collective-permute-done.3.refs_7_ = bf16[256,8,128]{2,1,0:T(8,128)(2,1)S(1)} collective-permute-done((bf16[256,8,128]{2,1,0:T(8,128)(2,1)S(1)}, bf16[256,8,128]{2,1,0:T(8,128)(2,1)S(1)}, u32[]{:S(2)}, u32[]{:S(2)}) %collective-permute-start.3) | collective-permute-done | bytes 524320 | tf_op jit(solution)/shard_map/ppermute | solution.py:322
  37.7 0.0 copy-start.2
  37.7 5.6 %collective-permute-start.4 = (bf16[256,8,128]{2,1,0:T(8,128)(2,1)S(1)}, bf16[256,8,128]{2,1,0:T(8,128)(2,1)S(1)}, u32[]{:S(2)}, u32[]{:S(2)}) collective-permute-start(bf16[256,8,128]{2,1,0:T(8,128)(2,1)S(1)} %collective-permute-done.3.refs_7_), channel_id=1, source_target_pairs={{0,64},{64,128},{128,192},{192,256},{256,320},{320,384},{384,448},... | collective-permute-start | bytes 1572872 | tf_op jit(solution)/shard_map/ppermute | solution.py:322
  43.3 0.0 collective-permute-done.refs_1_
  43.3 0.0 copy-start.3
  43.3 1.9 collective-permute-start.1
  45.2 4.7 %collective-permute-done.4.refs_6_ = bf16[256,8,128]{2,1,0:T(8,128)(2,1)S(1)} collective-permute-done((bf16[256,8,128]{2,1,0:T(8,128)(2,1)S(1)}, bf16[256,8,128]{2,1,0:T(8,128)(2,1)S(1)}, u32[]{:S(2)}, u32[]{:S(2)}) %collective-permute-start.4) | collective-permute-done | bytes 524320 | tf_op jit(solution)/shard_map/ppermute | solution.py:322
  50.0 0.0 copy-start.4
  50.0 5.6 %collective-permute-start.5 = (bf16[256,8,128]{2,1,0:T(8,128)(2,1)S(1)}, bf16[256,8,128]{2,1,0:T(8,128)(2,1)S(1)}, u32[]{:S(2)}, u32[]{:S(2)}) collective-permute-start(bf16[256,8,128]{2,1,0:T(8,128)(2,1)S(1)} %collective-permute-done.4.refs_6_), channel_id=1, source_target_pairs={{0,64},{64,128},{128,192},{192,256},{256,320},{320,384},{384,448},... | collective-permute-start | bytes 1572872 | tf_op jit(solution)/shard_map/ppermute | solution.py:322
  55.6 0.0 collective-permute-done.1.refs_2_
  55.6 0.0 copy-start.5
  55.6 1.9 collective-permute-start.2
  57.5 4.7 %collective-permute-done.5.refs_5_ = bf16[256,8,128]{2,1,0:T(8,128)(2,1)S(1)} collective-permute-done((bf16[256,8,128]{2,1,0:T(8,128)(2,1)S(1)}, bf16[256,8,128]{2,1,0:T(8,128)(2,1)S(1)}, u32[]{:S(2)}, u32[]{:S(2)}) %collective-permute-start.5) | collective-permute-done | bytes 524320 | tf_op jit(solution)/shard_map/ppermute | solution.py:322
  62.2 0.0 copy-start.6
  62.2 5.6 %collective-permute-start.6 = (bf16[256,8,128]{2,1,0:T(8,128)(2,1)S(1)}, bf16[256,8,128]{2,1,0:T(8,128)(2,1)}, u32[]{:S(2)}, u32[]{:S(2)}) collective-permute-start(bf16[256,8,128]{2,1,0:T(8,128)(2,1)S(1)} %collective-permute-done.5.refs_5_), channel_id=1, source_target_pairs={{0,64},{64,128},{128,192},{192,256},{256,320},{320,384},{384,448},... | collective-permute-start | bytes 1572872 | tf_op jit(solution)/shard_map/ppermute | solution.py:322
  67.9 0.7 pad_add_fusion.where
  68.5 4.9 %plan.1 = (s32[8,128]{1,0:T(8,128)}, s32[8,64]{1,0:T(8,128)}, s32[8,16]{1,0:T(8,128)}) custom-call(s32[2]{0:T(128)} %pad_add_fusion.where, s32[8,64]{1,0:T(8,128)} %bitcast.29, s32[8,64]{1,0:T(8,128)} %bitcast.30, s32[32,128]{1,0:T(8,128)} %bitcast.28, s32[8,16]{1,0:T(8,128)} %bitcast.31, s32[8,16]{1,0:T(8,128)} %bitcast.32, s32[8,128]{1,0:T(8,128)} %bitcast.33), custom_call_target="tpu_custom_call" | custom-call | tf_op jit(solution)/shard_map/plan/pallas_call | solution.py:110
  73.4 18.0 %all_to_all.37 = s32[8,1,128]{2,1,0:T(1,128)} all-to-all(s32[8,1,128]{2,1,0:T(1,128)} %bitcast.34), channel_id=1, replica_groups={{0,8,16,24,32,40,48,56},{64,72,80,88,96,104,112,120},{128,136,144,152,1..., dimensions={0} | all-to-all | bytes 8192 | tf_op jit(solution)/shard_map/all_to_all | solution.py:326
  91.4 0.0 collective-permute-done.2.refs_3_
  91.4 0.0 collective-permute-done.6.refs_4_
  91.5 0.0 copy-done.1
  91.5 0.0 copy-done.2
  91.5 0.0 copy-done.3
  91.5 0.0 copy-done.4
  91.5 0.0 copy-done.5
  91.5 0.0 copy-done.6
  91.5 3.8 %select.11 = bf16[8,16,8,8,128]{4,3,2,1,0:T(8,128)(2,1)} custom-call(s32[8,128]{1,0:T(8,128)} %bitcast.26, bf16[256,8,128]{2,1,0:T(8,128)(2,1)} %copy-done.1, bf16[256,8,128]{2,1,0:T(8,128)(2,1)} %copy-done.3, bf16[256,8,128]{2,1,0:T(8,128)(2,1)} %copy-done.5, bf16[256,8,128]{2,1,0:T(8,128)(2,1)} %collective-permute-done.2.refs_3_, ...), custom_call_target="tpu_custom_call" | custom-call | tf_op jit(solution)/shard_map/select/pallas_call | solution.py:180
  95.3 34.5 %all_to_all.38 = bf16[8,16,8,8,128]{4,3,2,1,0:T(8,128)(2,1)} all-to-all(bf16[8,16,8,8,128]{4,3,2,1,0:T(8,128)(2,1)} %select.11), channel_id=1, replica_groups={{0,8,16,24,32,40,48,56},{64,72,80,88,96,104,112,120},{128,136,144,152,1..., dimensions={0} | all-to-all | bytes 4194304 | tf_op jit(solution)/shard_map/all_to_all | solution.py:326
  129.8 4.4 %far_parents.1 = bf16[16,8,8,128]{3,2,1,0:T(8,128)(2,1)} custom-call(s32[8,16]{1,0:T(8,128)} %get-tuple-element.10.code, bf16[128,8,8,128]{3,2,1,0:T(8,128)(2,1)} %bitcast.20, bf16[40,2,16,256]{3,2,1,0:T(8,128)(2,1)} %ops_hbm.2), custom_call_target="tpu_custom_call" | custom-call | tf_op jit(solution)/shard_map/far_parents/pallas_call | solution.py:219
  134.1 3.4 %all-to-all-start.5 = ((bf16[16,8,8,128]{3,2,1,0:T(8,128)(2,1)}), bf16[16,8,8,128]{3,2,1,0:T(8,128)(2,1)S(1)}, u32[]{:S(2)}, u32[]{:S(2)}) async-start(bf16[16,8,8,128]{3,2,1,0:T(8,128)(2,1)} %far_parents.1), calls=%async_computation.5 | async-start | bytes 524288 | tf_op jit(solution)/shard_map/all_to_all | solution.py:326
  137.6 4.2 %select.10 = bf16[8,64,2,8,128]{4,3,2,1,0:T(8,128)(2,1)} custom-call(s32[8,128]{1,0:T(8,128)} %bitcast.27, bf16[256,8,128]{2,1,0:T(8,128)(2,1)} %copy-done.1, bf16[256,8,128]{2,1,0:T(8,128)(2,1)} %copy-done.3, bf16[256,8,128]{2,1,0:T(8,128)(2,1)} %copy-done.5, bf16[256,8,128]{2,1,0:T(8,128)(2,1)} %collective-permute-done.2.refs_3_, ...), custom_call_target="tpu_custom_call" | custom-call | tf_op jit(solution)/shard_map/select/pallas_call | solution.py:180
  141.8 3.2 %all-to-all-done.5 = bf16[16,8,8,128]{3,2,1,0:T(8,128)(2,1)S(1)} async-done(((bf16[16,8,8,128]{3,2,1,0:T(8,128)(2,1)}), bf16[16,8,8,128]{3,2,1,0:T(8,128)(2,1)S(1)}, u32[]{:S(2)}, u32[]{:S(2)}) %all-to-all-start.5) | async-done | bytes 262176 | tf_op jit(solution)/shard_map/all_to_all | solution.py:326
  145.0 0.0 copy-start.7
  145.0 3.6 %all-to-all-start.3 = ((bf16[8,64,2,8,128]{4,3,2,1,0:T(8,128)(2,1)}), bf16[8,64,2,8,128]{4,3,2,1,0:T(8,128)(2,1)S(1)}, u32[]{:S(2)}, u32[]{:S(2)}) async-start(bf16[8,64,2,8,128]{4,3,2,1,0:T(8,128)(2,1)} %select.10), calls=%async_computation.3 | async-start | bytes 4194304 | tf_op jit(solution)/shard_map/all_to_all | solution.py:326
  148.6 0.0 copy-done.7
  148.6 4.6 %lower.1 = bf16[8,8,2,8,128]{4,3,2,1,0:T(8,128)(2,1)} custom-call(bf16[8,2,8,8,128]{4,3,2,1,0:T(8,128)(2,1)} %bitcast.21, bf16[64,128]{1,0:T(8,128)(2,1)} %constant.67.theta, bf16[256,128]{1,0:T(8,128)(2,1)} %constant.68.phi, f32[2,128,256]{2,1,0:T(8,128)} %constant.61.clone.cos_t, f32[2,128,256]{2,1,0:T(8,128)} %constant.62.clone.sin_t), custom_call_target="tpu_custom_call" | custom-call | tf_op jit(solution)/shard_map/lower/pallas_call | solution.py:298
  153.2 25.6 %all-to-all-done.3 = bf16[8,64,2,8,128]{4,3,2,1,0:T(8,128)(2,1)S(1)} async-done(((bf16[8,64,2,8,128]{4,3,2,1,0:T(8,128)(2,1)}), bf16[8,64,2,8,128]{4,3,2,1,0:T(8,128)(2,1)S(1)}, u32[]{:S(2)}, u32[]{:S(2)}) %all-to-all-start.3) | async-done | bytes 2097184 | tf_op jit(solution)/shard_map/all_to_all | solution.py:326
  178.8 0.0 copy-start
  178.8 11.5 %all_to_all.39 = bf16[8,8,2,8,128]{4,3,2,1,0:T(8,128)(2,1)} all-to-all(bf16[8,8,2,8,128]{4,3,2,1,0:T(8,128)(2,1)} %lower.1), channel_id=1, replica_groups=mesh['box'=64,'angle'=8] {'angle'}, dimensions={0} | all-to-all | bytes 524288 | tf_op jit(solution)/shard_map/all_to_all | solution.py:326
  190.4 0.0 copy-done
  190.4 4.8 %far_children.1 = bf16[64,2,8,128]{3,2,1,0:T(8,128)(2,1)} custom-call(s32[8,64]{1,0:T(8,128)} %get-tuple-element.8.code, bf16[512,2,8,128]{3,2,1,0:T(8,128)(2,1)} %bitcast.19, bf16[40,2,8,128]{3,2,1,0:T(8,128)(2,1)} %ops_hbm.3, bf16[64,2,8,128]{3,2,1,0:T(8,128)(2,1)} %bitcast.25), custom_call_target="tpu_custom_call" | custom-call | tf_op jit(solution)/shard_map/far_children/pallas_call | solution.py:257
  (1 shorter events, 0.0 us)
Async XLA Ops:
  0.0 26.2 %copy-start.8 = (bf16[64,2,8,128]{3,2,1,0:T(8,128)(2,1)S(1)}, bf16[64,2,8,128]{3,2,1,0:T(8,128)(2,1)}, u32[]{:S(2)}) copy-start(bf16[64,2,8,128]{3,2,1,0:T(8,128)(2,1)} %param.15) | copy-start | bytes 786436
  26.3 65.2 %copy-start.1 = (bf16[256,8,128]{2,1,0:T(8,128)(2,1)}, bf16[256,8,128]{2,1,0:T(8,128)(2,1)S(1)}, u32[]{:S(2)}) copy-start(bf16[256,8,128]{2,1,0:T(8,128)(2,1)S(1)} %pad_maximum_fusion.refs_0_) | copy-start | bytes 1572868
  26.3 11.4 %collective-permute-start.3 = (bf16[256,8,128]{2,1,0:T(8,128)(2,1)S(1)}, bf16[256,8,128]{2,1,0:T(8,128)(2,1)S(1)}, u32[]{:S(2)}, u32[]{:S(2)}) collective-permute-start(bf16[256,8,128]{2,1,0:T(8,128)(2,1)S(1)} %pad_maximum_fusion.refs_0_), channel_id=1, source_target_pairs={{0,64},{64,128},{128,192},{192,256},{256,320},{320,384},{384,448},... | collective-permute-start | bytes 1572872 | tf_op jit(solution)/shard_map/ppermute | solution.py:322
  31.0 12.3 %collective-permute-start = (bf16[256,8,128]{2,1,0:T(8,128)(2,1)S(1)}, bf16[256,8,128]{2,1,0:T(8,128)(2,1)S(1)}, u32[]{:S(2)}, u32[]{:S(2)}) collective-permute-start(bf16[256,8,128]{2,1,0:T(8,128)(2,1)S(1)} %pad_maximum_fusion.refs_0_), channel_id=1, source_target_pairs={{0,448},{64,0},{128,64},{192,128},{256,192},{320,256},{384,320},{4... | collective-permute-start | bytes 1572872 | tf_op jit(solution)/shard_map/ppermute | solution.py:322
  37.7 53.8 %copy-start.2 = (bf16[256,8,128]{2,1,0:T(8,128)(2,1)}, bf16[256,8,128]{2,1,0:T(8,128)(2,1)S(1)}, u32[]{:S(2)}) copy-start(bf16[256,8,128]{2,1,0:T(8,128)(2,1)S(1)} %collective-permute-done.3.refs_7_) | copy-start | bytes 1572868
  37.7 12.3 %collective-permute-start.4 = (bf16[256,8,128]{2,1,0:T(8,128)(2,1)S(1)}, bf16[256,8,128]{2,1,0:T(8,128)(2,1)S(1)}, u32[]{:S(2)}, u32[]{:S(2)}) collective-permute-start(bf16[256,8,128]{2,1,0:T(8,128)(2,1)S(1)} %collective-permute-done.3.refs_7_), channel_id=1, source_target_pairs={{0,64},{64,128},{128,192},{192,256},{256,320},{320,384},{384,448},... | collective-permute-start | bytes 1572872 | tf_op jit(solution)/shard_map/ppermute | solution.py:322
  43.3 48.2 %copy-start.3 = (bf16[256,8,128]{2,1,0:T(8,128)(2,1)}, bf16[256,8,128]{2,1,0:T(8,128)(2,1)S(1)}, u32[]{:S(2)}) copy-start(bf16[256,8,128]{2,1,0:T(8,128)(2,1)S(1)} %collective-permute-done.refs_1_) | copy-start | bytes 1572868
  43.3 12.3 %collective-permute-start.1 = (bf16[256,8,128]{2,1,0:T(8,128)(2,1)S(1)}, bf16[256,8,128]{2,1,0:T(8,128)(2,1)S(1)}, u32[]{:S(2)}, u32[]{:S(2)}) collective-permute-start(bf16[256,8,128]{2,1,0:T(8,128)(2,1)S(1)} %collective-permute-done.refs_1_), channel_id=1, source_target_pairs={{0,448},{64,0},{128,64},{192,128},{256,192},{320,256},{384,320},{4... | collective-permute-start | bytes 1572872 | tf_op jit(solution)/shard_map/ppermute | solution.py:322
  50.0 41.5 %copy-start.4 = (bf16[256,8,128]{2,1,0:T(8,128)(2,1)}, bf16[256,8,128]{2,1,0:T(8,128)(2,1)S(1)}, u32[]{:S(2)}) copy-start(bf16[256,8,128]{2,1,0:T(8,128)(2,1)S(1)} %collective-permute-done.4.refs_6_) | copy-start | bytes 1572868
  50.0 12.3 %collective-permute-start.5 = (bf16[256,8,128]{2,1,0:T(8,128)(2,1)S(1)}, bf16[256,8,128]{2,1,0:T(8,128)(2,1)S(1)}, u32[]{:S(2)}, u32[]{:S(2)}) collective-permute-start(bf16[256,8,128]{2,1,0:T(8,128)(2,1)S(1)} %collective-permute-done.4.refs_6_), channel_id=1, source_target_pairs={{0,64},{64,128},{128,192},{192,256},{256,320},{320,384},{384,448},... | collective-permute-start | bytes 1572872 | tf_op jit(solution)/shard_map/ppermute | solution.py:322
  55.6 35.9 %copy-start.5 = (bf16[256,8,128]{2,1,0:T(8,128)(2,1)}, bf16[256,8,128]{2,1,0:T(8,128)(2,1)S(1)}, u32[]{:S(2)}) copy-start(bf16[256,8,128]{2,1,0:T(8,128)(2,1)S(1)} %collective-permute-done.1.refs_2_) | copy-start | bytes 1572868
  55.6 35.9 %collective-permute-start.2 = (bf16[256,8,128]{2,1,0:T(8,128)(2,1)S(1)}, bf16[256,8,128]{2,1,0:T(8,128)(2,1)}, u32[]{:S(2)}, u32[]{:S(2)}) collective-permute-start(bf16[256,8,128]{2,1,0:T(8,128)(2,1)S(1)} %collective-permute-done.1.refs_2_), channel_id=1, source_target_pairs={{0,448},{64,0},{128,64},{192,128},{256,192},{320,256},{384,320},{4... | collective-permute-start | bytes 1572872 | tf_op jit(solution)/shard_map/ppermute | solution.py:322
  62.2 29.3 %copy-start.6 = (bf16[256,8,128]{2,1,0:T(8,128)(2,1)}, bf16[256,8,128]{2,1,0:T(8,128)(2,1)S(1)}, u32[]{:S(2)}) copy-start(bf16[256,8,128]{2,1,0:T(8,128)(2,1)S(1)} %collective-permute-done.5.refs_5_) | copy-start | bytes 1572868
  62.2 29.2 %collective-permute-start.6 = (bf16[256,8,128]{2,1,0:T(8,128)(2,1)S(1)}, bf16[256,8,128]{2,1,0:T(8,128)(2,1)}, u32[]{:S(2)}, u32[]{:S(2)}) collective-permute-start(bf16[256,8,128]{2,1,0:T(8,128)(2,1)S(1)} %collective-permute-done.5.refs_5_), channel_id=1, source_target_pairs={{0,64},{64,128},{128,192},{192,256},{256,320},{320,384},{384,448},... | collective-permute-start | bytes 1572872 | tf_op jit(solution)/shard_map/ppermute | solution.py:322
  134.1 10.9 %all-to-all-start.5 = ((bf16[16,8,8,128]{3,2,1,0:T(8,128)(2,1)}), bf16[16,8,8,128]{3,2,1,0:T(8,128)(2,1)S(1)}, u32[]{:S(2)}, u32[]{:S(2)}) async-start(bf16[16,8,8,128]{3,2,1,0:T(8,128)(2,1)} %far_parents.1), calls=%async_computation.5 | async-start | bytes 524288 | tf_op jit(solution)/shard_map/all_to_all | solution.py:326
  145.0 3.6 %copy-start.7 = (bf16[16,8,8,128]{3,2,1,0:T(8,128)(2,1)}, bf16[16,8,8,128]{3,2,1,0:T(8,128)(2,1)S(1)}, u32[]{:S(2)}) copy-start(bf16[16,8,8,128]{3,2,1,0:T(8,128)(2,1)S(1)} %all-to-all-done.5) | copy-start | bytes 786436
  145.0 33.8 %all-to-all-start.3 = ((bf16[8,64,2,8,128]{4,3,2,1,0:T(8,128)(2,1)}), bf16[8,64,2,8,128]{4,3,2,1,0:T(8,128)(2,1)S(1)}, u32[]{:S(2)}, u32[]{:S(2)}) async-start(bf16[8,64,2,8,128]{4,3,2,1,0:T(8,128)(2,1)} %select.10), calls=%async_computation.3 | async-start | bytes 4194304 | tf_op jit(solution)/shard_map/all_to_all | solution.py:326
  178.8 11.5 %copy-start = (bf16[8,64,2,8,128]{4,3,2,1,0:T(8,128)(2,1)}, bf16[8,64,2,8,128]{4,3,2,1,0:T(8,128)(2,1)S(1)}, u32[]{:S(2)}) copy-start(bf16[8,64,2,8,128]{4,3,2,1,0:T(8,128)(2,1)S(1)} %all-to-all-done.3) | copy-start | bytes 6291460

commit v2 on v1

--- a/solution.py
+++ b/solution.py
@@ -20,6 +20,7 @@
 F32, BF16, I32 = jnp.float32, jnp.bfloat16, jnp.int32
 VM = pltpu.VMEM
 ANY = pl.ANY
+GRANT = 12 << 20
 
 
 def fourier_table(fine_count, coarse_count, offset):
@@ -116,6 +117,7 @@
         ),
         in_specs=[pl.BlockSpec(memory_space=pltpu.SMEM)] + [pl.BlockSpec(memory_space=VM)] * 6,
         out_specs=(pl.BlockSpec(memory_space=VM),) * 3,
+        compiler_params=pltpu.CompilerParams(vmem_limit_bytes=GRANT),
         name="plan",
     )(*args)
 
@@ -149,6 +151,7 @@
         in_specs=[pl.BlockSpec(memory_space=VM)] * 5,
         out_specs=pl.BlockSpec(memory_space=VM),
         scratch_shapes=[pltpu.VMEM((16, PT, PP), F32)],
+        compiler_params=pltpu.CompilerParams(vmem_limit_bytes=GRANT),
         name="lift",
     )(field, theta, phi, cos_t, sin_t)
 
@@ -183,104 +186,139 @@
         in_specs=[pl.BlockSpec(memory_space=pltpu.SMEM)] + [pl.BlockSpec(memory_space=ANY)] * 8,
         out_specs=pl.BlockSpec(memory_space=VM),
         scratch_shapes=[pltpu.VMEM((8 * rows * tiles, 8, 128), BF16), pltpu.SemaphoreType.DMA((8,))],
+        compiler_params=pltpu.CompilerParams(vmem_limit_bytes=GRANT),
         name="select",
     )(asked, *blocks)
 
 
-def parent_far_body(code, recv, ops_hbm, out, ops, sem):
+def parent_far_body(angle, code, recv, ops_hbm, keep, send, ops, sem):
     copy = pltpu.make_async_copy(ops_hbm, ops.at[pl.ds(0, 40)], sem)
     copy.start()
     ops[40] = jnp.zeros(ops.shape[1:], BF16)
     copy.wait()
 
-    def row(r, carry):
-        real = [jnp.zeros((8, 128), F32) for _ in range(4)]
-        imag = [jnp.zeros((8, 128), F32) for _ in range(4)]
-        for j in range(8):
-            both = code[j, r]
-            at, op = both >> 6, both & 63
-            for t in range(4):
-                u, v = t // 2, t % 2
-                a = ops[op, 0, u * 8 : u * 8 + 8, v * 128 : v * 128 + 128].astype(F32)
-                b = ops[op, 1, u * 8 : u * 8 + 8, v * 128 : v * 128 + 128].astype(F32)
-                c = recv[at, t].astype(F32)
-                d = recv[at, 4 + t].astype(F32)
-                real[t] = real[t] + (a * c - b * d)
-                imag[t] = imag[t] + (a * d + b * c)
-        for t in range(4):
-            out[r, t] = real[t].astype(BF16)
-            out[r, 4 + t] = imag[t].astype(BF16)
+    def pair(i, carry):
+        for odd, out in enumerate((keep, send)):
+            for q in range(2):
+                r = (angle[0] ^ (2 * i + odd)) * 2 + q
+                real = [jnp.zeros((8, 128), F32) for _ in range(4)]
+                imag = [jnp.zeros((8, 128), F32) for _ in range(4)]
+                for j in range(8):
+                    both = code[j, r]
+                    at, op = both >> 6, both & 63
+                    for t in range(4):
+                        u, v = t // 2, t % 2
+                        a = ops[op, 0, u * 8 : u * 8 + 8, v * 128 : v * 128 + 128].astype(F32)
+                        b = ops[op, 1, u * 8 : u * 8 + 8, v * 128 : v * 128 + 128].astype(F32)
+                        c = recv[at, t].astype(F32)
+                        d = recv[at, 4 + t].astype(F32)
+                        real[t] = real[t] + (a * c - b * d)
+                        imag[t] = imag[t] + (a * d + b * c)
+                for t in range(4):
+                    out[i, q, t] = real[t].astype(BF16)
+                    out[i, q, 4 + t] = imag[t].astype(BF16)
         return carry
 
-    lax.fori_loop(0, 16, row, 0)
-
-
-def far_parents(code, recv, ops):
+    lax.fori_loop(0, 4, pair, 0)
+
+
+def far_parents(angle, code, recv, ops):
     return pl.pallas_call(
         parent_far_body,
-        out_shape=jax.ShapeDtypeStruct((16, 8, 8, 128), BF16),
+        out_shape=(jax.ShapeDtypeStruct((4, 2, 8, 8, 128), BF16),) * 2,
         in_specs=[
+            pl.BlockSpec(memory_space=pltpu.SMEM),
             pl.BlockSpec(memory_space=pltpu.SMEM),
             pl.BlockSpec(memory_space=VM),
             pl.BlockSpec(memory_space=ANY),
         ],
-        out_specs=pl.BlockSpec(memory_space=VM),
+        out_specs=(pl.BlockSpec(memory_space=VM),) * 2,
         scratch_shapes=[pltpu.VMEM((41, 2, 16, PP), BF16), pltpu.SemaphoreType.DMA],
+        cost_estimate=pl.CostEstimate(flops=10_000_000, bytes_accessed=3_500_000, transcendentals=0),
+        compiler_params=pltpu.CompilerParams(vmem_limit_bytes=GRANT),
         name="far_parents",
-    )(code, recv, ops)
-
-
-def child_far_body(code, recv, ops_hbm, term, out, ops, sem):
+    )(angle, code, recv, ops)
+
+
+CUBE = ((0, 0), (1, 0), (2, 0), (2, 2), (3, 0), (3, 1), (3, 2), (3, 3))
+
+
+def cube(keep, send):
+    def across(x, bit):
+        return lax.ppermute(x, "angle", [(i, i ^ bit) for i in range(8)])
+
+    first = across(send, 1)
+    second = across(jnp.concatenate([keep[1:2], keep[3:4], first[1:2], first[3:4]]), 2)
+    third = across(jnp.concatenate([keep[2:3], first[2:3], second[1:2], second[3:4]]), 4)
+    return keep, first, second, third
+
+
+def child_far_body(angle, code, recv, ops_hbm, t0, t1, t2, t3, out, ops, sem):
     copy = pltpu.make_async_copy(ops_hbm, ops.at[pl.ds(0, 40)], sem)
     copy.start()
     ops[40] = jnp.zeros(ops.shape[1:], BF16)
     copy.wait()
-
-    def row(r, carry):
-        real = jnp.zeros((8, 128), F32)
-        imag = jnp.zeros((8, 128), F32)
-        for j in range(8):
-            both = code[j, r]
-            at, op = both >> 6, both & 63
-            a, b = ops[op, 0].astype(F32), ops[op, 1].astype(F32)
-            c, d = recv[at, 0].astype(F32), recv[at, 1].astype(F32)
-            real = real + (a * c - b * d)
-            imag = imag + (a * d + b * c)
-        out[r, 0] = (real + term[r, 0].astype(F32)).astype(BF16)
-        out[r, 1] = (imag + term[r, 1].astype(F32)).astype(BF16)
-        return carry
-
-    lax.fori_loop(0, 64, row, 0, unroll=2)
-
-
-def far_children(code, recv, ops, term):
+    terms = (t0, t1, t2, t3)
+
+    for s, (which, place) in enumerate(CUBE):
+
+        def row(k, carry):
+            r = (angle[0] ^ s) * 8 + k
+            real = jnp.zeros((8, 128), F32)
+            imag = jnp.zeros((8, 128), F32)
+            for j in range(8):
+                both = code[j, r]
+                at, op = both >> 6, both & 63
+                a, b = ops[op, 0].astype(F32), ops[op, 1].astype(F32)
+                c, d = recv[at, 0].astype(F32), recv[at, 1].astype(F32)
+                real = real + (a * c - b * d)
+                imag = imag + (a * d + b * c)
+            out[r, 0] = (real + terms[which][place, k, 0].astype(F32)).astype(BF16)
+            out[r, 1] = (imag + terms[which][place, k, 1].astype(F32)).astype(BF16)
+            return carry
+
+        lax.fori_loop(0, 8, row, 0, unroll=2)
+
+
+def far_children(angle, code, recv, ops, terms):
     return pl.pallas_call(
         child_far_body,
         out_shape=jax.ShapeDtypeStruct((64, 2, 8, 128), BF16),
         in_specs=[
             pl.BlockSpec(memory_space=pltpu.SMEM),
+            pl.BlockSpec(memory_space=pltpu.SMEM),
             pl.BlockSpec(memory_space=VM),
             pl.BlockSpec(memory_space=ANY),
-            pl.BlockSpec(memory_space=VM),
-        ],
+        ]
+        + [pl.BlockSpec(memory_space=VM)] * 4,
         out_specs=pl.BlockSpec(memory_space=VM),
         scratch_shapes=[pltpu.VMEM((41, 2, 8, 128), BF16), pltpu.SemaphoreType.DMA],
+        compiler_params=pltpu.CompilerParams(vmem_limit_bytes=GRANT),
         name="far_children",
-    )(code, recv, ops, term)
-
-
-def down_body(far, theta, phi, cos_t, sin_t, out, turned):
-    for q in range(2):
-        for u in range(PT // 8):
-            at = pl.ds(u * 8, 8)
+    )(angle, code, recv, ops, *terms)
+
+
+def down_body(angle, f0, f1, f2, f3, theta, phi, cos_t, sin_t, keep, send, turned, whole):
+    far = (f0, f1, f2, f3)
+    for s, (which, place) in enumerate(CUBE):
+        at = pl.ds(pl.multiple_of((angle[0] ^ s) * 16, 16), 16)
+        cos_s = [cos_t[t, at, :] for t in range(2)]
+        sin_s = [sin_t[t, at, :] for t in range(2)]
+        for q in range(2):
             re, im = (
                 jnp.concatenate(
-                    [far[u // 2, q, c * 4 + (u % 2) * 2 + v].astype(F32) for v in range(2)], axis=1
+                    [
+                        jnp.concatenate(
+                            [far[which][place, q, c * 4 + u * 2 + v].astype(F32) for v in range(2)], axis=1
+                        )
+                        for u in range(2)
+                    ],
+                    axis=0,
                 )
                 for c in range(2)
             )
             for t, (k, m) in enumerate(((0, 3), (1, 2))):
-                cs, sn = cos_t[t, at, :], sin_t[t, at, :]
+                cs, sn = cos_s[t], sin_s[t]
                 cr, si, ci, sr = cs * re, sn * im, cs * im, sn * re
                 turned[(q * 4 + k) * 2, at, :] = (cr + si).astype(BF16)
                 turned[(q * 4 + k) * 2 + 1, at, :] = (ci - sr).astype(BF16)
@@ -289,20 +327,25 @@
     for r in range(8):
         for c in range(2):
             narrowed = bmm(turned[r * 2 + c], phi[...]).astype(BF16)
-            term = bmm(theta[...], narrowed).astype(BF16)
-            for s in range(8):
-                out[s, r, c] = term[s * 8 : s * 8 + 8, :]
-
-
-def lower(far, theta, phi, cos_t, sin_t):
+            whole[r * 2 + c] = bmm(theta[...], narrowed)
+    for s in range(8):
+        at = pl.ds(pl.multiple_of((angle[0] ^ s) * 8, 8), 8)
+        for r in range(8):
+            for c in range(2):
+                (keep, send)[s % 2][s // 2, r, c] = whole[r * 2 + c, at, :].astype(BF16)
+
+
+def lower(angle, far, theta, phi, cos_t, sin_t):
     return pl.pallas_call(
         down_body,
-        out_shape=jax.ShapeDtypeStruct((8, 8, 2, 8, 128), BF16),
-        in_specs=[pl.BlockSpec(memory_space=VM)] * 5,
-        out_specs=pl.BlockSpec(memory_space=VM),
-        scratch_shapes=[pltpu.VMEM((16, PT, PP), BF16)],
+        out_shape=(jax.ShapeDtypeStruct((4, 8, 2, 8, 128), BF16),) * 2,
+        in_specs=[pl.BlockSpec(memory_space=pltpu.SMEM)] + [pl.BlockSpec(memory_space=VM)] * 8,
+        out_specs=(pl.BlockSpec(memory_space=VM),) * 2,
+        scratch_shapes=[pltpu.VMEM((16, PT, PP), BF16), pltpu.VMEM((16, CT, SUBBOX_HEADINGS), F32)],
+        cost_estimate=pl.CostEstimate(flops=300_000_000, bytes_accessed=2_000_000, transcendentals=0),
+        compiler_params=pltpu.CompilerParams(vmem_limit_bytes=GRANT),
         name="lower",
-    )(far, theta, phi, cos_t, sin_t)
+    )(angle, *far, theta, phi, cos_t, sin_t)
 
 
 def groups(straight):
@@ -354,28 +397,27 @@
     wanted, child_code, parent_code = plan(
         where, child_list, child_op, child_home, parent_list, parent_op, parent_home
     )
-    asked = swap(wanted.reshape(SIDE, 1, 128), BOTH, axis_index_groups=TRADE).reshape(SIDE, 128)
-
     whole = swap(child_field, "angle").reshape(8, 8, 2, 8, 128)
     parents = swap(lift(whole, theta_up, phi_up, cos_t, sin_t), "angle")
     own = jnp.concatenate([child_field.reshape(128, 8, 128), parents.reshape(128, 8, 128)])
     forth, back = [own], [own]
     for step in range(4):
+        if step == 1:
+            forth[1], wanted = lax.optimization_barrier((forth[1], wanted))
         forth.append(hop(forth[-1], 1))
         if step < 3:
             back.append(hop(back[-1], -1))
+    asked = swap(wanted.reshape(SIDE, 1, 128), BOTH, axis_index_groups=TRADE).reshape(SIDE, 128)
     blocks = back + [forth[8 - p] for p in range(4, 8)]
 
     parents_out = select(asked, blocks, (64, 128), 16, 8, 16)
     children_out = select(asked, blocks, (0, 0), 64, 2, 64)
     parents_in = swap(parents_out, BOTH, axis_index_groups=TRADE)
     children_in = swap(children_out, BOTH, axis_index_groups=TRADE)
-    parent_far = far_parents(parent_code, parents_in.reshape(128, 8, 8, 128), parent_ops)
-    turned = swap(parent_far, "angle").reshape(8, 2, 8, 8, 128)
-    terms = swap(lower(turned, theta_down, phi_down, cos_t, sin_t), "angle")
-    return far_children(
-        child_code, children_in.reshape(512, 2, 8, 128), child_ops, terms.reshape(64, 2, 8, 128)
-    )
+    here = angle.reshape(1).astype(I32)
+    far = cube(*far_parents(here, parent_code, parents_in.reshape(128, 8, 8, 128), parent_ops))
+    terms = cube(*lower(here, far, theta_down, phi_down, cos_t, sin_t))
+    return far_children(here, child_code, children_in.reshape(512, 2, 8, 128), child_ops, terms)
 
 
 def solution(mesh):

time: 196 us -> 182 us (0.929)
  blocking collectives: 86.9 us -> 39.7 us
  local copies, waits for them, and re-layouts: 0.03 us -> 20.2 us
  starting transfers between devices: 34.2 us -> 49.1 us
  Pallas kernels: 30 us -> 15.9 us
  waiting for transfers between devices: 43 us -> 54.9 us
    all_to_all x5 -> x3, blocking collectives: 86.9 us -> 39.7 us  [swap(): lax.all_to_all(x, axis, split_axis=0, concat_axis=0, tiled=True, **kw)]
    ppermute x0 -> x6, waiting for transfers between devices: none -> 23.6 us  [across(): return lax.ppermute(x, 'angle', [(i, i ^ bit) for i in range(8)])]
    unnamed x18 -> x66, local copies, waits for them, and re-layouts: 0.03 us -> 20.2 us
    ppermute x0 -> x6, starting transfers between devices: none -> 14.5 us  [across(): return lax.ppermute(x, 'angle', [(i, i ^ bit) for i in range(8)])]
    all_to_all x2, waiting for transfers between devices: 28.8 us -> 21.2 us  [swap(): lax.all_to_all(x, axis, split_axis=0, concat_axis=0, tiled=True, **kw)]
    pallas_call x2, Pallas kernels: 7.99 us -> 2.42 us  [select(): pl.pallas_call(functools.partial(select_body, first, rows, tiles), out_sh...]
    pallas_call x2, Pallas kernels: 8.98 us -> 4.75 us  [the longest x1 3.02 us: lower(): pl.pallas_call(down_body, out_shape=(jax.ShapeDtypeStruct((4, 8, 2, 8, 12...]
    ppermute x7, waiting for transfers between devices: 14.2 us -> 10.1 us  [hop(): return lax.ppermute(x, BOTH, pairs)]
  transfers between devices with their start and end apart: 9 -> 15, of which waited for: 5 -> 12; matrix products, arithmetic and copies ran while one was open for 0% -> 0% of each run, Pallas kernels for 7% -> 6%
where the time goes in v2:
time: 182 us; the launch traced here: 180 us
  waiting for transfers between devices  54.9 us (30%)
  starting transfers between devices  49.1 us (27%)
  blocking collectives  39.7 us (22%)
  local copies, waits for them, and re-layouts  20.2 us (11%)
  Pallas kernels  15.9 us (9%)
    all_to_all x3, blocking collectives, swap(): lax.all_to_all(x, axis, split_axis=0, concat_axis=0, tiled=True, **kw)  39.7 us
    ppermute x7, starting transfers between devices, hop(): return lax.ppermute(x, BOTH, pairs)  27.2 us
    ppermute x6, waiting for transfers between devices, across(): return lax.ppermute(x, 'angle', [(i, i ^ bit) for i in range(8)])  23.6 us
    all_to_all x2, waiting for transfers between devices, swap(): lax.all_to_all(x, axis, split_axis=0, concat_axis=0, tiled=True, **kw)  21.2 us
    unnamed x66, local copies, waits for them, and re-layouts  20.2 us
    ppermute x6, starting transfers between devices, across(): return lax.ppermute(x, 'angle', [(i, i ^ bit) for i in range(8)])  14.5 us
    ppermute x7, waiting for transfers between devices, hop(): return lax.ppermute(x, BOTH, pairs)  10.1 us
    all_to_all x2, starting transfers between devices, swap(): lax.all_to_all(x, axis, split_axis=0, concat_axis=0, tiled=True, **kw)  7.35 us
  transfers between devices with their start and end apart: 15, of which 12 were waited for; matrix products, arithmetic and copies ran while one was open for 0% of the time, Pallas kernels for 6%

profile of v2, /device:TPU:24, one launch (start us, length us, event | category | flops | bytes accessed | tf_op | source)
XLA Modules:
  0.0 180.4 jit_solution(10148416621828899752)
XLA Ops:
  0.0 0.0 copy-start.29
  0.0 0.0 copy-start.26
  0.0 11.9 %all_to_all.25 = bf16[64,2,8,128]{3,2,1,0:T(8,128)(2,1)S(1)} all-to-all(bf16[64,2,8,128]{3,2,1,0:T(8,128)(2,1)} %param.15), channel_id=1, replica_groups=mesh['box'=64,'angle'=8] {'angle'}, dimensions={0} | all-to-all | bytes 524288 | tf_op jit(solution)/shard_map/all_to_all | solution.py:369
  12.0 0.9 copy-done.16
  12.9 0.9 copy-done.18
  13.9 0.8 copy-done.23
  14.7 0.8 copy-done.24
  15.5 1.5 lift.1
  17.0 9.9 %all_to_all.26 = bf16[8,2,8,8,128]{4,3,2,1,0:T(8,128)(2,1)S(1)} all-to-all(bf16[8,2,8,8,128]{4,3,2,1,0:T(8,128)(2,1)S(1)} %lift.1), channel_id=1, replica_groups=mesh['box'=64,'angle'=8] {'angle'}, dimensions={0} | all-to-all | bytes 524288 | tf_op jit(solution)/shard_map/all_to_all | solution.py:369
  27.0 4.7 %collective-permute-start = (bf16[256,8,128]{2,1,0:T(8,128)(2,1)S(1)}, bf16[256,8,128]{2,1,0:T(8,128)(2,1)S(1)}, u32[]{:S(2)}, u32[]{:S(2)}) collective-permute-start(bf16[256,8,128]{2,1,0:T(8,128)(2,1)S(1)} %pad_maximum_fusion.refs_0_), channel_id=1, source_target_pairs={{0,64},{64,128},{128,192},{192,256},{256,320},{320,384},{384,448},... | collective-permute-start | bytes 1572872 | tf_op jit(solution)/shard_map/ppermute | solution.py:365
  31.7 0.1 pad_add_fusion.where
  31.8 4.0 %plan.1 = (s32[8,128]{1,0:T(8,128)S(1)}, s32[8,64]{1,0:T(8,128)S(1)}, s32[8,16]{1,0:T(8,128)S(1)}) custom-call(s32[2]{0:T(128)S(1)} %pad_add_fusion.where, s32[8,64]{1,0:T(8,128)S(1)} %bitcast.24, s32[8,64]{1,0:T(8,128)S(1)} %bitcast.25, s32[32,128]{1,0:T(8,128)S(1)} %bitcast.23, s32[8,16]{1,0:T(8,128)S(1)} %bitcast.26, s32[8,16]{1,0:T(8,128)S(1)} %bitcast.27, ...), custom_call_target="tpu_custom_call" | custom-call | tf_op jit(solution)/shard_map/plan/pallas_call | solution.py:111
  35.8 1.9 %collective-permute-start.1 = (bf16[256,8,128]{2,1,0:T(8,128)(2,1)S(1)}, bf16[256,8,128]{2,1,0:T(8,128)(2,1)S(1)}, u32[]{:S(2)}, u32[]{:S(2)}) collective-permute-start(bf16[256,8,128]{2,1,0:T(8,128)(2,1)S(1)} %pad_maximum_fusion.refs_0_), channel_id=1, source_target_pairs={{0,448},{64,0},{128,64},{192,128},{256,192},{320,256},{384,320},{4... | collective-permute-start | bytes 1572872 | tf_op jit(solution)/shard_map/ppermute | solution.py:365
  37.8 0.6 collective-permute-done.refs_7_
  38.4 5.6 %collective-permute-start.4 = (bf16[256,8,128]{2,1,0:T(8,128)(2,1)S(1)}, bf16[256,8,128]{2,1,0:T(8,128)(2,1)S(1)}, u32[]{:S(2)}, u32[]{:S(2)}) collective-permute-start(bf16[256,8,128]{2,1,0:T(8,128)(2,1)S(1)} %collective-permute-done.refs_7_), channel_id=1, source_target_pairs={{0,64},{64,128},{128,192},{192,256},{256,320},{320,384},{384,448},... | collective-permute-start | bytes 1572872 | tf_op jit(solution)/shard_map/ppermute | solution.py:365
  44.0 4.2 %collective-permute-done.1.refs_1_ = bf16[256,8,128]{2,1,0:T(8,128)(2,1)S(1)} collective-permute-done((bf16[256,8,128]{2,1,0:T(8,128)(2,1)S(1)}, bf16[256,8,128]{2,1,0:T(8,128)(2,1)S(1)}, u32[]{:S(2)}, u32[]{:S(2)}) %collective-permute-start.1) | collective-permute-done | bytes 524320 | tf_op jit(solution)/shard_map/ppermute | solution.py:365
  48.1 1.9 %collective-permute-start.2 = (bf16[256,8,128]{2,1,0:T(8,128)(2,1)S(1)}, bf16[256,8,128]{2,1,0:T(8,128)(2,1)S(1)}, u32[]{:S(2)}, u32[]{:S(2)}) collective-permute-start(bf16[256,8,128]{2,1,0:T(8,128)(2,1)S(1)} %collective-permute-done.1.refs_1_), channel_id=1, source_target_pairs={{0,448},{64,0},{128,64},{192,128},{256,192},{320,256},{384,320},{4... | collective-permute-start | bytes 1572872 | tf_op jit(solution)/shard_map/ppermute | solution.py:365
  50.0 0.6 collective-permute-done.4.refs_6_
  50.6 5.6 %collective-permute-start.5 = (bf16[256,8,128]{2,1,0:T(8,128)(2,1)S(1)}, bf16[256,8,128]{2,1,0:T(8,128)(2,1)S(1)}, u32[]{:S(2)}, u32[]{:S(2)}) collective-permute-start(bf16[256,8,128]{2,1,0:T(8,128)(2,1)S(1)} %collective-permute-done.4.refs_6_), channel_id=1, source_target_pairs={{0,64},{64,128},{128,192},{192,256},{256,320},{320,384},{384,448},... | collective-permute-start | bytes 1572872 | tf_op jit(solution)/shard_map/ppermute | solution.py:365
  56.2 4.2 %collective-permute-done.2.refs_2_ = bf16[256,8,128]{2,1,0:T(8,128)(2,1)S(1)} collective-permute-done((bf16[256,8,128]{2,1,0:T(8,128)(2,1)S(1)}, bf16[256,8,128]{2,1,0:T(8,128)(2,1)S(1)}, u32[]{:S(2)}, u32[]{:S(2)}) %collective-permute-start.2) | collective-permute-done | bytes 524320 | tf_op jit(solution)/shard_map/ppermute | solution.py:365
  60.4 1.9 %collective-permute-start.3 = (bf16[256,8,128]{2,1,0:T(8,128)(2,1)S(1)}, bf16[256,8,128]{2,1,0:T(8,128)(2,1)S(1)}, u32[]{:S(2)}, u32[]{:S(2)}) collective-permute-start(bf16[256,8,128]{2,1,0:T(8,128)(2,1)S(1)} %collective-permute-done.2.refs_2_), channel_id=1, source_target_pairs={{0,448},{64,0},{128,64},{192,128},{256,192},{320,256},{384,320},{4... | collective-permute-start | bytes 1572872 | tf_op jit(solution)/shard_map/ppermute | solution.py:365
  62.3 0.6 collective-permute-done.5.refs_5_
  62.9 5.6 %collective-permute-start.6 = (bf16[256,8,128]{2,1,0:T(8,128)(2,1)S(1)}, bf16[256,8,128]{2,1,0:T(8,128)(2,1)S(1)}, u32[]{:S(2)}, u32[]{:S(2)}) collective-permute-start(bf16[256,8,128]{2,1,0:T(8,128)(2,1)S(1)} %collective-permute-done.5.refs_5_), channel_id=1, source_target_pairs={{0,64},{64,128},{128,192},{192,256},{256,320},{320,384},{384,448},... | collective-permute-start | bytes 1572872 | tf_op jit(solution)/shard_map/ppermute | solution.py:365
  68.5 17.8 %all_to_all.27 = s32[8,1,128]{2,1,0:T(1,128)S(1)} all-to-all(s32[8,1,128]{2,1,0:T(1,128)S(1)} %bitcast.29), channel_id=1, replica_groups={{0,8,16,24,32,40,48,56},{64,72,80,88,96,104,112,120},{128,136,144,152,1..., dimensions={0} | all-to-all | bytes 8192 | tf_op jit(solution)/shard_map/all_to_all | solution.py:369
  86.3 0.0 collective-permute-done.3.refs_3_
  86.3 0.0 collective-permute-done.6.refs_4_
  86.3 1.0 select.11
  87.4 1.3 copy-done.3
  88.7 0.8 copy-done.4
  89.5 0.8 copy-done.6
  90.3 0.8 copy-done.8
  91.1 0.8 copy-done.10
  91.9 0.8 copy-done.12
  92.7 0.8 copy-done.14
  93.5 3.6 %all-to-all-start.4 = ((bf16[8,16,8,8,128]{4,3,2,1,0:T(8,128)(2,1)}), bf16[8,16,8,8,128]{4,3,2,1,0:T(8,128)(2,1)S(1)}, u32[]{:S(2)}, u32[]{:S(2)}) async-start(bf16[8,16,8,8,128]{4,3,2,1,0:T(8,128)(2,1)} %copy-done.3), calls=%async_computation.4 | async-start | bytes 4194304 | tf_op jit(solution)/shard_map/all_to_all | solution.py:369
  97.1 1.0 copy-done.5
  98.1 1.0 copy-done.7
  99.2 1.0 copy-done.9
  100.2 1.0 copy-done.11
  101.3 1.0 copy-done.13
  102.3 1.0 copy-done.15
  103.3 1.4 select.10
  104.8 1.4 copy-done.2
  106.1 21.2 %all-to-all-done.4 = bf16[8,16,8,8,128]{4,3,2,1,0:T(8,128)(2,1)S(1)} async-done(((bf16[8,16,8,8,128]{4,3,2,1,0:T(8,128)(2,1)}), bf16[8,16,8,8,128]{4,3,2,1,0:T(8,128)(2,1)S(1)}, u32[]{:S(2)}, u32[]{:S(2)}) %all-to-all-start.4) | async-done | bytes 2097184 | tf_op jit(solution)/shard_map/all_to_all | solution.py:369
  127.3 1.3 copy-done
  128.6 3.7 %all-to-all-start.3 = ((bf16[8,64,2,8,128]{4,3,2,1,0:T(8,128)(2,1)}), bf16[8,64,2,8,128]{4,3,2,1,0:T(8,128)(2,1)S(1)}, u32[]{:S(2)}, u32[]{:S(2)}) async-start(bf16[8,64,2,8,128]{4,3,2,1,0:T(8,128)(2,1)} %copy-done.2), calls=%async_computation.3 | async-start | bytes 4194304 | tf_op jit(solution)/shard_map/all_to_all | solution.py:369
  132.4 1.6 copy-done.1
  134.0 1.7 far_parents.1
  135.7 0.0 copy-start.21
  135.8 2.1 %collective-permute-start.7 = (bf16[4,2,8,8,128]{4,3,2,1,0:T(8,128)(2,1)S(1)}, bf16[4,2,8,8,128]{4,3,2,1,0:T(8,128)(2,1)S(1)}, u32[]{:S(2)}, u32[]{:S(2)}) collective-permute-start(bf16[4,2,8,8,128]{4,3,2,1,0:T(8,128)(2,1)S(1)} %get-tuple-element.20), channel_id=1, source_target_pairs={{0,1},{1,0},{2,3},{3,2},{4,5},{5,4},{6,7},{7,6},{8,9},{9,8},{10,11... | collective-permute-start | bytes 393224 | tf_op jit(solution)/shard_map/ppermute | solution.py:248
  137.8 1.3 collective-permute-done.7.f1
  139.2 2.5 %collective-permute-start.8 = (bf16[4,2,8,8,128]{4,3,2,1,0:T(8,128)(2,1)S(1)}, bf16[4,2,8,8,128]{4,3,2,1,0:T(8,128)(2,1)S(1)}, u32[]{:S(2)}, u32[]{:S(2)}) collective-permute-start(bf16[4,2,8,8,128]{4,3,2,1,0:T(8,128)(2,1)S(1)} %pad_maximum_fusion.1), channel_id=1, source_target_pairs={{0,2},{1,3},{2,0},{3,1},{4,6},{5,7},{6,4},{7,5},{8,10},{9,11},{10,... | collective-permute-start | bytes 393224 | tf_op jit(solution)/shard_map/ppermute | solution.py:248
  141.7 4.9 %collective-permute-done.8.f2 = bf16[4,2,8,8,128]{4,3,2,1,0:T(8,128)(2,1)S(1)} collective-permute-done((bf16[4,2,8,8,128]{4,3,2,1,0:T(8,128)(2,1)S(1)}, bf16[4,2,8,8,128]{4,3,2,1,0:T(8,128)(2,1)S(1)}, u32[]{:S(2)}, u32[]{:S(2)}) %collective-permute-start.8) | collective-permute-done | bytes 131104 | tf_op jit(solution)/shard_map/ppermute | solution.py:248
  146.6 2.8 %collective-permute-start.9 = (bf16[4,2,8,8,128]{4,3,2,1,0:T(8,128)(2,1)S(1)}, bf16[4,2,8,8,128]{4,3,2,1,0:T(8,128)(2,1)S(1)}, u32[]{:S(2)}, u32[]{:S(2)}) collective-permute-start(bf16[4,2,8,8,128]{4,3,2,1,0:T(8,128)(2,1)S(1)} %pad_maximum_fusion.2), channel_id=1, source_target_pairs={{0,4},{1,5},{2,6},{3,7},{4,0},{5,1},{6,2},{7,3},{8,12},{9,13},{10,... | collective-permute-start | bytes 393224 | tf_op jit(solution)/shard_map/ppermute | solution.py:248
  149.4 5.6 %collective-permute-done.9.f3 = bf16[4,2,8,8,128]{4,3,2,1,0:T(8,128)(2,1)S(1)} collective-permute-done((bf16[4,2,8,8,128]{4,3,2,1,0:T(8,128)(2,1)S(1)}, bf16[4,2,8,8,128]{4,3,2,1,0:T(8,128)(2,1)S(1)}, u32[]{:S(2)}, u32[]{:S(2)}) %collective-permute-start.9) | collective-permute-done | bytes 131104 | tf_op jit(solution)/shard_map/ppermute | solution.py:248
  155.0 3.0 %lower.1 = (bf16[4,8,2,8,128]{4,3,2,1,0:T(8,128)(2,1)S(1)}, bf16[4,8,2,8,128]{4,3,2,1,0:T(8,128)(2,1)S(1)}) custom-call(s32[1]{0:T(128)} %bitcast.angle, bf16[4,2,8,8,128]{4,3,2,1,0:T(8,128)(2,1)S(1)} %get-tuple-element.19.f0, bf16[4,2,8,8,128]{4,3,2,1,0:T(8,128)(2,1)S(1)} %collective-permute-done.7.f1, ...), custom_call_target="tpu_custom_call" | custom-call | flops 300000000 | bytes 2000000 | tf_op jit(solution)/shard_map/lower/pallas_call | solution.py:339
  158.0 1.9 %collective-permute-start.10 = (bf16[4,8,2,8,128]{4,3,2,1,0:T(8,128)(2,1)S(1)}, bf16[4,8,2,8,128]{4,3,2,1,0:T(8,128)(2,1)S(1)}, u32[]{:S(2)}, u32[]{:S(2)}) collective-permute-start(bf16[4,8,2,8,128]{4,3,2,1,0:T(8,128)(2,1)S(1)} %get-tuple-element.22), channel_id=1, source_target_pairs={{0,1},{1,0},{2,3},{3,2},{4,5},{5,4},{6,7},{7,6},{8,9},{9,8},{10,11... | collective-permute-start | bytes 393224 | tf_op jit(solution)/shard_map/ppermute | solution.py:248
  160.0 1.3 collective-permute-done.10.t1
  161.3 2.5 %collective-permute-start.11 = (bf16[4,8,2,8,128]{4,3,2,1,0:T(8,128)(2,1)S(1)}, bf16[4,8,2,8,128]{4,3,2,1,0:T(8,128)(2,1)S(1)}, u32[]{:S(2)}, u32[]{:S(2)}) collective-permute-start(bf16[4,8,2,8,128]{4,3,2,1,0:T(8,128)(2,1)S(1)} %pad_maximum_fusion.3), channel_id=1, source_target_pairs={{0,2},{1,3},{2,0},{3,1},{4,6},{5,7},{6,4},{7,5},{8,10},{9,11},{10,... | collective-permute-start | bytes 393224 | tf_op jit(solution)/shard_map/ppermute | solution.py:248
  163.8 4.9 %collective-permute-done.11.t2 = bf16[4,8,2,8,128]{4,3,2,1,0:T(8,128)(2,1)S(1)} collective-permute-done((bf16[4,8,2,8,128]{4,3,2,1,0:T(8,128)(2,1)S(1)}, bf16[4,8,2,8,128]{4,3,2,1,0:T(8,128)(2,1)S(1)}, u32[]{:S(2)}, u32[]{:S(2)}) %collective-permute-start.11) | collective-permute-done | bytes 131104 | tf_op jit(solution)/shard_map/ppermute | solution.py:248
  168.8 2.8 %collective-permute-start.12 = (bf16[4,8,2,8,128]{4,3,2,1,0:T(8,128)(2,1)S(1)}, bf16[4,8,2,8,128]{4,3,2,1,0:T(8,128)(2,1)S(1)}, u32[]{:S(2)}, u32[]{:S(2)}) collective-permute-start(bf16[4,8,2,8,128]{4,3,2,1,0:T(8,128)(2,1)S(1)} %pad_maximum_fusion.4), channel_id=1, source_target_pairs={{0,4},{1,5},{2,6},{3,7},{4,0},{5,1},{6,2},{7,3},{8,12},{9,13},{10,... | collective-permute-start | bytes 393224 | tf_op jit(solution)/shard_map/ppermute | solution.py:248
  171.6 0.0 all-to-all-done.3
  171.6 5.5 %collective-permute-done.12.t3 = bf16[4,8,2,8,128]{4,3,2,1,0:T(8,128)(2,1)S(1)} collective-permute-done((bf16[4,8,2,8,128]{4,3,2,1,0:T(8,128)(2,1)S(1)}, bf16[4,8,2,8,128]{4,3,2,1,0:T(8,128)(2,1)S(1)}, u32[]{:S(2)}, u32[]{:S(2)}) %collective-permute-start.12) | collective-permute-done | bytes 131104 | tf_op jit(solution)/shard_map/ppermute | solution.py:248
  177.2 3.2 %far_children.1 = bf16[64,2,8,128]{3,2,1,0:T(8,128)(2,1)} custom-call(s32[1]{0:T(128)} %bitcast.angle, s32[8,64]{1,0:T(8,128)S(1)} %get-tuple-element.14.code, bf16[512,2,8,128]{3,2,1,0:T(8,128)(2,1)S(1)} %bitcast.18, bf16[40,2,8,128]{3,2,1,0:T(8,128)(2,1)S(1)} %copy-done.21, bf16[4,8,2,8,128]{4,3,2,1,0:T(8,128)(2,1)S(1)} %get-tuple-element.21.t0, ...), custom_call_target="tpu_custom_call" | custom-call | tf_op jit(solution)/shard_map/far_children/pallas_call | solution.py:284
  (54 shorter events, 0.2 us)
Async XLA Ops:
  0.0 26.9 %copy-start.32 = (bf16[64,2,8,128]{3,2,1,0:T(8,128)(2,1)S(1)}, bf16[64,2,8,128]{3,2,1,0:T(8,128)(2,1)}, u32[]{:S(2)}) copy-start(bf16[64,2,8,128]{3,2,1,0:T(8,128)(2,1)} %param.15) | copy-start | bytes 786436
  0.0 31.8 %copy-start.31 = (s32[1024]{0:T(1024)S(1)}, s32[1024]{0:T(1024)}, u32[]{:S(2)}) copy-start(s32[1024]{0:T(1024)} %param.22) | copy-start | bytes 12292
  0.0 31.8 %copy-start.30 = (s32[16,8]{0,1:T(8,128)S(1)}, s32[16,8]{0,1:T(8,128)}, u32[]{:S(2)}) copy-start(s32[16,8]{0,1:T(8,128)} %param.21) | copy-start | bytes 1540
  0.0 31.8 %copy-start.29 = (s32[16,8]{0,1:T(8,128)S(1)}, s32[16,8]{0,1:T(8,128)}, u32[]{:S(2)}) copy-start(s32[16,8]{0,1:T(8,128)} %param.20) | copy-start | bytes 1540
  0.0 31.8 %copy-start.26 = (s32[4096]{0:T(1024)S(1)}, s32[4096]{0:T(1024)}, u32[]{:S(2)}) copy-start(s32[4096]{0:T(1024)} %param.18) | copy-start | bytes 49156
  0.0 31.8 %copy-start.28 = (s32[64,8]{0,1:T(8,128)S(1)}, s32[64,8]{0,1:T(8,128)}, u32[]{:S(2)}) copy-start(s32[64,8]{0,1:T(8,128)} %param.17) | copy-start | bytes 6148
  0.0 31.8 %copy-start.27 = (s32[64,8]{0,1:T(8,128)S(1)}, s32[64,8]{0,1:T(8,128)}, u32[]{:S(2)}) copy-start(s32[64,8]{0,1:T(8,128)} %param.16) | copy-start | bytes 6148
  12.0 1.0 copy-start.16
  12.9 0.9 copy-start.18
  13.9 0.8 copy-start.23
  14.7 0.8 copy-start.24
  27.0 11.4 %collective-permute-start = (bf16[256,8,128]{2,1,0:T(8,128)(2,1)S(1)}, bf16[256,8,128]{2,1,0:T(8,128)(2,1)S(1)}, u32[]{:S(2)}, u32[]{:S(2)}) collective-permute-start(bf16[256,8,128]{2,1,0:T(8,128)(2,1)S(1)} %pad_maximum_fusion.refs_0_), channel_id=1, source_target_pairs={{0,64},{64,128},{128,192},{192,256},{256,320},{320,384},{384,448},... | collective-permute-start | bytes 1572872 | tf_op jit(solution)/shard_map/ppermute | solution.py:365
  35.8 12.3 %collective-permute-start.1 = (bf16[256,8,128]{2,1,0:T(8,128)(2,1)S(1)}, bf16[256,8,128]{2,1,0:T(8,128)(2,1)S(1)}, u32[]{:S(2)}, u32[]{:S(2)}) collective-permute-start(bf16[256,8,128]{2,1,0:T(8,128)(2,1)S(1)} %pad_maximum_fusion.refs_0_), channel_id=1, source_target_pairs={{0,448},{64,0},{128,64},{192,128},{256,192},{320,256},{384,320},{4... | collective-permute-start | bytes 1572872 | tf_op jit(solution)/shard_map/ppermute | solution.py:365
  38.4 12.3 %collective-permute-start.4 = (bf16[256,8,128]{2,1,0:T(8,128)(2,1)S(1)}, bf16[256,8,128]{2,1,0:T(8,128)(2,1)S(1)}, u32[]{:S(2)}, u32[]{:S(2)}) collective-permute-start(bf16[256,8,128]{2,1,0:T(8,128)(2,1)S(1)} %collective-permute-done.refs_7_), channel_id=1, source_target_pairs={{0,64},{64,128},{128,192},{192,256},{256,320},{320,384},{384,448},... | collective-permute-start | bytes 1572872 | tf_op jit(solution)/shard_map/ppermute | solution.py:365
  48.1 12.3 %collective-permute-start.2 = (bf16[256,8,128]{2,1,0:T(8,128)(2,1)S(1)}, bf16[256,8,128]{2,1,0:T(8,128)(2,1)S(1)}, u32[]{:S(2)}, u32[]{:S(2)}) collective-permute-start(bf16[256,8,128]{2,1,0:T(8,128)(2,1)S(1)} %collective-permute-done.1.refs_1_), channel_id=1, source_target_pairs={{0,448},{64,0},{128,64},{192,128},{256,192},{320,256},{384,320},{4... | collective-permute-start | bytes 1572872 | tf_op jit(solution)/shard_map/ppermute | solution.py:365
  50.6 12.3 %collective-permute-start.5 = (bf16[256,8,128]{2,1,0:T(8,128)(2,1)S(1)}, bf16[256,8,128]{2,1,0:T(8,128)(2,1)S(1)}, u32[]{:S(2)}, u32[]{:S(2)}) collective-permute-start(bf16[256,8,128]{2,1,0:T(8,128)(2,1)S(1)} %collective-permute-done.4.refs_6_), channel_id=1, source_target_pairs={{0,64},{64,128},{128,192},{192,256},{256,320},{320,384},{384,448},... | collective-permute-start | bytes 1572872 | tf_op jit(solution)/shard_map/ppermute | solution.py:365
  60.4 25.9 %collective-permute-start.3 = (bf16[256,8,128]{2,1,0:T(8,128)(2,1)S(1)}, bf16[256,8,128]{2,1,0:T(8,128)(2,1)S(1)}, u32[]{:S(2)}, u32[]{:S(2)}) collective-permute-start(bf16[256,8,128]{2,1,0:T(8,128)(2,1)S(1)} %collective-permute-done.2.refs_2_), channel_id=1, source_target_pairs={{0,448},{64,0},{128,64},{192,128},{256,192},{320,256},{384,320},{4... | collective-permute-start | bytes 1572872 | tf_op jit(solution)/shard_map/ppermute | solution.py:365
  62.9 23.4 %collective-permute-start.6 = (bf16[256,8,128]{2,1,0:T(8,128)(2,1)S(1)}, bf16[256,8,128]{2,1,0:T(8,128)(2,1)S(1)}, u32[]{:S(2)}, u32[]{:S(2)}) collective-permute-start(bf16[256,8,128]{2,1,0:T(8,128)(2,1)S(1)} %collective-permute-done.5.refs_5_), channel_id=1, source_target_pairs={{0,64},{64,128},{128,192},{192,256},{256,320},{320,384},{384,448},... | collective-permute-start | bytes 1572872 | tf_op jit(solution)/shard_map/ppermute | solution.py:365
  87.4 1.3 copy-start.3
  88.7 0.8 copy-start.4
  89.5 0.8 copy-start.6
  90.3 0.8 copy-start.8
  91.1 0.8 copy-start.10
  91.9 0.8 copy-start.12
  92.7 0.8 copy-start.14
  93.5 33.8 %all-to-all-start.4 = ((bf16[8,16,8,8,128]{4,3,2,1,0:T(8,128)(2,1)}), bf16[8,16,8,8,128]{4,3,2,1,0:T(8,128)(2,1)S(1)}, u32[]{:S(2)}, u32[]{:S(2)}) async-start(bf16[8,16,8,8,128]{4,3,2,1,0:T(8,128)(2,1)} %copy-done.3), calls=%async_computation.4 | async-start | bytes 4194304 | tf_op jit(solution)/shard_map/all_to_all | solution.py:369
  97.1 1.0 copy-start.5
  98.1 1.0 copy-start.7
  99.2 1.0 copy-start.9
  100.2 1.0 copy-start.11
  101.3 1.0 copy-start.13
  102.3 1.0 copy-start.15
  104.8 1.4 copy-start.2
  106.1 26.3 %copy-start.20 = (bf16[40,2,16,256]{3,2,1,0:T(8,128)(2,1)S(1)}, bf16[40,2,16,256]{3,2,1,0:T(8,128)(2,1)}, u32[]{:S(2)}) copy-start(bf16[40,2,16,256]{3,2,1,0:T(8,128)(2,1)} %ops_hbm.2) | copy-start | bytes 1966084
  127.3 1.3 copy-start
  128.6 26.4 %copy-start.17 = (f32[2,128,256]{2,1,0:T(8,128)S(1)}, f32[2,128,256]{2,1,0:T(8,128)}, u32[]{:S(2)}) copy-start(f32[2,128,256]{2,1,0:T(8,128)} %constant.62.clone.sin_t) | copy-start | bytes 786436
  128.6 26.4 %copy-start.19 = (f32[2,128,256]{2,1,0:T(8,128)S(1)}, f32[2,128,256]{2,1,0:T(8,128)}, u32[]{:S(2)}) copy-start(f32[2,128,256]{2,1,0:T(8,128)} %constant.61.clone.cos_t) | copy-start | bytes 786436
  128.6 26.4 %copy-start.22 = (bf16[256,128]{1,0:T(8,128)(2,1)S(1)}, bf16[256,128]{1,0:T(8,128)(2,1)}, u32[]{:S(2)}) copy-start(bf16[256,128]{1,0:T(8,128)(2,1)} %constant.68.phi) | copy-start | bytes 196612
  128.6 26.4 %copy-start.25 = (bf16[64,128]{1,0:T(8,128)(2,1)S(1)}, bf16[64,128]{1,0:T(8,128)(2,1)}, u32[]{:S(2)}) copy-start(bf16[64,128]{1,0:T(8,128)(2,1)} %constant.67.theta) | copy-start | bytes 49156
  128.6 43.0 %all-to-all-start.3 = ((bf16[8,64,2,8,128]{4,3,2,1,0:T(8,128)(2,1)}), bf16[8,64,2,8,128]{4,3,2,1,0:T(8,128)(2,1)S(1)}, u32[]{:S(2)}, u32[]{:S(2)}) async-start(bf16[8,64,2,8,128]{4,3,2,1,0:T(8,128)(2,1)} %copy-done.2), calls=%async_computation.3 | async-start | bytes 4194304 | tf_op jit(solution)/shard_map/all_to_all | solution.py:369
  132.4 1.6 copy-start.1
  135.7 41.4 %copy-start.21 = (bf16[40,2,8,128]{3,2,1,0:T(8,128)(2,1)S(1)}, bf16[40,2,8,128]{3,2,1,0:T(8,128)(2,1)}, u32[]{:S(2)}) copy-start(bf16[40,2,8,128]{3,2,1,0:T(8,128)(2,1)} %ops_hbm.3) | copy-start | bytes 491524
  135.8 3.4 %collective-permute-start.7 = (bf16[4,2,8,8,128]{4,3,2,1,0:T(8,128)(2,1)S(1)}, bf16[4,2,8,8,128]{4,3,2,1,0:T(8,128)(2,1)S(1)}, u32[]{:S(2)}, u32[]{:S(2)}) collective-permute-start(bf16[4,2,8,8,128]{4,3,2,1,0:T(8,128)(2,1)S(1)} %get-tuple-element.20), channel_id=1, source_target_pairs={{0,1},{1,0},{2,3},{3,2},{4,5},{5,4},{6,7},{7,6},{8,9},{9,8},{10,11... | collective-permute-start | bytes 393224 | tf_op jit(solution)/shard_map/ppermute | solution.py:248
  139.2 7.4 %collective-permute-start.8 = (bf16[4,2,8,8,128]{4,3,2,1,0:T(8,128)(2,1)S(1)}, bf16[4,2,8,8,128]{4,3,2,1,0:T(8,128)(2,1)S(1)}, u32[]{:S(2)}, u32[]{:S(2)}) collective-permute-start(bf16[4,2,8,8,128]{4,3,2,1,0:T(8,128)(2,1)S(1)} %pad_maximum_fusion.1), channel_id=1, source_target_pairs={{0,2},{1,3},{2,0},{3,1},{4,6},{5,7},{6,4},{7,5},{8,10},{9,11},{10,... | collective-permute-start | bytes 393224 | tf_op jit(solution)/shard_map/ppermute | solution.py:248
  146.6 8.4 %collective-permute-start.9 = (bf16[4,2,8,8,128]{4,3,2,1,0:T(8,128)(2,1)S(1)}, bf16[4,2,8,8,128]{4,3,2,1,0:T(8,128)(2,1)S(1)}, u32[]{:S(2)}, u32[]{:S(2)}) collective-permute-start(bf16[4,2,8,8,128]{4,3,2,1,0:T(8,128)(2,1)S(1)} %pad_maximum_fusion.2), channel_id=1, source_target_pairs={{0,4},{1,5},{2,6},{3,7},{4,0},{5,1},{6,2},{7,3},{8,12},{9,13},{10,... | collective-permute-start | bytes 393224 | tf_op jit(solution)/shard_map/ppermute | solution.py:248
  158.0 3.2 %collective-permute-start.10 = (bf16[4,8,2,8,128]{4,3,2,1,0:T(8,128)(2,1)S(1)}, bf16[4,8,2,8,128]{4,3,2,1,0:T(8,128)(2,1)S(1)}, u32[]{:S(2)}, u32[]{:S(2)}) collective-permute-start(bf16[4,8,2,8,128]{4,3,2,1,0:T(8,128)(2,1)S(1)} %get-tuple-element.22), channel_id=1, source_target_pairs={{0,1},{1,0},{2,3},{3,2},{4,5},{5,4},{6,7},{7,6},{8,9},{9,8},{10,11... | collective-permute-start | bytes 393224 | tf_op jit(solution)/shard_map/ppermute | solution.py:248
  161.3 7.4 %collective-permute-start.11 = (bf16[4,8,2,8,128]{4,3,2,1,0:T(8,128)(2,1)S(1)}, bf16[4,8,2,8,128]{4,3,2,1,0:T(8,128)(2,1)S(1)}, u32[]{:S(2)}, u32[]{:S(2)}) collective-permute-start(bf16[4,8,2,8,128]{4,3,2,1,0:T(8,128)(2,1)S(1)} %pad_maximum_fusion.3), channel_id=1, source_target_pairs={{0,2},{1,3},{2,0},{3,1},{4,6},{5,7},{6,4},{7,5},{8,10},{9,11},{10,... | collective-permute-start | bytes 393224 | tf_op jit(solution)/shard_map/ppermute | solution.py:248
  168.8 8.4 %collective-permute-start.12 = (bf16[4,8,2,8,128]{4,3,2,1,0:T(8,128)(2,1)S(1)}, bf16[4,8,2,8,128]{4,3,2,1,0:T(8,128)(2,1)S(1)}, u32[]{:S(2)}, u32[]{:S(2)}) collective-permute-start(bf16[4,8,2,8,128]{4,3,2,1,0:T(8,128)(2,1)S(1)} %pad_maximum_fusion.4), channel_id=1, source_target_pairs={{0,4},{1,5},{2,6},{3,7},{4,0},{5,1},{6,2},{7,3},{8,12},{9,13},{10,... | collective-permute-start | bytes 393224 | tf_op jit(solution)/shard_map/ppermute | solution.py:248

commit v3 on v2

--- a/solution.py
+++ b/solution.py
@@ -9,11 +9,11 @@
 from jax.experimental.pallas import tpu as pltpu
 from jax.sharding import PartitionSpec as P
 
+
 CT = 64
 SUBBOX_HEADINGS = 128
 PT = 128
 PP = 256
-KIDS = 4
 WAVE_NUMBER = 6.0
 SIDE = 8
 BOTH = ("box", "angle")
@@ -122,12 +122,17 @@
     )(*args)
 
 
-def up_body(field, theta, phi, cos_t, sin_t, out, wide):
+def up_body(field, theta_h, phi_h, cos_h, sin_h, out, theta, phi, cos_t, sin_t, wide, sems):
+    copies = fetch((theta_h, phi_h, cos_h, sin_h), (theta, phi, cos_t, sin_t), sems)
+    copies[0].wait()
+    copies[1].wait()
     for r in range(8):
         for c in range(2):
             rows = jnp.concatenate([field[s, r, c] for s in range(8)], axis=0)
             stretched = bmm(theta[...], rows).astype(BF16)
             wide[r * 2 + c] = bmm(stretched, phi[...])
+    copies[2].wait()
+    copies[3].wait()
     for q in range(2):
         for u in range(PT // 8):
             at = pl.ds(u * 8, 8)
@@ -144,50 +149,65 @@
                     out[u // 2, q, c * 4 + (u % 2) * 2 + v] = part[:, v * 128 : (v + 1) * 128]
 
 
-def lift(field, theta, phi, cos_t, sin_t):
+def fetch(sources, targets, sems):
+    copies = [pltpu.make_async_copy(a, b, sems.at[i]) for i, (a, b) in enumerate(zip(sources, targets))]
+    for copy in copies:
+        copy.start()
+    return copies
+
+
+def lift(field, tables):
     return pl.pallas_call(
         up_body,
         out_shape=jax.ShapeDtypeStruct((8, 2, 8, 8, 128), BF16),
-        in_specs=[pl.BlockSpec(memory_space=VM)] * 5,
+        in_specs=[pl.BlockSpec(memory_space=VM)] + [pl.BlockSpec(memory_space=pltpu.HBM)] * 4,
         out_specs=pl.BlockSpec(memory_space=VM),
-        scratch_shapes=[pltpu.VMEM((16, PT, PP), F32)],
+        scratch_shapes=[pltpu.VMEM(t.shape, t.dtype) for t in tables]
+        + [pltpu.VMEM((16, PT, PP), F32), pltpu.SemaphoreType.DMA((4,))],
         compiler_params=pltpu.CompilerParams(vmem_limit_bytes=GRANT),
         name="lift",
-    )(field, theta, phi, cos_t, sin_t)
-
-
-def select_body(first, rows, tiles, asked, *refs):
-    blocks, out, pool, sems = refs[:8], refs[8], refs[9], refs[10]
-    count = rows * tiles
-    copies = [
-        pltpu.make_async_copy(b.at[pl.ds(first[1], count)], pool.at[pl.ds(i * count, count)], sems.at[i])
-        for i, b in enumerate(blocks)
-    ]
-    for copy in copies:
-        copy.start()
-    for copy in copies:
+    )(field, *tables)
+
+
+def select_body(first, asked, *refs):
+    blocks, out, pool, buf, sems, out_sems = refs[:8], *refs[8:]
+    for copy in fetch(blocks, [pool.at[i] for i in range(8)], sems):
         copy.wait()
-    per_peer = out.shape[1]
+    _, per_peer, tiles = buf.shape[:3]
+    rows = pool.shape[1] // tiles
+    shift = rows.bit_length() - 1
+
+    def copy_out(h):
+        return pltpu.make_async_copy(buf.at[h], out.at[h], out_sems.at[h])
 
     def step(h, carry):
         for k in range(per_peer):
-            row = asked[h, first[0] + k]
-            at = pl.multiple_of(row * tiles, tiles)
-            out[h, k] = pool[pl.ds(at, tiles)]
+            row = asked[h, first + k]
+            at = pl.multiple_of((row & (rows - 1)) * tiles, tiles)
+            buf[h, k] = pool[row >> shift, pl.ds(at, tiles)]
+        copy_out(h).start()
         return carry
 
     lax.fori_loop(0, SIDE, step, 0)
-
-
-def select(asked, blocks, first, rows, tiles, per_peer):
-    return pl.pallas_call(
-        functools.partial(select_body, first, rows, tiles),
-        out_shape=jax.ShapeDtypeStruct((SIDE, per_peer, tiles, 8, 128), BF16),
+    for h in range(SIDE):
+        copy_out(h).wait()
+
+
+def select(asked, blocks, first, tiles, per_peer):
+    shape = (SIDE, per_peer, tiles, 8, 128)
+    return pl.pallas_call(
+        functools.partial(select_body, first),
+        out_shape=jax.ShapeDtypeStruct(shape, BF16),
         in_specs=[pl.BlockSpec(memory_space=pltpu.SMEM)] + [pl.BlockSpec(memory_space=ANY)] * 8,
-        out_specs=pl.BlockSpec(memory_space=VM),
-        scratch_shapes=[pltpu.VMEM((8 * rows * tiles, 8, 128), BF16), pltpu.SemaphoreType.DMA((8,))],
-        compiler_params=pltpu.CompilerParams(vmem_limit_bytes=GRANT),
-        name="select",
+        out_specs=pl.BlockSpec(memory_space=pltpu.HBM),
+        scratch_shapes=[
+            pltpu.VMEM((8, 128, 8, 128), BF16),
+            pltpu.VMEM(shape, BF16),
+            pltpu.SemaphoreType.DMA((8,)),
+            pltpu.SemaphoreType.DMA((8,)),
+        ],
+        compiler_params=pltpu.CompilerParams(vmem_limit_bytes=GRANT),
+        cost_estimate=pl.CostEstimate(flops=0, bytes_accessed=4_000_000, transcendentals=0),
     )(asked, *blocks)
 
 
@@ -240,27 +260,25 @@
     )(angle, code, recv, ops)
 
 
-CUBE = ((0, 0), (1, 0), (2, 0), (2, 2), (3, 0), (3, 1), (3, 2), (3, 3))
-
-
-def cube(keep, send):
+CAME = ((0, 0), (1, 0), (2, 0), (2, 1), (3, 0), (3, 1), (4, 0), (4, 1))
+
+
+def trade(keep, send):
     def across(x, bit):
         return lax.ppermute(x, "angle", [(i, i ^ bit) for i in range(8)])
 
-    first = across(send, 1)
-    second = across(jnp.concatenate([keep[1:2], keep[3:4], first[1:2], first[3:4]]), 2)
-    third = across(jnp.concatenate([keep[2:3], first[2:3], second[1:2], second[3:4]]), 4)
-    return keep, first, second, third
-
-
-def child_far_body(angle, code, recv, ops_hbm, t0, t1, t2, t3, out, ops, sem):
+    other = across(send, 1)
+    return keep, other, *(across(jnp.concatenate([keep[i : i + 1], other[i : i + 1]]), 2 * i) for i in (1, 2, 3))
+
+
+def child_far_body(angle, code, recv, ops_hbm, t0, t1, t2, t3, t4, out, ops, sem):
     copy = pltpu.make_async_copy(ops_hbm, ops.at[pl.ds(0, 40)], sem)
     copy.start()
     ops[40] = jnp.zeros(ops.shape[1:], BF16)
     copy.wait()
-    terms = (t0, t1, t2, t3)
-
-    for s, (which, place) in enumerate(CUBE):
+    terms = (t0, t1, t2, t3, t4)
+
+    for s, (which, place) in enumerate(CAME):
 
         def row(k, carry):
             r = (angle[0] ^ s) * 8 + k
@@ -290,7 +308,7 @@
             pl.BlockSpec(memory_space=VM),
             pl.BlockSpec(memory_space=ANY),
         ]
-        + [pl.BlockSpec(memory_space=VM)] * 4,
+        + [pl.BlockSpec(memory_space=VM)] * 5,
         out_specs=pl.BlockSpec(memory_space=VM),
         scratch_shapes=[pltpu.VMEM((41, 2, 8, 128), BF16), pltpu.SemaphoreType.DMA],
         compiler_params=pltpu.CompilerParams(vmem_limit_bytes=GRANT),
@@ -298,9 +316,11 @@
     )(angle, code, recv, ops, *terms)
 
 
-def down_body(angle, f0, f1, f2, f3, theta, phi, cos_t, sin_t, keep, send, turned, whole):
-    far = (f0, f1, f2, f3)
-    for s, (which, place) in enumerate(CUBE):
+def down_body(angle, f0, f1, f2, f3, f4, theta_h, phi_h, cos_h, sin_h, keep, send, theta, phi, cos_t, sin_t, turned, whole, sems):
+    far = (f0, f1, f2, f3, f4)
+    for copy in fetch((theta_h, phi_h, cos_h, sin_h), (theta, phi, cos_t, sin_t), sems):
+        copy.wait()
+    for s, (which, place) in enumerate(CAME):
         at = pl.ds(pl.multiple_of((angle[0] ^ s) * 16, 16), 16)
         cos_s = [cos_t[t, at, :] for t in range(2)]
         sin_s = [sin_t[t, at, :] for t in range(2)]
@@ -335,17 +355,24 @@
                 (keep, send)[s % 2][s // 2, r, c] = whole[r * 2 + c, at, :].astype(BF16)
 
 
-def lower(angle, far, theta, phi, cos_t, sin_t):
+def lower(angle, far, tables):
     return pl.pallas_call(
         down_body,
         out_shape=(jax.ShapeDtypeStruct((4, 8, 2, 8, 128), BF16),) * 2,
-        in_specs=[pl.BlockSpec(memory_space=pltpu.SMEM)] + [pl.BlockSpec(memory_space=VM)] * 8,
+        in_specs=[pl.BlockSpec(memory_space=pltpu.SMEM)]
+        + [pl.BlockSpec(memory_space=VM)] * 5
+        + [pl.BlockSpec(memory_space=pltpu.HBM)] * 4,
         out_specs=(pl.BlockSpec(memory_space=VM),) * 2,
-        scratch_shapes=[pltpu.VMEM((16, PT, PP), BF16), pltpu.VMEM((16, CT, SUBBOX_HEADINGS), F32)],
+        scratch_shapes=[pltpu.VMEM(t.shape, t.dtype) for t in tables]
+        + [
+            pltpu.VMEM((16, PT, PP), BF16),
+            pltpu.VMEM((16, CT, SUBBOX_HEADINGS), F32),
+            pltpu.SemaphoreType.DMA((4,)),
+        ],
         cost_estimate=pl.CostEstimate(flops=300_000_000, bytes_accessed=2_000_000, transcendentals=0),
         compiler_params=pltpu.CompilerParams(vmem_limit_bytes=GRANT),
         name="lower",
-    )(angle, *far, theta, phi, cos_t, sin_t)
+    )(angle, *far, *tables)
 
 
 def groups(straight):
@@ -363,6 +390,15 @@
 def hop(x, step):
     pairs = [(g[i], g[(i + step) % SIDE]) for g in SPREAD for i in range(SIDE)]
     return lax.ppermute(x, BOTH, pairs)
+
+
+def ring(own):
+    forth, back = [own], [own]
+    for step in range(4):
+        forth.append(hop(forth[-1], 1))
+        if step < 3:
+            back.append(hop(back[-1], -1))
+    return back + [forth[8 - p] for p in range(4, 8)]
 
 
 def swap(x, axis, **kw):
@@ -394,29 +430,22 @@
     mine = jnp.where(core == 0, box // SIDE, box % SIDE)
     where = jnp.stack([core, mine]).astype(I32)
 
-    wanted, child_code, parent_code = plan(
-        where, child_list, child_op, child_home, parent_list, parent_op, parent_home
-    )
     whole = swap(child_field, "angle").reshape(8, 8, 2, 8, 128)
-    parents = swap(lift(whole, theta_up, phi_up, cos_t, sin_t), "angle")
-    own = jnp.concatenate([child_field.reshape(128, 8, 128), parents.reshape(128, 8, 128)])
-    forth, back = [own], [own]
-    for step in range(4):
-        if step == 1:
-            forth[1], wanted = lax.optimization_barrier((forth[1], wanted))
-        forth.append(hop(forth[-1], 1))
-        if step < 3:
-            back.append(hop(back[-1], -1))
+    wanted, child_code, parent_code = plan(where, child_list, child_op, child_home, parent_list, parent_op, parent_home)
+    parents = swap(lift(whole, (theta_up, phi_up, cos_t, sin_t)), "angle").reshape(128, 8, 128)
+    parent_blocks = ring(parents)
     asked = swap(wanted.reshape(SIDE, 1, 128), BOTH, axis_index_groups=TRADE).reshape(SIDE, 128)
-    blocks = back + [forth[8 - p] for p in range(4, 8)]
-
-    parents_out = select(asked, blocks, (64, 128), 16, 8, 16)
-    children_out = select(asked, blocks, (0, 0), 64, 2, 64)
+    parents_out = select(asked, parent_blocks, 64, 8, 16)
+    field, parents_out = lax.optimization_barrier((child_field, parents_out))
     parents_in = swap(parents_out, BOTH, axis_index_groups=TRADE)
+    child_blocks = ring(field.reshape(128, 8, 128))
+    children_out = select(asked, child_blocks, 0, 2, 64)
+    here = angle.reshape(1).astype(I32)
+    sums = far_parents(here, parent_code, parents_in.reshape(128, 8, 8, 128), parent_ops)
+    children_out, sums = lax.optimization_barrier((children_out, sums))
     children_in = swap(children_out, BOTH, axis_index_groups=TRADE)
-    here = angle.reshape(1).astype(I32)
-    far = cube(*far_parents(here, parent_code, parents_in.reshape(128, 8, 8, 128), parent_ops))
-    terms = cube(*lower(here, far, theta_down, phi_down, cos_t, sin_t))
+    far = trade(*sums)
+    terms = trade(*lower(here, far, (theta_down, phi_down, cos_t, sin_t)))
     return far_children(here, child_code, children_in.reshape(512, 2, 8, 128), child_ops, terms)
 
 

time: 182 us -> 187 us (1.027)
  the two profiles are of different devices: /device:TPU:24 before, /device:TPU:64 now
where the time goes in v3:
time: 187 us; the launch traced here: 186 us
  starting transfers between devices  81.2 us (43%)
  waiting for transfers between devices  43.7 us (23%)
  blocking collectives  37.9 us (20%)
  Pallas kernels  19.2 us (10%)
  local copies, waits for them, and re-layouts  3.59 us (2%)
    ppermute x14, starting transfers between devices, hop(): return lax.ppermute(x, BOTH, pairs)  43.6 us
    all_to_all x3, blocking collectives, swap(): lax.all_to_all(x, axis, split_axis=0, concat_axis=0, tiled=True, **kw)  37.9 us
    ppermute x14, waiting for transfers between devices, hop(): return lax.ppermute(x, BOTH, pairs)  33.4 us
    ppermute x8, starting transfers between devices, across(): return lax.ppermute(x, 'angle', [(i, i ^ bit) for i in range(8)])  24.8 us
    all_to_all x2, starting transfers between devices, swap(): lax.all_to_all(x, axis, split_axis=0, concat_axis=0, tiled=True, **kw)  12.8 us
    ppermute x8, waiting for transfers between devices, across(): return lax.ppermute(x, 'angle', [(i, i ^ bit) for i in range(8)])  10.2 us
    pallas_call x2, Pallas kernels, select(): pl.pallas_call(functools.partial(select_body, first), out_shape=jax.Shape...  5.15 us
    pallas_call x1, Pallas kernels, plan(): pl.pallas_call(plan_body, out_shape=(jax.ShapeDtypeStruct((SIDE, 128), I3...  4.01 us
  transfers between devices with their start and end apart: 24, of which 12 were waited for; matrix products, arithmetic and copies ran while one was open for 0% of the time, Pallas kernels for 5%

profile of v3, /device:TPU:64, one launch (start us, length us, event | category | flops | bytes accessed | tf_op | source)
XLA Modules:
  0.0 186.2 jit_solution(7434602435317611267)
XLA Ops:
  0.0 11.9 %all_to_all.25 = bf16[64,2,8,128]{3,2,1,0:T(8,128)(2,1)S(1)} all-to-all(bf16[64,2,8,128]{3,2,1,0:T(8,128)(2,1)} %param.15), channel_id=1, replica_groups=mesh['box'=64,'angle'=8] {'angle'}, dimensions={0} | all-to-all | bytes 524288 | tf_op jit(solution)/shard_map/all_to_all | solution.py:405
  12.0 0.9 copy-done.2
  12.9 0.9 copy-done.4
  13.9 0.8 copy-done.7
  14.7 0.8 copy-done.8
  15.5 1.8 lift.1
  17.3 9.9 %all_to_all.26 = bf16[8,2,8,8,128]{4,3,2,1,0:T(8,128)(2,1)S(1)} all-to-all(bf16[8,2,8,8,128]{4,3,2,1,0:T(8,128)(2,1)S(1)} %lift.1), channel_id=1, replica_groups=mesh['box'=64,'angle'=8] {'angle'}, dimensions={0} | all-to-all | bytes 524288 | tf_op jit(solution)/shard_map/all_to_all | solution.py:405
  27.2 3.5 %collective-permute-start.3 = (bf16[128,8,128]{2,1,0:T(8,128)(2,1)S(1)}, bf16[128,8,128]{2,1,0:T(8,128)(2,1)S(1)}, u32[]{:S(2)}, u32[]{:S(2)}) collective-permute-start(bf16[128,8,128]{2,1,0:T(8,128)(2,1)S(1)} %bitcast.23), channel_id=1, source_target_pairs={{0,64},{64,128},{128,192},{192,256},{256,320},{320,384},{384,448},... | collective-permute-start | bytes 786440 | tf_op jit(solution)/shard_map/ppermute | solution.py:392
  30.7 3.8 %collective-permute-start = (bf16[128,8,128]{2,1,0:T(8,128)(2,1)S(1)}, bf16[128,8,128]{2,1,0:T(8,128)(2,1)S(1)}, u32[]{:S(2)}, u32[]{:S(2)}) collective-permute-start(bf16[128,8,128]{2,1,0:T(8,128)(2,1)S(1)} %bitcast.24), channel_id=1, source_target_pairs={{0,448},{64,0},{128,64},{192,128},{256,192},{320,256},{384,320},{4... | collective-permute-start | bytes 786440 | tf_op jit(solution)/shard_map/ppermute | solution.py:392
  34.5 2.4 %collective-permute-done.3.refs_7_ = bf16[128,8,128]{2,1,0:T(8,128)(2,1)S(1)} collective-permute-done((bf16[128,8,128]{2,1,0:T(8,128)(2,1)S(1)}, bf16[128,8,128]{2,1,0:T(8,128)(2,1)S(1)}, u32[]{:S(2)}, u32[]{:S(2)}) %collective-permute-start.3) | collective-permute-done | bytes 262176 | tf_op jit(solution)/shard_map/ppermute | solution.py:392
  36.9 2.0 %collective-permute-start.4 = (bf16[128,8,128]{2,1,0:T(8,128)(2,1)S(1)}, bf16[128,8,128]{2,1,0:T(8,128)(2,1)S(1)}, u32[]{:S(2)}, u32[]{:S(2)}) collective-permute-start(bf16[128,8,128]{2,1,0:T(8,128)(2,1)S(1)} %collective-permute-done.3.refs_7_), channel_id=1, source_target_pairs={{0,64},{64,128},{128,192},{192,256},{256,320},{320,384},{384,448},... | collective-permute-start | bytes 786440 | tf_op jit(solution)/shard_map/ppermute | solution.py:392
  39.0 0.0 collective-permute-done.refs_1_
  39.0 5.0 %collective-permute-start.1 = (bf16[128,8,128]{2,1,0:T(8,128)(2,1)S(1)}, bf16[128,8,128]{2,1,0:T(8,128)(2,1)S(1)}, u32[]{:S(2)}, u32[]{:S(2)}) collective-permute-start(bf16[128,8,128]{2,1,0:T(8,128)(2,1)S(1)} %collective-permute-done.refs_1_), channel_id=1, source_target_pairs={{0,448},{64,0},{128,64},{192,128},{256,192},{320,256},{384,320},{4... | collective-permute-start | bytes 786440 | tf_op jit(solution)/shard_map/ppermute | solution.py:392
  44.0 2.4 %collective-permute-done.4.refs_6_ = bf16[128,8,128]{2,1,0:T(8,128)(2,1)S(1)} collective-permute-done((bf16[128,8,128]{2,1,0:T(8,128)(2,1)S(1)}, bf16[128,8,128]{2,1,0:T(8,128)(2,1)S(1)}, u32[]{:S(2)}, u32[]{:S(2)}) %collective-permute-start.4) | collective-permute-done | bytes 262176 | tf_op jit(solution)/shard_map/ppermute | solution.py:392
  46.4 1.9 %collective-permute-start.5 = (bf16[128,8,128]{2,1,0:T(8,128)(2,1)S(1)}, bf16[128,8,128]{2,1,0:T(8,128)(2,1)S(1)}, u32[]{:S(2)}, u32[]{:S(2)}) collective-permute-start(bf16[128,8,128]{2,1,0:T(8,128)(2,1)S(1)} %collective-permute-done.4.refs_6_), channel_id=1, source_target_pairs={{0,64},{64,128},{128,192},{192,256},{256,320},{320,384},{384,448},... | collective-permute-start | bytes 786440 | tf_op jit(solution)/shard_map/ppermute | solution.py:392
  48.3 5.1 %collective-permute-start.2 = (bf16[128,8,128]{2,1,0:T(8,128)(2,1)S(1)}, bf16[128,8,128]{2,1,0:T(8,128)(2,1)S(1)}, u32[]{:S(2)}, u32[]{:S(2)}) collective-permute-start(bf16[128,8,128]{2,1,0:T(8,128)(2,1)S(1)} %collective-permute-done.1.refs_2_), channel_id=1, source_target_pairs={{0,448},{64,0},{128,64},{192,128},{256,192},{320,256},{384,320},{4... | collective-permute-start | bytes 786440 | tf_op jit(solution)/shard_map/ppermute | solution.py:392
  53.5 2.4 %collective-permute-done.5.refs_5_ = bf16[128,8,128]{2,1,0:T(8,128)(2,1)S(1)} collective-permute-done((bf16[128,8,128]{2,1,0:T(8,128)(2,1)S(1)}, bf16[128,8,128]{2,1,0:T(8,128)(2,1)S(1)}, u32[]{:S(2)}, u32[]{:S(2)}) %collective-permute-start.5) | collective-permute-done | bytes 262176 | tf_op jit(solution)/shard_map/ppermute | solution.py:392
  55.9 1.9 %collective-permute-start.6 = (bf16[128,8,128]{2,1,0:T(8,128)(2,1)S(1)}, bf16[128,8,128]{2,1,0:T(8,128)(2,1)S(1)}, u32[]{:S(2)}, u32[]{:S(2)}) collective-permute-start(bf16[128,8,128]{2,1,0:T(8,128)(2,1)S(1)} %collective-permute-done.5.refs_5_), channel_id=1, source_target_pairs={{0,64},{64,128},{128,192},{192,256},{256,320},{320,384},{384,448},... | collective-permute-start | bytes 786440 | tf_op jit(solution)/shard_map/ppermute | solution.py:392
  57.8 0.1 pad_add_fusion.where
  57.9 4.0 %plan.1 = (s32[8,128]{1,0:T(8,128)S(1)}, s32[8,64]{1,0:T(8,128)S(1)}, s32[8,16]{1,0:T(8,128)S(1)}) custom-call(s32[2]{0:T(128)S(1)} %pad_add_fusion.where, s32[8,64]{1,0:T(8,128)S(1)} %bitcast.30, s32[8,64]{1,0:T(8,128)S(1)} %bitcast.31, s32[32,128]{1,0:T(8,128)S(1)} %bitcast.29, s32[8,16]{1,0:T(8,128)S(1)} %bitcast.32, s32[8,16]{1,0:T(8,128)S(1)} %bitcast.33, ...), custom_call_target="tpu_custom_call" | custom-call | tf_op jit(solution)/shard_map/plan/pallas_call | solution.py:111
  61.9 16.0 %all_to_all.27 = s32[8,1,128]{2,1,0:T(1,128)S(1)} all-to-all(s32[8,1,128]{2,1,0:T(1,128)S(1)} %bitcast.35), channel_id=1, replica_groups={{0,8,16,24,32,40,48,56},{64,72,80,88,96,104,112,120},{128,136,144,152,1..., dimensions={0} | all-to-all | bytes 8192 | tf_op jit(solution)/shard_map/all_to_all | solution.py:405
  78.0 0.0 collective-permute-done.2.refs_3_
  78.0 0.0 collective-permute-done.6.refs_4_
  78.0 2.3 %shard_map.145 = bf16[8,16,8,8,128]{4,3,2,1,0:T(8,128)(2,1)} custom-call(s32[8,128]{1,0:T(8,128)S(1)} %bitcast.27, bf16[128,8,128]{2,1,0:T(8,128)(2,1)S(1)} %bitcast.25, bf16[128,8,128]{2,1,0:T(8,128)(2,1)S(1)} %collective-permute-done.refs_1_, bf16[128,8,128]{2,1,0:T(8,128)(2,1)S(1)} %collective-permute-done.1.refs_2_, ...), custom_call_target="tpu_custom_call" | custom-call | bytes 4000000 | tf_op jit(solution)/shard_map/pallas_call | solution.py:198
  80.3 0.0 copy-start
  80.3 5.1 %all-to-all-start.3 = ((bf16[8,16,8,8,128]{4,3,2,1,0:T(8,128)(2,1)}), bf16[8,16,8,8,128]{4,3,2,1,0:T(8,128)(2,1)S(1)}, u32[]{:S(2)}, u32[]{:S(2)}) async-start(bf16[8,16,8,8,128]{4,3,2,1,0:T(8,128)(2,1)} %shard_map.145), calls=%async_computation.3 | async-start | bytes 4194304 | tf_op jit(solution)/shard_map/all_to_all | solution.py:405
  85.4 2.0 %collective-permute-start.10 = (bf16[128,8,128]{2,1,0:T(8,128)(2,1)S(1)}, bf16[128,8,128]{2,1,0:T(8,128)(2,1)S(1)}, u32[]{:S(2)}, u32[]{:S(2)}) collective-permute-start(bf16[128,8,128]{2,1,0:T(8,128)(2,1)S(1)} %bitcast.20), channel_id=1, source_target_pairs={{0,64},{64,128},{128,192},{192,256},{256,320},{320,384},{384,448},... | collective-permute-start | bytes 786440 | tf_op jit(solution)/shard_map/ppermute | solution.py:392
  87.4 5.1 %collective-permute-start.7 = (bf16[128,8,128]{2,1,0:T(8,128)(2,1)S(1)}, bf16[128,8,128]{2,1,0:T(8,128)(2,1)S(1)}, u32[]{:S(2)}, u32[]{:S(2)}) collective-permute-start(bf16[128,8,128]{2,1,0:T(8,128)(2,1)S(1)} %bitcast.21), channel_id=1, source_target_pairs={{0,448},{64,0},{128,64},{192,128},{256,192},{320,256},{384,320},{4... | collective-permute-start | bytes 786440 | tf_op jit(solution)/shard_map/ppermute | solution.py:392
  92.6 7.6 %collective-permute-done.10.refs_7_ = bf16[128,8,128]{2,1,0:T(8,128)(2,1)S(1)} collective-permute-done((bf16[128,8,128]{2,1,0:T(8,128)(2,1)S(1)}, bf16[128,8,128]{2,1,0:T(8,128)(2,1)S(1)}, u32[]{:S(2)}, u32[]{:S(2)}) %collective-permute-start.10) | collective-permute-done | bytes 262176 | tf_op jit(solution)/shard_map/ppermute | solution.py:392
  100.2 1.9 %collective-permute-start.11 = (bf16[128,8,128]{2,1,0:T(8,128)(2,1)S(1)}, bf16[128,8,128]{2,1,0:T(8,128)(2,1)S(1)}, u32[]{:S(2)}, u32[]{:S(2)}) collective-permute-start(bf16[128,8,128]{2,1,0:T(8,128)(2,1)S(1)} %collective-permute-done.10.refs_7_), channel_id=1, source_target_pairs={{0,64},{64,128},{128,192},{192,256},{256,320},{320,384},{384,448},... | collective-permute-start | bytes 786440 | tf_op jit(solution)/shard_map/ppermute | solution.py:392
  102.1 3.4 %collective-permute-done.7.refs_1_ = bf16[128,8,128]{2,1,0:T(8,128)(2,1)S(1)} collective-permute-done((bf16[128,8,128]{2,1,0:T(8,128)(2,1)S(1)}, bf16[128,8,128]{2,1,0:T(8,128)(2,1)S(1)}, u32[]{:S(2)}, u32[]{:S(2)}) %collective-permute-start.7) | collective-permute-done | bytes 262176 | tf_op jit(solution)/shard_map/ppermute | solution.py:392
  105.5 2.3 %collective-permute-start.8 = (bf16[128,8,128]{2,1,0:T(8,128)(2,1)S(1)}, bf16[128,8,128]{2,1,0:T(8,128)(2,1)S(1)}, u32[]{:S(2)}, u32[]{:S(2)}) collective-permute-start(bf16[128,8,128]{2,1,0:T(8,128)(2,1)S(1)} %collective-permute-done.7.refs_1_), channel_id=1, source_target_pairs={{0,448},{64,0},{128,64},{192,128},{256,192},{320,256},{384,320},{4... | collective-permute-start | bytes 786440 | tf_op jit(solution)/shard_map/ppermute | solution.py:392
  107.8 5.3 %collective-permute-done.11.refs_6_ = bf16[128,8,128]{2,1,0:T(8,128)(2,1)S(1)} collective-permute-done((bf16[128,8,128]{2,1,0:T(8,128)(2,1)S(1)}, bf16[128,8,128]{2,1,0:T(8,128)(2,1)S(1)}, u32[]{:S(2)}, u32[]{:S(2)}) %collective-permute-start.11) | collective-permute-done | bytes 262176 | tf_op jit(solution)/shard_map/ppermute | solution.py:392
  113.0 1.9 %collective-permute-start.12 = (bf16[128,8,128]{2,1,0:T(8,128)(2,1)S(1)}, bf16[128,8,128]{2,1,0:T(8,128)(2,1)S(1)}, u32[]{:S(2)}, u32[]{:S(2)}) collective-permute-start(bf16[128,8,128]{2,1,0:T(8,128)(2,1)S(1)} %collective-permute-done.11.refs_6_), channel_id=1, source_target_pairs={{0,64},{64,128},{128,192},{192,256},{256,320},{320,384},{384,448},... | collective-permute-start | bytes 786440 | tf_op jit(solution)/shard_map/ppermute | solution.py:392
  115.0 5.1 %collective-permute-start.9 = (bf16[128,8,128]{2,1,0:T(8,128)(2,1)S(1)}, bf16[128,8,128]{2,1,0:T(8,128)(2,1)S(1)}, u32[]{:S(2)}, u32[]{:S(2)}) collective-permute-start(bf16[128,8,128]{2,1,0:T(8,128)(2,1)S(1)} %collective-permute-done.8.refs_2_), channel_id=1, source_target_pairs={{0,448},{64,0},{128,64},{192,128},{256,192},{320,256},{384,320},{4... | collective-permute-start | bytes 786440 | tf_op jit(solution)/shard_map/ppermute | solution.py:392
  120.1 2.4 %collective-permute-done.12.refs_5_ = bf16[128,8,128]{2,1,0:T(8,128)(2,1)S(1)} collective-permute-done((bf16[128,8,128]{2,1,0:T(8,128)(2,1)S(1)}, bf16[128,8,128]{2,1,0:T(8,128)(2,1)S(1)}, u32[]{:S(2)}, u32[]{:S(2)}) %collective-permute-start.12) | collective-permute-done | bytes 262176 | tf_op jit(solution)/shard_map/ppermute | solution.py:392
  122.5 1.9 %collective-permute-start.13 = (bf16[128,8,128]{2,1,0:T(8,128)(2,1)S(1)}, bf16[128,8,128]{2,1,0:T(8,128)(2,1)S(1)}, u32[]{:S(2)}, u32[]{:S(2)}) collective-permute-start(bf16[128,8,128]{2,1,0:T(8,128)(2,1)S(1)} %collective-permute-done.12.refs_5_), channel_id=1, source_target_pairs={{0,64},{64,128},{128,192},{192,256},{256,320},{320,384},{384,448},... | collective-permute-start | bytes 786440 | tf_op jit(solution)/shard_map/ppermute | solution.py:392
  124.4 7.5 %collective-permute-done.13.refs_4_ = bf16[128,8,128]{2,1,0:T(8,128)(2,1)S(1)} collective-permute-done((bf16[128,8,128]{2,1,0:T(8,128)(2,1)S(1)}, bf16[128,8,128]{2,1,0:T(8,128)(2,1)S(1)}, u32[]{:S(2)}, u32[]{:S(2)}) %collective-permute-start.13) | collective-permute-done | bytes 262176 | tf_op jit(solution)/shard_map/ppermute | solution.py:392
  132.0 2.9 %shard_map.146 = bf16[8,64,2,8,128]{4,3,2,1,0:T(8,128)(2,1)} custom-call(s32[8,128]{1,0:T(8,128)S(1)} %bitcast.28, bf16[128,8,128]{2,1,0:T(8,128)(2,1)S(1)} %bitcast.22, bf16[128,8,128]{2,1,0:T(8,128)(2,1)S(1)} %collective-permute-done.7.refs_1_, bf16[128,8,128]{2,1,0:T(8,128)(2,1)S(1)} %collective-permute-done.8.refs_2_, ...), custom_call_target="tpu_custom_call" | custom-call | bytes 4000000 | tf_op jit(solution)/shard_map/pallas_call | solution.py:198
  134.8 0.0 all-to-all-done.3
  134.9 1.7 far_parents.1
  136.6 0.0 copy-start.3
  136.6 0.0 copy-start.5
  136.6 0.0 copy-start.15
  136.7 0.0 copy-start.16
  136.7 7.7 %all-to-all-start.4 = ((bf16[8,64,2,8,128]{4,3,2,1,0:T(8,128)(2,1)}), bf16[8,64,2,8,128]{4,3,2,1,0:T(8,128)(2,1)S(1)}, u32[]{:S(2)}, u32[]{:S(2)}) async-start(bf16[8,64,2,8,128]{4,3,2,1,0:T(8,128)(2,1)} %shard_map.146), calls=%async_computation.4 | async-start | bytes 4194304 | tf_op jit(solution)/shard_map/all_to_all | solution.py:405
  144.4 2.0 %collective-permute-start.14 = (bf16[4,2,8,8,128]{4,3,2,1,0:T(8,128)(2,1)S(1)}, bf16[4,2,8,8,128]{4,3,2,1,0:T(8,128)(2,1)S(1)}, u32[]{:S(2)}, u32[]{:S(2)}) collective-permute-start(bf16[4,2,8,8,128]{4,3,2,1,0:T(8,128)(2,1)S(1)} %get-tuple-element.26), channel_id=1, source_target_pairs={{0,1},{1,0},{2,3},{3,2},{4,5},{5,4},{6,7},{7,6},{8,9},{9,8},{10,11... | collective-permute-start | bytes 393224 | tf_op jit(solution)/shard_map/ppermute | solution.py:268
  146.4 1.3 collective-permute-done.14.f1
  147.8 2.5 %collective-permute-start.15 = (bf16[2,2,8,8,128]{4,3,2,1,0:T(8,128)(2,1)S(1)}, bf16[2,2,8,8,128]{4,3,2,1,0:T(8,128)(2,1)S(1)}, u32[]{:S(2)}, u32[]{:S(2)}) collective-permute-start(bf16[2,2,8,8,128]{4,3,2,1,0:T(8,128)(2,1)S(1)} %pad_maximum_fusion), channel_id=1, source_target_pairs={{0,2},{1,3},{2,0},{3,1},{4,6},{5,7},{6,4},{7,5},{8,10},{9,11},{10,... | collective-permute-start | bytes 196616 | tf_op jit(solution)/shard_map/ppermute | solution.py:268
  150.3 4.0 %collective-permute-start.16 = (bf16[2,2,8,8,128]{4,3,2,1,0:T(8,128)(2,1)S(1)}, bf16[2,2,8,8,128]{4,3,2,1,0:T(8,128)(2,1)S(1)}, u32[]{:S(2)}, u32[]{:S(2)}) collective-permute-start(bf16[2,2,8,8,128]{4,3,2,1,0:T(8,128)(2,1)S(1)} %pad_maximum_fusion.1), channel_id=1, source_target_pairs={{0,4},{1,5},{2,6},{3,7},{4,0},{5,1},{6,2},{7,3},{8,12},{9,13},{10,... | collective-permute-start | bytes 196616 | tf_op jit(solution)/shard_map/ppermute | solution.py:268
  154.3 4.0 %collective-permute-start.17 = (bf16[2,2,8,8,128]{4,3,2,1,0:T(8,128)(2,1)S(1)}, bf16[2,2,8,8,128]{4,3,2,1,0:T(8,128)(2,1)S(1)}, u32[]{:S(2)}, u32[]{:S(2)}) collective-permute-start(bf16[2,2,8,8,128]{4,3,2,1,0:T(8,128)(2,1)S(1)} %pad_maximum_fusion.2), channel_id=1, source_target_pairs={{0,6},{1,7},{2,4},{3,5},{4,2},{5,3},{6,0},{7,1},{8,14},{9,15},{10,... | collective-permute-start | bytes 196616 | tf_op jit(solution)/shard_map/ppermute | solution.py:268
  158.2 0.0 collective-permute-done.15.f2
  158.3 0.0 collective-permute-done.16.f3
  158.3 3.4 %collective-permute-done.17.f4 = bf16[2,2,8,8,128]{4,3,2,1,0:T(8,128)(2,1)S(1)} collective-permute-done((bf16[2,2,8,8,128]{4,3,2,1,0:T(8,128)(2,1)S(1)}, bf16[2,2,8,8,128]{4,3,2,1,0:T(8,128)(2,1)S(1)}, u32[]{:S(2)}, u32[]{:S(2)}) %collective-permute-start.17) | collective-permute-done | bytes 65568 | tf_op jit(solution)/shard_map/ppermute | solution.py:268
  161.6 3.2 %lower.1 = (bf16[4,8,2,8,128]{4,3,2,1,0:T(8,128)(2,1)S(1)}, bf16[4,8,2,8,128]{4,3,2,1,0:T(8,128)(2,1)S(1)}) custom-call(s32[1]{0:T(128)} %bitcast.angle, bf16[4,2,8,8,128]{4,3,2,1,0:T(8,128)(2,1)S(1)} %get-tuple-element.25.f0, bf16[4,2,8,8,128]{4,3,2,1,0:T(8,128)(2,1)S(1)} %collective-permute-done.14.f1, ...), custom_call_target="tpu_custom_call" | custom-call | flops 300000000 | bytes 2000000 | tf_op jit(solution)/shard_map/lower/pallas_call | solution.py:359
  164.9 1.9 %collective-permute-start.18 = (bf16[4,8,2,8,128]{4,3,2,1,0:T(8,128)(2,1)S(1)}, bf16[4,8,2,8,128]{4,3,2,1,0:T(8,128)(2,1)S(1)}, u32[]{:S(2)}, u32[]{:S(2)}) collective-permute-start(bf16[4,8,2,8,128]{4,3,2,1,0:T(8,128)(2,1)S(1)} %get-tuple-element.28), channel_id=1, source_target_pairs={{0,1},{1,0},{2,3},{3,2},{4,5},{5,4},{6,7},{7,6},{8,9},{9,8},{10,11... | collective-permute-start | bytes 393224 | tf_op jit(solution)/shard_map/ppermute | solution.py:268
  166.8 1.3 collective-permute-done.18.t1
  168.1 1.9 %collective-permute-start.19 = (bf16[2,8,2,8,128]{4,3,2,1,0:T(8,128)(2,1)S(1)}, bf16[2,8,2,8,128]{4,3,2,1,0:T(8,128)(2,1)S(1)}, u32[]{:S(2)}, u32[]{:S(2)}) collective-permute-start(bf16[2,8,2,8,128]{4,3,2,1,0:T(8,128)(2,1)S(1)} %pad_maximum_fusion.3), channel_id=1, source_target_pairs={{0,2},{1,3},{2,0},{3,1},{4,6},{5,7},{6,4},{7,5},{8,10},{9,11},{10,... | collective-permute-start | bytes 196616 | tf_op jit(solution)/shard_map/ppermute | solution.py:268
  170.1 5.4 %collective-permute-start.20 = (bf16[2,8,2,8,128]{4,3,2,1,0:T(8,128)(2,1)S(1)}, bf16[2,8,2,8,128]{4,3,2,1,0:T(8,128)(2,1)S(1)}, u32[]{:S(2)}, u32[]{:S(2)}) collective-permute-start(bf16[2,8,2,8,128]{4,3,2,1,0:T(8,128)(2,1)S(1)} %pad_maximum_fusion.4), channel_id=1, source_target_pairs={{0,4},{1,5},{2,6},{3,7},{4,0},{5,1},{6,2},{7,3},{8,12},{9,13},{10,... | collective-permute-start | bytes 196616 | tf_op jit(solution)/shard_map/ppermute | solution.py:268
  175.5 3.1 %collective-permute-start.21 = (bf16[2,8,2,8,128]{4,3,2,1,0:T(8,128)(2,1)S(1)}, bf16[2,8,2,8,128]{4,3,2,1,0:T(8,128)(2,1)S(1)}, u32[]{:S(2)}, u32[]{:S(2)}) collective-permute-start(bf16[2,8,2,8,128]{4,3,2,1,0:T(8,128)(2,1)S(1)} %pad_maximum_fusion.5), channel_id=1, source_target_pairs={{0,6},{1,7},{2,4},{3,5},{4,2},{5,3},{6,0},{7,1},{8,14},{9,15},{10,... | collective-permute-start | bytes 196616 | tf_op jit(solution)/shard_map/ppermute | solution.py:268
  178.6 0.0 collective-permute-done.19.t2
  178.6 4.3 %collective-permute-done.21.t4 = bf16[2,8,2,8,128]{4,3,2,1,0:T(8,128)(2,1)S(1)} collective-permute-done((bf16[2,8,2,8,128]{4,3,2,1,0:T(8,128)(2,1)S(1)}, bf16[2,8,2,8,128]{4,3,2,1,0:T(8,128)(2,1)S(1)}, u32[]{:S(2)}, u32[]{:S(2)}) %collective-permute-start.21) | collective-permute-done | bytes 65568 | tf_op jit(solution)/shard_map/ppermute | solution.py:268
  182.9 0.0 all-to-all-done.4
  182.9 3.2 %far_children.1 = bf16[64,2,8,128]{3,2,1,0:T(8,128)(2,1)} custom-call(s32[1]{0:T(128)} %bitcast.angle, s32[8,64]{1,0:T(8,128)S(1)} %get-tuple-element.17.code, bf16[512,2,8,128]{3,2,1,0:T(8,128)(2,1)S(1)} %bitcast.18, bf16[40,2,8,128]{3,2,1,0:T(8,128)(2,1)S(1)} %copy-done.6, bf16[4,8,2,8,128]{4,3,2,1,0:T(8,128)(2,1)S(1)} %get-tuple-element.27.t0, ...), custom_call_target="tpu_custom_call" | custom-call | tf_op jit(solution)/shard_map/far_children/pallas_call | solution.py:302
  (39 shorter events, 0.1 us)
Async XLA Ops:
  0.0 57.9 %copy-start.14 = (s32[1024]{0:T(1024)S(1)}, s32[1024]{0:T(1024)}, u32[]{:S(2)}) copy-start(s32[1024]{0:T(1024)} %param.22) | copy-start | bytes 12292
  0.0 57.9 %copy-start.13 = (s32[16,8]{0,1:T(8,128)S(1)}, s32[16,8]{0,1:T(8,128)}, u32[]{:S(2)}) copy-start(s32[16,8]{0,1:T(8,128)} %param.21) | copy-start | bytes 1540
  0.0 57.9 %copy-start.12 = (s32[16,8]{0,1:T(8,128)S(1)}, s32[16,8]{0,1:T(8,128)}, u32[]{:S(2)}) copy-start(s32[16,8]{0,1:T(8,128)} %param.20) | copy-start | bytes 1540
  0.0 57.9 %copy-start.9 = (s32[4096]{0:T(1024)S(1)}, s32[4096]{0:T(1024)}, u32[]{:S(2)}) copy-start(s32[4096]{0:T(1024)} %param.18) | copy-start | bytes 49156
  0.0 57.9 %copy-start.11 = (s32[64,8]{0,1:T(8,128)S(1)}, s32[64,8]{0,1:T(8,128)}, u32[]{:S(2)}) copy-start(s32[64,8]{0,1:T(8,128)} %param.17) | copy-start | bytes 6148
  0.0 57.9 %copy-start.10 = (s32[64,8]{0,1:T(8,128)S(1)}, s32[64,8]{0,1:T(8,128)}, u32[]{:S(2)}) copy-start(s32[64,8]{0,1:T(8,128)} %param.16) | copy-start | bytes 6148
  12.0 1.0 copy-start.2
  12.9 0.9 copy-start.4
  13.9 0.8 copy-start.7
  14.7 0.8 copy-start.8
  27.2 9.7 %collective-permute-start.3 = (bf16[128,8,128]{2,1,0:T(8,128)(2,1)S(1)}, bf16[128,8,128]{2,1,0:T(8,128)(2,1)S(1)}, u32[]{:S(2)}, u32[]{:S(2)}) collective-permute-start(bf16[128,8,128]{2,1,0:T(8,128)(2,1)S(1)} %bitcast.23), channel_id=1, source_target_pairs={{0,64},{64,128},{128,192},{192,256},{256,320},{320,384},{384,448},... | collective-permute-start | bytes 786440 | tf_op jit(solution)/shard_map/ppermute | solution.py:392
  30.7 8.3 %collective-permute-start = (bf16[128,8,128]{2,1,0:T(8,128)(2,1)S(1)}, bf16[128,8,128]{2,1,0:T(8,128)(2,1)S(1)}, u32[]{:S(2)}, u32[]{:S(2)}) collective-permute-start(bf16[128,8,128]{2,1,0:T(8,128)(2,1)S(1)} %bitcast.24), channel_id=1, source_target_pairs={{0,448},{64,0},{128,64},{192,128},{256,192},{320,256},{384,320},{4... | collective-permute-start | bytes 786440 | tf_op jit(solution)/shard_map/ppermute | solution.py:392
  36.9 9.5 %collective-permute-start.4 = (bf16[128,8,128]{2,1,0:T(8,128)(2,1)S(1)}, bf16[128,8,128]{2,1,0:T(8,128)(2,1)S(1)}, u32[]{:S(2)}, u32[]{:S(2)}) collective-permute-start(bf16[128,8,128]{2,1,0:T(8,128)(2,1)S(1)} %collective-permute-done.3.refs_7_), channel_id=1, source_target_pairs={{0,64},{64,128},{128,192},{192,256},{256,320},{320,384},{384,448},... | collective-permute-start | bytes 786440 | tf_op jit(solution)/shard_map/ppermute | solution.py:392
  39.0 9.3 %collective-permute-start.1 = (bf16[128,8,128]{2,1,0:T(8,128)(2,1)S(1)}, bf16[128,8,128]{2,1,0:T(8,128)(2,1)S(1)}, u32[]{:S(2)}, u32[]{:S(2)}) collective-permute-start(bf16[128,8,128]{2,1,0:T(8,128)(2,1)S(1)} %collective-permute-done.refs_1_), channel_id=1, source_target_pairs={{0,448},{64,0},{128,64},{192,128},{256,192},{320,256},{384,320},{4... | collective-permute-start | bytes 786440 | tf_op jit(solution)/shard_map/ppermute | solution.py:392
  46.4 9.5 %collective-permute-start.5 = (bf16[128,8,128]{2,1,0:T(8,128)(2,1)S(1)}, bf16[128,8,128]{2,1,0:T(8,128)(2,1)S(1)}, u32[]{:S(2)}, u32[]{:S(2)}) collective-permute-start(bf16[128,8,128]{2,1,0:T(8,128)(2,1)S(1)} %collective-permute-done.4.refs_6_), channel_id=1, source_target_pairs={{0,64},{64,128},{128,192},{192,256},{256,320},{320,384},{384,448},... | collective-permute-start | bytes 786440 | tf_op jit(solution)/shard_map/ppermute | solution.py:392
  48.3 29.6 %collective-permute-start.2 = (bf16[128,8,128]{2,1,0:T(8,128)(2,1)S(1)}, bf16[128,8,128]{2,1,0:T(8,128)(2,1)S(1)}, u32[]{:S(2)}, u32[]{:S(2)}) collective-permute-start(bf16[128,8,128]{2,1,0:T(8,128)(2,1)S(1)} %collective-permute-done.1.refs_2_), channel_id=1, source_target_pairs={{0,448},{64,0},{128,64},{192,128},{256,192},{320,256},{384,320},{4... | collective-permute-start | bytes 786440 | tf_op jit(solution)/shard_map/ppermute | solution.py:392
  55.9 22.1 %collective-permute-start.6 = (bf16[128,8,128]{2,1,0:T(8,128)(2,1)S(1)}, bf16[128,8,128]{2,1,0:T(8,128)(2,1)S(1)}, u32[]{:S(2)}, u32[]{:S(2)}) collective-permute-start(bf16[128,8,128]{2,1,0:T(8,128)(2,1)S(1)} %collective-permute-done.5.refs_5_), channel_id=1, source_target_pairs={{0,64},{64,128},{128,192},{192,256},{256,320},{320,384},{384,448},... | collective-permute-start | bytes 786440 | tf_op jit(solution)/shard_map/ppermute | solution.py:392
  80.3 5.1 %copy-start = (bf16[64,2,8,128]{3,2,1,0:T(8,128)(2,1)S(1)}, bf16[64,2,8,128]{3,2,1,0:T(8,128)(2,1)}, u32[]{:S(2)}) copy-start(bf16[64,2,8,128]{3,2,1,0:T(8,128)(2,1)} %param.15) | copy-start | bytes 786436
  80.3 54.6 %all-to-all-start.3 = ((bf16[8,16,8,8,128]{4,3,2,1,0:T(8,128)(2,1)}), bf16[8,16,8,8,128]{4,3,2,1,0:T(8,128)(2,1)S(1)}, u32[]{:S(2)}, u32[]{:S(2)}) async-start(bf16[8,16,8,8,128]{4,3,2,1,0:T(8,128)(2,1)} %shard_map.145), calls=%async_computation.3 | async-start | bytes 4194304 | tf_op jit(solution)/shard_map/all_to_all | solution.py:405
  85.4 49.5 %copy-start.1 = (bf16[40,2,16,256]{3,2,1,0:T(8,128)(2,1)S(1)}, bf16[40,2,16,256]{3,2,1,0:T(8,128)(2,1)}, u32[]{:S(2)}) copy-start(bf16[40,2,16,256]{3,2,1,0:T(8,128)(2,1)} %ops_hbm.2) | copy-start | bytes 1966084
  85.4 14.8 %collective-permute-start.10 = (bf16[128,8,128]{2,1,0:T(8,128)(2,1)S(1)}, bf16[128,8,128]{2,1,0:T(8,128)(2,1)S(1)}, u32[]{:S(2)}, u32[]{:S(2)}) collective-permute-start(bf16[128,8,128]{2,1,0:T(8,128)(2,1)S(1)} %bitcast.20), channel_id=1, source_target_pairs={{0,64},{64,128},{128,192},{192,256},{256,320},{320,384},{384,448},... | collective-permute-start | bytes 786440 | tf_op jit(solution)/shard_map/ppermute | solution.py:392
  87.4 18.1 %collective-permute-start.7 = (bf16[128,8,128]{2,1,0:T(8,128)(2,1)S(1)}, bf16[128,8,128]{2,1,0:T(8,128)(2,1)S(1)}, u32[]{:S(2)}, u32[]{:S(2)}) collective-permute-start(bf16[128,8,128]{2,1,0:T(8,128)(2,1)S(1)} %bitcast.21), channel_id=1, source_target_pairs={{0,448},{64,0},{128,64},{192,128},{256,192},{320,256},{384,320},{4... | collective-permute-start | bytes 786440 | tf_op jit(solution)/shard_map/ppermute | solution.py:392
  100.2 12.8 %collective-permute-start.11 = (bf16[128,8,128]{2,1,0:T(8,128)(2,1)S(1)}, bf16[128,8,128]{2,1,0:T(8,128)(2,1)S(1)}, u32[]{:S(2)}, u32[]{:S(2)}) collective-permute-start(bf16[128,8,128]{2,1,0:T(8,128)(2,1)S(1)} %collective-permute-done.10.refs_7_), channel_id=1, source_target_pairs={{0,64},{64,128},{128,192},{192,256},{256,320},{320,384},{384,448},... | collective-permute-start | bytes 786440 | tf_op jit(solution)/shard_map/ppermute | solution.py:392
  105.5 9.4 %collective-permute-start.8 = (bf16[128,8,128]{2,1,0:T(8,128)(2,1)S(1)}, bf16[128,8,128]{2,1,0:T(8,128)(2,1)S(1)}, u32[]{:S(2)}, u32[]{:S(2)}) collective-permute-start(bf16[128,8,128]{2,1,0:T(8,128)(2,1)S(1)} %collective-permute-done.7.refs_1_), channel_id=1, source_target_pairs={{0,448},{64,0},{128,64},{192,128},{256,192},{320,256},{384,320},{4... | collective-permute-start | bytes 786440 | tf_op jit(solution)/shard_map/ppermute | solution.py:392
  113.0 9.5 %collective-permute-start.12 = (bf16[128,8,128]{2,1,0:T(8,128)(2,1)S(1)}, bf16[128,8,128]{2,1,0:T(8,128)(2,1)S(1)}, u32[]{:S(2)}, u32[]{:S(2)}) collective-permute-start(bf16[128,8,128]{2,1,0:T(8,128)(2,1)S(1)} %collective-permute-done.11.refs_6_), channel_id=1, source_target_pairs={{0,64},{64,128},{128,192},{192,256},{256,320},{320,384},{384,448},... | collective-permute-start | bytes 786440 | tf_op jit(solution)/shard_map/ppermute | solution.py:392
  115.0 9.5 %collective-permute-start.9 = (bf16[128,8,128]{2,1,0:T(8,128)(2,1)S(1)}, bf16[128,8,128]{2,1,0:T(8,128)(2,1)S(1)}, u32[]{:S(2)}, u32[]{:S(2)}) collective-permute-start(bf16[128,8,128]{2,1,0:T(8,128)(2,1)S(1)} %collective-permute-done.8.refs_2_), channel_id=1, source_target_pairs={{0,448},{64,0},{128,64},{192,128},{256,192},{320,256},{384,320},{4... | collective-permute-start | bytes 786440 | tf_op jit(solution)/shard_map/ppermute | solution.py:392
  122.5 9.5 %collective-permute-start.13 = (bf16[128,8,128]{2,1,0:T(8,128)(2,1)S(1)}, bf16[128,8,128]{2,1,0:T(8,128)(2,1)S(1)}, u32[]{:S(2)}, u32[]{:S(2)}) collective-permute-start(bf16[128,8,128]{2,1,0:T(8,128)(2,1)S(1)} %collective-permute-done.12.refs_5_), channel_id=1, source_target_pairs={{0,64},{64,128},{128,192},{192,256},{256,320},{320,384},{384,448},... | collective-permute-start | bytes 786440 | tf_op jit(solution)/shard_map/ppermute | solution.py:392
  136.6 25.0 %copy-start.3 = (f32[2,128,256]{2,1,0:T(8,128)S(1)}, f32[2,128,256]{2,1,0:T(8,128)}, u32[]{:S(2)}) copy-start(f32[2,128,256]{2,1,0:T(8,128)} %constant.62.clone.sin_h) | copy-start | bytes 786436
  136.6 25.0 %copy-start.5 = (f32[2,128,256]{2,1,0:T(8,128)S(1)}, f32[2,128,256]{2,1,0:T(8,128)}, u32[]{:S(2)}) copy-start(f32[2,128,256]{2,1,0:T(8,128)} %constant.61.clone.cos_h) | copy-start | bytes 786436
  136.6 25.0 %copy-start.15 = (bf16[256,128]{1,0:T(8,128)(2,1)S(1)}, bf16[256,128]{1,0:T(8,128)(2,1)}, u32[]{:S(2)}) copy-start(bf16[256,128]{1,0:T(8,128)(2,1)} %constant.68.phi_h) | copy-start | bytes 196612
  136.7 25.0 %copy-start.16 = (bf16[64,128]{1,0:T(8,128)(2,1)S(1)}, bf16[64,128]{1,0:T(8,128)(2,1)}, u32[]{:S(2)}) copy-start(bf16[64,128]{1,0:T(8,128)(2,1)} %constant.67.theta_h) | copy-start | bytes 49156
  136.7 46.2 %all-to-all-start.4 = ((bf16[8,64,2,8,128]{4,3,2,1,0:T(8,128)(2,1)}), bf16[8,64,2,8,128]{4,3,2,1,0:T(8,128)(2,1)S(1)}, u32[]{:S(2)}, u32[]{:S(2)}) async-start(bf16[8,64,2,8,128]{4,3,2,1,0:T(8,128)(2,1)} %shard_map.146), calls=%async_computation.4 | async-start | bytes 4194304 | tf_op jit(solution)/shard_map/all_to_all | solution.py:405
  144.4 38.5 %copy-start.6 = (bf16[40,2,8,128]{3,2,1,0:T(8,128)(2,1)S(1)}, bf16[40,2,8,128]{3,2,1,0:T(8,128)(2,1)}, u32[]{:S(2)}) copy-start(bf16[40,2,8,128]{3,2,1,0:T(8,128)(2,1)} %ops_hbm.3) | copy-start | bytes 491524
  144.4 3.4 %collective-permute-start.14 = (bf16[4,2,8,8,128]{4,3,2,1,0:T(8,128)(2,1)S(1)}, bf16[4,2,8,8,128]{4,3,2,1,0:T(8,128)(2,1)S(1)}, u32[]{:S(2)}, u32[]{:S(2)}) collective-permute-start(bf16[4,2,8,8,128]{4,3,2,1,0:T(8,128)(2,1)S(1)} %get-tuple-element.26), channel_id=1, source_target_pairs={{0,1},{1,0},{2,3},{3,2},{4,5},{5,4},{6,7},{7,6},{8,9},{9,8},{10,11... | collective-permute-start | bytes 393224 | tf_op jit(solution)/shard_map/ppermute | solution.py:268
  147.8 10.5 %collective-permute-start.15 = (bf16[2,2,8,8,128]{4,3,2,1,0:T(8,128)(2,1)S(1)}, bf16[2,2,8,8,128]{4,3,2,1,0:T(8,128)(2,1)S(1)}, u32[]{:S(2)}, u32[]{:S(2)}) collective-permute-start(bf16[2,2,8,8,128]{4,3,2,1,0:T(8,128)(2,1)S(1)} %pad_maximum_fusion), channel_id=1, source_target_pairs={{0,2},{1,3},{2,0},{3,1},{4,6},{5,7},{6,4},{7,5},{8,10},{9,11},{10,... | collective-permute-start | bytes 196616 | tf_op jit(solution)/shard_map/ppermute | solution.py:268
  150.3 8.0 %collective-permute-start.16 = (bf16[2,2,8,8,128]{4,3,2,1,0:T(8,128)(2,1)S(1)}, bf16[2,2,8,8,128]{4,3,2,1,0:T(8,128)(2,1)S(1)}, u32[]{:S(2)}, u32[]{:S(2)}) collective-permute-start(bf16[2,2,8,8,128]{4,3,2,1,0:T(8,128)(2,1)S(1)} %pad_maximum_fusion.1), channel_id=1, source_target_pairs={{0,4},{1,5},{2,6},{3,7},{4,0},{5,1},{6,2},{7,3},{8,12},{9,13},{10,... | collective-permute-start | bytes 196616 | tf_op jit(solution)/shard_map/ppermute | solution.py:268
  154.3 7.4 %collective-permute-start.17 = (bf16[2,2,8,8,128]{4,3,2,1,0:T(8,128)(2,1)S(1)}, bf16[2,2,8,8,128]{4,3,2,1,0:T(8,128)(2,1)S(1)}, u32[]{:S(2)}, u32[]{:S(2)}) collective-permute-start(bf16[2,2,8,8,128]{4,3,2,1,0:T(8,128)(2,1)S(1)} %pad_maximum_fusion.2), channel_id=1, source_target_pairs={{0,6},{1,7},{2,4},{3,5},{4,2},{5,3},{6,0},{7,1},{8,14},{9,15},{10,... | collective-permute-start | bytes 196616 | tf_op jit(solution)/shard_map/ppermute | solution.py:268
  164.9 3.2 %collective-permute-start.18 = (bf16[4,8,2,8,128]{4,3,2,1,0:T(8,128)(2,1)S(1)}, bf16[4,8,2,8,128]{4,3,2,1,0:T(8,128)(2,1)S(1)}, u32[]{:S(2)}, u32[]{:S(2)}) collective-permute-start(bf16[4,8,2,8,128]{4,3,2,1,0:T(8,128)(2,1)S(1)} %get-tuple-element.28), channel_id=1, source_target_pairs={{0,1},{1,0},{2,3},{3,2},{4,5},{5,4},{6,7},{7,6},{8,9},{9,8},{10,11... | collective-permute-start | bytes 393224 | tf_op jit(solution)/shard_map/ppermute | solution.py:268
  168.1 10.5 %collective-permute-start.19 = (bf16[2,8,2,8,128]{4,3,2,1,0:T(8,128)(2,1)S(1)}, bf16[2,8,2,8,128]{4,3,2,1,0:T(8,128)(2,1)S(1)}, u32[]{:S(2)}, u32[]{:S(2)}) collective-permute-start(bf16[2,8,2,8,128]{4,3,2,1,0:T(8,128)(2,1)S(1)} %pad_maximum_fusion.3), channel_id=1, source_target_pairs={{0,2},{1,3},{2,0},{3,1},{4,6},{5,7},{6,4},{7,5},{8,10},{9,11},{10,... | collective-permute-start | bytes 196616 | tf_op jit(solution)/shard_map/ppermute | solution.py:268
  170.1 8.5 %collective-permute-start.20 = (bf16[2,8,2,8,128]{4,3,2,1,0:T(8,128)(2,1)S(1)}, bf16[2,8,2,8,128]{4,3,2,1,0:T(8,128)(2,1)S(1)}, u32[]{:S(2)}, u32[]{:S(2)}) collective-permute-start(bf16[2,8,2,8,128]{4,3,2,1,0:T(8,128)(2,1)S(1)} %pad_maximum_fusion.4), channel_id=1, source_target_pairs={{0,4},{1,5},{2,6},{3,7},{4,0},{5,1},{6,2},{7,3},{8,12},{9,13},{10,... | collective-permute-start | bytes 196616 | tf_op jit(solution)/shard_map/ppermute | solution.py:268
  175.5 7.4 %collective-permute-start.21 = (bf16[2,8,2,8,128]{4,3,2,1,0:T(8,128)(2,1)S(1)}, bf16[2,8,2,8,128]{4,3,2,1,0:T(8,128)(2,1)S(1)}, u32[]{:S(2)}, u32[]{:S(2)}) collective-permute-start(bf16[2,8,2,8,128]{4,3,2,1,0:T(8,128)(2,1)S(1)} %pad_maximum_fusion.5), channel_id=1, source_target_pairs={{0,6},{1,7},{2,4},{3,5},{4,2},{5,3},{6,0},{7,1},{8,14},{9,15},{10,... | collective-permute-start | bytes 196616 | tf_op jit(solution)/shard_map/ppermute | solution.py:268

commit v4 on v1

--- a/solution.py
+++ b/solution.py
@@ -1,4 +1,3 @@
-import functools
 import math
 
 import jax
@@ -9,17 +8,18 @@
 from jax.experimental.pallas import tpu as pltpu
 from jax.sharding import PartitionSpec as P
 
+
 CT = 64
 SUBBOX_HEADINGS = 128
 PT = 128
 PP = 256
-KIDS = 4
 WAVE_NUMBER = 6.0
 SIDE = 8
 BOTH = ("box", "angle")
 F32, BF16, I32 = jnp.float32, jnp.bfloat16, jnp.int32
 VM = pltpu.VMEM
 ANY = pl.ANY
+GRANT = 12 << 20
 
 
 def fourier_table(fine_count, coarse_count, offset):
@@ -51,7 +51,7 @@
     return lax.broadcasted_iota(I32, shape, dim)
 
 
-def plan_level(ids_ref, op_ref, home_ref, core, mine, rows_device, cap, empty_op, code_ref):
+def plan_level(ids_ref, op_ref, home_ref, core, mine, other, rows_device, cap, empty_op, code_ref):
     slots, rows = ids_ref.shape
     home = home_ref[...]
     owner = home // rows_device
@@ -78,7 +78,8 @@
         prefix = bmm(hot_b, before) + carry
         carry = carry + jnp.sum(hot, axis=1, keepdims=True)
         rank = jnp.sum(hot * prefix, axis=0, keepdims=True).astype(I32)
-        position = column * cap + rank
+        lane = column if other is None else (other - column) & 7
+        position = lane * cap + rank
         code_ref[pl.ds(j, 1), pl.ds(0, rows)] = jnp.where(
             usable, position * 64 + op_ref[pl.ds(j, 1), :], empty_op
         )
@@ -91,10 +92,10 @@
 
 
 def plan_body(where, cl, co, ch, plist, po, ph, want_ref, ccode_ref, pcode_ref):
-    core, mine = where[0], where[1]
+    core, mine, other = where[0], where[1], where[2]
     want_ref[...] = jnp.zeros(want_ref.shape, I32)
-    want_ref[:, pl.ds(0, 64)] = plan_level(cl, co, ch, core, mine, 64, 64, 40, ccode_ref)
-    want_ref[:, pl.ds(64, 16)] = plan_level(plist, po, ph, core, mine, 16, 16, 40, pcode_ref)
+    want_ref[:, pl.ds(0, 64)] = plan_level(cl, co, ch, core, mine, other, 64, 64, 40, ccode_ref)
+    want_ref[:, pl.ds(64, 16)] = plan_level(plist, po, ph, core, mine, None, 16, 16, 40, pcode_ref)
 
 
 def plan(where, child_list, child_op, child_home, parent_list, parent_op, parent_home):
@@ -116,16 +117,22 @@
         ),
         in_specs=[pl.BlockSpec(memory_space=pltpu.SMEM)] + [pl.BlockSpec(memory_space=VM)] * 6,
         out_specs=(pl.BlockSpec(memory_space=VM),) * 3,
+        compiler_params=pltpu.CompilerParams(vmem_limit_bytes=GRANT),
         name="plan",
     )(*args)
 
 
-def up_body(field, theta, phi, cos_t, sin_t, out, wide):
+def up_body(field, theta_h, phi_h, cos_h, sin_h, out, theta, phi, cos_t, sin_t, wide, sems):
+    copies = fetch((theta_h, phi_h, cos_h, sin_h), (theta, phi, cos_t, sin_t), sems)
+    copies[0].wait()
+    copies[1].wait()
     for r in range(8):
         for c in range(2):
             rows = jnp.concatenate([field[s, r, c] for s in range(8)], axis=0)
             stretched = bmm(theta[...], rows).astype(BF16)
             wide[r * 2 + c] = bmm(stretched, phi[...])
+    copies[2].wait()
+    copies[3].wait()
     for q in range(2):
         for u in range(PT // 8):
             at = pl.ds(u * 8, 8)
@@ -142,49 +149,96 @@
                     out[u // 2, q, c * 4 + (u % 2) * 2 + v] = part[:, v * 128 : (v + 1) * 128]
 
 
-def lift(field, theta, phi, cos_t, sin_t):
+def fetch(sources, targets, sems):
+    copies = [pltpu.make_async_copy(a, b, sems.at[i]) for i, (a, b) in enumerate(zip(sources, targets))]
+    for copy in copies:
+        copy.start()
+    return copies
+
+
+def lift(field, tables):
     return pl.pallas_call(
         up_body,
         out_shape=jax.ShapeDtypeStruct((8, 2, 8, 8, 128), BF16),
-        in_specs=[pl.BlockSpec(memory_space=VM)] * 5,
+        in_specs=[pl.BlockSpec(memory_space=VM)] + [pl.BlockSpec(memory_space=pltpu.HBM)] * 4,
         out_specs=pl.BlockSpec(memory_space=VM),
-        scratch_shapes=[pltpu.VMEM((16, PT, PP), F32)],
+        scratch_shapes=[pltpu.VMEM(t.shape, t.dtype) for t in tables]
+        + [pltpu.VMEM((16, PT, PP), F32), pltpu.SemaphoreType.DMA((4,))],
+        compiler_params=pltpu.CompilerParams(vmem_limit_bytes=GRANT),
         name="lift",
-    )(field, theta, phi, cos_t, sin_t)
-
-
-def select_body(first, rows, tiles, asked, *refs):
-    blocks, out, pool, sems = refs[:8], refs[8], refs[9], refs[10]
-    count = rows * tiles
+    )(field, *tables)
+
+
+def select_body(where, asked, *refs):
+    blocks, parents, children = refs[:8], refs[8], refs[9:17]
+    pool, parent_buf, child_buf, sems, parent_sems, child_sems = refs[17:]
     copies = [
-        pltpu.make_async_copy(b.at[pl.ds(first[1], count)], pool.at[pl.ds(i * count, count)], sems.at[i])
+        pltpu.make_async_copy(
+            b.at[pl.ds(128 * half, 128)], pool.at[half, i], sems.at[half, i]
+        )
+        for half in (1, 0)
         for i, b in enumerate(blocks)
     ]
     for copy in copies:
         copy.start()
-    for copy in copies:
+
+    def child_out(d):
+        return pltpu.make_async_copy(child_buf.at[d], children[d], child_sems.at[d])
+
+    def parent_out(h):
+        return pltpu.make_async_copy(parent_buf.at[h], parents.at[h], parent_sems.at[h])
+
+    for copy in copies[:8]:
         copy.wait()
-    per_peer = out.shape[1]
-
-    def step(h, carry):
-        for k in range(per_peer):
-            row = asked[h, first[0] + k]
-            at = pl.multiple_of(row * tiles, tiles)
-            out[h, k] = pool[pl.ds(at, tiles)]
+
+    def peer(h, carry):
+        for k in range(16):
+            row = asked[h, 64 + k]
+            at = pl.multiple_of((row & 15) * 8, 8)
+            parent_buf[h, k] = pool[1, row >> 4, pl.ds(at, 8)]
+        parent_out(h).start()
         return carry
 
-    lax.fori_loop(0, SIDE, step, 0)
-
-
-def select(asked, blocks, first, rows, tiles, per_peer):
-    return pl.pallas_call(
-        functools.partial(select_body, first, rows, tiles),
-        out_shape=jax.ShapeDtypeStruct((SIDE, per_peer, tiles, 8, 128), BF16),
-        in_specs=[pl.BlockSpec(memory_space=pltpu.SMEM)] + [pl.BlockSpec(memory_space=ANY)] * 8,
-        out_specs=pl.BlockSpec(memory_space=VM),
-        scratch_shapes=[pltpu.VMEM((8 * rows * tiles, 8, 128), BF16), pltpu.SemaphoreType.DMA((8,))],
+    lax.fori_loop(0, SIDE, peer, 0)
+    for copy in copies[8:]:
+        copy.wait()
+    for d in range(SIDE):
+        h = (where[2] + d) & 7
+
+        def some(i, carry):
+            for j in range(16):
+                k = i * 16 + j
+                row = asked[h, k]
+                at = pl.multiple_of((row & 63) * 2, 2)
+                child_buf[d, k] = pool[0, row >> 6, pl.ds(at, 2)]
+            return carry
+
+        lax.fori_loop(0, 4, some, 0)
+        child_out(d).start()
+    for h in range(SIDE):
+        parent_out(h).wait()
+    for d in range(SIDE):
+        child_out(d).wait()
+
+
+def select(where, asked, blocks):
+    hbm = pl.BlockSpec(memory_space=pltpu.HBM)
+    return pl.pallas_call(
+        select_body,
+        out_shape=(pltpu.HBM((SIDE, 16, 8, 8, 128), BF16),) + (pltpu.HBM((64, 2, 8, 128), BF16),) * SIDE,
+        in_specs=[pl.BlockSpec(memory_space=pltpu.SMEM)] * 2 + [pl.BlockSpec(memory_space=ANY)] * 8,
+        out_specs=(hbm,) * 9,
+        scratch_shapes=[
+            pltpu.VMEM((2, 8, 128, 8, 128), BF16),
+            pltpu.VMEM((SIDE, 16, 8, 8, 128), BF16),
+            pltpu.VMEM((SIDE, 64, 2, 8, 128), BF16),
+            pltpu.SemaphoreType.DMA((2, 8)),
+            pltpu.SemaphoreType.DMA((8,)),
+            pltpu.SemaphoreType.DMA((8,)),
+        ],
+        compiler_params=pltpu.CompilerParams(vmem_limit_bytes=GRANT),
         name="select",
-    )(asked, *blocks)
+    )(where, asked, *blocks)
 
 
 def parent_far_body(code, recv, ops_hbm, out, ops, sem):
@@ -226,24 +280,26 @@
         ],
         out_specs=pl.BlockSpec(memory_space=VM),
         scratch_shapes=[pltpu.VMEM((41, 2, 16, PP), BF16), pltpu.SemaphoreType.DMA],
+        compiler_params=pltpu.CompilerParams(vmem_limit_bytes=GRANT),
         name="far_parents",
     )(code, recv, ops)
 
 
-def child_far_body(code, recv, ops_hbm, term, out, ops, sem):
-    copy = pltpu.make_async_copy(ops_hbm, ops.at[pl.ds(0, 40)], sem)
-    copy.start()
+def child_far_body(code, *refs):
+    blocks, ops_hbm, term, out, recv, ops, sems = refs[:8], *refs[8:]
+    copies = fetch((ops_hbm, *blocks), (ops.at[pl.ds(0, 40)], *(recv.at[i] for i in range(8))), sems)
     ops[40] = jnp.zeros(ops.shape[1:], BF16)
-    copy.wait()
+    for copy in copies:
+        copy.wait()
 
     def row(r, carry):
         real = jnp.zeros((8, 128), F32)
         imag = jnp.zeros((8, 128), F32)
         for j in range(8):
             both = code[j, r]
-            at, op = both >> 6, both & 63
+            lane, at, op = both >> 12, (both >> 6) & 63, both & 63
             a, b = ops[op, 0].astype(F32), ops[op, 1].astype(F32)
-            c, d = recv[at, 0].astype(F32), recv[at, 1].astype(F32)
+            c, d = recv[lane, at, 0].astype(F32), recv[lane, at, 1].astype(F32)
             real = real + (a * c - b * d)
             imag = imag + (a * d + b * c)
         out[r, 0] = (real + term[r, 0].astype(F32)).astype(BF16)
@@ -253,23 +309,27 @@
     lax.fori_loop(0, 64, row, 0, unroll=2)
 
 
-def far_children(code, recv, ops, term):
+def far_children(code, blocks, ops, term):
     return pl.pallas_call(
         child_far_body,
         out_shape=jax.ShapeDtypeStruct((64, 2, 8, 128), BF16),
-        in_specs=[
-            pl.BlockSpec(memory_space=pltpu.SMEM),
-            pl.BlockSpec(memory_space=VM),
-            pl.BlockSpec(memory_space=ANY),
-            pl.BlockSpec(memory_space=VM),
+        in_specs=[pl.BlockSpec(memory_space=pltpu.SMEM)]
+        + [pl.BlockSpec(memory_space=ANY)] * 9
+        + [pl.BlockSpec(memory_space=VM)],
+        out_specs=pl.BlockSpec(memory_space=VM),
+        scratch_shapes=[
+            pltpu.VMEM((SIDE, 64, 2, 8, 128), BF16),
+            pltpu.VMEM((41, 2, 8, 128), BF16),
+            pltpu.SemaphoreType.DMA((9,)),
         ],
-        out_specs=pl.BlockSpec(memory_space=VM),
-        scratch_shapes=[pltpu.VMEM((41, 2, 8, 128), BF16), pltpu.SemaphoreType.DMA],
+        compiler_params=pltpu.CompilerParams(vmem_limit_bytes=GRANT),
         name="far_children",
-    )(code, recv, ops, term)
-
-
-def down_body(far, theta, phi, cos_t, sin_t, out, turned):
+    )(code, *blocks, ops, term)
+
+
+def down_body(far, theta_h, phi_h, cos_h, sin_h, out, theta, phi, cos_t, sin_t, turned, sems):
+    for copy in fetch((theta_h, phi_h, cos_h, sin_h), (theta, phi, cos_t, sin_t), sems):
+        copy.wait()
     for q in range(2):
         for u in range(PT // 8):
             at = pl.ds(u * 8, 8)
@@ -294,15 +354,17 @@
                 out[s, r, c] = term[s * 8 : s * 8 + 8, :]
 
 
-def lower(far, theta, phi, cos_t, sin_t):
+def lower(far, tables):
     return pl.pallas_call(
         down_body,
         out_shape=jax.ShapeDtypeStruct((8, 8, 2, 8, 128), BF16),
-        in_specs=[pl.BlockSpec(memory_space=VM)] * 5,
+        in_specs=[pl.BlockSpec(memory_space=VM)] + [pl.BlockSpec(memory_space=pltpu.HBM)] * 4,
         out_specs=pl.BlockSpec(memory_space=VM),
-        scratch_shapes=[pltpu.VMEM((16, PT, PP), BF16)],
+        scratch_shapes=[pltpu.VMEM(t.shape, t.dtype) for t in tables]
+        + [pltpu.VMEM((16, PT, PP), BF16), pltpu.SemaphoreType.DMA((4,))],
+        compiler_params=pltpu.CompilerParams(vmem_limit_bytes=GRANT),
         name="lower",
-    )(far, theta, phi, cos_t, sin_t)
+    )(far, *tables)
 
 
 def groups(straight):
@@ -317,8 +379,8 @@
 SPREAD, TRADE = groups(1), groups(0)
 
 
-def hop(x, step):
-    pairs = [(g[i], g[(i + step) % SIDE]) for g in SPREAD for i in range(SIDE)]
+def hop(x, step, lines=SPREAD):
+    pairs = [(g[i], g[(i + step) % SIDE]) for g in lines for i in range(SIDE)]
     return lax.ppermute(x, BOTH, pairs)
 
 
@@ -349,32 +411,35 @@
     box, angle = lax.axis_index("box"), lax.axis_index("angle")
     core = angle % 2
     mine = jnp.where(core == 0, box // SIDE, box % SIDE)
-    where = jnp.stack([core, mine]).astype(I32)
-
+    other = jnp.where(core == 0, box % SIDE, box // SIDE)
+    where = jnp.stack([core, mine, other]).astype(I32)
+
+    hold = lambda x: pltpu.with_memory_space_constraint(x, pltpu.HBM)
+    whole = swap(child_field, "angle").reshape(8, 8, 2, 8, 128)
+    parents = swap(lift(whole, tuple(map(hold, (theta_up, phi_up, cos_t, sin_t)))), "angle")
     wanted, child_code, parent_code = plan(
         where, child_list, child_op, child_home, parent_list, parent_op, parent_home
     )
-    asked = swap(wanted.reshape(SIDE, 1, 128), BOTH, axis_index_groups=TRADE).reshape(SIDE, 128)
-
-    whole = swap(child_field, "angle").reshape(8, 8, 2, 8, 128)
-    parents = swap(lift(whole, theta_up, phi_up, cos_t, sin_t), "angle")
     own = jnp.concatenate([child_field.reshape(128, 8, 128), parents.reshape(128, 8, 128)])
     forth, back = [own], [own]
     for step in range(4):
+        if step == 1:
+            forth[1], wanted = lax.optimization_barrier((forth[1], wanted))
         forth.append(hop(forth[-1], 1))
         if step < 3:
             back.append(hop(back[-1], -1))
     blocks = back + [forth[8 - p] for p in range(4, 8)]
-
-    parents_out = select(asked, blocks, (64, 128), 16, 8, 16)
-    children_out = select(asked, blocks, (0, 0), 64, 2, 64)
+    asked = swap(wanted.reshape(SIDE, 1, 128), BOTH, axis_index_groups=TRADE).reshape(SIDE, 128)
+    parents_out, *children_out = select(where, asked, blocks)
     parents_in = swap(parents_out, BOTH, axis_index_groups=TRADE)
-    children_in = swap(children_out, BOTH, axis_index_groups=TRADE)
-    parent_far = far_parents(parent_code, parents_in.reshape(128, 8, 8, 128), parent_ops)
-    turned = swap(parent_far, "angle").reshape(8, 2, 8, 8, 128)
-    terms = swap(lower(turned, theta_down, phi_down, cos_t, sin_t), "angle")
+    children_in = {0: children_out[0]}
+    for d in (4, 3, 5, 2, 6, 1, 7):
+        children_in[d] = hop(children_out[d], d, TRADE)
+    sums = far_parents(parent_code, parents_in.reshape(128, 8, 8, 128), parent_ops)
+    turned = swap(sums, "angle").reshape(8, 2, 8, 8, 128)
+    terms = swap(lower(turned, tuple(map(hold, (theta_down, phi_down, cos_t, sin_t)))), "angle")
     return far_children(
-        child_code, children_in.reshape(512, 2, 8, 128), child_ops, terms.reshape(64, 2, 8, 128)
+        child_code, [children_in[d] for d in range(SIDE)], child_ops, terms.reshape(64, 2, 8, 128)
     )
 
 

time: 196 us -> 170 us (0.87)
  blocking collectives: 86.9 us -> 39.7 us
  starting transfers between devices: 34.2 us -> 67.3 us
  Pallas kernels: 30 us -> 22 us
  waiting for transfers between devices: 43 us -> 39.8 us
    all_to_all x5 -> x3, blocking collectives: 86.9 us -> 39.7 us  [swap(): lax.all_to_all(x, axis, split_axis=0, concat_axis=0, tiled=True, **kw)]
    ppermute x7 -> x14, starting transfers between devices: 27.2 us -> 55.3 us  [hop(): return lax.ppermute(x, BOTH, pairs)]
    all_to_all x2 -> x3, starting transfers between devices: 7.03 us -> 12 us  [swap(): lax.all_to_all(x, axis, split_axis=0, concat_axis=0, tiled=True, **kw)]
    all_to_all x2 -> x3, waiting for transfers between devices: 28.8 us -> 24.6 us  [swap(): lax.all_to_all(x, axis, split_axis=0, concat_axis=0, tiled=True, **kw)]
    pallas_call x2 -> x1, Pallas kernels: 7.99 us -> 4.34 us  [select(): pl.pallas_call(select_body, out_shape=(pltpu.HBM((SIDE, 16, 8, 8, 128), B...]
    ppermute x7 -> x14, waiting for transfers between devices: 14.2 us -> 15.2 us  [hop(): return lax.ppermute(x, BOTH, pairs)]
  transfers between devices with their start and end apart: 9 -> 17, of which waited for: 5 -> 9; matrix products, arithmetic and copies ran while one was open for 0% -> 0% of each run, Pallas kernels for 7% -> 7%
where the time goes in v4:
time: 170 us; the launch traced here: 169 us
  starting transfers between devices  67.3 us (40%)
  waiting for transfers between devices  39.8 us (23%)
  blocking collectives  39.7 us (23%)
  Pallas kernels  22 us (13%)
    ppermute x14, starting transfers between devices, hop(): return lax.ppermute(x, BOTH, pairs)  55.3 us
    all_to_all x3, blocking collectives, swap(): lax.all_to_all(x, axis, split_axis=0, concat_axis=0, tiled=True, **kw)  39.7 us
    all_to_all x3, waiting for transfers between devices, swap(): lax.all_to_all(x, axis, split_axis=0, concat_axis=0, tiled=True, **kw)  24.6 us
    ppermute x14, waiting for transfers between devices, hop(): return lax.ppermute(x, BOTH, pairs)  15.2 us
    all_to_all x3, starting transfers between devices, swap(): lax.all_to_all(x, axis, split_axis=0, concat_axis=0, tiled=True, **kw)  12 us
    pallas_call x1, Pallas kernels, lower(): pl.pallas_call(down_body, out_shape=jax.ShapeDtypeStruct((8, 8, 2, 8, 128...  4.59 us
    pallas_call x1, Pallas kernels, select(): pl.pallas_call(select_body, out_shape=(pltpu.HBM((SIDE, 16, 8, 8, 128), B...  4.34 us
    pallas_call x1, Pallas kernels, plan(): pl.pallas_call(plan_body, out_shape=(jax.ShapeDtypeStruct((SIDE, 128), I3...  4.01 us
  transfers between devices with their start and end apart: 17, of which 9 were waited for; matrix products, arithmetic and copies ran while one was open for 0% of the time, Pallas kernels for 7%

profile of v4, /device:TPU:24, one launch (start us, length us, event | category | flops | bytes accessed | tf_op | source)
XLA Modules:
  0.0 169.2 jit_solution(4801995665681791493)
XLA Ops:
  0.0 0.0 copy-start.9
  0.0 0.0 copy-start.8
  0.0 0.0 copy-start.7
  0.0 0.0 copy-start.6
  0.0 0.0 copy-start.3
  0.0 0.0 copy-start.5
  0.0 0.0 copy-start.4
  0.0 11.9 %all_to_all.30 = bf16[64,2,8,128]{3,2,1,0:T(8,128)(2,1)S(1)} all-to-all(bf16[64,2,8,128]{3,2,1,0:T(8,128)(2,1)} %param.15), channel_id=1, replica_groups=mesh['box'=64,'angle'=8] {'angle'}, dimensions={0} | all-to-all | bytes 524288 | tf_op jit(solution)/shard_map/all_to_all | solution.py:388
  12.0 2.6 %lift.1 = bf16[8,2,8,8,128]{4,3,2,1,0:T(8,128)(2,1)S(1)} custom-call(bf16[8,8,2,8,128]{4,3,2,1,0:T(8,128)(2,1)S(1)} %bitcast.21, bf16[128,64]{1,0:T(8,128)(2,1)} %constant.69.theta_h, bf16[128,256]{1,0:T(8,128)(2,1)} %constant.70.phi_h, f32[2,128,256]{2,1,0:T(8,128)} %constant.65.clone.cos_h, f32[2,128,256]{2,1,0:T(8,128)} %constant.66.clone.sin_h), custom_call_target="tpu_custom_call" | custom-call | tf_op jit(solution)/shard_map/lift/pallas_call | solution.py:160
  14.6 9.9 %all_to_all.31 = bf16[8,2,8,8,128]{4,3,2,1,0:T(8,128)(2,1)S(1)} all-to-all(bf16[8,2,8,8,128]{4,3,2,1,0:T(8,128)(2,1)S(1)} %lift.1), channel_id=1, replica_groups=mesh['box'=64,'angle'=8] {'angle'}, dimensions={0} | all-to-all | bytes 524288 | tf_op jit(solution)/shard_map/all_to_all | solution.py:388
  24.5 0.0 copy-done.9
  24.5 4.7 %collective-permute-start = (bf16[256,8,128]{2,1,0:T(8,128)(2,1)S(1)}, bf16[256,8,128]{2,1,0:T(8,128)(2,1)S(1)}, u32[]{:S(2)}, u32[]{:S(2)}) collective-permute-start(bf16[256,8,128]{2,1,0:T(8,128)(2,1)S(1)} %pad_maximum_fusion.refs_0_), channel_id=1, source_target_pairs={{0,64},{64,128},{128,192},{192,256},{256,320},{320,384},{384,448},... | collective-permute-start | bytes 1572872 | tf_op jit(solution)/shard_map/ppermute | solution.py:384
  29.3 0.1 pad_add_fusion.where
  29.3 0.0 copy-done.8
  29.3 0.0 copy-done.7
  29.3 0.0 copy-done.6
  29.4 0.0 copy-done.3
  29.4 0.0 copy-done.5
  29.4 0.0 copy-done.4
  29.4 4.0 %plan.1 = (s32[8,128]{1,0:T(8,128)S(1)}, s32[8,64]{1,0:T(8,128)S(1)}, s32[8,16]{1,0:T(8,128)S(1)}) custom-call(s32[3]{0:T(128)S(1)} %pad_add_fusion.where, s32[8,64]{1,0:T(8,128)S(1)} %bitcast.25, s32[8,64]{1,0:T(8,128)S(1)} %bitcast.26, s32[32,128]{1,0:T(8,128)S(1)} %bitcast.24, s32[8,16]{1,0:T(8,128)S(1)} %bitcast.27, s32[8,16]{1,0:T(8,128)S(1)} %bitcast.28, ...), custom_call_target="tpu_custom_call" | custom-call | tf_op jit(solution)/shard_map/plan/pallas_call | solution.py:111
  33.4 1.9 %collective-permute-start.1 = (bf16[256,8,128]{2,1,0:T(8,128)(2,1)S(1)}, bf16[256,8,128]{2,1,0:T(8,128)(2,1)S(1)}, u32[]{:S(2)}, u32[]{:S(2)}) collective-permute-start(bf16[256,8,128]{2,1,0:T(8,128)(2,1)S(1)} %pad_maximum_fusion.refs_0_), channel_id=1, source_target_pairs={{0,448},{64,0},{128,64},{192,128},{256,192},{320,256},{384,320},{4... | collective-permute-start | bytes 1572872 | tf_op jit(solution)/shard_map/ppermute | solution.py:384
  35.3 0.6 collective-permute-done.refs_7_
  35.9 5.6 %collective-permute-start.4 = (bf16[256,8,128]{2,1,0:T(8,128)(2,1)S(1)}, bf16[256,8,128]{2,1,0:T(8,128)(2,1)S(1)}, u32[]{:S(2)}, u32[]{:S(2)}) collective-permute-start(bf16[256,8,128]{2,1,0:T(8,128)(2,1)S(1)} %collective-permute-done.refs_7_), channel_id=1, source_target_pairs={{0,64},{64,128},{128,192},{192,256},{256,320},{320,384},{384,448},... | collective-permute-start | bytes 1572872 | tf_op jit(solution)/shard_map/ppermute | solution.py:384
  41.5 4.2 %collective-permute-done.1.refs_1_ = bf16[256,8,128]{2,1,0:T(8,128)(2,1)S(1)} collective-permute-done((bf16[256,8,128]{2,1,0:T(8,128)(2,1)S(1)}, bf16[256,8,128]{2,1,0:T(8,128)(2,1)S(1)}, u32[]{:S(2)}, u32[]{:S(2)}) %collective-permute-start.1) | collective-permute-done | bytes 524320 | tf_op jit(solution)/shard_map/ppermute | solution.py:384
  45.7 1.9 %collective-permute-start.2 = (bf16[256,8,128]{2,1,0:T(8,128)(2,1)S(1)}, bf16[256,8,128]{2,1,0:T(8,128)(2,1)S(1)}, u32[]{:S(2)}, u32[]{:S(2)}) collective-permute-start(bf16[256,8,128]{2,1,0:T(8,128)(2,1)S(1)} %collective-permute-done.1.refs_1_), channel_id=1, source_target_pairs={{0,448},{64,0},{128,64},{192,128},{256,192},{320,256},{384,320},{4... | collective-permute-start | bytes 1572872 | tf_op jit(solution)/shard_map/ppermute | solution.py:384
  47.6 0.6 collective-permute-done.4.refs_6_
  48.2 5.6 %collective-permute-start.5 = (bf16[256,8,128]{2,1,0:T(8,128)(2,1)S(1)}, bf16[256,8,128]{2,1,0:T(8,128)(2,1)S(1)}, u32[]{:S(2)}, u32[]{:S(2)}) collective-permute-start(bf16[256,8,128]{2,1,0:T(8,128)(2,1)S(1)} %collective-permute-done.4.refs_6_), channel_id=1, source_target_pairs={{0,64},{64,128},{128,192},{192,256},{256,320},{320,384},{384,448},... | collective-permute-start | bytes 1572872 | tf_op jit(solution)/shard_map/ppermute | solution.py:384
  53.8 4.2 %collective-permute-done.2.refs_2_ = bf16[256,8,128]{2,1,0:T(8,128)(2,1)S(1)} collective-permute-done((bf16[256,8,128]{2,1,0:T(8,128)(2,1)S(1)}, bf16[256,8,128]{2,1,0:T(8,128)(2,1)S(1)}, u32[]{:S(2)}, u32[]{:S(2)}) %collective-permute-start.2) | collective-permute-done | bytes 524320 | tf_op jit(solution)/shard_map/ppermute | solution.py:384
  58.0 1.9 %collective-permute-start.3 = (bf16[256,8,128]{2,1,0:T(8,128)(2,1)S(1)}, bf16[256,8,128]{2,1,0:T(8,128)(2,1)S(1)}, u32[]{:S(2)}, u32[]{:S(2)}) collective-permute-start(bf16[256,8,128]{2,1,0:T(8,128)(2,1)S(1)} %collective-permute-done.2.refs_2_), channel_id=1, source_target_pairs={{0,448},{64,0},{128,64},{192,128},{256,192},{320,256},{384,320},{4... | collective-permute-start | bytes 1572872 | tf_op jit(solution)/shard_map/ppermute | solution.py:384
  59.9 0.6 collective-permute-done.5.refs_5_
  60.5 5.6 %collective-permute-start.6 = (bf16[256,8,128]{2,1,0:T(8,128)(2,1)S(1)}, bf16[256,8,128]{2,1,0:T(8,128)(2,1)S(1)}, u32[]{:S(2)}, u32[]{:S(2)}) collective-permute-start(bf16[256,8,128]{2,1,0:T(8,128)(2,1)S(1)} %collective-permute-done.5.refs_5_), channel_id=1, source_target_pairs={{0,64},{64,128},{128,192},{192,256},{256,320},{320,384},{384,448},... | collective-permute-start | bytes 1572872 | tf_op jit(solution)/shard_map/ppermute | solution.py:384
  66.1 17.8 %all_to_all.32 = s32[8,1,128]{2,1,0:T(1,128)S(1)} all-to-all(s32[8,1,128]{2,1,0:T(1,128)S(1)} %bitcast.30), channel_id=1, replica_groups={{0,8,16,24,32,40,48,56},{64,72,80,88,96,104,112,120},{128,136,144,152,1..., dimensions={0} | all-to-all | bytes 8192 | tf_op jit(solution)/shard_map/all_to_all | solution.py:388
  83.9 0.0 collective-permute-done.3.refs_3_
  83.9 0.0 collective-permute-done.6.refs_4_
  83.9 4.3 %select.9 = (bf16[8,16,8,8,128]{4,3,2,1,0:T(8,128)(2,1)}, bf16[64,2,8,128]{3,2,1,0:T(8,128)(2,1)}, bf16[64,2,8,128]{3,2,1,0:T(8,128)(2,1)}, bf16[64,2,8,128]{3,2...) custom-call(s32[3]{0:T(128)S(1)} %pad_add_fusion.where, ...), custom_call_target="tpu_custom_call" | custom-call | tf_op jit(solution)/shard_map/select/pallas_call | solution.py:226
  88.2 0.0 copy-start
  88.2 3.7 %all-to-all-start.3 = ((bf16[8,16,8,8,128]{4,3,2,1,0:T(8,128)(2,1)}), bf16[8,16,8,8,128]{4,3,2,1,0:T(8,128)(2,1)S(1)}, u32[]{:S(2)}, u32[]{:S(2)}) async-start(bf16[8,16,8,8,128]{4,3,2,1,0:T(8,128)(2,1)} %get-tuple-element.32), calls=%async_computation.3 | async-start | bytes 4194304 | tf_op jit(solution)/shard_map/all_to_all | solution.py:388
  92.0 3.8 %collective-permute-start.7 = (bf16[64,2,8,128]{3,2,1,0:T(8,128)(2,1)}, bf16[64,2,8,128]{3,2,1,0:T(8,128)(2,1)S(1)}, u32[]{:S(2)}, u32[]{:S(2)}) collective-permute-start(bf16[64,2,8,128]{3,2,1,0:T(8,128)(2,1)} %get-tuple-element.24), channel_id=1, source_target_pairs={{0,8},{8,16},{16,24},{24,32},{32,40},{40,48},{48,56},{56,0},{64,72... | collective-permute-start | bytes 786440 | tf_op jit(solution)/shard_map/ppermute | solution.py:384
  95.8 4.3 %collective-permute-start.8 = (bf16[64,2,8,128]{3,2,1,0:T(8,128)(2,1)}, bf16[64,2,8,128]{3,2,1,0:T(8,128)(2,1)S(1)}, u32[]{:S(2)}, u32[]{:S(2)}) collective-permute-start(bf16[64,2,8,128]{3,2,1,0:T(8,128)(2,1)} %get-tuple-element.25), channel_id=1, source_target_pairs={{0,16},{8,24},{16,32},{24,40},{32,48},{40,56},{48,0},{56,8},{64,80... | collective-permute-start | bytes 786440 | tf_op jit(solution)/shard_map/ppermute | solution.py:384
  100.1 22.2 %all-to-all-done.3 = bf16[8,16,8,8,128]{4,3,2,1,0:T(8,128)(2,1)S(1)} async-done(((bf16[8,16,8,8,128]{4,3,2,1,0:T(8,128)(2,1)}), bf16[8,16,8,8,128]{4,3,2,1,0:T(8,128)(2,1)S(1)}, u32[]{:S(2)}, u32[]{:S(2)}) %all-to-all-start.3) | async-done | bytes 2097184 | tf_op jit(solution)/shard_map/all_to_all | solution.py:388
  122.3 0.0 copy-done
  122.3 0.0 copy-start.1
  122.3 2.5 %far_parents.1 = bf16[16,8,8,128]{3,2,1,0:T(8,128)(2,1)} custom-call(s32[8,16]{1,0:T(8,128)S(1)} %get-tuple-element.31.code, bf16[128,8,8,128]{3,2,1,0:T(8,128)(2,1)S(1)} %bitcast.19, bf16[40,2,16,256]{3,2,1,0:T(8,128)(2,1)S(1)} %copy-done), custom_call_target="tpu_custom_call" | custom-call | tf_op jit(solution)/shard_map/far_parents/pallas_call | solution.py:273
  124.8 0.0 copy-start.2
  124.8 3.6 %all-to-all-start.4 = ((bf16[16,8,8,128]{3,2,1,0:T(8,128)(2,1)}), bf16[16,8,8,128]{3,2,1,0:T(8,128)(2,1)S(1)}, u32[]{:S(2)}, u32[]{:S(2)}) async-start(bf16[16,8,8,128]{3,2,1,0:T(8,128)(2,1)} %far_parents.1), calls=%async_computation.4 | async-start | bytes 524288 | tf_op jit(solution)/shard_map/all_to_all | solution.py:388
  128.4 1.9 %collective-permute-start.9 = (bf16[64,2,8,128]{3,2,1,0:T(8,128)(2,1)}, bf16[64,2,8,128]{3,2,1,0:T(8,128)(2,1)S(1)}, u32[]{:S(2)}, u32[]{:S(2)}) collective-permute-start(bf16[64,2,8,128]{3,2,1,0:T(8,128)(2,1)} %get-tuple-element.26), channel_id=1, source_target_pairs={{0,24},{8,32},{16,40},{24,48},{32,56},{40,0},{48,8},{56,16},{64,88... | collective-permute-start | bytes 786440 | tf_op jit(solution)/shard_map/ppermute | solution.py:384
  130.3 3.0 %collective-permute-start.10 = (bf16[64,2,8,128]{3,2,1,0:T(8,128)(2,1)}, bf16[64,2,8,128]{3,2,1,0:T(8,128)(2,1)S(1)}, u32[]{:S(2)}, u32[]{:S(2)}) collective-permute-start(bf16[64,2,8,128]{3,2,1,0:T(8,128)(2,1)} %get-tuple-element.27), channel_id=1, source_target_pairs={{0,32},{8,40},{16,48},{24,56},{32,0},{40,8},{48,16},{56,24},{64,96... | collective-permute-start | bytes 786440 | tf_op jit(solution)/shard_map/ppermute | solution.py:384
  133.4 6.2 %collective-permute-start.11 = (bf16[64,2,8,128]{3,2,1,0:T(8,128)(2,1)}, bf16[64,2,8,128]{3,2,1,0:T(8,128)(2,1)S(1)}, u32[]{:S(2)}, u32[]{:S(2)}) collective-permute-start(bf16[64,2,8,128]{3,2,1,0:T(8,128)(2,1)} %get-tuple-element.28), channel_id=1, source_target_pairs={{0,40},{8,48},{16,56},{24,0},{32,8},{40,16},{48,24},{56,32},{64,10... | collective-permute-start | bytes 786440 | tf_op jit(solution)/shard_map/ppermute | solution.py:384
  139.5 0.0 collective-permute-done.7.refs_1_
  139.5 5.4 %collective-permute-start.12 = (bf16[64,2,8,128]{3,2,1,0:T(8,128)(2,1)}, bf16[64,2,8,128]{3,2,1,0:T(8,128)(2,1)S(1)}, u32[]{:S(2)}, u32[]{:S(2)}) collective-permute-start(bf16[64,2,8,128]{3,2,1,0:T(8,128)(2,1)} %get-tuple-element.29), channel_id=1, source_target_pairs={{0,48},{8,56},{16,0},{24,8},{32,16},{40,24},{48,32},{56,40},{64,11... | collective-permute-start | bytes 786440 | tf_op jit(solution)/shard_map/ppermute | solution.py:384
  145.0 0.0 collective-permute-done.8.refs_2_
  145.0 3.4 %collective-permute-start.13 = (bf16[64,2,8,128]{3,2,1,0:T(8,128)(2,1)}, bf16[64,2,8,128]{3,2,1,0:T(8,128)(2,1)S(1)}, u32[]{:S(2)}, u32[]{:S(2)}) collective-permute-start(bf16[64,2,8,128]{3,2,1,0:T(8,128)(2,1)} %get-tuple-element.30), channel_id=1, source_target_pairs={{0,56},{8,0},{16,8},{24,16},{32,24},{40,32},{48,40},{56,48},{64,12... | collective-permute-start | bytes 786440 | tf_op jit(solution)/shard_map/ppermute | solution.py:384
  148.4 0.0 all-to-all-done.4
  148.4 4.6 %lower.1 = bf16[8,8,2,8,128]{4,3,2,1,0:T(8,128)(2,1)} custom-call(bf16[8,2,8,8,128]{4,3,2,1,0:T(8,128)(2,1)S(1)} %bitcast.20, bf16[64,128]{1,0:T(8,128)(2,1)} %constant.71.theta_h, bf16[256,128]{1,0:T(8,128)(2,1)} %constant.72.phi_h, f32[2,128,256]{2,1,0:T(8,128)} %constant.65.clone.cos_h, f32[2,128,256]{2,1,0:T(8,128)} %constant.66.clone.sin_h), custom_call_target="tpu_custom_call" | custom-call | tf_op jit(solution)/shard_map/lower/pallas_call | solution.py:358
  153.0 4.7 %all-to-all-start.5 = ((bf16[8,8,2,8,128]{4,3,2,1,0:T(8,128)(2,1)}), bf16[8,8,2,8,128]{4,3,2,1,0:T(8,128)(2,1)S(1)}, u32[]{:S(2)}, u32[]{:S(2)}) async-start(bf16[8,8,2,8,128]{4,3,2,1,0:T(8,128)(2,1)} %lower.1), calls=%async_computation.5 | async-start | bytes 524288 | tf_op jit(solution)/shard_map/all_to_all | solution.py:388
  157.7 0.0 collective-permute-done.9.refs_3_
  157.8 0.0 collective-permute-done.10.refs_4_
  157.8 0.0 collective-permute-done.11.refs_5_
  157.8 2.2 %collective-permute-done.12.refs_6_ = bf16[64,2,8,128]{3,2,1,0:T(8,128)(2,1)S(1)} collective-permute-done((bf16[64,2,8,128]{3,2,1,0:T(8,128)(2,1)}, bf16[64,2,8,128]{3,2,1,0:T(8,128)(2,1)S(1)}, u32[]{:S(2)}, u32[]{:S(2)}) %collective-permute-start.12) | collective-permute-done | bytes 262176 | tf_op jit(solution)/shard_map/ppermute | solution.py:384
  159.9 2.9 %collective-permute-done.13.refs_7_ = bf16[64,2,8,128]{3,2,1,0:T(8,128)(2,1)S(1)} collective-permute-done((bf16[64,2,8,128]{3,2,1,0:T(8,128)(2,1)}, bf16[64,2,8,128]{3,2,1,0:T(8,128)(2,1)S(1)}, u32[]{:S(2)}, u32[]{:S(2)}) %collective-permute-start.13) | collective-permute-done | bytes 262176 | tf_op jit(solution)/shard_map/ppermute | solution.py:384
  162.8 2.4 %all-to-all-done.5 = bf16[8,8,2,8,128]{4,3,2,1,0:T(8,128)(2,1)S(1)} async-done(((bf16[8,8,2,8,128]{4,3,2,1,0:T(8,128)(2,1)}), bf16[8,8,2,8,128]{4,3,2,1,0:T(8,128)(2,1)S(1)}, u32[]{:S(2)}, u32[]{:S(2)}) %all-to-all-start.5) | async-done | bytes 262176 | tf_op jit(solution)/shard_map/all_to_all | solution.py:388
  165.3 0.0 copy-done.1
  165.3 0.0 copy-done.2
  165.3 4.0 %far_children.1 = bf16[64,2,8,128]{3,2,1,0:T(8,128)(2,1)} custom-call(s32[8,64]{1,0:T(8,128)S(1)} %get-tuple-element.19.code, bf16[64,2,8,128]{3,2,1,0:T(8,128)(2,1)S(1)} %copy-done.1, bf16[64,2,8,128]{3,2,1,0:T(8,128)(2,1)S(1)} %collective-permute-done.7.refs_1_, bf16[64,2,8,128]{3,2,1,0:T(8,128)(2,1)S(1)} %collective-permute-done.8.refs_2_, ...), custom_call_target="tpu_custom_call" | custom-call | tf_op jit(solution)/shard_map/far_children/pallas_call | solution.py:313
  (1 shorter events, 0.0 us)
Async XLA Ops:
  0.0 24.5 %copy-start.9 = (bf16[64,2,8,128]{3,2,1,0:T(8,128)(2,1)S(1)}, bf16[64,2,8,128]{3,2,1,0:T(8,128)(2,1)}, u32[]{:S(2)}) copy-start(bf16[64,2,8,128]{3,2,1,0:T(8,128)(2,1)} %param.15) | copy-start | bytes 786436
  0.0 29.3 %copy-start.8 = (s32[1024]{0:T(1024)S(1)}, s32[1024]{0:T(1024)}, u32[]{:S(2)}) copy-start(s32[1024]{0:T(1024)} %param.22) | copy-start | bytes 12292
  0.0 29.3 %copy-start.7 = (s32[16,8]{0,1:T(8,128)S(1)}, s32[16,8]{0,1:T(8,128)}, u32[]{:S(2)}) copy-start(s32[16,8]{0,1:T(8,128)} %param.21) | copy-start | bytes 1540
  0.0 29.3 %copy-start.6 = (s32[16,8]{0,1:T(8,128)S(1)}, s32[16,8]{0,1:T(8,128)}, u32[]{:S(2)}) copy-start(s32[16,8]{0,1:T(8,128)} %param.20) | copy-start | bytes 1540
  0.0 29.3 %copy-start.3 = (s32[4096]{0:T(1024)S(1)}, s32[4096]{0:T(1024)}, u32[]{:S(2)}) copy-start(s32[4096]{0:T(1024)} %param.18) | copy-start | bytes 49156
  0.0 29.3 %copy-start.5 = (s32[64,8]{0,1:T(8,128)S(1)}, s32[64,8]{0,1:T(8,128)}, u32[]{:S(2)}) copy-start(s32[64,8]{0,1:T(8,128)} %param.17) | copy-start | bytes 6148
  0.0 29.3 %copy-start.4 = (s32[64,8]{0,1:T(8,128)S(1)}, s32[64,8]{0,1:T(8,128)}, u32[]{:S(2)}) copy-start(s32[64,8]{0,1:T(8,128)} %param.16) | copy-start | bytes 6148
  24.5 11.4 %collective-permute-start = (bf16[256,8,128]{2,1,0:T(8,128)(2,1)S(1)}, bf16[256,8,128]{2,1,0:T(8,128)(2,1)S(1)}, u32[]{:S(2)}, u32[]{:S(2)}) collective-permute-start(bf16[256,8,128]{2,1,0:T(8,128)(2,1)S(1)} %pad_maximum_fusion.refs_0_), channel_id=1, source_target_pairs={{0,64},{64,128},{128,192},{192,256},{256,320},{320,384},{384,448},... | collective-permute-start | bytes 1572872 | tf_op jit(solution)/shard_map/ppermute | solution.py:384
  33.4 12.3 %collective-permute-start.1 = (bf16[256,8,128]{2,1,0:T(8,128)(2,1)S(1)}, bf16[256,8,128]{2,1,0:T(8,128)(2,1)S(1)}, u32[]{:S(2)}, u32[]{:S(2)}) collective-permute-start(bf16[256,8,128]{2,1,0:T(8,128)(2,1)S(1)} %pad_maximum_fusion.refs_0_), channel_id=1, source_target_pairs={{0,448},{64,0},{128,64},{192,128},{256,192},{320,256},{384,320},{4... | collective-permute-start | bytes 1572872 | tf_op jit(solution)/shard_map/ppermute | solution.py:384
  35.9 12.3 %collective-permute-start.4 = (bf16[256,8,128]{2,1,0:T(8,128)(2,1)S(1)}, bf16[256,8,128]{2,1,0:T(8,128)(2,1)S(1)}, u32[]{:S(2)}, u32[]{:S(2)}) collective-permute-start(bf16[256,8,128]{2,1,0:T(8,128)(2,1)S(1)} %collective-permute-done.refs_7_), channel_id=1, source_target_pairs={{0,64},{64,128},{128,192},{192,256},{256,320},{320,384},{384,448},... | collective-permute-start | bytes 1572872 | tf_op jit(solution)/shard_map/ppermute | solution.py:384
  45.7 12.3 %collective-permute-start.2 = (bf16[256,8,128]{2,1,0:T(8,128)(2,1)S(1)}, bf16[256,8,128]{2,1,0:T(8,128)(2,1)S(1)}, u32[]{:S(2)}, u32[]{:S(2)}) collective-permute-start(bf16[256,8,128]{2,1,0:T(8,128)(2,1)S(1)} %collective-permute-done.1.refs_1_), channel_id=1, source_target_pairs={{0,448},{64,0},{128,64},{192,128},{256,192},{320,256},{384,320},{4... | collective-permute-start | bytes 1572872 | tf_op jit(solution)/shard_map/ppermute | solution.py:384
  48.2 12.3 %collective-permute-start.5 = (bf16[256,8,128]{2,1,0:T(8,128)(2,1)S(1)}, bf16[256,8,128]{2,1,0:T(8,128)(2,1)S(1)}, u32[]{:S(2)}, u32[]{:S(2)}) collective-permute-start(bf16[256,8,128]{2,1,0:T(8,128)(2,1)S(1)} %collective-permute-done.4.refs_6_), channel_id=1, source_target_pairs={{0,64},{64,128},{128,192},{192,256},{256,320},{320,384},{384,448},... | collective-permute-start | bytes 1572872 | tf_op jit(solution)/shard_map/ppermute | solution.py:384
  58.0 25.9 %collective-permute-start.3 = (bf16[256,8,128]{2,1,0:T(8,128)(2,1)S(1)}, bf16[256,8,128]{2,1,0:T(8,128)(2,1)S(1)}, u32[]{:S(2)}, u32[]{:S(2)}) collective-permute-start(bf16[256,8,128]{2,1,0:T(8,128)(2,1)S(1)} %collective-permute-done.2.refs_2_), channel_id=1, source_target_pairs={{0,448},{64,0},{128,64},{192,128},{256,192},{320,256},{384,320},{4... | collective-permute-start | bytes 1572872 | tf_op jit(solution)/shard_map/ppermute | solution.py:384
  60.5 23.4 %collective-permute-start.6 = (bf16[256,8,128]{2,1,0:T(8,128)(2,1)S(1)}, bf16[256,8,128]{2,1,0:T(8,128)(2,1)S(1)}, u32[]{:S(2)}, u32[]{:S(2)}) collective-permute-start(bf16[256,8,128]{2,1,0:T(8,128)(2,1)S(1)} %collective-permute-done.5.refs_5_), channel_id=1, source_target_pairs={{0,64},{64,128},{128,192},{192,256},{256,320},{320,384},{384,448},... | collective-permute-start | bytes 1572872 | tf_op jit(solution)/shard_map/ppermute | solution.py:384
  88.2 34.1 %copy-start = (bf16[40,2,16,256]{3,2,1,0:T(8,128)(2,1)S(1)}, bf16[40,2,16,256]{3,2,1,0:T(8,128)(2,1)}, u32[]{:S(2)}) copy-start(bf16[40,2,16,256]{3,2,1,0:T(8,128)(2,1)} %ops_hbm.1) | copy-start | bytes 1966084
  88.2 34.0 %all-to-all-start.3 = ((bf16[8,16,8,8,128]{4,3,2,1,0:T(8,128)(2,1)}), bf16[8,16,8,8,128]{4,3,2,1,0:T(8,128)(2,1)S(1)}, u32[]{:S(2)}, u32[]{:S(2)}) async-start(bf16[8,16,8,8,128]{4,3,2,1,0:T(8,128)(2,1)} %get-tuple-element.32), calls=%async_computation.3 | async-start | bytes 4194304 | tf_op jit(solution)/shard_map/all_to_all | solution.py:388
  92.0 47.5 %collective-permute-start.7 = (bf16[64,2,8,128]{3,2,1,0:T(8,128)(2,1)}, bf16[64,2,8,128]{3,2,1,0:T(8,128)(2,1)S(1)}, u32[]{:S(2)}, u32[]{:S(2)}) collective-permute-start(bf16[64,2,8,128]{3,2,1,0:T(8,128)(2,1)} %get-tuple-element.24), channel_id=1, source_target_pairs={{0,8},{8,16},{16,24},{24,32},{32,40},{40,48},{48,56},{56,0},{64,72... | collective-permute-start | bytes 786440 | tf_op jit(solution)/shard_map/ppermute | solution.py:384
  95.8 49.2 %collective-permute-start.8 = (bf16[64,2,8,128]{3,2,1,0:T(8,128)(2,1)}, bf16[64,2,8,128]{3,2,1,0:T(8,128)(2,1)S(1)}, u32[]{:S(2)}, u32[]{:S(2)}) collective-permute-start(bf16[64,2,8,128]{3,2,1,0:T(8,128)(2,1)} %get-tuple-element.25), channel_id=1, source_target_pairs={{0,16},{8,24},{16,32},{24,40},{32,48},{40,56},{48,0},{56,8},{64,80... | collective-permute-start | bytes 786440 | tf_op jit(solution)/shard_map/ppermute | solution.py:384
  122.3 43.0 %copy-start.1 = (bf16[64,2,8,128]{3,2,1,0:T(8,128)(2,1)S(1)}, bf16[64,2,8,128]{3,2,1,0:T(8,128)(2,1)}, u32[]{:S(2)}) copy-start(bf16[64,2,8,128]{3,2,1,0:T(8,128)(2,1)} %get-tuple-element.23.refs_0_) | copy-start | bytes 786436
  124.8 40.5 %copy-start.2 = (bf16[40,2,8,128]{3,2,1,0:T(8,128)(2,1)S(1)}, bf16[40,2,8,128]{3,2,1,0:T(8,128)(2,1)}, u32[]{:S(2)}) copy-start(bf16[40,2,8,128]{3,2,1,0:T(8,128)(2,1)} %refs_8_.1) | copy-start | bytes 491524
  124.8 23.6 %all-to-all-start.4 = ((bf16[16,8,8,128]{3,2,1,0:T(8,128)(2,1)}), bf16[16,8,8,128]{3,2,1,0:T(8,128)(2,1)S(1)}, u32[]{:S(2)}, u32[]{:S(2)}) async-start(bf16[16,8,8,128]{3,2,1,0:T(8,128)(2,1)} %far_parents.1), calls=%async_computation.4 | async-start | bytes 524288 | tf_op jit(solution)/shard_map/all_to_all | solution.py:388
  128.4 29.4 %collective-permute-start.9 = (bf16[64,2,8,128]{3,2,1,0:T(8,128)(2,1)}, bf16[64,2,8,128]{3,2,1,0:T(8,128)(2,1)S(1)}, u32[]{:S(2)}, u32[]{:S(2)}) collective-permute-start(bf16[64,2,8,128]{3,2,1,0:T(8,128)(2,1)} %get-tuple-element.26), channel_id=1, source_target_pairs={{0,24},{8,32},{16,40},{24,48},{32,56},{40,0},{48,8},{56,16},{64,88... | collective-permute-start | bytes 786440 | tf_op jit(solution)/shard_map/ppermute | solution.py:384
  130.3 27.5 %collective-permute-start.10 = (bf16[64,2,8,128]{3,2,1,0:T(8,128)(2,1)}, bf16[64,2,8,128]{3,2,1,0:T(8,128)(2,1)S(1)}, u32[]{:S(2)}, u32[]{:S(2)}) collective-permute-start(bf16[64,2,8,128]{3,2,1,0:T(8,128)(2,1)} %get-tuple-element.27), channel_id=1, source_target_pairs={{0,32},{8,40},{16,48},{24,56},{32,0},{40,8},{48,16},{56,24},{64,96... | collective-permute-start | bytes 786440 | tf_op jit(solution)/shard_map/ppermute | solution.py:384
  133.4 24.4 %collective-permute-start.11 = (bf16[64,2,8,128]{3,2,1,0:T(8,128)(2,1)}, bf16[64,2,8,128]{3,2,1,0:T(8,128)(2,1)S(1)}, u32[]{:S(2)}, u32[]{:S(2)}) collective-permute-start(bf16[64,2,8,128]{3,2,1,0:T(8,128)(2,1)} %get-tuple-element.28), channel_id=1, source_target_pairs={{0,40},{8,48},{16,56},{24,0},{32,8},{40,16},{48,24},{56,32},{64,10... | collective-permute-start | bytes 786440 | tf_op jit(solution)/shard_map/ppermute | solution.py:384
  139.5 20.4 %collective-permute-start.12 = (bf16[64,2,8,128]{3,2,1,0:T(8,128)(2,1)}, bf16[64,2,8,128]{3,2,1,0:T(8,128)(2,1)S(1)}, u32[]{:S(2)}, u32[]{:S(2)}) collective-permute-start(bf16[64,2,8,128]{3,2,1,0:T(8,128)(2,1)} %get-tuple-element.29), channel_id=1, source_target_pairs={{0,48},{8,56},{16,0},{24,8},{32,16},{40,24},{48,32},{56,40},{64,11... | collective-permute-start | bytes 786440 | tf_op jit(solution)/shard_map/ppermute | solution.py:384
  145.0 17.9 %collective-permute-start.13 = (bf16[64,2,8,128]{3,2,1,0:T(8,128)(2,1)}, bf16[64,2,8,128]{3,2,1,0:T(8,128)(2,1)S(1)}, u32[]{:S(2)}, u32[]{:S(2)}) collective-permute-start(bf16[64,2,8,128]{3,2,1,0:T(8,128)(2,1)} %get-tuple-element.30), channel_id=1, source_target_pairs={{0,56},{8,0},{16,8},{24,16},{32,24},{40,32},{48,40},{56,48},{64,12... | collective-permute-start | bytes 786440 | tf_op jit(solution)/shard_map/ppermute | solution.py:384
  153.0 12.2 %all-to-all-start.5 = ((bf16[8,8,2,8,128]{4,3,2,1,0:T(8,128)(2,1)}), bf16[8,8,2,8,128]{4,3,2,1,0:T(8,128)(2,1)S(1)}, u32[]{:S(2)}, u32[]{:S(2)}) async-start(bf16[8,8,2,8,128]{4,3,2,1,0:T(8,128)(2,1)} %lower.1), calls=%async_computation.5 | async-start | bytes 524288 | tf_op jit(solution)/shard_map/all_to_all | solution.py:388

commit v5 on v4

--- a/solution.py
+++ b/solution.py
@@ -112,8 +112,8 @@
         plan_body,
         out_shape=(
             jax.ShapeDtypeStruct((SIDE, 128), I32),
-            jax.ShapeDtypeStruct((8, 64), I32),
-            jax.ShapeDtypeStruct((8, 16), I32),
+            pltpu.HBM((8, 64), I32),
+            pltpu.HBM((8, 16), I32),
         ),
         in_specs=[pl.BlockSpec(memory_space=pltpu.SMEM)] + [pl.BlockSpec(memory_space=VM)] * 6,
         out_specs=(pl.BlockSpec(memory_space=VM),) * 3,
@@ -286,7 +286,7 @@
 
 
 def child_far_body(code, *refs):
-    blocks, ops_hbm, term, out, recv, ops, sems = refs[:8], *refs[8:]
+    blocks, ops_hbm, out, recv, ops, sems = refs[:8], *refs[8:]
     copies = fetch((ops_hbm, *blocks), (ops.at[pl.ds(0, 40)], *(recv.at[i] for i in range(8))), sems)
     ops[40] = jnp.zeros(ops.shape[1:], BF16)
     for copy in copies:
@@ -302,20 +302,18 @@
             c, d = recv[lane, at, 0].astype(F32), recv[lane, at, 1].astype(F32)
             real = real + (a * c - b * d)
             imag = imag + (a * d + b * c)
-        out[r, 0] = (real + term[r, 0].astype(F32)).astype(BF16)
-        out[r, 1] = (imag + term[r, 1].astype(F32)).astype(BF16)
+        out[r, 0] = real
+        out[r, 1] = imag
         return carry
 
     lax.fori_loop(0, 64, row, 0, unroll=2)
 
 
-def far_children(code, blocks, ops, term):
+def far_children(code, blocks, ops):
     return pl.pallas_call(
         child_far_body,
-        out_shape=jax.ShapeDtypeStruct((64, 2, 8, 128), BF16),
-        in_specs=[pl.BlockSpec(memory_space=pltpu.SMEM)]
-        + [pl.BlockSpec(memory_space=ANY)] * 9
-        + [pl.BlockSpec(memory_space=VM)],
+        out_shape=pltpu.HBM((64, 2, 8, 128), F32),
+        in_specs=[pl.BlockSpec(memory_space=pltpu.SMEM)] + [pl.BlockSpec(memory_space=ANY)] * 9,
         out_specs=pl.BlockSpec(memory_space=VM),
         scratch_shapes=[
             pltpu.VMEM((SIDE, 64, 2, 8, 128), BF16),
@@ -324,12 +322,12 @@
         ],
         compiler_params=pltpu.CompilerParams(vmem_limit_bytes=GRANT),
         name="far_children",
-    )(code, *blocks, ops, term)
-
-
-def down_body(far, theta_h, phi_h, cos_h, sin_h, out, theta, phi, cos_t, sin_t, turned, sems):
-    for copy in fetch((theta_h, phi_h, cos_h, sin_h), (theta, phi, cos_t, sin_t), sems):
-        copy.wait()
+    )(code, *blocks, ops)
+
+
+def down_body(far, theta, phi_h, cos_t, sin_t, out, phi, turned, sem):
+    copy = pltpu.make_async_copy(phi_h, phi, sem)
+    copy.start()
     for q in range(2):
         for u in range(PT // 8):
             at = pl.ds(u * 8, 8)
@@ -346,6 +344,7 @@
                 turned[(q * 4 + k) * 2 + 1, at, :] = (ci - sr).astype(BF16)
                 turned[(q * 4 + m) * 2, at, :] = (cr - si).astype(BF16)
                 turned[(q * 4 + m) * 2 + 1, at, :] = (ci + sr).astype(BF16)
+    copy.wait()
     for r in range(8):
         for c in range(2):
             narrowed = bmm(turned[r * 2 + c], phi[...]).astype(BF16)
@@ -358,10 +357,13 @@
     return pl.pallas_call(
         down_body,
         out_shape=jax.ShapeDtypeStruct((8, 8, 2, 8, 128), BF16),
-        in_specs=[pl.BlockSpec(memory_space=VM)] + [pl.BlockSpec(memory_space=pltpu.HBM)] * 4,
+        in_specs=[pl.BlockSpec(memory_space=ANY if i == 2 else VM) for i in range(5)],
         out_specs=pl.BlockSpec(memory_space=VM),
-        scratch_shapes=[pltpu.VMEM(t.shape, t.dtype) for t in tables]
-        + [pltpu.VMEM((16, PT, PP), BF16), pltpu.SemaphoreType.DMA((4,))],
+        scratch_shapes=[
+            pltpu.VMEM(tables[1].shape, BF16),
+            pltpu.VMEM((16, PT, PP), BF16),
+            pltpu.SemaphoreType.DMA,
+        ],
         compiler_params=pltpu.CompilerParams(vmem_limit_bytes=GRANT),
         name="lower",
     )(far, *tables)
@@ -435,12 +437,12 @@
     children_in = {0: children_out[0]}
     for d in (4, 3, 5, 2, 6, 1, 7):
         children_in[d] = hop(children_out[d], d, TRADE)
-    sums = far_parents(parent_code, parents_in.reshape(128, 8, 8, 128), parent_ops)
+    sums = far_parents(hold(parent_code), parents_in.reshape(128, 8, 8, 128), parent_ops)
     turned = swap(sums, "angle").reshape(8, 2, 8, 8, 128)
-    terms = swap(lower(turned, tuple(map(hold, (theta_down, phi_down, cos_t, sin_t)))), "angle")
-    return far_children(
-        child_code, [children_in[d] for d in range(SIDE)], child_ops, terms.reshape(64, 2, 8, 128)
-    )
+    term = lower(turned, (theta_down, hold(phi_down), cos_t, sin_t))
+    term = swap(term, "angle").reshape(64, 2, 8, 128)
+    child_far = far_children(hold(child_code), [children_in[d] for d in range(SIDE)], child_ops)
+    return (child_far + term.astype(F32)).astype(BF16)
 
 
 def solution(mesh):

time: 170 us -> 172 us (1.012)
  the two profiles are of different devices: /device:TPU:24 before, /device:TPU:26 now
where the time goes in v5:
time: 172 us; the launch traced here: 170 us
  starting transfers between devices  68.9 us (40%)
  blocking collectives  38.8 us (23%)
  waiting for transfers between devices  37 us (22%)
  Pallas kernels  23.4 us (14%)
  other arithmetic  1.92 us (1%)
    ppermute x14, starting transfers between devices, hop(): return lax.ppermute(x, BOTH, pairs)  55.4 us
    all_to_all x3, blocking collectives, swap(): lax.all_to_all(x, axis, split_axis=0, concat_axis=0, tiled=True, **kw)  38.8 us
    all_to_all x3, waiting for transfers between devices, swap(): lax.all_to_all(x, axis, split_axis=0, concat_axis=0, tiled=True, **kw)  22 us
    ppermute x14, waiting for transfers between devices, hop(): return lax.ppermute(x, BOTH, pairs)  14.9 us
    all_to_all x3, starting transfers between devices, swap(): lax.all_to_all(x, axis, split_axis=0, concat_axis=0, tiled=True, **kw)  13.5 us
    pallas_call x1, Pallas kernels, far_children(): pl.pallas_call(child_far_body, out_shape=pltpu.HBM((64, 2, 8, 128), F32),...  5.05 us
    pallas_call x1, Pallas kernels, plan(): pl.pallas_call(plan_body, out_shape=(jax.ShapeDtypeStruct((SIDE, 128), I3...  4.43 us
    pallas_call x1, Pallas kernels, select(): pl.pallas_call(select_body, out_shape=(pltpu.HBM((SIDE, 16, 8, 8, 128), B...  4.33 us
  transfers between devices with their start and end apart: 17, of which 8 were waited for; matrix products, arithmetic and copies ran while one was open for 0% of the time, Pallas kernels for 10%

profile of v5, /device:TPU:26, one launch (start us, length us, event | category | flops | bytes accessed | tf_op | source)
XLA Modules:
  0.0 170.4 jit_solution(12786094886037128315)
XLA Ops:
  0.0 0.0 copy-start.9
  0.0 0.0 copy-start.6
  0.0 0.0 copy-start.8
  0.0 0.0 copy-start.7
  0.0 11.0 %all_to_all.30 = bf16[64,2,8,128]{3,2,1,0:T(8,128)(2,1)S(1)} all-to-all(bf16[64,2,8,128]{3,2,1,0:T(8,128)(2,1)} %param.15), channel_id=1, replica_groups=mesh['box'=64,'angle'=8] {'angle'}, dimensions={0} | all-to-all | bytes 524288 | tf_op jit(solution)/shard_map/all_to_all | solution.py:390
  11.1 2.6 %lift.1 = bf16[8,2,8,8,128]{4,3,2,1,0:T(8,128)(2,1)S(1)} custom-call(bf16[8,8,2,8,128]{4,3,2,1,0:T(8,128)(2,1)S(1)} %bitcast.23, bf16[128,64]{1,0:T(8,128)(2,1)} %constant.69.theta_h, bf16[128,256]{1,0:T(8,128)(2,1)} %constant.70.phi_h, f32[2,128,256]{2,1,0:T(8,128)} %constant.65.clone.cos_h.cos_t, f32[2,128,256]{2,1,0:T(8,128)} %constant.66.clone.sin_h.sin_t), custom_call_target="tpu_custom_call" | custom-call | tf_op jit(solution)/shard_map/lift/pallas_call | solution.py:160
  13.6 9.9 %all_to_all.31 = bf16[8,2,8,8,128]{4,3,2,1,0:T(8,128)(2,1)S(1)} all-to-all(bf16[8,2,8,8,128]{4,3,2,1,0:T(8,128)(2,1)S(1)} %lift.1), channel_id=1, replica_groups=mesh['box'=64,'angle'=8] {'angle'}, dimensions={0} | all-to-all | bytes 524288 | tf_op jit(solution)/shard_map/all_to_all | solution.py:390
  23.6 0.0 copy-done.12
  23.6 4.7 %collective-permute-start = (bf16[256,8,128]{2,1,0:T(8,128)(2,1)S(1)}, bf16[256,8,128]{2,1,0:T(8,128)(2,1)S(1)}, u32[]{:S(2)}, u32[]{:S(2)}) collective-permute-start(bf16[256,8,128]{2,1,0:T(8,128)(2,1)S(1)} %pad_maximum_fusion.refs_0_), channel_id=1, source_target_pairs={{0,64},{64,128},{128,192},{192,256},{256,320},{320,384},{384,448},... | collective-permute-start | bytes 1572872 | tf_op jit(solution)/shard_map/ppermute | solution.py:386
  28.3 0.1 pad_add_fusion.where
  28.4 0.0 copy-done.11
  28.4 0.0 copy-done.10
  28.4 0.0 copy-done.9
  28.4 0.0 copy-done.6
  28.4 0.0 copy-done.8
  28.5 0.0 copy-done.7
  28.5 4.4 %plan.1 = (s32[8,128]{1,0:T(8,128)S(1)}, s32[8,64]{1,0:T(8,128)}, s32[8,16]{1,0:T(8,128)}) custom-call(s32[3]{0:T(128)S(1)} %pad_add_fusion.where, s32[8,64]{1,0:T(8,128)S(1)} %bitcast.26, s32[8,64]{1,0:T(8,128)S(1)} %bitcast.27, s32[32,128]{1,0:T(8,128)S(1)} %bitcast.25, s32[8,16]{1,0:T(8,128)S(1)} %bitcast.28, s32[8,16]{1,0:T(8,128)S(1)} %bitcast.29, ...), custom_call_target="tpu_custom_call" | custom-call | tf_op jit(solution)/shard_map/plan/pallas_call | solution.py:111
  32.9 1.9 %collective-permute-start.1 = (bf16[256,8,128]{2,1,0:T(8,128)(2,1)S(1)}, bf16[256,8,128]{2,1,0:T(8,128)(2,1)S(1)}, u32[]{:S(2)}, u32[]{:S(2)}) collective-permute-start(bf16[256,8,128]{2,1,0:T(8,128)(2,1)S(1)} %pad_maximum_fusion.refs_0_), channel_id=1, source_target_pairs={{0,448},{64,0},{128,64},{192,128},{256,192},{320,256},{384,320},{4... | collective-permute-start | bytes 1572872 | tf_op jit(solution)/shard_map/ppermute | solution.py:386
  34.8 0.2 collective-permute-done.refs_7_
  35.0 5.6 %collective-permute-start.4 = (bf16[256,8,128]{2,1,0:T(8,128)(2,1)S(1)}, bf16[256,8,128]{2,1,0:T(8,128)(2,1)S(1)}, u32[]{:S(2)}, u32[]{:S(2)}) collective-permute-start(bf16[256,8,128]{2,1,0:T(8,128)(2,1)S(1)} %collective-permute-done.refs_7_), channel_id=1, source_target_pairs={{0,64},{64,128},{128,192},{192,256},{256,320},{320,384},{384,448},... | collective-permute-start | bytes 1572872 | tf_op jit(solution)/shard_map/ppermute | solution.py:386
  40.6 4.6 %collective-permute-done.1.refs_1_ = bf16[256,8,128]{2,1,0:T(8,128)(2,1)S(1)} collective-permute-done((bf16[256,8,128]{2,1,0:T(8,128)(2,1)S(1)}, bf16[256,8,128]{2,1,0:T(8,128)(2,1)S(1)}, u32[]{:S(2)}, u32[]{:S(2)}) %collective-permute-start.1) | collective-permute-done | bytes 524320 | tf_op jit(solution)/shard_map/ppermute | solution.py:386
  45.2 1.9 %collective-permute-start.2 = (bf16[256,8,128]{2,1,0:T(8,128)(2,1)S(1)}, bf16[256,8,128]{2,1,0:T(8,128)(2,1)S(1)}, u32[]{:S(2)}, u32[]{:S(2)}) collective-permute-start(bf16[256,8,128]{2,1,0:T(8,128)(2,1)S(1)} %collective-permute-done.1.refs_1_), channel_id=1, source_target_pairs={{0,448},{64,0},{128,64},{192,128},{256,192},{320,256},{384,320},{4... | collective-permute-start | bytes 1572872 | tf_op jit(solution)/shard_map/ppermute | solution.py:386
  47.1 0.2 collective-permute-done.4.refs_6_
  47.3 5.6 %collective-permute-start.5 = (bf16[256,8,128]{2,1,0:T(8,128)(2,1)S(1)}, bf16[256,8,128]{2,1,0:T(8,128)(2,1)S(1)}, u32[]{:S(2)}, u32[]{:S(2)}) collective-permute-start(bf16[256,8,128]{2,1,0:T(8,128)(2,1)S(1)} %collective-permute-done.4.refs_6_), channel_id=1, source_target_pairs={{0,64},{64,128},{128,192},{192,256},{256,320},{320,384},{384,448},... | collective-permute-start | bytes 1572872 | tf_op jit(solution)/shard_map/ppermute | solution.py:386
  52.9 4.6 %collective-permute-done.2.refs_2_ = bf16[256,8,128]{2,1,0:T(8,128)(2,1)S(1)} collective-permute-done((bf16[256,8,128]{2,1,0:T(8,128)(2,1)S(1)}, bf16[256,8,128]{2,1,0:T(8,128)(2,1)S(1)}, u32[]{:S(2)}, u32[]{:S(2)}) %collective-permute-start.2) | collective-permute-done | bytes 524320 | tf_op jit(solution)/shard_map/ppermute | solution.py:386
  57.4 1.9 %collective-permute-start.3 = (bf16[256,8,128]{2,1,0:T(8,128)(2,1)S(1)}, bf16[256,8,128]{2,1,0:T(8,128)(2,1)S(1)}, u32[]{:S(2)}, u32[]{:S(2)}) collective-permute-start(bf16[256,8,128]{2,1,0:T(8,128)(2,1)S(1)} %collective-permute-done.2.refs_2_), channel_id=1, source_target_pairs={{0,448},{64,0},{128,64},{192,128},{256,192},{320,256},{384,320},{4... | collective-permute-start | bytes 1572872 | tf_op jit(solution)/shard_map/ppermute | solution.py:386
  59.4 0.2 collective-permute-done.5.refs_5_
  59.5 5.6 %collective-permute-start.6 = (bf16[256,8,128]{2,1,0:T(8,128)(2,1)S(1)}, bf16[256,8,128]{2,1,0:T(8,128)(2,1)S(1)}, u32[]{:S(2)}, u32[]{:S(2)}) collective-permute-start(bf16[256,8,128]{2,1,0:T(8,128)(2,1)S(1)} %collective-permute-done.5.refs_5_), channel_id=1, source_target_pairs={{0,64},{64,128},{128,192},{192,256},{256,320},{320,384},{384,448},... | collective-permute-start | bytes 1572872 | tf_op jit(solution)/shard_map/ppermute | solution.py:386
  65.1 17.8 %all_to_all.32 = s32[8,1,128]{2,1,0:T(1,128)S(1)} all-to-all(s32[8,1,128]{2,1,0:T(1,128)S(1)} %bitcast.31), channel_id=1, replica_groups={{0,8,16,24,32,40,48,56},{64,72,80,88,96,104,112,120},{128,136,144,152,1..., dimensions={0} | all-to-all | bytes 8192 | tf_op jit(solution)/shard_map/all_to_all | solution.py:390
  83.0 0.0 collective-permute-done.3.refs_3_
  83.0 0.0 collective-permute-done.6.refs_4_
  83.0 4.3 %select.9 = (bf16[8,16,8,8,128]{4,3,2,1,0:T(8,128)(2,1)}, bf16[64,2,8,128]{3,2,1,0:T(8,128)(2,1)}, bf16[64,2,8,128]{3,2,1,0:T(8,128)(2,1)}, bf16[64,2,8,128]{3,2...) custom-call(s32[3]{0:T(128)S(1)} %pad_add_fusion.where, ...), custom_call_target="tpu_custom_call" | custom-call | tf_op jit(solution)/shard_map/select/pallas_call | solution.py:226
  87.3 0.0 copy-start.2
  87.3 3.7 %all-to-all-start.3 = ((bf16[8,16,8,8,128]{4,3,2,1,0:T(8,128)(2,1)}), bf16[8,16,8,8,128]{4,3,2,1,0:T(8,128)(2,1)S(1)}, u32[]{:S(2)}, u32[]{:S(2)}) async-start(bf16[8,16,8,8,128]{4,3,2,1,0:T(8,128)(2,1)} %get-tuple-element.32), calls=%async_computation.3 | async-start | bytes 4194304 | tf_op jit(solution)/shard_map/all_to_all | solution.py:390
  91.1 0.0 copy-start
  91.1 0.0 copy-start.1
  91.1 0.0 copy-start.5
  91.1 3.9 %collective-permute-start.7 = (bf16[64,2,8,128]{3,2,1,0:T(8,128)(2,1)}, bf16[64,2,8,128]{3,2,1,0:T(8,128)(2,1)}, u32[]{:S(2)}, u32[]{:S(2)}) collective-permute-start(bf16[64,2,8,128]{3,2,1,0:T(8,128)(2,1)} %get-tuple-element.24), channel_id=1, source_target_pairs={{0,8},{8,16},{16,24},{24,32},{32,40},{40,48},{48,56},{56,0},{64,72... | collective-permute-start | bytes 786440 | tf_op jit(solution)/shard_map/ppermute | solution.py:386
  95.0 4.3 %collective-permute-start.8 = (bf16[64,2,8,128]{3,2,1,0:T(8,128)(2,1)}, bf16[64,2,8,128]{3,2,1,0:T(8,128)(2,1)}, u32[]{:S(2)}, u32[]{:S(2)}) collective-permute-start(bf16[64,2,8,128]{3,2,1,0:T(8,128)(2,1)} %get-tuple-element.25), channel_id=1, source_target_pairs={{0,16},{8,24},{16,32},{24,40},{32,48},{40,56},{48,0},{56,8},{64,80... | collective-permute-start | bytes 786440 | tf_op jit(solution)/shard_map/ppermute | solution.py:386
  99.3 22.0 %all-to-all-done.3 = bf16[8,16,8,8,128]{4,3,2,1,0:T(8,128)(2,1)S(1)} async-done(((bf16[8,16,8,8,128]{4,3,2,1,0:T(8,128)(2,1)}), bf16[8,16,8,8,128]{4,3,2,1,0:T(8,128)(2,1)S(1)}, u32[]{:S(2)}, u32[]{:S(2)}) %all-to-all-start.3) | async-done | bytes 2097184 | tf_op jit(solution)/shard_map/all_to_all | solution.py:390
  121.4 0.0 copy-done.2
  121.4 2.7 %far_parents.1 = bf16[16,8,8,128]{3,2,1,0:T(8,128)(2,1)} custom-call(s32[8,16]{1,0:T(8,128)} %get-tuple-element.31.code, bf16[128,8,8,128]{3,2,1,0:T(8,128)(2,1)S(1)} %bitcast.21, bf16[40,2,16,256]{3,2,1,0:T(8,128)(2,1)S(1)} %copy-done.2), custom_call_target="tpu_custom_call" | custom-call | tf_op jit(solution)/shard_map/far_parents/pallas_call | solution.py:273
  124.1 0.0 copy-start.4
  124.1 4.9 %all-to-all-start.4 = ((bf16[16,8,8,128]{3,2,1,0:T(8,128)(2,1)}), bf16[16,8,8,128]{3,2,1,0:T(8,128)(2,1)S(1)}, u32[]{:S(2)}, u32[]{:S(2)}) async-start(bf16[16,8,8,128]{3,2,1,0:T(8,128)(2,1)} %far_parents.1), calls=%async_computation.4 | async-start | bytes 524288 | tf_op jit(solution)/shard_map/all_to_all | solution.py:390
  129.0 1.9 %collective-permute-start.9 = (bf16[64,2,8,128]{3,2,1,0:T(8,128)(2,1)}, bf16[64,2,8,128]{3,2,1,0:T(8,128)(2,1)S(1)}, u32[]{:S(2)}, u32[]{:S(2)}) collective-permute-start(bf16[64,2,8,128]{3,2,1,0:T(8,128)(2,1)} %get-tuple-element.26), channel_id=1, source_target_pairs={{0,24},{8,32},{16,40},{24,48},{32,56},{40,0},{48,8},{56,16},{64,88... | collective-permute-start | bytes 786440 | tf_op jit(solution)/shard_map/ppermute | solution.py:386
  131.0 3.0 %collective-permute-start.10 = (bf16[64,2,8,128]{3,2,1,0:T(8,128)(2,1)}, bf16[64,2,8,128]{3,2,1,0:T(8,128)(2,1)S(1)}, u32[]{:S(2)}, u32[]{:S(2)}) collective-permute-start(bf16[64,2,8,128]{3,2,1,0:T(8,128)(2,1)} %get-tuple-element.27), channel_id=1, source_target_pairs={{0,32},{8,40},{16,48},{24,56},{32,0},{40,8},{48,16},{56,24},{64,96... | collective-permute-start | bytes 786440 | tf_op jit(solution)/shard_map/ppermute | solution.py:386
  134.0 6.2 %collective-permute-start.11 = (bf16[64,2,8,128]{3,2,1,0:T(8,128)(2,1)}, bf16[64,2,8,128]{3,2,1,0:T(8,128)(2,1)S(1)}, u32[]{:S(2)}, u32[]{:S(2)}) collective-permute-start(bf16[64,2,8,128]{3,2,1,0:T(8,128)(2,1)} %get-tuple-element.28), channel_id=1, source_target_pairs={{0,40},{8,48},{16,56},{24,0},{32,8},{40,16},{48,24},{56,32},{64,10... | collective-permute-start | bytes 786440 | tf_op jit(solution)/shard_map/ppermute | solution.py:386
  140.2 0.0 collective-permute-done.7.refs_1_
  140.2 5.4 %collective-permute-start.12 = (bf16[64,2,8,128]{3,2,1,0:T(8,128)(2,1)}, bf16[64,2,8,128]{3,2,1,0:T(8,128)(2,1)S(1)}, u32[]{:S(2)}, u32[]{:S(2)}) collective-permute-start(bf16[64,2,8,128]{3,2,1,0:T(8,128)(2,1)} %get-tuple-element.29), channel_id=1, source_target_pairs={{0,48},{8,56},{16,0},{24,8},{32,16},{40,24},{48,32},{56,40},{64,11... | collective-permute-start | bytes 786440 | tf_op jit(solution)/shard_map/ppermute | solution.py:386
  145.6 0.0 collective-permute-done.8.refs_2_
  145.7 3.4 %collective-permute-start.13 = (bf16[64,2,8,128]{3,2,1,0:T(8,128)(2,1)}, bf16[64,2,8,128]{3,2,1,0:T(8,128)(2,1)S(1)}, u32[]{:S(2)}, u32[]{:S(2)}) collective-permute-start(bf16[64,2,8,128]{3,2,1,0:T(8,128)(2,1)} %get-tuple-element.30), channel_id=1, source_target_pairs={{0,56},{8,0},{16,8},{24,16},{32,24},{40,32},{48,40},{56,48},{64,12... | collective-permute-start | bytes 786440 | tf_op jit(solution)/shard_map/ppermute | solution.py:386
  149.1 0.0 all-to-all-done.4
  149.1 0.0 copy-done
  149.1 4.3 %lower.1 = bf16[8,8,2,8,128]{4,3,2,1,0:T(8,128)(2,1)} custom-call(bf16[8,2,8,8,128]{4,3,2,1,0:T(8,128)(2,1)S(1)} %bitcast.22, bf16[64,128]{1,0:T(8,128)(2,1)S(1)} %copy-done.5, bf16[256,128]{1,0:T(8,128)(2,1)} %constant.72.phi_h, f32[2,128,256]{2,1,0:T(8,128)S(1)} %copy-done.1, f32[2,128,256]{2,1,0:T(8,128)S(1)} %copy-done), custom_call_target="tpu_custom_call" | custom-call | tf_op jit(solution)/shard_map/lower/pallas_call | solution.py:357
  153.4 4.8 %all-to-all-start.5 = ((bf16[8,8,2,8,128]{4,3,2,1,0:T(8,128)(2,1)}), bf16[8,8,2,8,128]{4,3,2,1,0:T(8,128)(2,1)S(1)}, u32[]{:S(2)}, u32[]{:S(2)}) async-start(bf16[8,8,2,8,128]{4,3,2,1,0:T(8,128)(2,1)} %lower.1), calls=%async_computation.5 | async-start | bytes 524288 | tf_op jit(solution)/shard_map/all_to_all | solution.py:390
  158.3 0.0 collective-permute-done.9.refs_3_
  158.3 0.0 collective-permute-done.10.refs_4_
  158.3 0.0 collective-permute-done.11.refs_5_
  158.3 2.3 %collective-permute-done.12.refs_6_ = bf16[64,2,8,128]{3,2,1,0:T(8,128)(2,1)S(1)} collective-permute-done((bf16[64,2,8,128]{3,2,1,0:T(8,128)(2,1)}, bf16[64,2,8,128]{3,2,1,0:T(8,128)(2,1)S(1)}, u32[]{:S(2)}, u32[]{:S(2)}) %collective-permute-start.12) | collective-permute-done | bytes 262176 | tf_op jit(solution)/shard_map/ppermute | solution.py:386
  160.6 2.9 %collective-permute-done.13.refs_7_ = bf16[64,2,8,128]{3,2,1,0:T(8,128)(2,1)S(1)} collective-permute-done((bf16[64,2,8,128]{3,2,1,0:T(8,128)(2,1)}, bf16[64,2,8,128]{3,2,1,0:T(8,128)(2,1)S(1)}, u32[]{:S(2)}, u32[]{:S(2)}) %collective-permute-start.13) | collective-permute-done | bytes 262176 | tf_op jit(solution)/shard_map/ppermute | solution.py:386
  163.5 0.0 copy-done.3
  163.5 5.1 %far_children.1 = f32[64,2,8,128]{3,2,1,0:T(8,128)} custom-call(s32[8,64]{1,0:T(8,128)} %get-tuple-element.19.code, bf16[64,2,8,128]{3,2,1,0:T(8,128)(2,1)S(1)} %copy-done.3, bf16[64,2,8,128]{3,2,1,0:T(8,128)(2,1)} %collective-permute-done.7.refs_1_, bf16[64,2,8,128]{3,2,1,0:T(8,128)(2,1)} %collective-permute-done.8.refs_2_, ...), custom_call_target="tpu_custom_call" | custom-call | tf_op jit(solution)/shard_map/far_children/pallas_call | solution.py:313
  168.6 0.0 all-to-all-done.5
  168.6 1.8 %fusion = bf16[64,2,8,128]{3,2,1,0:T(8,128)(2,1)} fusion(f32[64,2,8,128]{3,2,1,0:T(8,128)} %far_children.1, bf16[8,8,2,8,128]{4,3,2,1,0:T(8,128)(2,1)S(1)} %all-to-all-done.5), kind=kLoop, calls=%fused_computation.2 | loop fusion | flops 393216 | bytes 1048576 | tf_op jit(solution)/shard_map/convert_element_type | solution.py:445
  (8 shorter events, 0.1 us)
Async XLA Ops:
  0.0 23.6 %copy-start.12 = (bf16[64,2,8,128]{3,2,1,0:T(8,128)(2,1)S(1)}, bf16[64,2,8,128]{3,2,1,0:T(8,128)(2,1)}, u32[]{:S(2)}) copy-start(bf16[64,2,8,128]{3,2,1,0:T(8,128)(2,1)} %param.15) | copy-start | bytes 786436
  0.0 28.4 %copy-start.11 = (s32[1024]{0:T(1024)S(1)}, s32[1024]{0:T(1024)}, u32[]{:S(2)}) copy-start(s32[1024]{0:T(1024)} %param.22) | copy-start | bytes 12292
  0.0 28.4 %copy-start.10 = (s32[16,8]{0,1:T(8,128)S(1)}, s32[16,8]{0,1:T(8,128)}, u32[]{:S(2)}) copy-start(s32[16,8]{0,1:T(8,128)} %param.21) | copy-start | bytes 1540
  0.0 28.4 %copy-start.9 = (s32[16,8]{0,1:T(8,128)S(1)}, s32[16,8]{0,1:T(8,128)}, u32[]{:S(2)}) copy-start(s32[16,8]{0,1:T(8,128)} %param.20) | copy-start | bytes 1540
  0.0 28.4 %copy-start.6 = (s32[4096]{0:T(1024)S(1)}, s32[4096]{0:T(1024)}, u32[]{:S(2)}) copy-start(s32[4096]{0:T(1024)} %param.18) | copy-start | bytes 49156
  0.0 28.4 %copy-start.8 = (s32[64,8]{0,1:T(8,128)S(1)}, s32[64,8]{0,1:T(8,128)}, u32[]{:S(2)}) copy-start(s32[64,8]{0,1:T(8,128)} %param.17) | copy-start | bytes 6148
  0.0 28.4 %copy-start.7 = (s32[64,8]{0,1:T(8,128)S(1)}, s32[64,8]{0,1:T(8,128)}, u32[]{:S(2)}) copy-start(s32[64,8]{0,1:T(8,128)} %param.16) | copy-start | bytes 6148
  23.6 11.4 %collective-permute-start = (bf16[256,8,128]{2,1,0:T(8,128)(2,1)S(1)}, bf16[256,8,128]{2,1,0:T(8,128)(2,1)S(1)}, u32[]{:S(2)}, u32[]{:S(2)}) collective-permute-start(bf16[256,8,128]{2,1,0:T(8,128)(2,1)S(1)} %pad_maximum_fusion.refs_0_), channel_id=1, source_target_pairs={{0,64},{64,128},{128,192},{192,256},{256,320},{320,384},{384,448},... | collective-permute-start | bytes 1572872 | tf_op jit(solution)/shard_map/ppermute | solution.py:386
  32.9 12.3 %collective-permute-start.1 = (bf16[256,8,128]{2,1,0:T(8,128)(2,1)S(1)}, bf16[256,8,128]{2,1,0:T(8,128)(2,1)S(1)}, u32[]{:S(2)}, u32[]{:S(2)}) collective-permute-start(bf16[256,8,128]{2,1,0:T(8,128)(2,1)S(1)} %pad_maximum_fusion.refs_0_), channel_id=1, source_target_pairs={{0,448},{64,0},{128,64},{192,128},{256,192},{320,256},{384,320},{4... | collective-permute-start | bytes 1572872 | tf_op jit(solution)/shard_map/ppermute | solution.py:386
  35.0 12.3 %collective-permute-start.4 = (bf16[256,8,128]{2,1,0:T(8,128)(2,1)S(1)}, bf16[256,8,128]{2,1,0:T(8,128)(2,1)S(1)}, u32[]{:S(2)}, u32[]{:S(2)}) collective-permute-start(bf16[256,8,128]{2,1,0:T(8,128)(2,1)S(1)} %collective-permute-done.refs_7_), channel_id=1, source_target_pairs={{0,64},{64,128},{128,192},{192,256},{256,320},{320,384},{384,448},... | collective-permute-start | bytes 1572872 | tf_op jit(solution)/shard_map/ppermute | solution.py:386
  45.2 12.3 %collective-permute-start.2 = (bf16[256,8,128]{2,1,0:T(8,128)(2,1)S(1)}, bf16[256,8,128]{2,1,0:T(8,128)(2,1)S(1)}, u32[]{:S(2)}, u32[]{:S(2)}) collective-permute-start(bf16[256,8,128]{2,1,0:T(8,128)(2,1)S(1)} %collective-permute-done.1.refs_1_), channel_id=1, source_target_pairs={{0,448},{64,0},{128,64},{192,128},{256,192},{320,256},{384,320},{4... | collective-permute-start | bytes 1572872 | tf_op jit(solution)/shard_map/ppermute | solution.py:386
  47.3 12.3 %collective-permute-start.5 = (bf16[256,8,128]{2,1,0:T(8,128)(2,1)S(1)}, bf16[256,8,128]{2,1,0:T(8,128)(2,1)S(1)}, u32[]{:S(2)}, u32[]{:S(2)}) collective-permute-start(bf16[256,8,128]{2,1,0:T(8,128)(2,1)S(1)} %collective-permute-done.4.refs_6_), channel_id=1, source_target_pairs={{0,64},{64,128},{128,192},{192,256},{256,320},{320,384},{384,448},... | collective-permute-start | bytes 1572872 | tf_op jit(solution)/shard_map/ppermute | solution.py:386
  57.4 25.5 %collective-permute-start.3 = (bf16[256,8,128]{2,1,0:T(8,128)(2,1)S(1)}, bf16[256,8,128]{2,1,0:T(8,128)(2,1)S(1)}, u32[]{:S(2)}, u32[]{:S(2)}) collective-permute-start(bf16[256,8,128]{2,1,0:T(8,128)(2,1)S(1)} %collective-permute-done.2.refs_2_), channel_id=1, source_target_pairs={{0,448},{64,0},{128,64},{192,128},{256,192},{320,256},{384,320},{4... | collective-permute-start | bytes 1572872 | tf_op jit(solution)/shard_map/ppermute | solution.py:386
  59.5 23.4 %collective-permute-start.6 = (bf16[256,8,128]{2,1,0:T(8,128)(2,1)S(1)}, bf16[256,8,128]{2,1,0:T(8,128)(2,1)S(1)}, u32[]{:S(2)}, u32[]{:S(2)}) collective-permute-start(bf16[256,8,128]{2,1,0:T(8,128)(2,1)S(1)} %collective-permute-done.5.refs_5_), channel_id=1, source_target_pairs={{0,64},{64,128},{128,192},{192,256},{256,320},{320,384},{384,448},... | collective-permute-start | bytes 1572872 | tf_op jit(solution)/shard_map/ppermute | solution.py:386
  87.3 34.1 %copy-start.2 = (bf16[40,2,16,256]{3,2,1,0:T(8,128)(2,1)S(1)}, bf16[40,2,16,256]{3,2,1,0:T(8,128)(2,1)}, u32[]{:S(2)}) copy-start(bf16[40,2,16,256]{3,2,1,0:T(8,128)(2,1)} %ops_hbm.1) | copy-start | bytes 1966084
  87.3 34.0 %all-to-all-start.3 = ((bf16[8,16,8,8,128]{4,3,2,1,0:T(8,128)(2,1)}), bf16[8,16,8,8,128]{4,3,2,1,0:T(8,128)(2,1)S(1)}, u32[]{:S(2)}, u32[]{:S(2)}) async-start(bf16[8,16,8,8,128]{4,3,2,1,0:T(8,128)(2,1)} %get-tuple-element.32), calls=%async_computation.3 | async-start | bytes 4194304 | tf_op jit(solution)/shard_map/all_to_all | solution.py:390
  91.1 58.0 %copy-start = (f32[2,128,256]{2,1,0:T(8,128)S(1)}, f32[2,128,256]{2,1,0:T(8,128)}, u32[]{:S(2)}) copy-start(f32[2,128,256]{2,1,0:T(8,128)} %constant.66.clone.sin_h.sin_t) | copy-start | bytes 786436
  91.1 58.0 %copy-start.1 = (f32[2,128,256]{2,1,0:T(8,128)S(1)}, f32[2,128,256]{2,1,0:T(8,128)}, u32[]{:S(2)}) copy-start(f32[2,128,256]{2,1,0:T(8,128)} %constant.65.clone.cos_h.cos_t) | copy-start | bytes 786436
  91.1 58.0 %copy-start.5 = (bf16[64,128]{1,0:T(8,128)(2,1)S(1)}, bf16[64,128]{1,0:T(8,128)(2,1)}, u32[]{:S(2)}) copy-start(bf16[64,128]{1,0:T(8,128)(2,1)} %constant.71.theta) | copy-start | bytes 49156
  91.1 49.1 %collective-permute-start.7 = (bf16[64,2,8,128]{3,2,1,0:T(8,128)(2,1)}, bf16[64,2,8,128]{3,2,1,0:T(8,128)(2,1)}, u32[]{:S(2)}, u32[]{:S(2)}) collective-permute-start(bf16[64,2,8,128]{3,2,1,0:T(8,128)(2,1)} %get-tuple-element.24), channel_id=1, source_target_pairs={{0,8},{8,16},{16,24},{24,32},{32,40},{40,48},{48,56},{56,0},{64,72... | collective-permute-start | bytes 786440 | tf_op jit(solution)/shard_map/ppermute | solution.py:386
  95.0 50.6 %collective-permute-start.8 = (bf16[64,2,8,128]{3,2,1,0:T(8,128)(2,1)}, bf16[64,2,8,128]{3,2,1,0:T(8,128)(2,1)}, u32[]{:S(2)}, u32[]{:S(2)}) collective-permute-start(bf16[64,2,8,128]{3,2,1,0:T(8,128)(2,1)} %get-tuple-element.25), channel_id=1, source_target_pairs={{0,16},{8,24},{16,32},{24,40},{32,48},{40,56},{48,0},{56,8},{64,80... | collective-permute-start | bytes 786440 | tf_op jit(solution)/shard_map/ppermute | solution.py:386
  121.4 42.1 %copy-start.3 = (bf16[64,2,8,128]{3,2,1,0:T(8,128)(2,1)S(1)}, bf16[64,2,8,128]{3,2,1,0:T(8,128)(2,1)}, u32[]{:S(2)}) copy-start(bf16[64,2,8,128]{3,2,1,0:T(8,128)(2,1)} %get-tuple-element.23.refs_0_) | copy-start | bytes 786436
  124.1 39.4 %copy-start.4 = (bf16[40,2,8,128]{3,2,1,0:T(8,128)(2,1)S(1)}, bf16[40,2,8,128]{3,2,1,0:T(8,128)(2,1)}, u32[]{:S(2)}) copy-start(bf16[40,2,8,128]{3,2,1,0:T(8,128)(2,1)} %refs_8_.1) | copy-start | bytes 491524
  124.1 25.0 %all-to-all-start.4 = ((bf16[16,8,8,128]{3,2,1,0:T(8,128)(2,1)}), bf16[16,8,8,128]{3,2,1,0:T(8,128)(2,1)S(1)}, u32[]{:S(2)}, u32[]{:S(2)}) async-start(bf16[16,8,8,128]{3,2,1,0:T(8,128)(2,1)} %far_parents.1), calls=%async_computation.4 | async-start | bytes 524288 | tf_op jit(solution)/shard_map/all_to_all | solution.py:390
  129.0 29.2 %collective-permute-start.9 = (bf16[64,2,8,128]{3,2,1,0:T(8,128)(2,1)}, bf16[64,2,8,128]{3,2,1,0:T(8,128)(2,1)S(1)}, u32[]{:S(2)}, u32[]{:S(2)}) collective-permute-start(bf16[64,2,8,128]{3,2,1,0:T(8,128)(2,1)} %get-tuple-element.26), channel_id=1, source_target_pairs={{0,24},{8,32},{16,40},{24,48},{32,56},{40,0},{48,8},{56,16},{64,88... | collective-permute-start | bytes 786440 | tf_op jit(solution)/shard_map/ppermute | solution.py:386
  131.0 27.3 %collective-permute-start.10 = (bf16[64,2,8,128]{3,2,1,0:T(8,128)(2,1)}, bf16[64,2,8,128]{3,2,1,0:T(8,128)(2,1)S(1)}, u32[]{:S(2)}, u32[]{:S(2)}) collective-permute-start(bf16[64,2,8,128]{3,2,1,0:T(8,128)(2,1)} %get-tuple-element.27), channel_id=1, source_target_pairs={{0,32},{8,40},{16,48},{24,56},{32,0},{40,8},{48,16},{56,24},{64,96... | collective-permute-start | bytes 786440 | tf_op jit(solution)/shard_map/ppermute | solution.py:386
  134.0 24.3 %collective-permute-start.11 = (bf16[64,2,8,128]{3,2,1,0:T(8,128)(2,1)}, bf16[64,2,8,128]{3,2,1,0:T(8,128)(2,1)S(1)}, u32[]{:S(2)}, u32[]{:S(2)}) collective-permute-start(bf16[64,2,8,128]{3,2,1,0:T(8,128)(2,1)} %get-tuple-element.28), channel_id=1, source_target_pairs={{0,40},{8,48},{16,56},{24,0},{32,8},{40,16},{48,24},{56,32},{64,10... | collective-permute-start | bytes 786440 | tf_op jit(solution)/shard_map/ppermute | solution.py:386
  140.2 20.4 %collective-permute-start.12 = (bf16[64,2,8,128]{3,2,1,0:T(8,128)(2,1)}, bf16[64,2,8,128]{3,2,1,0:T(8,128)(2,1)S(1)}, u32[]{:S(2)}, u32[]{:S(2)}) collective-permute-start(bf16[64,2,8,128]{3,2,1,0:T(8,128)(2,1)} %get-tuple-element.29), channel_id=1, source_target_pairs={{0,48},{8,56},{16,0},{24,8},{32,16},{40,24},{48,32},{56,40},{64,11... | collective-permute-start | bytes 786440 | tf_op jit(solution)/shard_map/ppermute | solution.py:386
  145.7 17.9 %collective-permute-start.13 = (bf16[64,2,8,128]{3,2,1,0:T(8,128)(2,1)}, bf16[64,2,8,128]{3,2,1,0:T(8,128)(2,1)S(1)}, u32[]{:S(2)}, u32[]{:S(2)}) collective-permute-start(bf16[64,2,8,128]{3,2,1,0:T(8,128)(2,1)} %get-tuple-element.30), channel_id=1, source_target_pairs={{0,56},{8,0},{16,8},{24,16},{32,24},{40,32},{48,40},{56,48},{64,12... | collective-permute-start | bytes 786440 | tf_op jit(solution)/shard_map/ppermute | solution.py:386
  153.4 15.1 %all-to-all-start.5 = ((bf16[8,8,2,8,128]{4,3,2,1,0:T(8,128)(2,1)}), bf16[8,8,2,8,128]{4,3,2,1,0:T(8,128)(2,1)S(1)}, u32[]{:S(2)}, u32[]{:S(2)}) async-start(bf16[8,8,2,8,128]{4,3,2,1,0:T(8,128)(2,1)} %lower.1), calls=%async_computation.5 | async-start | bytes 524288 | tf_op jit(solution)/shard_map/all_to_all | solution.py:390

commit v6 on v5

--- a/solution.py
+++ b/solution.py
@@ -15,6 +15,7 @@
 PP = 256
 WAVE_NUMBER = 6.0
 SIDE = 8
+ORDER = (4, 3, 5, 2, 6, 1, 7, 0)
 BOTH = ("box", "angle")
 F32, BF16, I32 = jnp.float32, jnp.bfloat16, jnp.int32
 VM = pltpu.VMEM
@@ -111,7 +112,7 @@
     return pl.pallas_call(
         plan_body,
         out_shape=(
-            jax.ShapeDtypeStruct((SIDE, 128), I32),
+            pltpu.HBM((SIDE, 128), I32),
             pltpu.HBM((8, 64), I32),
             pltpu.HBM((8, 16), I32),
         ),
@@ -169,40 +170,35 @@
     )(field, *tables)
 
 
-def select_body(where, asked, *refs):
-    blocks, parents, children = refs[:8], refs[8], refs[9:17]
-    pool, parent_buf, child_buf, sems, parent_sems, child_sems = refs[17:]
-    copies = [
-        pltpu.make_async_copy(
-            b.at[pl.ds(128 * half, 128)], pool.at[half, i], sems.at[half, i]
-        )
-        for half in (1, 0)
-        for i, b in enumerate(blocks)
-    ]
-    for copy in copies:
-        copy.start()
-
-    def child_out(d):
-        return pltpu.make_async_copy(child_buf.at[d], children[d], child_sems.at[d])
-
-    def parent_out(h):
-        return pltpu.make_async_copy(parent_buf.at[h], parents.at[h], parent_sems.at[h])
-
-    for copy in copies[:8]:
+def pooled(blocks, first, pool, sems):
+    for copy in fetch([b.at[pl.ds(first, 128)] for b in blocks], [pool.at[i] for i in range(8)], sems):
         copy.wait()
+
+
+def parents_body(asked, *refs):
+    blocks, out, pool, buf, sems, out_sems = refs[:8], *refs[8:]
+    pooled(blocks, 128, pool, sems)
+
+    def copy_out(h):
+        return pltpu.make_async_copy(buf.at[h], out.at[h], out_sems.at[h])
 
     def peer(h, carry):
         for k in range(16):
             row = asked[h, 64 + k]
             at = pl.multiple_of((row & 15) * 8, 8)
-            parent_buf[h, k] = pool[1, row >> 4, pl.ds(at, 8)]
-        parent_out(h).start()
+            buf[h, k] = pool[row >> 4, pl.ds(at, 8)]
+        copy_out(h).start()
         return carry
 
     lax.fori_loop(0, SIDE, peer, 0)
-    for copy in copies[8:]:
-        copy.wait()
-    for d in range(SIDE):
+    for h in range(SIDE):
+        copy_out(h).wait()
+
+
+def children_body(where, asked, *refs):
+    blocks, outs, pool, buf, sems, out_sems = refs[:8], refs[8:16], *refs[16:]
+    pooled(blocks, 0, pool, sems)
+    for d in ORDER:
         h = (where[2] + d) & 7
 
         def some(i, carry):
@@ -210,35 +206,40 @@
                 k = i * 16 + j
                 row = asked[h, k]
                 at = pl.multiple_of((row & 63) * 2, 2)
-                child_buf[d, k] = pool[0, row >> 6, pl.ds(at, 2)]
+                buf[d, k] = pool[row >> 6, pl.ds(at, 2)]
             return carry
 
         lax.fori_loop(0, 4, some, 0)
-        child_out(d).start()
-    for h in range(SIDE):
-        parent_out(h).wait()
-    for d in range(SIDE):
-        child_out(d).wait()
-
-
-def select(where, asked, blocks):
-    hbm = pl.BlockSpec(memory_space=pltpu.HBM)
-    return pl.pallas_call(
-        select_body,
-        out_shape=(pltpu.HBM((SIDE, 16, 8, 8, 128), BF16),) + (pltpu.HBM((64, 2, 8, 128), BF16),) * SIDE,
-        in_specs=[pl.BlockSpec(memory_space=pltpu.SMEM)] * 2 + [pl.BlockSpec(memory_space=ANY)] * 8,
-        out_specs=(hbm,) * 9,
+        pltpu.make_async_copy(buf.at[d], outs[d], out_sems.at[d]).start()
+    for d in ORDER:
+        pltpu.make_async_copy(buf.at[d], outs[d], out_sems.at[d]).wait()
+
+
+def select_call(body, smem, blocks, shape, outs):
+    return pl.pallas_call(
+        body,
+        out_shape=outs,
+        in_specs=[pl.BlockSpec(memory_space=pltpu.SMEM)] * len(smem) + [pl.BlockSpec(memory_space=ANY)] * 8,
+        out_specs=jax.tree.map(lambda _: pl.BlockSpec(memory_space=pltpu.HBM), outs),
         scratch_shapes=[
-            pltpu.VMEM((2, 8, 128, 8, 128), BF16),
-            pltpu.VMEM((SIDE, 16, 8, 8, 128), BF16),
-            pltpu.VMEM((SIDE, 64, 2, 8, 128), BF16),
-            pltpu.SemaphoreType.DMA((2, 8)),
+            pltpu.VMEM((8, 128, 8, 128), BF16),
+            pltpu.VMEM(shape, BF16),
             pltpu.SemaphoreType.DMA((8,)),
             pltpu.SemaphoreType.DMA((8,)),
         ],
         compiler_params=pltpu.CompilerParams(vmem_limit_bytes=GRANT),
-        name="select",
-    )(where, asked, *blocks)
+        cost_estimate=pl.CostEstimate(flops=0, bytes_accessed=4_000_000, transcendentals=0),
+    )(*smem, *blocks)
+
+
+def select_parents(asked, blocks):
+    shape = (SIDE, 16, 8, 8, 128)
+    return select_call(parents_body, (asked,), blocks, shape, pltpu.HBM(shape, BF16))
+
+
+def select_children(where, asked, blocks):
+    outs = tuple(pltpu.HBM((64, 2, 8, 128), BF16) for _ in range(SIDE))
+    return select_call(children_body, (where, asked), blocks, (SIDE, 64, 2, 8, 128), outs)
 
 
 def parent_far_body(code, recv, ops_hbm, out, ops, sem):
@@ -328,12 +329,16 @@
 def down_body(far, theta, phi_h, cos_t, sin_t, out, phi, turned, sem):
     copy = pltpu.make_async_copy(phi_h, phi, sem)
     copy.start()
-    for q in range(2):
-        for u in range(PT // 8):
-            at = pl.ds(u * 8, 8)
+    for s in range(8):
+        at = pl.ds(s * 16, 16)
+        for q in range(2):
             re, im = (
                 jnp.concatenate(
-                    [far[u // 2, q, c * 4 + (u % 2) * 2 + v].astype(F32) for v in range(2)], axis=1
+                    [
+                        jnp.concatenate([far[s, q, c * 4 + u * 2 + v].astype(F32) for v in range(2)], axis=1)
+                        for u in range(2)
+                    ],
+                    axis=0,
                 )
                 for c in range(2)
             )
@@ -422,20 +427,21 @@
     wanted, child_code, parent_code = plan(
         where, child_list, child_op, child_home, parent_list, parent_op, parent_home
     )
-    own = jnp.concatenate([child_field.reshape(128, 8, 128), parents.reshape(128, 8, 128)])
+    own = hold(jnp.concatenate([child_field.reshape(128, 8, 128), parents.reshape(128, 8, 128)]))
     forth, back = [own], [own]
     for step in range(4):
         if step == 1:
             forth[1], wanted = lax.optimization_barrier((forth[1], wanted))
-        forth.append(hop(forth[-1], 1))
+        forth.append(hold(hop(forth[-1], 1)))
         if step < 3:
-            back.append(hop(back[-1], -1))
+            back.append(hold(hop(back[-1], -1)))
     blocks = back + [forth[8 - p] for p in range(4, 8)]
     asked = swap(wanted.reshape(SIDE, 1, 128), BOTH, axis_index_groups=TRADE).reshape(SIDE, 128)
-    parents_out, *children_out = select(where, asked, blocks)
+    parents_out = select_parents(asked, blocks)
     parents_in = swap(parents_out, BOTH, axis_index_groups=TRADE)
+    children_out = select_children(where, hold(asked), blocks)
     children_in = {0: children_out[0]}
-    for d in (4, 3, 5, 2, 6, 1, 7):
+    for d in ORDER[:-1]:
         children_in[d] = hop(children_out[d], d, TRADE)
     sums = far_parents(hold(parent_code), parents_in.reshape(128, 8, 8, 128), parent_ops)
     turned = swap(sums, "angle").reshape(8, 2, 8, 8, 128)

time: 172 us -> 172 us (level)
  waiting for transfers between devices: 37 us -> 31.5 us
  Pallas kernels: 23.4 us -> 28.2 us
    all_to_all x3, waiting for transfers between devices: 22 us -> 16.7 us  [swap(): lax.all_to_all(x, axis, split_axis=0, concat_axis=0, tiled=True, **kw)]
    pallas_call x2 -> x3, Pallas kernels: 8.76 us -> 13.5 us  [the longest x2 8.9 us: select_call(): pl.pallas_call(body, out_shape=outs, in_specs=[pl.BlockSpec(memory_space=...]
  transfers between devices with their start and end apart: 17 -> 17, of which waited for: 8 -> 5; matrix products, arithmetic and copies ran while one was open for 0% -> 0% of each run, Pallas kernels for 10% -> 13%
where the time goes in v6:
time: 172 us; the launch traced here: 171 us
  starting transfers between devices  68.7 us (40%)
  blocking collectives  38.9 us (23%)
  waiting for transfers between devices  31.5 us (18%)
  Pallas kernels  28.2 us (16%)
  other arithmetic  1.92 us (1%)
    ppermute x14, starting transfers between devices, hop(): return lax.ppermute(x, BOTH, pairs)  55.3 us
    all_to_all x3, blocking collectives, swap(): lax.all_to_all(x, axis, split_axis=0, concat_axis=0, tiled=True, **kw)  38.9 us
    all_to_all x3, waiting for transfers between devices, swap(): lax.all_to_all(x, axis, split_axis=0, concat_axis=0, tiled=True, **kw)  16.7 us
    ppermute x14, waiting for transfers between devices, hop(): return lax.ppermute(x, BOTH, pairs)  14.8 us
    all_to_all x3, starting transfers between devices, swap(): lax.all_to_all(x, axis, split_axis=0, concat_axis=0, tiled=True, **kw)  13.4 us
    pallas_call x2, Pallas kernels, select_call(): pl.pallas_call(body, out_shape=outs, in_specs=[pl.BlockSpec(memory_space=...  8.9 us
    pallas_call x1, Pallas kernels, far_children(): pl.pallas_call(child_far_body, out_shape=pltpu.HBM((64, 2, 8, 128), F32),...  5.04 us
    pallas_call x1, Pallas kernels, plan(): pl.pallas_call(plan_body, out_shape=(pltpu.HBM((SIDE, 128), I32), pltpu.H...  4.61 us
  transfers between devices with their start and end apart: 17, of which 5 were waited for; matrix products, arithmetic and copies ran while one was open for 0% of the time, Pallas kernels for 13%

profile of v6, /device:TPU:26, one launch (start us, length us, event | category | flops | bytes accessed | tf_op | source)
XLA Modules:
  0.0 170.7 jit_solution(9928920174161359911)
XLA Ops:
  0.0 0.0 copy-start.7
  0.0 0.0 copy-start.10
  0.0 0.0 copy-start.11
  0.0 0.0 copy-start.12
  0.0 11.0 %all_to_all.30 = bf16[64,2,8,128]{3,2,1,0:T(8,128)(2,1)S(1)} all-to-all(bf16[64,2,8,128]{3,2,1,0:T(8,128)(2,1)} %param.15), channel_id=1, replica_groups=mesh['box'=64,'angle'=8] {'angle'}, dimensions={0} | all-to-all | bytes 524288 | tf_op jit(solution)/shard_map/all_to_all | solution.py:395
  11.1 2.6 %lift.1 = bf16[8,2,8,8,128]{4,3,2,1,0:T(8,128)(2,1)S(1)} custom-call(bf16[8,8,2,8,128]{4,3,2,1,0:T(8,128)(2,1)S(1)} %bitcast.23, bf16[128,64]{1,0:T(8,128)(2,1)} %constant.69.theta_h, bf16[128,256]{1,0:T(8,128)(2,1)} %constant.70.phi_h, f32[2,128,256]{2,1,0:T(8,128)} %constant.65.clone.cos_h.cos_t, f32[2,128,256]{2,1,0:T(8,128)} %constant.66.clone.sin_h.sin_t), custom_call_target="tpu_custom_call" | custom-call | tf_op jit(solution)/shard_map/lift/pallas_call | solution.py:161
  13.6 9.9 %all_to_all.31 = bf16[8,2,8,8,128]{4,3,2,1,0:T(8,128)(2,1)S(1)} all-to-all(bf16[8,2,8,8,128]{4,3,2,1,0:T(8,128)(2,1)S(1)} %lift.1), channel_id=1, replica_groups=mesh['box'=64,'angle'=8] {'angle'}, dimensions={0} | all-to-all | bytes 524288 | tf_op jit(solution)/shard_map/all_to_all | solution.py:395
  23.6 0.0 copy-done.21
  23.6 0.0 copy-start.13
  23.6 4.7 %collective-permute-start = (bf16[256,8,128]{2,1,0:T(8,128)(2,1)S(1)}, bf16[256,8,128]{2,1,0:T(8,128)(2,1)S(1)}, u32[]{:S(2)}, u32[]{:S(2)}) collective-permute-start(bf16[256,8,128]{2,1,0:T(8,128)(2,1)S(1)} %pad_maximum_fusion.refs_0_), channel_id=1, source_target_pairs={{0,64},{64,128},{128,192},{192,256},{256,320},{320,384},{384,448},... | collective-permute-start | bytes 1572872 | tf_op jit(solution)/shard_map/ppermute | solution.py:391
  28.4 0.1 pad_add_fusion.where
  28.4 0.0 copy-done.8
  28.4 0.0 copy-done.9
  28.4 0.0 copy-done.7
  28.5 4.6 %plan.1 = (s32[8,128]{1,0:T(8,128)}, s32[8,64]{1,0:T(8,128)}, s32[8,16]{1,0:T(8,128)}) custom-call(s32[3]{0:T(128)S(1)} %pad_add_fusion.where, s32[8,64]{1,0:T(8,128)S(1)} %bitcast.27, s32[8,64]{1,0:T(8,128)S(1)} %bitcast.28, s32[32,128]{1,0:T(8,128)S(1)} %bitcast.26, s32[8,16]{1,0:T(8,128)S(1)} %bitcast.29, s32[8,16]{1,0:T(8,128)S(1)} %bitcast.30, ...), custom_call_target="tpu_custom_call" | custom-call | tf_op jit(solution)/shard_map/plan/pallas_call | solution.py:112
  33.1 1.9 %collective-permute-start.1 = (bf16[256,8,128]{2,1,0:T(8,128)(2,1)S(1)}, bf16[256,8,128]{2,1,0:T(8,128)(2,1)S(1)}, u32[]{:S(2)}, u32[]{:S(2)}) collective-permute-start(bf16[256,8,128]{2,1,0:T(8,128)(2,1)S(1)} %pad_maximum_fusion.refs_0_), channel_id=1, source_target_pairs={{0,448},{64,0},{128,64},{192,128},{256,192},{320,256},{384,320},{4... | collective-permute-start | bytes 1572872 | tf_op jit(solution)/shard_map/ppermute | solution.py:391
  35.0 0.0 collective-permute-done.refs_7_
  35.0 5.6 %collective-permute-start.4 = (bf16[256,8,128]{2,1,0:T(8,128)(2,1)S(1)}, bf16[256,8,128]{2,1,0:T(8,128)(2,1)S(1)}, u32[]{:S(2)}, u32[]{:S(2)}) collective-permute-start(bf16[256,8,128]{2,1,0:T(8,128)(2,1)S(1)} %collective-permute-done.refs_7_), channel_id=1, source_target_pairs={{0,64},{64,128},{128,192},{192,256},{256,320},{320,384},{384,448},... | collective-permute-start | bytes 1572872 | tf_op jit(solution)/shard_map/ppermute | solution.py:391
  40.6 4.8 %collective-permute-done.1.refs_1_ = bf16[256,8,128]{2,1,0:T(8,128)(2,1)S(1)} collective-permute-done((bf16[256,8,128]{2,1,0:T(8,128)(2,1)S(1)}, bf16[256,8,128]{2,1,0:T(8,128)(2,1)S(1)}, u32[]{:S(2)}, u32[]{:S(2)}) %collective-permute-start.1) | collective-permute-done | bytes 524320 | tf_op jit(solution)/shard_map/ppermute | solution.py:391
  45.4 1.9 %collective-permute-start.2 = (bf16[256,8,128]{2,1,0:T(8,128)(2,1)S(1)}, bf16[256,8,128]{2,1,0:T(8,128)(2,1)S(1)}, u32[]{:S(2)}, u32[]{:S(2)}) collective-permute-start(bf16[256,8,128]{2,1,0:T(8,128)(2,1)S(1)} %collective-permute-done.1.refs_1_), channel_id=1, source_target_pairs={{0,448},{64,0},{128,64},{192,128},{256,192},{320,256},{384,320},{4... | collective-permute-start | bytes 1572872 | tf_op jit(solution)/shard_map/ppermute | solution.py:391
  47.3 0.0 collective-permute-done.4.refs_6_
  47.3 5.6 %collective-permute-start.5 = (bf16[256,8,128]{2,1,0:T(8,128)(2,1)S(1)}, bf16[256,8,128]{2,1,0:T(8,128)(2,1)S(1)}, u32[]{:S(2)}, u32[]{:S(2)}) collective-permute-start(bf16[256,8,128]{2,1,0:T(8,128)(2,1)S(1)} %collective-permute-done.4.refs_6_), channel_id=1, source_target_pairs={{0,64},{64,128},{128,192},{192,256},{256,320},{320,384},{384,448},... | collective-permute-start | bytes 1572872 | tf_op jit(solution)/shard_map/ppermute | solution.py:391
  52.9 4.8 %collective-permute-done.2.refs_2_ = bf16[256,8,128]{2,1,0:T(8,128)(2,1)S(1)} collective-permute-done((bf16[256,8,128]{2,1,0:T(8,128)(2,1)S(1)}, bf16[256,8,128]{2,1,0:T(8,128)(2,1)S(1)}, u32[]{:S(2)}, u32[]{:S(2)}) %collective-permute-start.2) | collective-permute-done | bytes 524320 | tf_op jit(solution)/shard_map/ppermute | solution.py:391
  57.6 1.9 %collective-permute-start.3 = (bf16[256,8,128]{2,1,0:T(8,128)(2,1)S(1)}, bf16[256,8,128]{2,1,0:T(8,128)(2,1)S(1)}, u32[]{:S(2)}, u32[]{:S(2)}) collective-permute-start(bf16[256,8,128]{2,1,0:T(8,128)(2,1)S(1)} %collective-permute-done.2.refs_2_), channel_id=1, source_target_pairs={{0,448},{64,0},{128,64},{192,128},{256,192},{320,256},{384,320},{4... | collective-permute-start | bytes 1572872 | tf_op jit(solution)/shard_map/ppermute | solution.py:391
  59.6 0.0 collective-permute-done.5.refs_5_
  59.6 0.0 copy-start.18
  59.6 5.6 %collective-permute-start.6 = (bf16[256,8,128]{2,1,0:T(8,128)(2,1)S(1)}, bf16[256,8,128]{2,1,0:T(8,128)(2,1)S(1)}, u32[]{:S(2)}, u32[]{:S(2)}) collective-permute-start(bf16[256,8,128]{2,1,0:T(8,128)(2,1)S(1)} %collective-permute-done.5.refs_5_), channel_id=1, source_target_pairs={{0,64},{64,128},{128,192},{192,256},{256,320},{320,384},{384,448},... | collective-permute-start | bytes 1572872 | tf_op jit(solution)/shard_map/ppermute | solution.py:391
  65.2 18.0 %all_to_all.32 = s32[8,1,128]{2,1,0:T(1,128)S(1)} all-to-all(s32[8,1,128]{2,1,0:T(1,128)} %bitcast.34), channel_id=1, replica_groups={{0,8,16,24,32,40,48,56},{64,72,80,88,96,104,112,120},{128,136,144,152,1..., dimensions={0} | all-to-all | bytes 8192 | tf_op jit(solution)/shard_map/all_to_all | solution.py:395
  83.1 0.0 collective-permute-done.3.refs_3_
  83.1 0.0 collective-permute-done.6.refs_4_
  83.2 0.7 copy-done.19
  83.9 0.2 copy-done.20
  84.1 3.6 %shard_map.146 = bf16[8,16,8,8,128]{4,3,2,1,0:T(8,128)(2,1)} custom-call(s32[8,128]{1,0:T(8,128)S(1)} %bitcast.24, bf16[256,8,128]{2,1,0:T(8,128)(2,1)} %copy-done.13, bf16[256,8,128]{2,1,0:T(8,128)(2,1)} %copy-done.15, bf16[256,8,128]{2,1,0:T(8,128)(2,1)} %copy-done.17, bf16[256,8,128]{2,1,0:T(8,128)(2,1)} %copy-done.19, bf16[256,8,128]{2,1,0:T(8,128)(2,1)} %copy-done.20, ...), custom_call_target="tpu_custom_call" | custom-call | bytes 4000000 | tf_op jit(solution)/shard_map/pallas_call | solution.py:219
  87.7 3.6 %all-to-all-start.3 = ((bf16[8,16,8,8,128]{4,3,2,1,0:T(8,128)(2,1)}), bf16[8,16,8,8,128]{4,3,2,1,0:T(8,128)(2,1)S(1)}, u32[]{:S(2)}, u32[]{:S(2)}) async-start(bf16[8,16,8,8,128]{4,3,2,1,0:T(8,128)(2,1)} %shard_map.146), calls=%async_computation.3 | async-start | bytes 4194304 | tf_op jit(solution)/shard_map/all_to_all | solution.py:395
  91.4 0.0 copy-start.2
  91.4 5.3 %shard_map.145 = (bf16[64,2,8,128]{3,2,1,0:T(8,128)(2,1)}, bf16[64,2,8,128]{3,2,1,0:T(8,128)(2,1)}, bf16[64,2,8,128]{3,2,1,0:T(8,128)(2,1)}, bf16[64,2,8,128]{3,...) custom-call(s32[3]{0:T(128)S(1)} %pad_add_fusion.where, ...), custom_call_target="tpu_custom_call" | custom-call | bytes 4000000 | tf_op jit(solution)/shard_map/pallas_call | solution.py:219
  96.6 0.0 copy-start
  96.7 0.0 copy-start.1
  96.7 0.0 copy-start.6
  96.7 3.9 %collective-permute-start.7 = (bf16[64,2,8,128]{3,2,1,0:T(8,128)(2,1)}, bf16[64,2,8,128]{3,2,1,0:T(8,128)(2,1)}, u32[]{:S(2)}, u32[]{:S(2)}) collective-permute-start(bf16[64,2,8,128]{3,2,1,0:T(8,128)(2,1)} %get-tuple-element.23), channel_id=1, source_target_pairs={{0,8},{8,16},{16,24},{24,32},{32,40},{40,48},{48,56},{56,0},{64,72... | collective-permute-start | bytes 786440 | tf_op jit(solution)/shard_map/ppermute | solution.py:391
  100.6 4.3 %collective-permute-start.8 = (bf16[64,2,8,128]{3,2,1,0:T(8,128)(2,1)}, bf16[64,2,8,128]{3,2,1,0:T(8,128)(2,1)}, u32[]{:S(2)}, u32[]{:S(2)}) collective-permute-start(bf16[64,2,8,128]{3,2,1,0:T(8,128)(2,1)} %get-tuple-element.24), channel_id=1, source_target_pairs={{0,16},{8,24},{16,32},{24,40},{32,48},{40,56},{48,0},{56,8},{64,80... | collective-permute-start | bytes 786440 | tf_op jit(solution)/shard_map/ppermute | solution.py:391
  104.9 16.7 %all-to-all-done.3 = bf16[8,16,8,8,128]{4,3,2,1,0:T(8,128)(2,1)S(1)} async-done(((bf16[8,16,8,8,128]{4,3,2,1,0:T(8,128)(2,1)}), bf16[8,16,8,8,128]{4,3,2,1,0:T(8,128)(2,1)S(1)}, u32[]{:S(2)}, u32[]{:S(2)}) %all-to-all-start.3) | async-done | bytes 2097184 | tf_op jit(solution)/shard_map/all_to_all | solution.py:395
  121.7 2.7 %far_parents.1 = bf16[16,8,8,128]{3,2,1,0:T(8,128)(2,1)} custom-call(s32[8,16]{1,0:T(8,128)} %get-tuple-element.30.code, bf16[128,8,8,128]{3,2,1,0:T(8,128)(2,1)S(1)} %bitcast.21, bf16[40,2,16,256]{3,2,1,0:T(8,128)(2,1)S(1)} %copy-done.2), custom_call_target="tpu_custom_call" | custom-call | tf_op jit(solution)/shard_map/far_parents/pallas_call | solution.py:274
  124.4 0.0 copy-start.4
  124.4 4.9 %all-to-all-start.4 = ((bf16[16,8,8,128]{3,2,1,0:T(8,128)(2,1)}), bf16[16,8,8,128]{3,2,1,0:T(8,128)(2,1)S(1)}, u32[]{:S(2)}, u32[]{:S(2)}) async-start(bf16[16,8,8,128]{3,2,1,0:T(8,128)(2,1)} %far_parents.1), calls=%async_computation.4 | async-start | bytes 524288 | tf_op jit(solution)/shard_map/all_to_all | solution.py:395
  129.3 1.9 %collective-permute-start.9 = (bf16[64,2,8,128]{3,2,1,0:T(8,128)(2,1)}, bf16[64,2,8,128]{3,2,1,0:T(8,128)(2,1)S(1)}, u32[]{:S(2)}, u32[]{:S(2)}) collective-permute-start(bf16[64,2,8,128]{3,2,1,0:T(8,128)(2,1)} %get-tuple-element.25), channel_id=1, source_target_pairs={{0,24},{8,32},{16,40},{24,48},{32,56},{40,0},{48,8},{56,16},{64,88... | collective-permute-start | bytes 786440 | tf_op jit(solution)/shard_map/ppermute | solution.py:391
  131.3 3.0 %collective-permute-start.10 = (bf16[64,2,8,128]{3,2,1,0:T(8,128)(2,1)}, bf16[64,2,8,128]{3,2,1,0:T(8,128)(2,1)S(1)}, u32[]{:S(2)}, u32[]{:S(2)}) collective-permute-start(bf16[64,2,8,128]{3,2,1,0:T(8,128)(2,1)} %get-tuple-element.26), channel_id=1, source_target_pairs={{0,32},{8,40},{16,48},{24,56},{32,0},{40,8},{48,16},{56,24},{64,96... | collective-permute-start | bytes 786440 | tf_op jit(solution)/shard_map/ppermute | solution.py:391
  134.3 6.2 %collective-permute-start.11 = (bf16[64,2,8,128]{3,2,1,0:T(8,128)(2,1)}, bf16[64,2,8,128]{3,2,1,0:T(8,128)(2,1)S(1)}, u32[]{:S(2)}, u32[]{:S(2)}) collective-permute-start(bf16[64,2,8,128]{3,2,1,0:T(8,128)(2,1)} %get-tuple-element.27), channel_id=1, source_target_pairs={{0,40},{8,48},{16,56},{24,0},{32,8},{40,16},{48,24},{56,32},{64,10... | collective-permute-start | bytes 786440 | tf_op jit(solution)/shard_map/ppermute | solution.py:391
  140.5 0.0 collective-permute-done.7.refs_1_
  140.5 5.4 %collective-permute-start.12 = (bf16[64,2,8,128]{3,2,1,0:T(8,128)(2,1)}, bf16[64,2,8,128]{3,2,1,0:T(8,128)(2,1)S(1)}, u32[]{:S(2)}, u32[]{:S(2)}) collective-permute-start(bf16[64,2,8,128]{3,2,1,0:T(8,128)(2,1)} %get-tuple-element.28), channel_id=1, source_target_pairs={{0,48},{8,56},{16,0},{24,8},{32,16},{40,24},{48,32},{56,40},{64,11... | collective-permute-start | bytes 786440 | tf_op jit(solution)/shard_map/ppermute | solution.py:391
  145.9 0.0 collective-permute-done.8.refs_2_
  146.0 3.4 %collective-permute-start.13 = (bf16[64,2,8,128]{3,2,1,0:T(8,128)(2,1)}, bf16[64,2,8,128]{3,2,1,0:T(8,128)(2,1)S(1)}, u32[]{:S(2)}, u32[]{:S(2)}) collective-permute-start(bf16[64,2,8,128]{3,2,1,0:T(8,128)(2,1)} %get-tuple-element.29), channel_id=1, source_target_pairs={{0,56},{8,0},{16,8},{24,16},{32,24},{40,32},{48,40},{56,48},{64,12... | collective-permute-start | bytes 786440 | tf_op jit(solution)/shard_map/ppermute | solution.py:391
  149.4 0.0 all-to-all-done.4
  149.4 4.3 %lower.1 = bf16[8,8,2,8,128]{4,3,2,1,0:T(8,128)(2,1)} custom-call(bf16[8,2,8,8,128]{4,3,2,1,0:T(8,128)(2,1)S(1)} %bitcast.22, bf16[64,128]{1,0:T(8,128)(2,1)S(1)} %copy-done.6, bf16[256,128]{1,0:T(8,128)(2,1)} %constant.72.phi_h, f32[2,128,256]{2,1,0:T(8,128)S(1)} %copy-done, f32[2,128,256]{2,1,0:T(8,128)S(1)} %copy-done.1), custom_call_target="tpu_custom_call" | custom-call | tf_op jit(solution)/shard_map/lower/pallas_call | solution.py:362
  153.7 4.8 %all-to-all-start.5 = ((bf16[8,8,2,8,128]{4,3,2,1,0:T(8,128)(2,1)}), bf16[8,8,2,8,128]{4,3,2,1,0:T(8,128)(2,1)S(1)}, u32[]{:S(2)}, u32[]{:S(2)}) async-start(bf16[8,8,2,8,128]{4,3,2,1,0:T(8,128)(2,1)} %lower.1), calls=%async_computation.5 | async-start | bytes 524288 | tf_op jit(solution)/shard_map/all_to_all | solution.py:395
  158.6 0.0 collective-permute-done.9.refs_3_
  158.6 0.0 collective-permute-done.10.refs_4_
  158.6 0.0 collective-permute-done.11.refs_5_
  158.6 2.3 %collective-permute-done.12.refs_6_ = bf16[64,2,8,128]{3,2,1,0:T(8,128)(2,1)S(1)} collective-permute-done((bf16[64,2,8,128]{3,2,1,0:T(8,128)(2,1)}, bf16[64,2,8,128]{3,2,1,0:T(8,128)(2,1)S(1)}, u32[]{:S(2)}, u32[]{:S(2)}) %collective-permute-start.12) | collective-permute-done | bytes 262176 | tf_op jit(solution)/shard_map/ppermute | solution.py:391
  160.9 2.9 %collective-permute-done.13.refs_7_ = bf16[64,2,8,128]{3,2,1,0:T(8,128)(2,1)S(1)} collective-permute-done((bf16[64,2,8,128]{3,2,1,0:T(8,128)(2,1)}, bf16[64,2,8,128]{3,2,1,0:T(8,128)(2,1)S(1)}, u32[]{:S(2)}, u32[]{:S(2)}) %collective-permute-start.13) | collective-permute-done | bytes 262176 | tf_op jit(solution)/shard_map/ppermute | solution.py:391
  163.8 0.0 copy-done.4
  163.8 5.0 %far_children.1 = f32[64,2,8,128]{3,2,1,0:T(8,128)} custom-call(s32[8,64]{1,0:T(8,128)} %get-tuple-element.18.code, bf16[64,2,8,128]{3,2,1,0:T(8,128)(2,1)S(1)} %copy-done.3, bf16[64,2,8,128]{3,2,1,0:T(8,128)(2,1)} %collective-permute-done.7.refs_1_, bf16[64,2,8,128]{3,2,1,0:T(8,128)(2,1)} %collective-permute-done.8.refs_2_, ...), custom_call_target="tpu_custom_call" | custom-call | tf_op jit(solution)/shard_map/far_children/pallas_call | solution.py:314
  168.9 0.0 all-to-all-done.5
  168.9 1.8 %fusion = bf16[64,2,8,128]{3,2,1,0:T(8,128)(2,1)} fusion(f32[64,2,8,128]{3,2,1,0:T(8,128)} %far_children.1, bf16[8,8,2,8,128]{4,3,2,1,0:T(8,128)(2,1)S(1)} %all-to-all-done.5), kind=kLoop, calls=%fused_computation.2 | loop fusion | flops 393216 | bytes 1048576 | tf_op jit(solution)/shard_map/convert_element_type | solution.py:451
  (27 shorter events, 0.1 us)
Async XLA Ops:
  0.0 23.6 %copy-start.21 = (bf16[64,2,8,128]{3,2,1,0:T(8,128)(2,1)S(1)}, bf16[64,2,8,128]{3,2,1,0:T(8,128)(2,1)}, u32[]{:S(2)}) copy-start(bf16[64,2,8,128]{3,2,1,0:T(8,128)(2,1)} %param.15) | copy-start | bytes 786436
  0.0 28.4 %copy-start.8 = (s32[64,8]{0,1:T(8,128)S(1)}, s32[64,8]{0,1:T(8,128)}, u32[]{:S(2)}) copy-start(s32[64,8]{0,1:T(8,128)} %param.16) | copy-start | bytes 6148
  0.0 28.4 %copy-start.9 = (s32[64,8]{0,1:T(8,128)S(1)}, s32[64,8]{0,1:T(8,128)}, u32[]{:S(2)}) copy-start(s32[64,8]{0,1:T(8,128)} %param.17) | copy-start | bytes 6148
  0.0 28.4 %copy-start.7 = (s32[4096]{0:T(1024)S(1)}, s32[4096]{0:T(1024)}, u32[]{:S(2)}) copy-start(s32[4096]{0:T(1024)} %param.18) | copy-start | bytes 49156
  0.0 28.4 %copy-start.10 = (s32[16,8]{0,1:T(8,128)S(1)}, s32[16,8]{0,1:T(8,128)}, u32[]{:S(2)}) copy-start(s32[16,8]{0,1:T(8,128)} %param.20) | copy-start | bytes 1540
  0.0 28.4 %copy-start.11 = (s32[16,8]{0,1:T(8,128)S(1)}, s32[16,8]{0,1:T(8,128)}, u32[]{:S(2)}) copy-start(s32[16,8]{0,1:T(8,128)} %param.21) | copy-start | bytes 1540
  0.0 28.4 %copy-start.12 = (s32[1024]{0:T(1024)S(1)}, s32[1024]{0:T(1024)}, u32[]{:S(2)}) copy-start(s32[1024]{0:T(1024)} %param.22) | copy-start | bytes 12292
  23.6 59.5 %copy-start.13 = (bf16[256,8,128]{2,1,0:T(8,128)(2,1)}, bf16[256,8,128]{2,1,0:T(8,128)(2,1)S(1)}, u32[]{:S(2)}) copy-start(bf16[256,8,128]{2,1,0:T(8,128)(2,1)S(1)} %pad_maximum_fusion.refs_0_) | copy-start | bytes 1572868
  23.6 11.4 %collective-permute-start = (bf16[256,8,128]{2,1,0:T(8,128)(2,1)S(1)}, bf16[256,8,128]{2,1,0:T(8,128)(2,1)S(1)}, u32[]{:S(2)}, u32[]{:S(2)}) collective-permute-start(bf16[256,8,128]{2,1,0:T(8,128)(2,1)S(1)} %pad_maximum_fusion.refs_0_), channel_id=1, source_target_pairs={{0,64},{64,128},{128,192},{192,256},{256,320},{320,384},{384,448},... | collective-permute-start | bytes 1572872 | tf_op jit(solution)/shard_map/ppermute | solution.py:391
  33.1 12.3 %collective-permute-start.1 = (bf16[256,8,128]{2,1,0:T(8,128)(2,1)S(1)}, bf16[256,8,128]{2,1,0:T(8,128)(2,1)S(1)}, u32[]{:S(2)}, u32[]{:S(2)}) collective-permute-start(bf16[256,8,128]{2,1,0:T(8,128)(2,1)S(1)} %pad_maximum_fusion.refs_0_), channel_id=1, source_target_pairs={{0,448},{64,0},{128,64},{192,128},{256,192},{320,256},{384,320},{4... | collective-permute-start | bytes 1572872 | tf_op jit(solution)/shard_map/ppermute | solution.py:391
  35.0 48.1 %copy-start.14 = (bf16[256,8,128]{2,1,0:T(8,128)(2,1)}, bf16[256,8,128]{2,1,0:T(8,128)(2,1)S(1)}, u32[]{:S(2)}) copy-start(bf16[256,8,128]{2,1,0:T(8,128)(2,1)S(1)} %collective-permute-done.refs_7_) | copy-start | bytes 1572868
  35.0 12.3 %collective-permute-start.4 = (bf16[256,8,128]{2,1,0:T(8,128)(2,1)S(1)}, bf16[256,8,128]{2,1,0:T(8,128)(2,1)S(1)}, u32[]{:S(2)}, u32[]{:S(2)}) collective-permute-start(bf16[256,8,128]{2,1,0:T(8,128)(2,1)S(1)} %collective-permute-done.refs_7_), channel_id=1, source_target_pairs={{0,64},{64,128},{128,192},{192,256},{256,320},{320,384},{384,448},... | collective-permute-start | bytes 1572872 | tf_op jit(solution)/shard_map/ppermute | solution.py:391
  45.4 37.8 %copy-start.15 = (bf16[256,8,128]{2,1,0:T(8,128)(2,1)}, bf16[256,8,128]{2,1,0:T(8,128)(2,1)S(1)}, u32[]{:S(2)}) copy-start(bf16[256,8,128]{2,1,0:T(8,128)(2,1)S(1)} %collective-permute-done.1.refs_1_) | copy-start | bytes 1572868
  45.4 12.3 %collective-permute-start.2 = (bf16[256,8,128]{2,1,0:T(8,128)(2,1)S(1)}, bf16[256,8,128]{2,1,0:T(8,128)(2,1)S(1)}, u32[]{:S(2)}, u32[]{:S(2)}) collective-permute-start(bf16[256,8,128]{2,1,0:T(8,128)(2,1)S(1)} %collective-permute-done.1.refs_1_), channel_id=1, source_target_pairs={{0,448},{64,0},{128,64},{192,128},{256,192},{320,256},{384,320},{4... | collective-permute-start | bytes 1572872 | tf_op jit(solution)/shard_map/ppermute | solution.py:391
  47.3 35.9 %copy-start.16 = (bf16[256,8,128]{2,1,0:T(8,128)(2,1)}, bf16[256,8,128]{2,1,0:T(8,128)(2,1)S(1)}, u32[]{:S(2)}) copy-start(bf16[256,8,128]{2,1,0:T(8,128)(2,1)S(1)} %collective-permute-done.4.refs_6_) | copy-start | bytes 1572868
  47.3 12.3 %collective-permute-start.5 = (bf16[256,8,128]{2,1,0:T(8,128)(2,1)S(1)}, bf16[256,8,128]{2,1,0:T(8,128)(2,1)S(1)}, u32[]{:S(2)}, u32[]{:S(2)}) collective-permute-start(bf16[256,8,128]{2,1,0:T(8,128)(2,1)S(1)} %collective-permute-done.4.refs_6_), channel_id=1, source_target_pairs={{0,64},{64,128},{128,192},{192,256},{256,320},{320,384},{384,448},... | collective-permute-start | bytes 1572872 | tf_op jit(solution)/shard_map/ppermute | solution.py:391
  57.6 25.5 %copy-start.17 = (bf16[256,8,128]{2,1,0:T(8,128)(2,1)}, bf16[256,8,128]{2,1,0:T(8,128)(2,1)S(1)}, u32[]{:S(2)}) copy-start(bf16[256,8,128]{2,1,0:T(8,128)(2,1)S(1)} %collective-permute-done.2.refs_2_) | copy-start | bytes 1572868
  57.6 25.5 %collective-permute-start.3 = (bf16[256,8,128]{2,1,0:T(8,128)(2,1)S(1)}, bf16[256,8,128]{2,1,0:T(8,128)(2,1)S(1)}, u32[]{:S(2)}, u32[]{:S(2)}) collective-permute-start(bf16[256,8,128]{2,1,0:T(8,128)(2,1)S(1)} %collective-permute-done.2.refs_2_), channel_id=1, source_target_pairs={{0,448},{64,0},{128,64},{192,128},{256,192},{320,256},{384,320},{4... | collective-permute-start | bytes 1572872 | tf_op jit(solution)/shard_map/ppermute | solution.py:391
  59.6 23.6 %copy-start.18 = (bf16[256,8,128]{2,1,0:T(8,128)(2,1)}, bf16[256,8,128]{2,1,0:T(8,128)(2,1)S(1)}, u32[]{:S(2)}) copy-start(bf16[256,8,128]{2,1,0:T(8,128)(2,1)S(1)} %collective-permute-done.5.refs_5_) | copy-start | bytes 1572868
  59.6 23.5 %collective-permute-start.6 = (bf16[256,8,128]{2,1,0:T(8,128)(2,1)S(1)}, bf16[256,8,128]{2,1,0:T(8,128)(2,1)S(1)}, u32[]{:S(2)}, u32[]{:S(2)}) collective-permute-start(bf16[256,8,128]{2,1,0:T(8,128)(2,1)S(1)} %collective-permute-done.5.refs_5_), channel_id=1, source_target_pairs={{0,64},{64,128},{128,192},{192,256},{256,320},{320,384},{384,448},... | collective-permute-start | bytes 1572872 | tf_op jit(solution)/shard_map/ppermute | solution.py:391
  83.1 4.6 %copy-start.5 = (s32[8,1,128]{2,1,0:T(1,128)}, s32[8,1,128]{2,1,0:T(1,128)S(1)}, u32[]{:S(2)}) copy-start(s32[8,1,128]{2,1,0:T(1,128)S(1)} %all_to_all.32) | copy-start | bytes 12292
  83.1 0.8 copy-start.19
  83.1 1.0 copy-start.20
  87.7 33.9 %all-to-all-start.3 = ((bf16[8,16,8,8,128]{4,3,2,1,0:T(8,128)(2,1)}), bf16[8,16,8,8,128]{4,3,2,1,0:T(8,128)(2,1)S(1)}, u32[]{:S(2)}, u32[]{:S(2)}) async-start(bf16[8,16,8,8,128]{4,3,2,1,0:T(8,128)(2,1)} %shard_map.146), calls=%async_computation.3 | async-start | bytes 4194304 | tf_op jit(solution)/shard_map/all_to_all | solution.py:395
  91.4 30.3 %copy-start.2 = (bf16[40,2,16,256]{3,2,1,0:T(8,128)(2,1)S(1)}, bf16[40,2,16,256]{3,2,1,0:T(8,128)(2,1)}, u32[]{:S(2)}) copy-start(bf16[40,2,16,256]{3,2,1,0:T(8,128)(2,1)} %ops_hbm.1) | copy-start | bytes 1966084
  96.6 52.7 %copy-start = (f32[2,128,256]{2,1,0:T(8,128)S(1)}, f32[2,128,256]{2,1,0:T(8,128)}, u32[]{:S(2)}) copy-start(f32[2,128,256]{2,1,0:T(8,128)} %constant.65.clone.cos_h.cos_t) | copy-start | bytes 786436
  96.7 52.7 %copy-start.1 = (f32[2,128,256]{2,1,0:T(8,128)S(1)}, f32[2,128,256]{2,1,0:T(8,128)}, u32[]{:S(2)}) copy-start(f32[2,128,256]{2,1,0:T(8,128)} %constant.66.clone.sin_h.sin_t) | copy-start | bytes 786436
  96.7 52.7 %copy-start.6 = (bf16[64,128]{1,0:T(8,128)(2,1)S(1)}, bf16[64,128]{1,0:T(8,128)(2,1)}, u32[]{:S(2)}) copy-start(bf16[64,128]{1,0:T(8,128)(2,1)} %constant.71.theta) | copy-start | bytes 49156
  96.7 43.8 %collective-permute-start.7 = (bf16[64,2,8,128]{3,2,1,0:T(8,128)(2,1)}, bf16[64,2,8,128]{3,2,1,0:T(8,128)(2,1)}, u32[]{:S(2)}, u32[]{:S(2)}) collective-permute-start(bf16[64,2,8,128]{3,2,1,0:T(8,128)(2,1)} %get-tuple-element.23), channel_id=1, source_target_pairs={{0,8},{8,16},{16,24},{24,32},{32,40},{40,48},{48,56},{56,0},{64,72... | collective-permute-start | bytes 786440 | tf_op jit(solution)/shard_map/ppermute | solution.py:391
  100.6 45.3 %collective-permute-start.8 = (bf16[64,2,8,128]{3,2,1,0:T(8,128)(2,1)}, bf16[64,2,8,128]{3,2,1,0:T(8,128)(2,1)}, u32[]{:S(2)}, u32[]{:S(2)}) collective-permute-start(bf16[64,2,8,128]{3,2,1,0:T(8,128)(2,1)} %get-tuple-element.24), channel_id=1, source_target_pairs={{0,16},{8,24},{16,32},{24,40},{32,48},{40,56},{48,0},{56,8},{64,80... | collective-permute-start | bytes 786440 | tf_op jit(solution)/shard_map/ppermute | solution.py:391
  121.7 42.2 %copy-start.3 = (bf16[64,2,8,128]{3,2,1,0:T(8,128)(2,1)S(1)}, bf16[64,2,8,128]{3,2,1,0:T(8,128)(2,1)}, u32[]{:S(2)}) copy-start(bf16[64,2,8,128]{3,2,1,0:T(8,128)(2,1)} %get-tuple-element.22.refs_0_) | copy-start | bytes 786436
  124.4 39.4 %copy-start.4 = (bf16[40,2,8,128]{3,2,1,0:T(8,128)(2,1)S(1)}, bf16[40,2,8,128]{3,2,1,0:T(8,128)(2,1)}, u32[]{:S(2)}) copy-start(bf16[40,2,8,128]{3,2,1,0:T(8,128)(2,1)} %refs_8_.1) | copy-start | bytes 491524
  124.4 25.0 %all-to-all-start.4 = ((bf16[16,8,8,128]{3,2,1,0:T(8,128)(2,1)}), bf16[16,8,8,128]{3,2,1,0:T(8,128)(2,1)S(1)}, u32[]{:S(2)}, u32[]{:S(2)}) async-start(bf16[16,8,8,128]{3,2,1,0:T(8,128)(2,1)} %far_parents.1), calls=%async_computation.4 | async-start | bytes 524288 | tf_op jit(solution)/shard_map/all_to_all | solution.py:395
  129.3 29.2 %collective-permute-start.9 = (bf16[64,2,8,128]{3,2,1,0:T(8,128)(2,1)}, bf16[64,2,8,128]{3,2,1,0:T(8,128)(2,1)S(1)}, u32[]{:S(2)}, u32[]{:S(2)}) collective-permute-start(bf16[64,2,8,128]{3,2,1,0:T(8,128)(2,1)} %get-tuple-element.25), channel_id=1, source_target_pairs={{0,24},{8,32},{16,40},{24,48},{32,56},{40,0},{48,8},{56,16},{64,88... | collective-permute-start | bytes 786440 | tf_op jit(solution)/shard_map/ppermute | solution.py:391
  131.3 27.3 %collective-permute-start.10 = (bf16[64,2,8,128]{3,2,1,0:T(8,128)(2,1)}, bf16[64,2,8,128]{3,2,1,0:T(8,128)(2,1)S(1)}, u32[]{:S(2)}, u32[]{:S(2)}) collective-permute-start(bf16[64,2,8,128]{3,2,1,0:T(8,128)(2,1)} %get-tuple-element.26), channel_id=1, source_target_pairs={{0,32},{8,40},{16,48},{24,56},{32,0},{40,8},{48,16},{56,24},{64,96... | collective-permute-start | bytes 786440 | tf_op jit(solution)/shard_map/ppermute | solution.py:391
  134.3 24.3 %collective-permute-start.11 = (bf16[64,2,8,128]{3,2,1,0:T(8,128)(2,1)}, bf16[64,2,8,128]{3,2,1,0:T(8,128)(2,1)S(1)}, u32[]{:S(2)}, u32[]{:S(2)}) collective-permute-start(bf16[64,2,8,128]{3,2,1,0:T(8,128)(2,1)} %get-tuple-element.27), channel_id=1, source_target_pairs={{0,40},{8,48},{16,56},{24,0},{32,8},{40,16},{48,24},{56,32},{64,10... | collective-permute-start | bytes 786440 | tf_op jit(solution)/shard_map/ppermute | solution.py:391
  140.5 20.4 %collective-permute-start.12 = (bf16[64,2,8,128]{3,2,1,0:T(8,128)(2,1)}, bf16[64,2,8,128]{3,2,1,0:T(8,128)(2,1)S(1)}, u32[]{:S(2)}, u32[]{:S(2)}) collective-permute-start(bf16[64,2,8,128]{3,2,1,0:T(8,128)(2,1)} %get-tuple-element.28), channel_id=1, source_target_pairs={{0,48},{8,56},{16,0},{24,8},{32,16},{40,24},{48,32},{56,40},{64,11... | collective-permute-start | bytes 786440 | tf_op jit(solution)/shard_map/ppermute | solution.py:391
  146.0 17.9 %collective-permute-start.13 = (bf16[64,2,8,128]{3,2,1,0:T(8,128)(2,1)}, bf16[64,2,8,128]{3,2,1,0:T(8,128)(2,1)S(1)}, u32[]{:S(2)}, u32[]{:S(2)}) collective-permute-start(bf16[64,2,8,128]{3,2,1,0:T(8,128)(2,1)} %get-tuple-element.29), channel_id=1, source_target_pairs={{0,56},{8,0},{16,8},{24,16},{32,24},{40,32},{48,40},{56,48},{64,12... | collective-permute-start | bytes 786440 | tf_op jit(solution)/shard_map/ppermute | solution.py:391
  153.7 15.1 %all-to-all-start.5 = ((bf16[8,8,2,8,128]{4,3,2,1,0:T(8,128)(2,1)}), bf16[8,8,2,8,128]{4,3,2,1,0:T(8,128)(2,1)S(1)}, u32[]{:S(2)}, u32[]{:S(2)}) async-start(bf16[8,8,2,8,128]{4,3,2,1,0:T(8,128)(2,1)} %lower.1), calls=%async_computation.5 | async-start | bytes 524288 | tf_op jit(solution)/shard_map/all_to_all | solution.py:395

commit v7 on v5

--- a/solution.py
+++ b/solution.py
@@ -423,14 +423,12 @@
         where, child_list, child_op, child_home, parent_list, parent_op, parent_home
     )
     own = jnp.concatenate([child_field.reshape(128, 8, 128), parents.reshape(128, 8, 128)])
-    forth, back = [own], [own]
-    for step in range(4):
-        if step == 1:
-            forth[1], wanted = lax.optimization_barrier((forth[1], wanted))
-        forth.append(hop(forth[-1], 1))
-        if step < 3:
-            back.append(hop(back[-1], -1))
-    blocks = back + [forth[8 - p] for p in range(4, 8)]
+    up2, down2 = hop(own, 2), hop(own, -2)
+    up1, down1 = hop(own, 1), hop(own, -1)
+    up2, wanted = lax.optimization_barrier((up2, wanted))
+    up4 = hop(up2, 2)
+    up3, down3 = hop(up2, 1), hop(down2, -1)
+    blocks = [own, down1, down2, down3, up4, up3, up2, up1]
     asked = swap(wanted.reshape(SIDE, 1, 128), BOTH, axis_index_groups=TRADE).reshape(SIDE, 128)
     parents_out, *children_out = select(where, asked, blocks)
     parents_in = swap(parents_out, BOTH, axis_index_groups=TRADE)

time: 172 us -> 170 us (0.988)
  the two profiles are of different devices: /device:TPU:26 before, /device:TPU:1 now
where the time goes in v7:
time: 170 us; the launch traced here: 169 us
  starting transfers between devices  80.6 us (47%)
  waiting for transfers between devices  34.5 us (20%)
  blocking collectives  26.7 us (16%)
  Pallas kernels  24.5 us (14%)
  other arithmetic  1.92 us (1%)
    ppermute x14, starting transfers between devices, hop(): return lax.ppermute(x, BOTH, pairs)  52.6 us
    all_to_all x4, waiting for transfers between devices, swap(): lax.all_to_all(x, axis, split_axis=0, concat_axis=0, tiled=True, **kw)  28.9 us
    all_to_all x4, starting transfers between devices, swap(): lax.all_to_all(x, axis, split_axis=0, concat_axis=0, tiled=True, **kw)  28 us
    all_to_all x2, blocking collectives, swap(): lax.all_to_all(x, axis, split_axis=0, concat_axis=0, tiled=True, **kw)  26.7 us
    ppermute x14, waiting for transfers between devices, hop(): return lax.ppermute(x, BOTH, pairs)  5.55 us
    pallas_call x1, Pallas kernels, select(): pl.pallas_call(select_body, out_shape=(pltpu.HBM((SIDE, 16, 8, 8, 128), B...  5.17 us
    pallas_call x1, Pallas kernels, far_children(): pl.pallas_call(child_far_body, out_shape=pltpu.HBM((64, 2, 8, 128), F32),...  5.05 us
    pallas_call x1, Pallas kernels, plan(): pl.pallas_call(plan_body, out_shape=(jax.ShapeDtypeStruct((SIDE, 128), I3...  4.61 us
  transfers between devices with their start and end apart: 18, of which 5 were waited for; matrix products, arithmetic and copies ran while one was open for 0% of the time, Pallas kernels for 10%

profile of v7, /device:TPU:1, one launch (start us, length us, event | category | flops | bytes accessed | tf_op | source)
XLA Modules:
  0.0 168.6 jit_solution(18038954537742263110)
XLA Ops:
  0.0 0.0 copy-start.9
  0.0 0.0 copy-start.6
  0.0 0.0 copy-start.8
  0.0 0.0 copy-start.7
  0.0 16.7 %all_to_all.30 = bf16[64,2,8,128]{3,2,1,0:T(8,128)(2,1)S(1)} all-to-all(bf16[64,2,8,128]{3,2,1,0:T(8,128)(2,1)} %param.15), channel_id=1, replica_groups=mesh['box'=64,'angle'=8] {'angle'}, dimensions={0} | all-to-all | bytes 524288 | tf_op jit(solution)/shard_map/all_to_all | solution.py:390
  16.8 2.6 %lift.1 = bf16[8,2,8,8,128]{4,3,2,1,0:T(8,128)(2,1)S(1)} custom-call(bf16[8,8,2,8,128]{4,3,2,1,0:T(8,128)(2,1)S(1)} %bitcast.23, bf16[128,64]{1,0:T(8,128)(2,1)} %constant.69.theta_h, bf16[128,256]{1,0:T(8,128)(2,1)} %constant.70.phi_h, f32[2,128,256]{2,1,0:T(8,128)} %constant.65.clone.cos_h.cos_t, f32[2,128,256]{2,1,0:T(8,128)} %constant.66.clone.sin_h.sin_t), custom_call_target="tpu_custom_call" | custom-call | tf_op jit(solution)/shard_map/lift/pallas_call | solution.py:160
  19.4 9.9 %all_to_all.31 = bf16[8,2,8,8,128]{4,3,2,1,0:T(8,128)(2,1)S(1)} all-to-all(bf16[8,2,8,8,128]{4,3,2,1,0:T(8,128)(2,1)S(1)} %lift.1), channel_id=1, replica_groups=mesh['box'=64,'angle'=8] {'angle'}, dimensions={0} | all-to-all | bytes 524288 | tf_op jit(solution)/shard_map/all_to_all | solution.py:390
  29.3 0.0 copy-done.12
  29.3 1.9 %collective-permute-start = (bf16[256,8,128]{2,1,0:T(8,128)(2,1)S(1)}, bf16[256,8,128]{2,1,0:T(8,128)(2,1)S(1)}, u32[]{:S(2)}, u32[]{:S(2)}) collective-permute-start(bf16[256,8,128]{2,1,0:T(8,128)(2,1)S(1)} %pad_maximum_fusion.refs_0_), channel_id=1, source_target_pairs={{0,128},{64,192},{128,256},{192,320},{256,384},{320,448},{384,0},{... | collective-permute-start | bytes 1572872 | tf_op jit(solution)/shard_map/ppermute | solution.py:386
  31.3 6.3 %collective-permute-start.2 = (bf16[256,8,128]{2,1,0:T(8,128)(2,1)S(1)}, bf16[256,8,128]{2,1,0:T(8,128)(2,1)S(1)}, u32[]{:S(2)}, u32[]{:S(2)}) collective-permute-start(bf16[256,8,128]{2,1,0:T(8,128)(2,1)S(1)} %pad_maximum_fusion.refs_0_), channel_id=1, source_target_pairs={{0,384},{64,448},{128,0},{192,64},{256,128},{320,192},{384,256},{4... | collective-permute-start | bytes 1572872 | tf_op jit(solution)/shard_map/ppermute | solution.py:386
  37.6 0.1 pad_add_fusion.where
  37.7 0.0 copy-done.11
  37.7 0.0 copy-done.10
  37.7 0.0 copy-done.9
  37.7 0.0 copy-done.6
  37.7 0.0 copy-done.8
  37.7 0.0 copy-done.7
  37.7 4.6 %plan.1 = (s32[8,128]{1,0:T(8,128)}, s32[8,64]{1,0:T(8,128)}, s32[8,16]{1,0:T(8,128)}) custom-call(s32[3]{0:T(128)S(1)} %pad_add_fusion.where, s32[8,64]{1,0:T(8,128)S(1)} %bitcast.26, s32[8,64]{1,0:T(8,128)S(1)} %bitcast.27, s32[32,128]{1,0:T(8,128)S(1)} %bitcast.25, s32[8,16]{1,0:T(8,128)S(1)} %bitcast.28, s32[8,16]{1,0:T(8,128)S(1)} %bitcast.29, ...), custom_call_target="tpu_custom_call" | custom-call | tf_op jit(solution)/shard_map/plan/pallas_call | solution.py:111
  42.3 3.1 %collective-permute-start.6 = (bf16[256,8,128]{2,1,0:T(8,128)(2,1)S(1)}, bf16[256,8,128]{2,1,0:T(8,128)(2,1)S(1)}, u32[]{:S(2)}, u32[]{:S(2)}) collective-permute-start(bf16[256,8,128]{2,1,0:T(8,128)(2,1)S(1)} %pad_maximum_fusion.refs_0_), channel_id=1, source_target_pairs={{0,64},{64,128},{128,192},{192,256},{256,320},{320,384},{384,448},... | collective-permute-start | bytes 1572872 | tf_op jit(solution)/shard_map/ppermute | solution.py:386
  45.4 3.4 %collective-permute-start.1 = (bf16[256,8,128]{2,1,0:T(8,128)(2,1)S(1)}, bf16[256,8,128]{2,1,0:T(8,128)(2,1)S(1)}, u32[]{:S(2)}, u32[]{:S(2)}) collective-permute-start(bf16[256,8,128]{2,1,0:T(8,128)(2,1)S(1)} %pad_maximum_fusion.refs_0_), channel_id=1, source_target_pairs={{0,448},{64,0},{128,64},{192,128},{256,192},{320,256},{384,320},{4... | collective-permute-start | bytes 1572872 | tf_op jit(solution)/shard_map/ppermute | solution.py:386
  48.8 0.0 collective-permute-done.refs_6_
  48.9 0.9 collective-permute-done.2.refs_2_
  49.7 4.7 %collective-permute-start.3 = (bf16[256,8,128]{2,1,0:T(8,128)(2,1)S(1)}, bf16[256,8,128]{2,1,0:T(8,128)(2,1)S(1)}, u32[]{:S(2)}, u32[]{:S(2)}) collective-permute-start(bf16[256,8,128]{2,1,0:T(8,128)(2,1)S(1)} %collective-permute-done.2.refs_2_), channel_id=1, source_target_pairs={{0,448},{64,0},{128,64},{192,128},{256,192},{320,256},{384,320},{4... | collective-permute-start | bytes 1572872 | tf_op jit(solution)/shard_map/ppermute | solution.py:386
  54.4 1.9 %collective-permute-start.5 = (bf16[256,8,128]{2,1,0:T(8,128)(2,1)S(1)}, bf16[256,8,128]{2,1,0:T(8,128)(2,1)}, u32[]{:S(2)}, u32[]{:S(2)}) collective-permute-start(bf16[256,8,128]{2,1,0:T(8,128)(2,1)S(1)} %collective-permute-done.refs_6_), channel_id=1, source_target_pairs={{0,64},{64,128},{128,192},{192,256},{256,320},{320,384},{384,448},... | collective-permute-start | bytes 1572872 | tf_op jit(solution)/shard_map/ppermute | solution.py:386
  56.3 4.0 %collective-permute-start.4 = (bf16[256,8,128]{2,1,0:T(8,128)(2,1)S(1)}, bf16[256,8,128]{2,1,0:T(8,128)(2,1)}, u32[]{:S(2)}, u32[]{:S(2)}) collective-permute-start(bf16[256,8,128]{2,1,0:T(8,128)(2,1)S(1)} %collective-permute-done.refs_6_), channel_id=1, source_target_pairs={{0,128},{64,192},{128,256},{192,320},{256,384},{320,448},{384,0},{... | collective-permute-start | bytes 1572872 | tf_op jit(solution)/shard_map/ppermute | solution.py:386
  60.4 6.8 %all-to-all-start.2 = ((s32[8,1,128]{2,1,0:T(1,128)}), s32[8,1,128]{2,1,0:T(1,128)S(1)}, u32[]{:S(2)}, u32[]{:S(2)}) async-start(s32[8,1,128]{2,1,0:T(1,128)} %bitcast.13), calls=%async_computation.2 | async-start | bytes 8192 | tf_op jit(solution)/shard_map/all_to_all | solution.py:390
  67.2 0.0 collective-permute-done.6.refs_7_
  67.2 0.0 collective-permute-done.1.refs_1_
  67.2 7.2 %all-to-all-done.2 = s32[8,1,128]{2,1,0:T(1,128)S(1)} async-done(((s32[8,1,128]{2,1,0:T(1,128)}), s32[8,1,128]{2,1,0:T(1,128)S(1)}, u32[]{:S(2)}, u32[]{:S(2)}) %all-to-all-start.2) | async-done | bytes 4128 | tf_op jit(solution)/shard_map/all_to_all | solution.py:390
  74.4 0.0 collective-permute-done.3.refs_3_
  74.4 0.0 collective-permute-done.5.refs_5_
  74.4 0.0 collective-permute-done.4.refs_4_
  74.4 5.2 %select.9 = (bf16[8,16,8,8,128]{4,3,2,1,0:T(8,128)(2,1)}, bf16[64,2,8,128]{3,2,1,0:T(8,128)(2,1)}, bf16[64,2,8,128]{3,2,1,0:T(8,128)(2,1)}, bf16[64,2,8,128]{3,2...) custom-call(s32[3]{0:T(128)S(1)} %pad_add_fusion.where, ...), custom_call_target="tpu_custom_call" | custom-call | tf_op jit(solution)/shard_map/select/pallas_call | solution.py:226
  79.6 0.0 copy-start.2
  79.6 4.5 %all-to-all-start.3 = ((bf16[8,16,8,8,128]{4,3,2,1,0:T(8,128)(2,1)}), bf16[8,16,8,8,128]{4,3,2,1,0:T(8,128)(2,1)S(1)}, u32[]{:S(2)}, u32[]{:S(2)}) async-start(bf16[8,16,8,8,128]{4,3,2,1,0:T(8,128)(2,1)} %get-tuple-element.32), calls=%async_computation.3 | async-start | bytes 4194304 | tf_op jit(solution)/shard_map/all_to_all | solution.py:390
  84.2 0.0 copy-start.1
  84.2 0.0 copy-start.5
  84.2 3.5 %collective-permute-start.7 = (bf16[64,2,8,128]{3,2,1,0:T(8,128)(2,1)}, bf16[64,2,8,128]{3,2,1,0:T(8,128)(2,1)}, u32[]{:S(2)}, u32[]{:S(2)}) collective-permute-start(bf16[64,2,8,128]{3,2,1,0:T(8,128)(2,1)} %get-tuple-element.24), channel_id=1, source_target_pairs={{0,8},{8,16},{16,24},{24,32},{32,40},{40,48},{48,56},{56,0},{64,72... | collective-permute-start | bytes 786440 | tf_op jit(solution)/shard_map/ppermute | solution.py:386
  87.7 4.0 %collective-permute-start.8 = (bf16[64,2,8,128]{3,2,1,0:T(8,128)(2,1)}, bf16[64,2,8,128]{3,2,1,0:T(8,128)(2,1)}, u32[]{:S(2)}, u32[]{:S(2)}) collective-permute-start(bf16[64,2,8,128]{3,2,1,0:T(8,128)(2,1)} %get-tuple-element.25), channel_id=1, source_target_pairs={{0,16},{8,24},{16,32},{24,40},{32,48},{40,56},{48,0},{56,8},{64,80... | collective-permute-start | bytes 786440 | tf_op jit(solution)/shard_map/ppermute | solution.py:386
  91.7 21.7 %all-to-all-done.3 = bf16[8,16,8,8,128]{4,3,2,1,0:T(8,128)(2,1)S(1)} async-done(((bf16[8,16,8,8,128]{4,3,2,1,0:T(8,128)(2,1)}), bf16[8,16,8,8,128]{4,3,2,1,0:T(8,128)(2,1)S(1)}, u32[]{:S(2)}, u32[]{:S(2)}) %all-to-all-start.3) | async-done | bytes 2097184 | tf_op jit(solution)/shard_map/all_to_all | solution.py:390
  113.4 0.0 copy-done.2
  113.4 2.7 %far_parents.1 = bf16[16,8,8,128]{3,2,1,0:T(8,128)(2,1)} custom-call(s32[8,16]{1,0:T(8,128)} %get-tuple-element.31.code, bf16[128,8,8,128]{3,2,1,0:T(8,128)(2,1)S(1)} %bitcast.21, bf16[40,2,16,256]{3,2,1,0:T(8,128)(2,1)S(1)} %copy-done.2), custom_call_target="tpu_custom_call" | custom-call | tf_op jit(solution)/shard_map/far_parents/pallas_call | solution.py:273
  116.1 0.0 copy-start.4
  116.2 11.7 %all-to-all-start.4 = ((bf16[16,8,8,128]{3,2,1,0:T(8,128)(2,1)}), bf16[16,8,8,128]{3,2,1,0:T(8,128)(2,1)S(1)}, u32[]{:S(2)}, u32[]{:S(2)}) async-start(bf16[16,8,8,128]{3,2,1,0:T(8,128)(2,1)} %far_parents.1), calls=%async_computation.4 | async-start | bytes 524288 | tf_op jit(solution)/shard_map/all_to_all | solution.py:390
  127.8 4.8 %collective-permute-start.9 = (bf16[64,2,8,128]{3,2,1,0:T(8,128)(2,1)}, bf16[64,2,8,128]{3,2,1,0:T(8,128)(2,1)S(1)}, u32[]{:S(2)}, u32[]{:S(2)}) collective-permute-start(bf16[64,2,8,128]{3,2,1,0:T(8,128)(2,1)} %get-tuple-element.26), channel_id=1, source_target_pairs={{0,24},{8,32},{16,40},{24,48},{32,56},{40,0},{48,8},{56,16},{64,88... | collective-permute-start | bytes 786440 | tf_op jit(solution)/shard_map/ppermute | solution.py:386
  132.6 4.5 %collective-permute-start.10 = (bf16[64,2,8,128]{3,2,1,0:T(8,128)(2,1)}, bf16[64,2,8,128]{3,2,1,0:T(8,128)(2,1)S(1)}, u32[]{:S(2)}, u32[]{:S(2)}) collective-permute-start(bf16[64,2,8,128]{3,2,1,0:T(8,128)(2,1)} %get-tuple-element.27), channel_id=1, source_target_pairs={{0,32},{8,40},{16,48},{24,56},{32,0},{40,8},{48,16},{56,24},{64,96... | collective-permute-start | bytes 786440 | tf_op jit(solution)/shard_map/ppermute | solution.py:386
  137.1 6.4 %collective-permute-start.11 = (bf16[64,2,8,128]{3,2,1,0:T(8,128)(2,1)}, bf16[64,2,8,128]{3,2,1,0:T(8,128)(2,1)S(1)}, u32[]{:S(2)}, u32[]{:S(2)}) collective-permute-start(bf16[64,2,8,128]{3,2,1,0:T(8,128)(2,1)} %get-tuple-element.28), channel_id=1, source_target_pairs={{0,40},{8,48},{16,56},{24,0},{32,8},{40,16},{48,24},{56,32},{64,10... | collective-permute-start | bytes 786440 | tf_op jit(solution)/shard_map/ppermute | solution.py:386
  143.5 0.0 collective-permute-done.7.refs_1_
  143.5 1.9 %collective-permute-start.12 = (bf16[64,2,8,128]{3,2,1,0:T(8,128)(2,1)}, bf16[64,2,8,128]{3,2,1,0:T(8,128)(2,1)S(1)}, u32[]{:S(2)}, u32[]{:S(2)}) collective-permute-start(bf16[64,2,8,128]{3,2,1,0:T(8,128)(2,1)} %get-tuple-element.29), channel_id=1, source_target_pairs={{0,48},{8,56},{16,0},{24,8},{32,16},{40,24},{48,32},{56,40},{64,11... | collective-permute-start | bytes 786440 | tf_op jit(solution)/shard_map/ppermute | solution.py:386
  145.4 0.0 collective-permute-done.8.refs_2_
  145.4 2.2 %collective-permute-start.13 = (bf16[64,2,8,128]{3,2,1,0:T(8,128)(2,1)}, bf16[64,2,8,128]{3,2,1,0:T(8,128)(2,1)S(1)}, u32[]{:S(2)}, u32[]{:S(2)}) collective-permute-start(bf16[64,2,8,128]{3,2,1,0:T(8,128)(2,1)} %get-tuple-element.30), channel_id=1, source_target_pairs={{0,56},{8,0},{16,8},{24,16},{32,24},{40,32},{48,40},{56,48},{64,12... | collective-permute-start | bytes 786440 | tf_op jit(solution)/shard_map/ppermute | solution.py:386
  147.6 0.0 all-to-all-done.4
  147.6 0.0 copy-done
  147.7 4.3 %lower.1 = bf16[8,8,2,8,128]{4,3,2,1,0:T(8,128)(2,1)} custom-call(bf16[8,2,8,8,128]{4,3,2,1,0:T(8,128)(2,1)S(1)} %bitcast.22, bf16[64,128]{1,0:T(8,128)(2,1)S(1)} %copy-done.5, bf16[256,128]{1,0:T(8,128)(2,1)} %constant.72.phi_h, f32[2,128,256]{2,1,0:T(8,128)S(1)} %copy-done.1, f32[2,128,256]{2,1,0:T(8,128)S(1)} %copy-done), custom_call_target="tpu_custom_call" | custom-call | tf_op jit(solution)/shard_map/lower/pallas_call | solution.py:357
  152.0 5.0 %all-to-all-start.5 = ((bf16[8,8,2,8,128]{4,3,2,1,0:T(8,128)(2,1)}), bf16[8,8,2,8,128]{4,3,2,1,0:T(8,128)(2,1)S(1)}, u32[]{:S(2)}, u32[]{:S(2)}) async-start(bf16[8,8,2,8,128]{4,3,2,1,0:T(8,128)(2,1)} %lower.1), calls=%async_computation.5 | async-start | bytes 524288 | tf_op jit(solution)/shard_map/all_to_all | solution.py:390
  157.0 0.0 collective-permute-done.9.refs_3_
  157.0 0.0 collective-permute-done.10.refs_4_
  157.0 0.0 collective-permute-done.11.refs_5_
  157.0 2.3 %collective-permute-done.12.refs_6_ = bf16[64,2,8,128]{3,2,1,0:T(8,128)(2,1)S(1)} collective-permute-done((bf16[64,2,8,128]{3,2,1,0:T(8,128)(2,1)}, bf16[64,2,8,128]{3,2,1,0:T(8,128)(2,1)S(1)}, u32[]{:S(2)}, u32[]{:S(2)}) %collective-permute-start.12) | collective-permute-done | bytes 262176 | tf_op jit(solution)/shard_map/ppermute | solution.py:386
  159.4 2.3 %collective-permute-done.13.refs_7_ = bf16[64,2,8,128]{3,2,1,0:T(8,128)(2,1)S(1)} collective-permute-done((bf16[64,2,8,128]{3,2,1,0:T(8,128)(2,1)}, bf16[64,2,8,128]{3,2,1,0:T(8,128)(2,1)S(1)}, u32[]{:S(2)}, u32[]{:S(2)}) %collective-permute-start.13) | collective-permute-done | bytes 262176 | tf_op jit(solution)/shard_map/ppermute | solution.py:386
  161.7 0.0 copy-done.4
  161.7 5.1 %far_children.1 = f32[64,2,8,128]{3,2,1,0:T(8,128)} custom-call(s32[8,64]{1,0:T(8,128)} %get-tuple-element.19.code, bf16[64,2,8,128]{3,2,1,0:T(8,128)(2,1)S(1)} %copy-done.3, bf16[64,2,8,128]{3,2,1,0:T(8,128)(2,1)} %collective-permute-done.7.refs_1_, bf16[64,2,8,128]{3,2,1,0:T(8,128)(2,1)} %collective-permute-done.8.refs_2_, ...), custom_call_target="tpu_custom_call" | custom-call | tf_op jit(solution)/shard_map/far_children/pallas_call | solution.py:313
  166.7 0.0 all-to-all-done.5
  166.8 1.8 %fusion = bf16[64,2,8,128]{3,2,1,0:T(8,128)(2,1)} fusion(f32[64,2,8,128]{3,2,1,0:T(8,128)} %far_children.1, bf16[8,8,2,8,128]{4,3,2,1,0:T(8,128)(2,1)S(1)} %all-to-all-done.5), kind=kLoop, calls=%fused_computation.2 | loop fusion | flops 393216 | bytes 1048576 | tf_op jit(solution)/shard_map/convert_element_type | solution.py:443
  (9 shorter events, 0.1 us)
Async XLA Ops:
  0.0 29.3 %copy-start.12 = (bf16[64,2,8,128]{3,2,1,0:T(8,128)(2,1)S(1)}, bf16[64,2,8,128]{3,2,1,0:T(8,128)(2,1)}, u32[]{:S(2)}) copy-start(bf16[64,2,8,128]{3,2,1,0:T(8,128)(2,1)} %param.15) | copy-start | bytes 786436
  0.0 37.7 %copy-start.11 = (s32[1024]{0:T(1024)S(1)}, s32[1024]{0:T(1024)}, u32[]{:S(2)}) copy-start(s32[1024]{0:T(1024)} %param.22) | copy-start | bytes 12292
  0.0 37.7 %copy-start.10 = (s32[16,8]{0,1:T(8,128)S(1)}, s32[16,8]{0,1:T(8,128)}, u32[]{:S(2)}) copy-start(s32[16,8]{0,1:T(8,128)} %param.21) | copy-start | bytes 1540
  0.0 37.7 %copy-start.9 = (s32[16,8]{0,1:T(8,128)S(1)}, s32[16,8]{0,1:T(8,128)}, u32[]{:S(2)}) copy-start(s32[16,8]{0,1:T(8,128)} %param.20) | copy-start | bytes 1540
  0.0 37.7 %copy-start.6 = (s32[4096]{0:T(1024)S(1)}, s32[4096]{0:T(1024)}, u32[]{:S(2)}) copy-start(s32[4096]{0:T(1024)} %param.18) | copy-start | bytes 49156
  0.0 37.7 %copy-start.8 = (s32[64,8]{0,1:T(8,128)S(1)}, s32[64,8]{0,1:T(8,128)}, u32[]{:S(2)}) copy-start(s32[64,8]{0,1:T(8,128)} %param.17) | copy-start | bytes 6148
  0.0 37.7 %copy-start.7 = (s32[64,8]{0,1:T(8,128)S(1)}, s32[64,8]{0,1:T(8,128)}, u32[]{:S(2)}) copy-start(s32[64,8]{0,1:T(8,128)} %param.16) | copy-start | bytes 6148
  29.3 19.5 %collective-permute-start = (bf16[256,8,128]{2,1,0:T(8,128)(2,1)S(1)}, bf16[256,8,128]{2,1,0:T(8,128)(2,1)S(1)}, u32[]{:S(2)}, u32[]{:S(2)}) collective-permute-start(bf16[256,8,128]{2,1,0:T(8,128)(2,1)S(1)} %pad_maximum_fusion.refs_0_), channel_id=1, source_target_pairs={{0,128},{64,192},{128,256},{192,320},{256,384},{320,448},{384,0},{... | collective-permute-start | bytes 1572872 | tf_op jit(solution)/shard_map/ppermute | solution.py:386
  31.3 18.4 %collective-permute-start.2 = (bf16[256,8,128]{2,1,0:T(8,128)(2,1)S(1)}, bf16[256,8,128]{2,1,0:T(8,128)(2,1)S(1)}, u32[]{:S(2)}, u32[]{:S(2)}) collective-permute-start(bf16[256,8,128]{2,1,0:T(8,128)(2,1)S(1)} %pad_maximum_fusion.refs_0_), channel_id=1, source_target_pairs={{0,384},{64,448},{128,0},{192,64},{256,128},{320,192},{384,256},{4... | collective-permute-start | bytes 1572872 | tf_op jit(solution)/shard_map/ppermute | solution.py:386
  42.3 24.9 %collective-permute-start.6 = (bf16[256,8,128]{2,1,0:T(8,128)(2,1)S(1)}, bf16[256,8,128]{2,1,0:T(8,128)(2,1)S(1)}, u32[]{:S(2)}, u32[]{:S(2)}) collective-permute-start(bf16[256,8,128]{2,1,0:T(8,128)(2,1)S(1)} %pad_maximum_fusion.refs_0_), channel_id=1, source_target_pairs={{0,64},{64,128},{128,192},{192,256},{256,320},{320,384},{384,448},... | collective-permute-start | bytes 1572872 | tf_op jit(solution)/shard_map/ppermute | solution.py:386
  45.4 21.8 %collective-permute-start.1 = (bf16[256,8,128]{2,1,0:T(8,128)(2,1)S(1)}, bf16[256,8,128]{2,1,0:T(8,128)(2,1)S(1)}, u32[]{:S(2)}, u32[]{:S(2)}) collective-permute-start(bf16[256,8,128]{2,1,0:T(8,128)(2,1)S(1)} %pad_maximum_fusion.refs_0_), channel_id=1, source_target_pairs={{0,448},{64,0},{128,64},{192,128},{256,192},{320,256},{384,320},{4... | collective-permute-start | bytes 1572872 | tf_op jit(solution)/shard_map/ppermute | solution.py:386
  49.7 24.7 %collective-permute-start.3 = (bf16[256,8,128]{2,1,0:T(8,128)(2,1)S(1)}, bf16[256,8,128]{2,1,0:T(8,128)(2,1)S(1)}, u32[]{:S(2)}, u32[]{:S(2)}) collective-permute-start(bf16[256,8,128]{2,1,0:T(8,128)(2,1)S(1)} %collective-permute-done.2.refs_2_), channel_id=1, source_target_pairs={{0,448},{64,0},{128,64},{192,128},{256,192},{320,256},{384,320},{4... | collective-permute-start | bytes 1572872 | tf_op jit(solution)/shard_map/ppermute | solution.py:386
  54.4 20.0 %collective-permute-start.5 = (bf16[256,8,128]{2,1,0:T(8,128)(2,1)S(1)}, bf16[256,8,128]{2,1,0:T(8,128)(2,1)}, u32[]{:S(2)}, u32[]{:S(2)}) collective-permute-start(bf16[256,8,128]{2,1,0:T(8,128)(2,1)S(1)} %collective-permute-done.refs_6_), channel_id=1, source_target_pairs={{0,64},{64,128},{128,192},{192,256},{256,320},{320,384},{384,448},... | collective-permute-start | bytes 1572872 | tf_op jit(solution)/shard_map/ppermute | solution.py:386
  56.3 18.1 %collective-permute-start.4 = (bf16[256,8,128]{2,1,0:T(8,128)(2,1)S(1)}, bf16[256,8,128]{2,1,0:T(8,128)(2,1)}, u32[]{:S(2)}, u32[]{:S(2)}) collective-permute-start(bf16[256,8,128]{2,1,0:T(8,128)(2,1)S(1)} %collective-permute-done.refs_6_), channel_id=1, source_target_pairs={{0,128},{64,192},{128,256},{192,320},{256,384},{320,448},{384,0},{... | collective-permute-start | bytes 1572872 | tf_op jit(solution)/shard_map/ppermute | solution.py:386
  60.4 14.1 %all-to-all-start.2 = ((s32[8,1,128]{2,1,0:T(1,128)}), s32[8,1,128]{2,1,0:T(1,128)S(1)}, u32[]{:S(2)}, u32[]{:S(2)}) async-start(s32[8,1,128]{2,1,0:T(1,128)} %bitcast.13), calls=%async_computation.2 | async-start | bytes 8192 | tf_op jit(solution)/shard_map/all_to_all | solution.py:390
  79.6 33.8 %copy-start.2 = (bf16[40,2,16,256]{3,2,1,0:T(8,128)(2,1)S(1)}, bf16[40,2,16,256]{3,2,1,0:T(8,128)(2,1)}, u32[]{:S(2)}) copy-start(bf16[40,2,16,256]{3,2,1,0:T(8,128)(2,1)} %ops_hbm.1) | copy-start | bytes 1966084
  79.6 33.7 %all-to-all-start.3 = ((bf16[8,16,8,8,128]{4,3,2,1,0:T(8,128)(2,1)}), bf16[8,16,8,8,128]{4,3,2,1,0:T(8,128)(2,1)S(1)}, u32[]{:S(2)}, u32[]{:S(2)}) async-start(bf16[8,16,8,8,128]{4,3,2,1,0:T(8,128)(2,1)} %get-tuple-element.32), calls=%async_computation.3 | async-start | bytes 4194304 | tf_op jit(solution)/shard_map/all_to_all | solution.py:390
  84.1 63.5 %copy-start = (f32[2,128,256]{2,1,0:T(8,128)S(1)}, f32[2,128,256]{2,1,0:T(8,128)}, u32[]{:S(2)}) copy-start(f32[2,128,256]{2,1,0:T(8,128)} %constant.66.clone.sin_h.sin_t) | copy-start | bytes 786436
  84.2 63.5 %copy-start.1 = (f32[2,128,256]{2,1,0:T(8,128)S(1)}, f32[2,128,256]{2,1,0:T(8,128)}, u32[]{:S(2)}) copy-start(f32[2,128,256]{2,1,0:T(8,128)} %constant.65.clone.cos_h.cos_t) | copy-start | bytes 786436
  84.2 63.5 %copy-start.5 = (bf16[64,128]{1,0:T(8,128)(2,1)S(1)}, bf16[64,128]{1,0:T(8,128)(2,1)}, u32[]{:S(2)}) copy-start(bf16[64,128]{1,0:T(8,128)(2,1)} %constant.71.theta) | copy-start | bytes 49156
  84.2 59.3 %collective-permute-start.7 = (bf16[64,2,8,128]{3,2,1,0:T(8,128)(2,1)}, bf16[64,2,8,128]{3,2,1,0:T(8,128)(2,1)}, u32[]{:S(2)}, u32[]{:S(2)}) collective-permute-start(bf16[64,2,8,128]{3,2,1,0:T(8,128)(2,1)} %get-tuple-element.24), channel_id=1, source_target_pairs={{0,8},{8,16},{16,24},{24,32},{32,40},{40,48},{48,56},{56,0},{64,72... | collective-permute-start | bytes 786440 | tf_op jit(solution)/shard_map/ppermute | solution.py:386
  87.7 57.8 %collective-permute-start.8 = (bf16[64,2,8,128]{3,2,1,0:T(8,128)(2,1)}, bf16[64,2,8,128]{3,2,1,0:T(8,128)(2,1)}, u32[]{:S(2)}, u32[]{:S(2)}) collective-permute-start(bf16[64,2,8,128]{3,2,1,0:T(8,128)(2,1)} %get-tuple-element.25), channel_id=1, source_target_pairs={{0,16},{8,24},{16,32},{24,40},{32,48},{40,56},{48,0},{56,8},{64,80... | collective-permute-start | bytes 786440 | tf_op jit(solution)/shard_map/ppermute | solution.py:386
  113.4 48.3 %copy-start.3 = (bf16[64,2,8,128]{3,2,1,0:T(8,128)(2,1)S(1)}, bf16[64,2,8,128]{3,2,1,0:T(8,128)(2,1)}, u32[]{:S(2)}) copy-start(bf16[64,2,8,128]{3,2,1,0:T(8,128)(2,1)} %get-tuple-element.23.refs_0_) | copy-start | bytes 786436
  116.1 45.5 %copy-start.4 = (bf16[40,2,8,128]{3,2,1,0:T(8,128)(2,1)S(1)}, bf16[40,2,8,128]{3,2,1,0:T(8,128)(2,1)}, u32[]{:S(2)}) copy-start(bf16[40,2,8,128]{3,2,1,0:T(8,128)(2,1)} %refs_8_.1) | copy-start | bytes 491524
  116.2 31.5 %all-to-all-start.4 = ((bf16[16,8,8,128]{3,2,1,0:T(8,128)(2,1)}), bf16[16,8,8,128]{3,2,1,0:T(8,128)(2,1)S(1)}, u32[]{:S(2)}, u32[]{:S(2)}) async-start(bf16[16,8,8,128]{3,2,1,0:T(8,128)(2,1)} %far_parents.1), calls=%async_computation.4 | async-start | bytes 524288 | tf_op jit(solution)/shard_map/all_to_all | solution.py:390
  127.8 29.2 %collective-permute-start.9 = (bf16[64,2,8,128]{3,2,1,0:T(8,128)(2,1)}, bf16[64,2,8,128]{3,2,1,0:T(8,128)(2,1)S(1)}, u32[]{:S(2)}, u32[]{:S(2)}) collective-permute-start(bf16[64,2,8,128]{3,2,1,0:T(8,128)(2,1)} %get-tuple-element.26), channel_id=1, source_target_pairs={{0,24},{8,32},{16,40},{24,48},{32,56},{40,0},{48,8},{56,16},{64,88... | collective-permute-start | bytes 786440 | tf_op jit(solution)/shard_map/ppermute | solution.py:386
  132.6 24.4 %collective-permute-start.10 = (bf16[64,2,8,128]{3,2,1,0:T(8,128)(2,1)}, bf16[64,2,8,128]{3,2,1,0:T(8,128)(2,1)S(1)}, u32[]{:S(2)}, u32[]{:S(2)}) collective-permute-start(bf16[64,2,8,128]{3,2,1,0:T(8,128)(2,1)} %get-tuple-element.27), channel_id=1, source_target_pairs={{0,32},{8,40},{16,48},{24,56},{32,0},{40,8},{48,16},{56,24},{64,96... | collective-permute-start | bytes 786440 | tf_op jit(solution)/shard_map/ppermute | solution.py:386
  137.1 19.9 %collective-permute-start.11 = (bf16[64,2,8,128]{3,2,1,0:T(8,128)(2,1)}, bf16[64,2,8,128]{3,2,1,0:T(8,128)(2,1)S(1)}, u32[]{:S(2)}, u32[]{:S(2)}) collective-permute-start(bf16[64,2,8,128]{3,2,1,0:T(8,128)(2,1)} %get-tuple-element.28), channel_id=1, source_target_pairs={{0,40},{8,48},{16,56},{24,0},{32,8},{40,16},{48,24},{56,32},{64,10... | collective-permute-start | bytes 786440 | tf_op jit(solution)/shard_map/ppermute | solution.py:386
  143.5 15.9 %collective-permute-start.12 = (bf16[64,2,8,128]{3,2,1,0:T(8,128)(2,1)}, bf16[64,2,8,128]{3,2,1,0:T(8,128)(2,1)S(1)}, u32[]{:S(2)}, u32[]{:S(2)}) collective-permute-start(bf16[64,2,8,128]{3,2,1,0:T(8,128)(2,1)} %get-tuple-element.29), channel_id=1, source_target_pairs={{0,48},{8,56},{16,0},{24,8},{32,16},{40,24},{48,32},{56,40},{64,11... | collective-permute-start | bytes 786440 | tf_op jit(solution)/shard_map/ppermute | solution.py:386
  145.4 16.2 %collective-permute-start.13 = (bf16[64,2,8,128]{3,2,1,0:T(8,128)(2,1)}, bf16[64,2,8,128]{3,2,1,0:T(8,128)(2,1)S(1)}, u32[]{:S(2)}, u32[]{:S(2)}) collective-permute-start(bf16[64,2,8,128]{3,2,1,0:T(8,128)(2,1)} %get-tuple-element.30), channel_id=1, source_target_pairs={{0,56},{8,0},{16,8},{24,16},{32,24},{40,32},{48,40},{56,48},{64,12... | collective-permute-start | bytes 786440 | tf_op jit(solution)/shard_map/ppermute | solution.py:386
  152.0 14.7 %all-to-all-start.5 = ((bf16[8,8,2,8,128]{4,3,2,1,0:T(8,128)(2,1)}), bf16[8,8,2,8,128]{4,3,2,1,0:T(8,128)(2,1)S(1)}, u32[]{:S(2)}, u32[]{:S(2)}) async-start(bf16[8,8,2,8,128]{4,3,2,1,0:T(8,128)(2,1)} %lower.1), calls=%async_computation.5 | async-start | bytes 524288 | tf_op jit(solution)/shard_map/all_to_all | solution.py:390

commit v8 on v7

--- a/solution.py
+++ b/solution.py
@@ -41,6 +41,10 @@
     across = np.stack([-cos_h - sin_h, cos_h - sin_h])
     arg = (f32(WAVE_NUMBER) * np.sin(polar))[None, :, None] * across[:, None, :]
     return np.cos(arg).astype(f32), np.sin(arg).astype(f32)
+
+
+def hold(x):
+    return pltpu.with_memory_space_constraint(x, pltpu.HBM)
 
 
 def bmm(a, b):
@@ -101,12 +105,17 @@
 def plan(where, child_list, child_op, child_home, parent_list, parent_op, parent_home):
     args = (
         where,
-        child_list.T,
-        child_op.T,
-        child_home.reshape(-1, 128),
-        parent_list.T,
-        parent_op.T,
-        parent_home.reshape(-1, 128),
+        *map(
+            hold,
+            (
+                child_list.T,
+                child_op.T,
+                child_home.reshape(-1, 128),
+                parent_list.T,
+                parent_op.T,
+                parent_home.reshape(-1, 128),
+            ),
+        ),
     )
     return pl.pallas_call(
         plan_body,
@@ -312,7 +321,7 @@
 def far_children(code, blocks, ops):
     return pl.pallas_call(
         child_far_body,
-        out_shape=pltpu.HBM((64, 2, 8, 128), F32),
+        out_shape=jax.ShapeDtypeStruct((64, 2, 8, 128), F32),
         in_specs=[pl.BlockSpec(memory_space=pltpu.SMEM)] + [pl.BlockSpec(memory_space=ANY)] * 9,
         out_specs=pl.BlockSpec(memory_space=VM),
         scratch_shapes=[
@@ -416,7 +425,6 @@
     other = jnp.where(core == 0, box % SIDE, box // SIDE)
     where = jnp.stack([core, mine, other]).astype(I32)
 
-    hold = lambda x: pltpu.with_memory_space_constraint(x, pltpu.HBM)
     whole = swap(child_field, "angle").reshape(8, 8, 2, 8, 128)
     parents = swap(lift(whole, tuple(map(hold, (theta_up, phi_up, cos_t, sin_t)))), "angle")
     wanted, child_code, parent_code = plan(
@@ -425,8 +433,9 @@
     own = jnp.concatenate([child_field.reshape(128, 8, 128), parents.reshape(128, 8, 128)])
     up2, down2 = hop(own, 2), hop(own, -2)
     up1, down1 = hop(own, 1), hop(own, -1)
-    up2, wanted = lax.optimization_barrier((up2, wanted))
-    up4 = hop(up2, 2)
+    onward = jnp.where(mine % 2 == 0, up2, down2)
+    pairs = [(g[i], g[(i + 2 - 4 * (i % 2)) % SIDE]) for g in SPREAD for i in range(SIDE)]
+    up4 = lax.ppermute(onward, BOTH, pairs)
     up3, down3 = hop(up2, 1), hop(down2, -1)
     blocks = [own, down1, down2, down3, up4, up3, up2, up1]
     asked = swap(wanted.reshape(SIDE, 1, 128), BOTH, axis_index_groups=TRADE).reshape(SIDE, 128)

time: 170 us -> 166 us (0.976)
  the two profiles are of different devices: /device:TPU:1 before, /device:TPU:10 now
where the time goes in v8:
time: 166 us; the launch traced here: 165 us
  starting transfers between devices  72.8 us (44%)
  blocking collectives  39 us (23%)
  waiting for transfers between devices  27.2 us (16%)
  Pallas kernels  23.7 us (14%)
  other arithmetic  1.77 us (1%)
    ppermute x13, starting transfers between devices, hop(): return lax.ppermute(x, BOTH, pairs)  52.3 us
    all_to_all x3, blocking collectives, swap(): lax.all_to_all(x, axis, split_axis=0, concat_axis=0, tiled=True, **kw)  39 us
    all_to_all x3, waiting for transfers between devices, swap(): lax.all_to_all(x, axis, split_axis=0, concat_axis=0, tiled=True, **kw)  22 us
    all_to_all x3, starting transfers between devices, swap(): lax.all_to_all(x, axis, split_axis=0, concat_axis=0, tiled=True, **kw)  13.5 us
    ppermute x1, starting transfers between devices, local(): up4 = lax.ppermute(onward, BOTH, pairs)  7.04 us
    ppermute x13, waiting for transfers between devices, hop(): return lax.ppermute(x, BOTH, pairs)  5.21 us
    pallas_call x1, Pallas kernels, select(): pl.pallas_call(select_body, out_shape=(pltpu.HBM((SIDE, 16, 8, 8, 128), B...  5.14 us
    pallas_call x1, Pallas kernels, plan(): pl.pallas_call(plan_body, out_shape=(jax.ShapeDtypeStruct((SIDE, 128), I3...  4.66 us
  transfers between devices with their start and end apart: 17, of which 3 were waited for; matrix products, arithmetic and copies ran while one was open for 1% of the time, Pallas kernels for 10%

profile of v8, /device:TPU:10, one launch (start us, length us, event | category | flops | bytes accessed | tf_op | source)
XLA Modules:
  0.0 164.9 jit_solution(17086674184076298186)
XLA Ops:
  0.0 0.0 copy-start.6
  0.0 11.0 %all_to_all.30 = bf16[64,2,8,128]{3,2,1,0:T(8,128)(2,1)S(1)} all-to-all(bf16[64,2,8,128]{3,2,1,0:T(8,128)(2,1)} %param.15), channel_id=1, replica_groups=mesh['box'=64,'angle'=8] {'angle'}, dimensions={0} | all-to-all | bytes 524288 | tf_op jit(solution)/shard_map/all_to_all | solution.py:399
  11.0 2.6 %lift.1 = bf16[8,2,8,8,128]{4,3,2,1,0:T(8,128)(2,1)S(1)} custom-call(bf16[8,8,2,8,128]{4,3,2,1,0:T(8,128)(2,1)S(1)} %bitcast.23, bf16[128,64]{1,0:T(8,128)(2,1)} %constant.73.theta_h, bf16[128,256]{1,0:T(8,128)(2,1)} %constant.74.phi_h, f32[2,128,256]{2,1,0:T(8,128)} %constant.69.clone.cos_h.cos_t, f32[2,128,256]{2,1,0:T(8,128)} %constant.70.clone.sin_h.sin_t), custom_call_target="tpu_custom_call" | custom-call | tf_op jit(solution)/shard_map/lift/pallas_call | solution.py:169
  13.6 9.9 %all_to_all.31 = bf16[8,2,8,8,128]{4,3,2,1,0:T(8,128)(2,1)S(1)} all-to-all(bf16[8,2,8,8,128]{4,3,2,1,0:T(8,128)(2,1)S(1)} %lift.1), channel_id=1, replica_groups=mesh['box'=64,'angle'=8] {'angle'}, dimensions={0} | all-to-all | bytes 524288 | tf_op jit(solution)/shard_map/all_to_all | solution.py:399
  23.5 0.0 copy-done.6
  23.6 4.5 %collective-permute-start.3 = (bf16[256,8,128]{2,1,0:T(8,128)(2,1)S(1)}, bf16[256,8,128]{2,1,0:T(8,128)(2,1)S(1)}, u32[]{:S(2)}, u32[]{:S(2)}) collective-permute-start(bf16[256,8,128]{2,1,0:T(8,128)(2,1)S(1)} %pad_maximum_fusion.refs_0_), channel_id=1, source_target_pairs={{0,128},{64,192},{128,256},{192,320},{256,384},{320,448},{384,0},{... | collective-permute-start | bytes 1572872 | tf_op jit(solution)/shard_map/ppermute | solution.py:395
  28.1 3.5 %collective-permute-start.1 = (bf16[256,8,128]{2,1,0:T(8,128)(2,1)S(1)}, bf16[256,8,128]{2,1,0:T(8,128)(2,1)S(1)}, u32[]{:S(2)}, u32[]{:S(2)}) collective-permute-start(bf16[256,8,128]{2,1,0:T(8,128)(2,1)S(1)} %pad_maximum_fusion.refs_0_), channel_id=1, source_target_pairs={{0,384},{64,448},{128,0},{192,64},{256,128},{320,192},{384,256},{4... | collective-permute-start | bytes 1572872 | tf_op jit(solution)/shard_map/ppermute | solution.py:395
  31.6 4.1 %collective-permute-start.6 = (bf16[256,8,128]{2,1,0:T(8,128)(2,1)S(1)}, bf16[256,8,128]{2,1,0:T(8,128)(2,1)S(1)}, u32[]{:S(2)}, u32[]{:S(2)}) collective-permute-start(bf16[256,8,128]{2,1,0:T(8,128)(2,1)S(1)} %pad_maximum_fusion.refs_0_), channel_id=1, source_target_pairs={{0,64},{64,128},{128,192},{192,256},{256,320},{320,384},{384,448},... | collective-permute-start | bytes 1572872 | tf_op jit(solution)/shard_map/ppermute | solution.py:395
  35.6 4.6 %collective-permute-start = (bf16[256,8,128]{2,1,0:T(8,128)(2,1)S(1)}, bf16[256,8,128]{2,1,0:T(8,128)(2,1)S(1)}, u32[]{:S(2)}, u32[]{:S(2)}) collective-permute-start(bf16[256,8,128]{2,1,0:T(8,128)(2,1)S(1)} %pad_maximum_fusion.refs_0_), channel_id=1, source_target_pairs={{0,448},{64,0},{128,64},{192,128},{256,192},{320,256},{384,320},{4... | collective-permute-start | bytes 1572872 | tf_op jit(solution)/shard_map/ppermute | solution.py:395
  40.2 0.0 collective-permute-done.3.refs_6_
  40.2 5.6 %collective-permute-start.5 = (bf16[256,8,128]{2,1,0:T(8,128)(2,1)S(1)}, bf16[256,8,128]{2,1,0:T(8,128)(2,1)S(1)}, u32[]{:S(2)}, u32[]{:S(2)}) collective-permute-start(bf16[256,8,128]{2,1,0:T(8,128)(2,1)S(1)} %collective-permute-done.3.refs_6_), channel_id=1, source_target_pairs={{0,64},{64,128},{128,192},{192,256},{256,320},{320,384},{384,448},... | collective-permute-start | bytes 1572872 | tf_op jit(solution)/shard_map/ppermute | solution.py:395
  45.8 0.0 collective-permute-done.1.refs_2_
  45.8 0.9 broadcast_select_fusion
  46.7 7.0 %collective-permute-start.4 = (bf16[256,8,128]{2,1,0:T(8,128)(2,1)}, bf16[256,8,128]{2,1,0:T(8,128)(2,1)}, u32[]{:S(2)}, u32[]{:S(2)}) collective-permute-start(bf16[256,8,128]{2,1,0:T(8,128)(2,1)} %broadcast_select_fusion), channel_id=1, source_target_pairs={{0,128},{64,448},{128,256},{192,64},{256,384},{320,192},{384,0},{4... | collective-permute-start | bytes 1572872 | tf_op jit(solution)/shard_map/ppermute | solution.py:438
  53.7 1.9 %collective-permute-start.2 = (bf16[256,8,128]{2,1,0:T(8,128)(2,1)S(1)}, bf16[256,8,128]{2,1,0:T(8,128)(2,1)}, u32[]{:S(2)}, u32[]{:S(2)}) collective-permute-start(bf16[256,8,128]{2,1,0:T(8,128)(2,1)S(1)} %collective-permute-done.1.refs_2_), channel_id=1, source_target_pairs={{0,448},{64,0},{128,64},{192,128},{256,192},{320,256},{384,320},{4... | collective-permute-start | bytes 1572872 | tf_op jit(solution)/shard_map/ppermute | solution.py:395
  55.7 0.1 pad_add_fusion.where
  55.8 4.7 %plan.1 = (s32[8,128]{1,0:T(8,128)S(1)}, s32[8,64]{1,0:T(8,128)}, s32[8,16]{1,0:T(8,128)}) custom-call(s32[3]{0:T(128)S(1)} %pad_add_fusion.where, s32[8,64]{1,0:T(8,128)} %bitcast.29, s32[8,64]{1,0:T(8,128)} %bitcast.30, s32[32,128]{1,0:T(8,128)} %bitcast.28, s32[8,16]{1,0:T(8,128)} %bitcast.31, s32[8,16]{1,0:T(8,128)} %bitcast.32, s32[8,128]{1,0:T(8,128)} %bitcast.33), custom_call_target="tpu_custom_call" | custom-call | tf_op jit(solution)/shard_map/plan/pallas_call | solution.py:120
  60.4 18.0 %all_to_all.32 = s32[8,1,128]{2,1,0:T(1,128)S(1)} all-to-all(s32[8,1,128]{2,1,0:T(1,128)S(1)} %bitcast.25), channel_id=1, replica_groups={{0,8,16,24,32,40,48,56},{64,72,80,88,96,104,112,120},{128,136,144,152,1..., dimensions={0} | all-to-all | bytes 8192 | tf_op jit(solution)/shard_map/all_to_all | solution.py:399
  78.5 0.0 collective-permute-done.6.refs_7_
  78.5 0.0 collective-permute-done.refs_1_
  78.5 0.0 collective-permute-done.5.refs_5_
  78.5 0.0 collective-permute-done.4.refs_4_
  78.5 0.0 collective-permute-done.2.refs_3_
  78.5 5.1 %select.11 = (bf16[8,16,8,8,128]{4,3,2,1,0:T(8,128)(2,1)}, bf16[64,2,8,128]{3,2,1,0:T(8,128)(2,1)}, bf16[64,2,8,128]{3,2,1,0:T(8,128)(2,1)}, bf16[64,2,8,128]{3,...) custom-call(s32[3]{0:T(128)S(1)} %pad_add_fusion.where, ...), custom_call_target="tpu_custom_call" | custom-call | tf_op jit(solution)/shard_map/select/pallas_call | solution.py:235
  83.6 0.0 copy-start.2
  83.6 3.7 %all-to-all-start.3 = ((bf16[8,16,8,8,128]{4,3,2,1,0:T(8,128)(2,1)}), bf16[8,16,8,8,128]{4,3,2,1,0:T(8,128)(2,1)S(1)}, u32[]{:S(2)}, u32[]{:S(2)}) async-start(bf16[8,16,8,8,128]{4,3,2,1,0:T(8,128)(2,1)} %get-tuple-element.28), calls=%async_computation.3 | async-start | bytes 4194304 | tf_op jit(solution)/shard_map/all_to_all | solution.py:399
  87.4 0.0 copy-start
  87.4 0.0 copy-start.1
  87.4 0.0 copy-start.5
  87.4 3.9 %collective-permute-start.7 = (bf16[64,2,8,128]{3,2,1,0:T(8,128)(2,1)}, bf16[64,2,8,128]{3,2,1,0:T(8,128)(2,1)}, u32[]{:S(2)}, u32[]{:S(2)}) collective-permute-start(bf16[64,2,8,128]{3,2,1,0:T(8,128)(2,1)} %get-tuple-element.20), channel_id=1, source_target_pairs={{0,8},{8,16},{16,24},{24,32},{32,40},{40,48},{48,56},{56,0},{64,72... | collective-permute-start | bytes 786440 | tf_op jit(solution)/shard_map/ppermute | solution.py:395
  91.4 4.3 %collective-permute-start.8 = (bf16[64,2,8,128]{3,2,1,0:T(8,128)(2,1)}, bf16[64,2,8,128]{3,2,1,0:T(8,128)(2,1)}, u32[]{:S(2)}, u32[]{:S(2)}) collective-permute-start(bf16[64,2,8,128]{3,2,1,0:T(8,128)(2,1)} %get-tuple-element.21), channel_id=1, source_target_pairs={{0,16},{8,24},{16,32},{24,40},{32,48},{40,56},{48,0},{56,8},{64,80... | collective-permute-start | bytes 786440 | tf_op jit(solution)/shard_map/ppermute | solution.py:395
  95.7 22.0 %all-to-all-done.3 = bf16[8,16,8,8,128]{4,3,2,1,0:T(8,128)(2,1)S(1)} async-done(((bf16[8,16,8,8,128]{4,3,2,1,0:T(8,128)(2,1)}), bf16[8,16,8,8,128]{4,3,2,1,0:T(8,128)(2,1)S(1)}, u32[]{:S(2)}, u32[]{:S(2)}) %all-to-all-start.3) | async-done | bytes 2097184 | tf_op jit(solution)/shard_map/all_to_all | solution.py:399
  117.7 0.0 copy-done.2
  117.7 0.0 copy-start.3
  117.7 2.8 %far_parents.1 = bf16[16,8,8,128]{3,2,1,0:T(8,128)(2,1)} custom-call(s32[8,16]{1,0:T(8,128)} %get-tuple-element.27.code, bf16[128,8,8,128]{3,2,1,0:T(8,128)(2,1)S(1)} %bitcast.21, bf16[40,2,16,256]{3,2,1,0:T(8,128)(2,1)S(1)} %copy-done.2), custom_call_target="tpu_custom_call" | custom-call | tf_op jit(solution)/shard_map/far_parents/pallas_call | solution.py:282
  120.5 0.0 copy-start.4
  120.5 4.9 %all-to-all-start.4 = ((bf16[16,8,8,128]{3,2,1,0:T(8,128)(2,1)}), bf16[16,8,8,128]{3,2,1,0:T(8,128)(2,1)S(1)}, u32[]{:S(2)}, u32[]{:S(2)}) async-start(bf16[16,8,8,128]{3,2,1,0:T(8,128)(2,1)} %far_parents.1), calls=%async_computation.4 | async-start | bytes 524288 | tf_op jit(solution)/shard_map/all_to_all | solution.py:399
  125.4 1.9 %collective-permute-start.9 = (bf16[64,2,8,128]{3,2,1,0:T(8,128)(2,1)}, bf16[64,2,8,128]{3,2,1,0:T(8,128)(2,1)S(1)}, u32[]{:S(2)}, u32[]{:S(2)}) collective-permute-start(bf16[64,2,8,128]{3,2,1,0:T(8,128)(2,1)} %get-tuple-element.22), channel_id=1, source_target_pairs={{0,24},{8,32},{16,40},{24,48},{32,56},{40,0},{48,8},{56,16},{64,88... | collective-permute-start | bytes 786440 | tf_op jit(solution)/shard_map/ppermute | solution.py:395
  127.3 3.0 %collective-permute-start.10 = (bf16[64,2,8,128]{3,2,1,0:T(8,128)(2,1)}, bf16[64,2,8,128]{3,2,1,0:T(8,128)(2,1)S(1)}, u32[]{:S(2)}, u32[]{:S(2)}) collective-permute-start(bf16[64,2,8,128]{3,2,1,0:T(8,128)(2,1)} %get-tuple-element.23), channel_id=1, source_target_pairs={{0,32},{8,40},{16,48},{24,56},{32,0},{40,8},{48,16},{56,24},{64,96... | collective-permute-start | bytes 786440 | tf_op jit(solution)/shard_map/ppermute | solution.py:395
  130.4 6.2 %collective-permute-start.11 = (bf16[64,2,8,128]{3,2,1,0:T(8,128)(2,1)}, bf16[64,2,8,128]{3,2,1,0:T(8,128)(2,1)S(1)}, u32[]{:S(2)}, u32[]{:S(2)}) collective-permute-start(bf16[64,2,8,128]{3,2,1,0:T(8,128)(2,1)} %get-tuple-element.24), channel_id=1, source_target_pairs={{0,40},{8,48},{16,56},{24,0},{32,8},{40,16},{48,24},{56,32},{64,10... | collective-permute-start | bytes 786440 | tf_op jit(solution)/shard_map/ppermute | solution.py:395
  136.6 0.0 collective-permute-done.7.refs_1_
  136.6 5.4 %collective-permute-start.12 = (bf16[64,2,8,128]{3,2,1,0:T(8,128)(2,1)}, bf16[64,2,8,128]{3,2,1,0:T(8,128)(2,1)S(1)}, u32[]{:S(2)}, u32[]{:S(2)}) collective-permute-start(bf16[64,2,8,128]{3,2,1,0:T(8,128)(2,1)} %get-tuple-element.25), channel_id=1, source_target_pairs={{0,48},{8,56},{16,0},{24,8},{32,16},{40,24},{48,32},{56,40},{64,11... | collective-permute-start | bytes 786440 | tf_op jit(solution)/shard_map/ppermute | solution.py:395
  142.0 0.0 collective-permute-done.8.refs_2_
  142.0 3.4 %collective-permute-start.13 = (bf16[64,2,8,128]{3,2,1,0:T(8,128)(2,1)}, bf16[64,2,8,128]{3,2,1,0:T(8,128)(2,1)S(1)}, u32[]{:S(2)}, u32[]{:S(2)}) collective-permute-start(bf16[64,2,8,128]{3,2,1,0:T(8,128)(2,1)} %get-tuple-element.26), channel_id=1, source_target_pairs={{0,56},{8,0},{16,8},{24,16},{32,24},{40,32},{48,40},{56,48},{64,12... | collective-permute-start | bytes 786440 | tf_op jit(solution)/shard_map/ppermute | solution.py:395
  145.5 0.0 all-to-all-done.4
  145.5 0.0 copy-done
  145.5 0.0 copy-done.1
  145.5 0.0 copy-done.5
  145.5 4.4 %lower.1 = bf16[8,8,2,8,128]{4,3,2,1,0:T(8,128)(2,1)} custom-call(bf16[8,2,8,8,128]{4,3,2,1,0:T(8,128)(2,1)S(1)} %bitcast.22, bf16[64,128]{1,0:T(8,128)(2,1)S(1)} %copy-done.5, bf16[256,128]{1,0:T(8,128)(2,1)} %constant.76.phi_h, f32[2,128,256]{2,1,0:T(8,128)S(1)} %copy-done.1, f32[2,128,256]{2,1,0:T(8,128)S(1)} %copy-done), custom_call_target="tpu_custom_call" | custom-call | tf_op jit(solution)/shard_map/lower/pallas_call | solution.py:366
  149.9 4.8 %all-to-all-start.5 = ((bf16[8,8,2,8,128]{4,3,2,1,0:T(8,128)(2,1)}), bf16[8,8,2,8,128]{4,3,2,1,0:T(8,128)(2,1)S(1)}, u32[]{:S(2)}, u32[]{:S(2)}) async-start(bf16[8,8,2,8,128]{4,3,2,1,0:T(8,128)(2,1)} %lower.1), calls=%async_computation.5 | async-start | bytes 524288 | tf_op jit(solution)/shard_map/all_to_all | solution.py:399
  154.7 0.0 collective-permute-done.9.refs_3_
  154.7 0.0 collective-permute-done.10.refs_4_
  154.7 0.0 collective-permute-done.11.refs_5_
  154.7 2.3 %collective-permute-done.12.refs_6_ = bf16[64,2,8,128]{3,2,1,0:T(8,128)(2,1)S(1)} collective-permute-done((bf16[64,2,8,128]{3,2,1,0:T(8,128)(2,1)}, bf16[64,2,8,128]{3,2,1,0:T(8,128)(2,1)S(1)}, u32[]{:S(2)}, u32[]{:S(2)}) %collective-permute-start.12) | collective-permute-done | bytes 262176 | tf_op jit(solution)/shard_map/ppermute | solution.py:395
  157.0 2.9 %collective-permute-done.13.refs_7_ = bf16[64,2,8,128]{3,2,1,0:T(8,128)(2,1)S(1)} collective-permute-done((bf16[64,2,8,128]{3,2,1,0:T(8,128)(2,1)}, bf16[64,2,8,128]{3,2,1,0:T(8,128)(2,1)S(1)}, u32[]{:S(2)}, u32[]{:S(2)}) %collective-permute-start.13) | collective-permute-done | bytes 262176 | tf_op jit(solution)/shard_map/ppermute | solution.py:395
  159.9 0.0 copy-done.3
  159.9 0.0 copy-done.4
  159.9 4.2 %far_children.1 = f32[64,2,8,128]{3,2,1,0:T(8,128)S(1)} custom-call(s32[8,64]{1,0:T(8,128)} %get-tuple-element.17.code, bf16[64,2,8,128]{3,2,1,0:T(8,128)(2,1)S(1)} %copy-done.3, bf16[64,2,8,128]{3,2,1,0:T(8,128)(2,1)} %collective-permute-done.7.refs_1_, bf16[64,2,8,128]{3,2,1,0:T(8,128)(2,1)} %collective-permute-done.8.refs_2_, ...), custom_call_target="tpu_custom_call" | custom-call | tf_op jit(solution)/shard_map/far_children/pallas_call | solution.py:322
  164.1 0.0 all-to-all-done.5
  164.1 0.8 fusion
  (1 shorter events, 0.0 us)
Async XLA Ops:
  0.0 23.5 %copy-start.6 = (bf16[64,2,8,128]{3,2,1,0:T(8,128)(2,1)S(1)}, bf16[64,2,8,128]{3,2,1,0:T(8,128)(2,1)}, u32[]{:S(2)}) copy-start(bf16[64,2,8,128]{3,2,1,0:T(8,128)(2,1)} %param.15) | copy-start | bytes 786436
  23.6 16.7 %collective-permute-start.3 = (bf16[256,8,128]{2,1,0:T(8,128)(2,1)S(1)}, bf16[256,8,128]{2,1,0:T(8,128)(2,1)S(1)}, u32[]{:S(2)}, u32[]{:S(2)}) collective-permute-start(bf16[256,8,128]{2,1,0:T(8,128)(2,1)S(1)} %pad_maximum_fusion.refs_0_), channel_id=1, source_target_pairs={{0,128},{64,192},{128,256},{192,320},{256,384},{320,448},{384,0},{... | collective-permute-start | bytes 1572872 | tf_op jit(solution)/shard_map/ppermute | solution.py:395
  28.1 17.8 %collective-permute-start.1 = (bf16[256,8,128]{2,1,0:T(8,128)(2,1)S(1)}, bf16[256,8,128]{2,1,0:T(8,128)(2,1)S(1)}, u32[]{:S(2)}, u32[]{:S(2)}) collective-permute-start(bf16[256,8,128]{2,1,0:T(8,128)(2,1)S(1)} %pad_maximum_fusion.refs_0_), channel_id=1, source_target_pairs={{0,384},{64,448},{128,0},{192,64},{256,128},{320,192},{384,256},{4... | collective-permute-start | bytes 1572872 | tf_op jit(solution)/shard_map/ppermute | solution.py:395
  31.6 46.9 %collective-permute-start.6 = (bf16[256,8,128]{2,1,0:T(8,128)(2,1)S(1)}, bf16[256,8,128]{2,1,0:T(8,128)(2,1)S(1)}, u32[]{:S(2)}, u32[]{:S(2)}) collective-permute-start(bf16[256,8,128]{2,1,0:T(8,128)(2,1)S(1)} %pad_maximum_fusion.refs_0_), channel_id=1, source_target_pairs={{0,64},{64,128},{128,192},{192,256},{256,320},{320,384},{384,448},... | collective-permute-start | bytes 1572872 | tf_op jit(solution)/shard_map/ppermute | solution.py:395
  35.6 42.8 %collective-permute-start = (bf16[256,8,128]{2,1,0:T(8,128)(2,1)S(1)}, bf16[256,8,128]{2,1,0:T(8,128)(2,1)S(1)}, u32[]{:S(2)}, u32[]{:S(2)}) collective-permute-start(bf16[256,8,128]{2,1,0:T(8,128)(2,1)S(1)} %pad_maximum_fusion.refs_0_), channel_id=1, source_target_pairs={{0,448},{64,0},{128,64},{192,128},{256,192},{320,256},{384,320},{4... | collective-permute-start | bytes 1572872 | tf_op jit(solution)/shard_map/ppermute | solution.py:395
  40.2 38.2 %collective-permute-start.5 = (bf16[256,8,128]{2,1,0:T(8,128)(2,1)S(1)}, bf16[256,8,128]{2,1,0:T(8,128)(2,1)S(1)}, u32[]{:S(2)}, u32[]{:S(2)}) collective-permute-start(bf16[256,8,128]{2,1,0:T(8,128)(2,1)S(1)} %collective-permute-done.3.refs_6_), channel_id=1, source_target_pairs={{0,64},{64,128},{128,192},{192,256},{256,320},{320,384},{384,448},... | collective-permute-start | bytes 1572872 | tf_op jit(solution)/shard_map/ppermute | solution.py:395
  46.7 31.8 %collective-permute-start.4 = (bf16[256,8,128]{2,1,0:T(8,128)(2,1)}, bf16[256,8,128]{2,1,0:T(8,128)(2,1)}, u32[]{:S(2)}, u32[]{:S(2)}) collective-permute-start(bf16[256,8,128]{2,1,0:T(8,128)(2,1)} %broadcast_select_fusion), channel_id=1, source_target_pairs={{0,128},{64,448},{128,256},{192,64},{256,384},{320,192},{384,0},{4... | collective-permute-start | bytes 1572872 | tf_op jit(solution)/shard_map/ppermute | solution.py:438
  53.7 24.7 %collective-permute-start.2 = (bf16[256,8,128]{2,1,0:T(8,128)(2,1)S(1)}, bf16[256,8,128]{2,1,0:T(8,128)(2,1)}, u32[]{:S(2)}, u32[]{:S(2)}) collective-permute-start(bf16[256,8,128]{2,1,0:T(8,128)(2,1)S(1)} %collective-permute-done.1.refs_2_), channel_id=1, source_target_pairs={{0,448},{64,0},{128,64},{192,128},{256,192},{320,256},{384,320},{4... | collective-permute-start | bytes 1572872 | tf_op jit(solution)/shard_map/ppermute | solution.py:395
  83.6 34.1 %copy-start.2 = (bf16[40,2,16,256]{3,2,1,0:T(8,128)(2,1)S(1)}, bf16[40,2,16,256]{3,2,1,0:T(8,128)(2,1)}, u32[]{:S(2)}) copy-start(bf16[40,2,16,256]{3,2,1,0:T(8,128)(2,1)} %ops_hbm.1) | copy-start | bytes 1966084
  83.6 34.0 %all-to-all-start.3 = ((bf16[8,16,8,8,128]{4,3,2,1,0:T(8,128)(2,1)}), bf16[8,16,8,8,128]{4,3,2,1,0:T(8,128)(2,1)S(1)}, u32[]{:S(2)}, u32[]{:S(2)}) async-start(bf16[8,16,8,8,128]{4,3,2,1,0:T(8,128)(2,1)} %get-tuple-element.28), calls=%async_computation.3 | async-start | bytes 4194304 | tf_op jit(solution)/shard_map/all_to_all | solution.py:399
  87.4 58.1 %copy-start = (f32[2,128,256]{2,1,0:T(8,128)S(1)}, f32[2,128,256]{2,1,0:T(8,128)}, u32[]{:S(2)}) copy-start(f32[2,128,256]{2,1,0:T(8,128)} %constant.70.clone.sin_h.sin_t) | copy-start | bytes 786436
  87.4 58.1 %copy-start.1 = (f32[2,128,256]{2,1,0:T(8,128)S(1)}, f32[2,128,256]{2,1,0:T(8,128)}, u32[]{:S(2)}) copy-start(f32[2,128,256]{2,1,0:T(8,128)} %constant.69.clone.cos_h.cos_t) | copy-start | bytes 786436
  87.4 58.1 %copy-start.5 = (bf16[64,128]{1,0:T(8,128)(2,1)S(1)}, bf16[64,128]{1,0:T(8,128)(2,1)}, u32[]{:S(2)}) copy-start(bf16[64,128]{1,0:T(8,128)(2,1)} %constant.75.theta) | copy-start | bytes 49156
  87.4 49.1 %collective-permute-start.7 = (bf16[64,2,8,128]{3,2,1,0:T(8,128)(2,1)}, bf16[64,2,8,128]{3,2,1,0:T(8,128)(2,1)}, u32[]{:S(2)}, u32[]{:S(2)}) collective-permute-start(bf16[64,2,8,128]{3,2,1,0:T(8,128)(2,1)} %get-tuple-element.20), channel_id=1, source_target_pairs={{0,8},{8,16},{16,24},{24,32},{32,40},{40,48},{48,56},{56,0},{64,72... | collective-permute-start | bytes 786440 | tf_op jit(solution)/shard_map/ppermute | solution.py:395
  91.4 50.6 %collective-permute-start.8 = (bf16[64,2,8,128]{3,2,1,0:T(8,128)(2,1)}, bf16[64,2,8,128]{3,2,1,0:T(8,128)(2,1)}, u32[]{:S(2)}, u32[]{:S(2)}) collective-permute-start(bf16[64,2,8,128]{3,2,1,0:T(8,128)(2,1)} %get-tuple-element.21), channel_id=1, source_target_pairs={{0,16},{8,24},{16,32},{24,40},{32,48},{40,56},{48,0},{56,8},{64,80... | collective-permute-start | bytes 786440 | tf_op jit(solution)/shard_map/ppermute | solution.py:395
  117.7 42.2 %copy-start.3 = (bf16[64,2,8,128]{3,2,1,0:T(8,128)(2,1)S(1)}, bf16[64,2,8,128]{3,2,1,0:T(8,128)(2,1)}, u32[]{:S(2)}) copy-start(bf16[64,2,8,128]{3,2,1,0:T(8,128)(2,1)} %get-tuple-element.19.refs_0_) | copy-start | bytes 786436
  120.5 39.4 %copy-start.4 = (bf16[40,2,8,128]{3,2,1,0:T(8,128)(2,1)S(1)}, bf16[40,2,8,128]{3,2,1,0:T(8,128)(2,1)}, u32[]{:S(2)}) copy-start(bf16[40,2,8,128]{3,2,1,0:T(8,128)(2,1)} %refs_8_.1) | copy-start | bytes 491524
  120.5 25.0 %all-to-all-start.4 = ((bf16[16,8,8,128]{3,2,1,0:T(8,128)(2,1)}), bf16[16,8,8,128]{3,2,1,0:T(8,128)(2,1)S(1)}, u32[]{:S(2)}, u32[]{:S(2)}) async-start(bf16[16,8,8,128]{3,2,1,0:T(8,128)(2,1)} %far_parents.1), calls=%async_computation.4 | async-start | bytes 524288 | tf_op jit(solution)/shard_map/all_to_all | solution.py:399
  125.4 29.3 %collective-permute-start.9 = (bf16[64,2,8,128]{3,2,1,0:T(8,128)(2,1)}, bf16[64,2,8,128]{3,2,1,0:T(8,128)(2,1)S(1)}, u32[]{:S(2)}, u32[]{:S(2)}) collective-permute-start(bf16[64,2,8,128]{3,2,1,0:T(8,128)(2,1)} %get-tuple-element.22), channel_id=1, source_target_pairs={{0,24},{8,32},{16,40},{24,48},{32,56},{40,0},{48,8},{56,16},{64,88... | collective-permute-start | bytes 786440 | tf_op jit(solution)/shard_map/ppermute | solution.py:395
  127.3 27.4 %collective-permute-start.10 = (bf16[64,2,8,128]{3,2,1,0:T(8,128)(2,1)}, bf16[64,2,8,128]{3,2,1,0:T(8,128)(2,1)S(1)}, u32[]{:S(2)}, u32[]{:S(2)}) collective-permute-start(bf16[64,2,8,128]{3,2,1,0:T(8,128)(2,1)} %get-tuple-element.23), channel_id=1, source_target_pairs={{0,32},{8,40},{16,48},{24,56},{32,0},{40,8},{48,16},{56,24},{64,96... | collective-permute-start | bytes 786440 | tf_op jit(solution)/shard_map/ppermute | solution.py:395
  130.4 24.3 %collective-permute-start.11 = (bf16[64,2,8,128]{3,2,1,0:T(8,128)(2,1)}, bf16[64,2,8,128]{3,2,1,0:T(8,128)(2,1)S(1)}, u32[]{:S(2)}, u32[]{:S(2)}) collective-permute-start(bf16[64,2,8,128]{3,2,1,0:T(8,128)(2,1)} %get-tuple-element.24), channel_id=1, source_target_pairs={{0,40},{8,48},{16,56},{24,0},{32,8},{40,16},{48,24},{56,32},{64,10... | collective-permute-start | bytes 786440 | tf_op jit(solution)/shard_map/ppermute | solution.py:395
  136.6 20.4 %collective-permute-start.12 = (bf16[64,2,8,128]{3,2,1,0:T(8,128)(2,1)}, bf16[64,2,8,128]{3,2,1,0:T(8,128)(2,1)S(1)}, u32[]{:S(2)}, u32[]{:S(2)}) collective-permute-start(bf16[64,2,8,128]{3,2,1,0:T(8,128)(2,1)} %get-tuple-element.25), channel_id=1, source_target_pairs={{0,48},{8,56},{16,0},{24,8},{32,16},{40,24},{48,32},{56,40},{64,11... | collective-permute-start | bytes 786440 | tf_op jit(solution)/shard_map/ppermute | solution.py:395
  142.0 17.9 %collective-permute-start.13 = (bf16[64,2,8,128]{3,2,1,0:T(8,128)(2,1)}, bf16[64,2,8,128]{3,2,1,0:T(8,128)(2,1)S(1)}, u32[]{:S(2)}, u32[]{:S(2)}) collective-permute-start(bf16[64,2,8,128]{3,2,1,0:T(8,128)(2,1)} %get-tuple-element.26), channel_id=1, source_target_pairs={{0,56},{8,0},{16,8},{24,16},{32,24},{40,32},{48,40},{56,48},{64,12... | collective-permute-start | bytes 786440 | tf_op jit(solution)/shard_map/ppermute | solution.py:395
  149.9 14.3 %all-to-all-start.5 = ((bf16[8,8,2,8,128]{4,3,2,1,0:T(8,128)(2,1)}), bf16[8,8,2,8,128]{4,3,2,1,0:T(8,128)(2,1)S(1)}, u32[]{:S(2)}, u32[]{:S(2)}) async-start(bf16[8,8,2,8,128]{4,3,2,1,0:T(8,128)(2,1)} %lower.1), calls=%async_computation.5 | async-start | bytes 524288 | tf_op jit(solution)/shard_map/all_to_all | solution.py:399

commit v9 on v8

--- a/solution.py
+++ b/solution.py
@@ -334,7 +334,7 @@
     )(code, *blocks, ops)
 
 
-def down_body(far, theta, phi_h, cos_t, sin_t, out, phi, turned, sem):
+def down_body(far, theta, phi_h, cos_t, sin_t, out, phi, turned, buf, sem, out_sems):
     copy = pltpu.make_async_copy(phi_h, phi, sem)
     copy.start()
     for q in range(2):
@@ -354,24 +354,32 @@
                 turned[(q * 4 + m) * 2, at, :] = (cr - si).astype(BF16)
                 turned[(q * 4 + m) * 2 + 1, at, :] = (ci + sr).astype(BF16)
     copy.wait()
+    pieces = [
+        pltpu.make_async_copy(buf.at[r], out.at[pl.ds(0, 8), r], out_sems.at[r]) for r in range(8)
+    ]
     for r in range(8):
         for c in range(2):
             narrowed = bmm(turned[r * 2 + c], phi[...]).astype(BF16)
             term = bmm(theta[...], narrowed).astype(BF16)
             for s in range(8):
-                out[s, r, c] = term[s * 8 : s * 8 + 8, :]
+                buf[r, s, c] = term[s * 8 : s * 8 + 8, :]
+        pieces[r].start()
+    for piece in pieces:
+        piece.wait()
 
 
 def lower(far, tables):
     return pl.pallas_call(
         down_body,
-        out_shape=jax.ShapeDtypeStruct((8, 8, 2, 8, 128), BF16),
+        out_shape=pltpu.HBM((8, 8, 2, 8, 128), BF16),
         in_specs=[pl.BlockSpec(memory_space=ANY if i == 2 else VM) for i in range(5)],
-        out_specs=pl.BlockSpec(memory_space=VM),
+        out_specs=pl.BlockSpec(memory_space=pltpu.HBM),
         scratch_shapes=[
             pltpu.VMEM(tables[1].shape, BF16),
             pltpu.VMEM((16, PT, PP), BF16),
+            pltpu.VMEM((8, 8, 2, 8, 128), BF16),
             pltpu.SemaphoreType.DMA,
+            pltpu.SemaphoreType.DMA((8,)),
         ],
         compiler_params=pltpu.CompilerParams(vmem_limit_bytes=GRANT),
         name="lower",

time: 166 us -> 166 us (level)
  no operation moved by 1% of the time
where the time goes in v9:
time: 166 us; the launch traced here: 165 us
  starting transfers between devices  72.8 us (44%)
  blocking collectives  39 us (23%)
  waiting for transfers between devices  27.3 us (16%)
  Pallas kernels  23.7 us (14%)
  other arithmetic  1.77 us (1%)
    ppermute x13, starting transfers between devices, hop(): return lax.ppermute(x, BOTH, pairs)  52.3 us
    all_to_all x3, blocking collectives, swap(): lax.all_to_all(x, axis, split_axis=0, concat_axis=0, tiled=True, **kw)  39 us
    all_to_all x3, waiting for transfers between devices, swap(): lax.all_to_all(x, axis, split_axis=0, concat_axis=0, tiled=True, **kw)  22 us
    all_to_all x3, starting transfers between devices, swap(): lax.all_to_all(x, axis, split_axis=0, concat_axis=0, tiled=True, **kw)  13.5 us
    ppermute x1, starting transfers between devices, local(): up4 = lax.ppermute(onward, BOTH, pairs)  7.04 us
    ppermute x13, waiting for transfers between devices, hop(): return lax.ppermute(x, BOTH, pairs)  5.26 us
    pallas_call x1, Pallas kernels, select(): pl.pallas_call(select_body, out_shape=(pltpu.HBM((SIDE, 16, 8, 8, 128), B...  5.14 us
    pallas_call x1, Pallas kernels, plan(): pl.pallas_call(plan_body, out_shape=(jax.ShapeDtypeStruct((SIDE, 128), I3...  4.66 us
  transfers between devices with their start and end apart: 17, of which 3 were waited for; matrix products, arithmetic and copies ran while one was open for 1% of the time, Pallas kernels for 10%

profile of v9, /device:TPU:10, one launch (start us, length us, event | category | flops | bytes accessed | tf_op | source)
XLA Modules:
  0.0 164.9 jit_solution(12337905294075942222)
XLA Ops:
  0.0 0.0 copy-start.6
  0.0 11.0 %all_to_all.30 = bf16[64,2,8,128]{3,2,1,0:T(8,128)(2,1)S(1)} all-to-all(bf16[64,2,8,128]{3,2,1,0:T(8,128)(2,1)} %param.15), channel_id=1, replica_groups=mesh['box'=64,'angle'=8] {'angle'}, dimensions={0} | all-to-all | bytes 524288 | tf_op jit(solution)/shard_map/all_to_all | solution.py:407
  11.0 2.6 %lift.1 = bf16[8,2,8,8,128]{4,3,2,1,0:T(8,128)(2,1)S(1)} custom-call(bf16[8,8,2,8,128]{4,3,2,1,0:T(8,128)(2,1)S(1)} %bitcast.23, bf16[128,64]{1,0:T(8,128)(2,1)} %constant.73.theta_h, bf16[128,256]{1,0:T(8,128)(2,1)} %constant.74.phi_h, f32[2,128,256]{2,1,0:T(8,128)} %constant.69.clone.cos_h.cos_t, f32[2,128,256]{2,1,0:T(8,128)} %constant.70.clone.sin_h.sin_t), custom_call_target="tpu_custom_call" | custom-call | tf_op jit(solution)/shard_map/lift/pallas_call | solution.py:169
  13.6 9.9 %all_to_all.31 = bf16[8,2,8,8,128]{4,3,2,1,0:T(8,128)(2,1)S(1)} all-to-all(bf16[8,2,8,8,128]{4,3,2,1,0:T(8,128)(2,1)S(1)} %lift.1), channel_id=1, replica_groups=mesh['box'=64,'angle'=8] {'angle'}, dimensions={0} | all-to-all | bytes 524288 | tf_op jit(solution)/shard_map/all_to_all | solution.py:407
  23.5 0.0 copy-done.6
  23.6 4.5 %collective-permute-start.3 = (bf16[256,8,128]{2,1,0:T(8,128)(2,1)S(1)}, bf16[256,8,128]{2,1,0:T(8,128)(2,1)S(1)}, u32[]{:S(2)}, u32[]{:S(2)}) collective-permute-start(bf16[256,8,128]{2,1,0:T(8,128)(2,1)S(1)} %pad_maximum_fusion.refs_0_), channel_id=1, source_target_pairs={{0,128},{64,192},{128,256},{192,320},{256,384},{320,448},{384,0},{... | collective-permute-start | bytes 1572872 | tf_op jit(solution)/shard_map/ppermute | solution.py:403
  28.1 3.5 %collective-permute-start.1 = (bf16[256,8,128]{2,1,0:T(8,128)(2,1)S(1)}, bf16[256,8,128]{2,1,0:T(8,128)(2,1)S(1)}, u32[]{:S(2)}, u32[]{:S(2)}) collective-permute-start(bf16[256,8,128]{2,1,0:T(8,128)(2,1)S(1)} %pad_maximum_fusion.refs_0_), channel_id=1, source_target_pairs={{0,384},{64,448},{128,0},{192,64},{256,128},{320,192},{384,256},{4... | collective-permute-start | bytes 1572872 | tf_op jit(solution)/shard_map/ppermute | solution.py:403
  31.6 4.1 %collective-permute-start.6 = (bf16[256,8,128]{2,1,0:T(8,128)(2,1)S(1)}, bf16[256,8,128]{2,1,0:T(8,128)(2,1)S(1)}, u32[]{:S(2)}, u32[]{:S(2)}) collective-permute-start(bf16[256,8,128]{2,1,0:T(8,128)(2,1)S(1)} %pad_maximum_fusion.refs_0_), channel_id=1, source_target_pairs={{0,64},{64,128},{128,192},{192,256},{256,320},{320,384},{384,448},... | collective-permute-start | bytes 1572872 | tf_op jit(solution)/shard_map/ppermute | solution.py:403
  35.6 4.6 %collective-permute-start = (bf16[256,8,128]{2,1,0:T(8,128)(2,1)S(1)}, bf16[256,8,128]{2,1,0:T(8,128)(2,1)S(1)}, u32[]{:S(2)}, u32[]{:S(2)}) collective-permute-start(bf16[256,8,128]{2,1,0:T(8,128)(2,1)S(1)} %pad_maximum_fusion.refs_0_), channel_id=1, source_target_pairs={{0,448},{64,0},{128,64},{192,128},{256,192},{320,256},{384,320},{4... | collective-permute-start | bytes 1572872 | tf_op jit(solution)/shard_map/ppermute | solution.py:403
  40.2 0.0 collective-permute-done.3.refs_6_
  40.2 5.6 %collective-permute-start.5 = (bf16[256,8,128]{2,1,0:T(8,128)(2,1)S(1)}, bf16[256,8,128]{2,1,0:T(8,128)(2,1)S(1)}, u32[]{:S(2)}, u32[]{:S(2)}) collective-permute-start(bf16[256,8,128]{2,1,0:T(8,128)(2,1)S(1)} %collective-permute-done.3.refs_6_), channel_id=1, source_target_pairs={{0,64},{64,128},{128,192},{192,256},{256,320},{320,384},{384,448},... | collective-permute-start | bytes 1572872 | tf_op jit(solution)/shard_map/ppermute | solution.py:403
  45.8 0.0 collective-permute-done.1.refs_2_
  45.8 0.9 broadcast_select_fusion
  46.7 7.0 %collective-permute-start.4 = (bf16[256,8,128]{2,1,0:T(8,128)(2,1)}, bf16[256,8,128]{2,1,0:T(8,128)(2,1)}, u32[]{:S(2)}, u32[]{:S(2)}) collective-permute-start(bf16[256,8,128]{2,1,0:T(8,128)(2,1)} %broadcast_select_fusion), channel_id=1, source_target_pairs={{0,128},{64,448},{128,256},{192,64},{256,384},{320,192},{384,0},{4... | collective-permute-start | bytes 1572872 | tf_op jit(solution)/shard_map/ppermute | solution.py:446
  53.7 1.9 %collective-permute-start.2 = (bf16[256,8,128]{2,1,0:T(8,128)(2,1)S(1)}, bf16[256,8,128]{2,1,0:T(8,128)(2,1)}, u32[]{:S(2)}, u32[]{:S(2)}) collective-permute-start(bf16[256,8,128]{2,1,0:T(8,128)(2,1)S(1)} %collective-permute-done.1.refs_2_), channel_id=1, source_target_pairs={{0,448},{64,0},{128,64},{192,128},{256,192},{320,256},{384,320},{4... | collective-permute-start | bytes 1572872 | tf_op jit(solution)/shard_map/ppermute | solution.py:403
  55.7 0.1 pad_add_fusion.where
  55.8 4.7 %plan.1 = (s32[8,128]{1,0:T(8,128)S(1)}, s32[8,64]{1,0:T(8,128)}, s32[8,16]{1,0:T(8,128)}) custom-call(s32[3]{0:T(128)S(1)} %pad_add_fusion.where, s32[8,64]{1,0:T(8,128)} %bitcast.29, s32[8,64]{1,0:T(8,128)} %bitcast.30, s32[32,128]{1,0:T(8,128)} %bitcast.28, s32[8,16]{1,0:T(8,128)} %bitcast.31, s32[8,16]{1,0:T(8,128)} %bitcast.32, s32[8,128]{1,0:T(8,128)} %bitcast.33), custom_call_target="tpu_custom_call" | custom-call | tf_op jit(solution)/shard_map/plan/pallas_call | solution.py:120
  60.4 18.0 %all_to_all.32 = s32[8,1,128]{2,1,0:T(1,128)S(1)} all-to-all(s32[8,1,128]{2,1,0:T(1,128)S(1)} %bitcast.25), channel_id=1, replica_groups={{0,8,16,24,32,40,48,56},{64,72,80,88,96,104,112,120},{128,136,144,152,1..., dimensions={0} | all-to-all | bytes 8192 | tf_op jit(solution)/shard_map/all_to_all | solution.py:407
  78.5 0.0 collective-permute-done.6.refs_7_
  78.5 0.0 collective-permute-done.refs_1_
  78.5 0.0 collective-permute-done.5.refs_5_
  78.5 0.0 collective-permute-done.4.refs_4_
  78.5 0.0 collective-permute-done.2.refs_3_
  78.5 5.1 %select.11 = (bf16[8,16,8,8,128]{4,3,2,1,0:T(8,128)(2,1)}, bf16[64,2,8,128]{3,2,1,0:T(8,128)(2,1)}, bf16[64,2,8,128]{3,2,1,0:T(8,128)(2,1)}, bf16[64,2,8,128]{3,...) custom-call(s32[3]{0:T(128)S(1)} %pad_add_fusion.where, ...), custom_call_target="tpu_custom_call" | custom-call | tf_op jit(solution)/shard_map/select/pallas_call | solution.py:235
  83.6 0.0 copy-start.2
  83.6 3.7 %all-to-all-start.3 = ((bf16[8,16,8,8,128]{4,3,2,1,0:T(8,128)(2,1)}), bf16[8,16,8,8,128]{4,3,2,1,0:T(8,128)(2,1)S(1)}, u32[]{:S(2)}, u32[]{:S(2)}) async-start(bf16[8,16,8,8,128]{4,3,2,1,0:T(8,128)(2,1)} %get-tuple-element.28), calls=%async_computation.3 | async-start | bytes 4194304 | tf_op jit(solution)/shard_map/all_to_all | solution.py:407
  87.4 0.0 copy-start
  87.4 0.0 copy-start.1
  87.4 0.0 copy-start.5
  87.4 3.9 %collective-permute-start.7 = (bf16[64,2,8,128]{3,2,1,0:T(8,128)(2,1)}, bf16[64,2,8,128]{3,2,1,0:T(8,128)(2,1)}, u32[]{:S(2)}, u32[]{:S(2)}) collective-permute-start(bf16[64,2,8,128]{3,2,1,0:T(8,128)(2,1)} %get-tuple-element.20), channel_id=1, source_target_pairs={{0,8},{8,16},{16,24},{24,32},{32,40},{40,48},{48,56},{56,0},{64,72... | collective-permute-start | bytes 786440 | tf_op jit(solution)/shard_map/ppermute | solution.py:403
  91.4 4.3 %collective-permute-start.8 = (bf16[64,2,8,128]{3,2,1,0:T(8,128)(2,1)}, bf16[64,2,8,128]{3,2,1,0:T(8,128)(2,1)}, u32[]{:S(2)}, u32[]{:S(2)}) collective-permute-start(bf16[64,2,8,128]{3,2,1,0:T(8,128)(2,1)} %get-tuple-element.21), channel_id=1, source_target_pairs={{0,16},{8,24},{16,32},{24,40},{32,48},{40,56},{48,0},{56,8},{64,80... | collective-permute-start | bytes 786440 | tf_op jit(solution)/shard_map/ppermute | solution.py:403
  95.7 22.0 %all-to-all-done.3 = bf16[8,16,8,8,128]{4,3,2,1,0:T(8,128)(2,1)S(1)} async-done(((bf16[8,16,8,8,128]{4,3,2,1,0:T(8,128)(2,1)}), bf16[8,16,8,8,128]{4,3,2,1,0:T(8,128)(2,1)S(1)}, u32[]{:S(2)}, u32[]{:S(2)}) %all-to-all-start.3) | async-done | bytes 2097184 | tf_op jit(solution)/shard_map/all_to_all | solution.py:407
  117.7 0.0 copy-done.2
  117.7 0.0 copy-start.3
  117.7 2.8 %far_parents.1 = bf16[16,8,8,128]{3,2,1,0:T(8,128)(2,1)} custom-call(s32[8,16]{1,0:T(8,128)} %get-tuple-element.27.code, bf16[128,8,8,128]{3,2,1,0:T(8,128)(2,1)S(1)} %bitcast.21, bf16[40,2,16,256]{3,2,1,0:T(8,128)(2,1)S(1)} %copy-done.2), custom_call_target="tpu_custom_call" | custom-call | tf_op jit(solution)/shard_map/far_parents/pallas_call | solution.py:282
  120.5 0.0 copy-start.4
  120.5 4.9 %all-to-all-start.4 = ((bf16[16,8,8,128]{3,2,1,0:T(8,128)(2,1)}), bf16[16,8,8,128]{3,2,1,0:T(8,128)(2,1)S(1)}, u32[]{:S(2)}, u32[]{:S(2)}) async-start(bf16[16,8,8,128]{3,2,1,0:T(8,128)(2,1)} %far_parents.1), calls=%async_computation.4 | async-start | bytes 524288 | tf_op jit(solution)/shard_map/all_to_all | solution.py:407
  125.4 1.9 %collective-permute-start.9 = (bf16[64,2,8,128]{3,2,1,0:T(8,128)(2,1)}, bf16[64,2,8,128]{3,2,1,0:T(8,128)(2,1)S(1)}, u32[]{:S(2)}, u32[]{:S(2)}) collective-permute-start(bf16[64,2,8,128]{3,2,1,0:T(8,128)(2,1)} %get-tuple-element.22), channel_id=1, source_target_pairs={{0,24},{8,32},{16,40},{24,48},{32,56},{40,0},{48,8},{56,16},{64,88... | collective-permute-start | bytes 786440 | tf_op jit(solution)/shard_map/ppermute | solution.py:403
  127.3 3.0 %collective-permute-start.10 = (bf16[64,2,8,128]{3,2,1,0:T(8,128)(2,1)}, bf16[64,2,8,128]{3,2,1,0:T(8,128)(2,1)S(1)}, u32[]{:S(2)}, u32[]{:S(2)}) collective-permute-start(bf16[64,2,8,128]{3,2,1,0:T(8,128)(2,1)} %get-tuple-element.23), channel_id=1, source_target_pairs={{0,32},{8,40},{16,48},{24,56},{32,0},{40,8},{48,16},{56,24},{64,96... | collective-permute-start | bytes 786440 | tf_op jit(solution)/shard_map/ppermute | solution.py:403
  130.4 6.2 %collective-permute-start.11 = (bf16[64,2,8,128]{3,2,1,0:T(8,128)(2,1)}, bf16[64,2,8,128]{3,2,1,0:T(8,128)(2,1)S(1)}, u32[]{:S(2)}, u32[]{:S(2)}) collective-permute-start(bf16[64,2,8,128]{3,2,1,0:T(8,128)(2,1)} %get-tuple-element.24), channel_id=1, source_target_pairs={{0,40},{8,48},{16,56},{24,0},{32,8},{40,16},{48,24},{56,32},{64,10... | collective-permute-start | bytes 786440 | tf_op jit(solution)/shard_map/ppermute | solution.py:403
  136.6 0.0 collective-permute-done.7.refs_1_
  136.6 5.4 %collective-permute-start.12 = (bf16[64,2,8,128]{3,2,1,0:T(8,128)(2,1)}, bf16[64,2,8,128]{3,2,1,0:T(8,128)(2,1)S(1)}, u32[]{:S(2)}, u32[]{:S(2)}) collective-permute-start(bf16[64,2,8,128]{3,2,1,0:T(8,128)(2,1)} %get-tuple-element.25), channel_id=1, source_target_pairs={{0,48},{8,56},{16,0},{24,8},{32,16},{40,24},{48,32},{56,40},{64,11... | collective-permute-start | bytes 786440 | tf_op jit(solution)/shard_map/ppermute | solution.py:403
  142.0 0.0 collective-permute-done.8.refs_2_
  142.0 3.4 %collective-permute-start.13 = (bf16[64,2,8,128]{3,2,1,0:T(8,128)(2,1)}, bf16[64,2,8,128]{3,2,1,0:T(8,128)(2,1)S(1)}, u32[]{:S(2)}, u32[]{:S(2)}) collective-permute-start(bf16[64,2,8,128]{3,2,1,0:T(8,128)(2,1)} %get-tuple-element.26), channel_id=1, source_target_pairs={{0,56},{8,0},{16,8},{24,16},{32,24},{40,32},{48,40},{56,48},{64,12... | collective-permute-start | bytes 786440 | tf_op jit(solution)/shard_map/ppermute | solution.py:403
  145.5 0.0 all-to-all-done.4
  145.5 0.0 copy-done
  145.5 0.0 copy-done.1
  145.5 0.0 copy-done.5
  145.5 4.3 %lower.1 = bf16[8,8,2,8,128]{4,3,2,1,0:T(8,128)(2,1)} custom-call(bf16[8,2,8,8,128]{4,3,2,1,0:T(8,128)(2,1)S(1)} %bitcast.22, bf16[64,128]{1,0:T(8,128)(2,1)S(1)} %copy-done.5, bf16[256,128]{1,0:T(8,128)(2,1)} %constant.76.phi_h, f32[2,128,256]{2,1,0:T(8,128)S(1)} %copy-done.1, f32[2,128,256]{2,1,0:T(8,128)S(1)} %copy-done), custom_call_target="tpu_custom_call" | custom-call | tf_op jit(solution)/shard_map/lower/pallas_call | solution.py:372
  149.8 4.8 %all-to-all-start.5 = ((bf16[8,8,2,8,128]{4,3,2,1,0:T(8,128)(2,1)}), bf16[8,8,2,8,128]{4,3,2,1,0:T(8,128)(2,1)S(1)}, u32[]{:S(2)}, u32[]{:S(2)}) async-start(bf16[8,8,2,8,128]{4,3,2,1,0:T(8,128)(2,1)} %lower.1), calls=%async_computation.5 | async-start | bytes 524288 | tf_op jit(solution)/shard_map/all_to_all | solution.py:407
  154.6 0.0 collective-permute-done.9.refs_3_
  154.6 0.0 collective-permute-done.10.refs_4_
  154.6 0.0 collective-permute-done.11.refs_5_
  154.7 2.3 %collective-permute-done.12.refs_6_ = bf16[64,2,8,128]{3,2,1,0:T(8,128)(2,1)S(1)} collective-permute-done((bf16[64,2,8,128]{3,2,1,0:T(8,128)(2,1)}, bf16[64,2,8,128]{3,2,1,0:T(8,128)(2,1)S(1)}, u32[]{:S(2)}, u32[]{:S(2)}) %collective-permute-start.12) | collective-permute-done | bytes 262176 | tf_op jit(solution)/shard_map/ppermute | solution.py:403
  157.0 2.9 %collective-permute-done.13.refs_7_ = bf16[64,2,8,128]{3,2,1,0:T(8,128)(2,1)S(1)} collective-permute-done((bf16[64,2,8,128]{3,2,1,0:T(8,128)(2,1)}, bf16[64,2,8,128]{3,2,1,0:T(8,128)(2,1)S(1)}, u32[]{:S(2)}, u32[]{:S(2)}) %collective-permute-start.13) | collective-permute-done | bytes 262176 | tf_op jit(solution)/shard_map/ppermute | solution.py:403
  159.9 0.0 copy-done.3
  159.9 0.0 copy-done.4
  159.9 4.2 %far_children.1 = f32[64,2,8,128]{3,2,1,0:T(8,128)S(1)} custom-call(s32[8,64]{1,0:T(8,128)} %get-tuple-element.17.code, bf16[64,2,8,128]{3,2,1,0:T(8,128)(2,1)S(1)} %copy-done.3, bf16[64,2,8,128]{3,2,1,0:T(8,128)(2,1)} %collective-permute-done.7.refs_1_, bf16[64,2,8,128]{3,2,1,0:T(8,128)(2,1)} %collective-permute-done.8.refs_2_, ...), custom_call_target="tpu_custom_call" | custom-call | tf_op jit(solution)/shard_map/far_children/pallas_call | solution.py:322
  164.1 0.0 all-to-all-done.5
  164.1 0.8 fusion
  (1 shorter events, 0.0 us)
Async XLA Ops:
  0.0 23.5 %copy-start.6 = (bf16[64,2,8,128]{3,2,1,0:T(8,128)(2,1)S(1)}, bf16[64,2,8,128]{3,2,1,0:T(8,128)(2,1)}, u32[]{:S(2)}) copy-start(bf16[64,2,8,128]{3,2,1,0:T(8,128)(2,1)} %param.15) | copy-start | bytes 786436
  23.6 16.7 %collective-permute-start.3 = (bf16[256,8,128]{2,1,0:T(8,128)(2,1)S(1)}, bf16[256,8,128]{2,1,0:T(8,128)(2,1)S(1)}, u32[]{:S(2)}, u32[]{:S(2)}) collective-permute-start(bf16[256,8,128]{2,1,0:T(8,128)(2,1)S(1)} %pad_maximum_fusion.refs_0_), channel_id=1, source_target_pairs={{0,128},{64,192},{128,256},{192,320},{256,384},{320,448},{384,0},{... | collective-permute-start | bytes 1572872 | tf_op jit(solution)/shard_map/ppermute | solution.py:403
  28.1 17.8 %collective-permute-start.1 = (bf16[256,8,128]{2,1,0:T(8,128)(2,1)S(1)}, bf16[256,8,128]{2,1,0:T(8,128)(2,1)S(1)}, u32[]{:S(2)}, u32[]{:S(2)}) collective-permute-start(bf16[256,8,128]{2,1,0:T(8,128)(2,1)S(1)} %pad_maximum_fusion.refs_0_), channel_id=1, source_target_pairs={{0,384},{64,448},{128,0},{192,64},{256,128},{320,192},{384,256},{4... | collective-permute-start | bytes 1572872 | tf_op jit(solution)/shard_map/ppermute | solution.py:403
  31.6 46.9 %collective-permute-start.6 = (bf16[256,8,128]{2,1,0:T(8,128)(2,1)S(1)}, bf16[256,8,128]{2,1,0:T(8,128)(2,1)S(1)}, u32[]{:S(2)}, u32[]{:S(2)}) collective-permute-start(bf16[256,8,128]{2,1,0:T(8,128)(2,1)S(1)} %pad_maximum_fusion.refs_0_), channel_id=1, source_target_pairs={{0,64},{64,128},{128,192},{192,256},{256,320},{320,384},{384,448},... | collective-permute-start | bytes 1572872 | tf_op jit(solution)/shard_map/ppermute | solution.py:403
  35.6 42.8 %collective-permute-start = (bf16[256,8,128]{2,1,0:T(8,128)(2,1)S(1)}, bf16[256,8,128]{2,1,0:T(8,128)(2,1)S(1)}, u32[]{:S(2)}, u32[]{:S(2)}) collective-permute-start(bf16[256,8,128]{2,1,0:T(8,128)(2,1)S(1)} %pad_maximum_fusion.refs_0_), channel_id=1, source_target_pairs={{0,448},{64,0},{128,64},{192,128},{256,192},{320,256},{384,320},{4... | collective-permute-start | bytes 1572872 | tf_op jit(solution)/shard_map/ppermute | solution.py:403
  40.2 38.2 %collective-permute-start.5 = (bf16[256,8,128]{2,1,0:T(8,128)(2,1)S(1)}, bf16[256,8,128]{2,1,0:T(8,128)(2,1)S(1)}, u32[]{:S(2)}, u32[]{:S(2)}) collective-permute-start(bf16[256,8,128]{2,1,0:T(8,128)(2,1)S(1)} %collective-permute-done.3.refs_6_), channel_id=1, source_target_pairs={{0,64},{64,128},{128,192},{192,256},{256,320},{320,384},{384,448},... | collective-permute-start | bytes 1572872 | tf_op jit(solution)/shard_map/ppermute | solution.py:403
  46.7 31.8 %collective-permute-start.4 = (bf16[256,8,128]{2,1,0:T(8,128)(2,1)}, bf16[256,8,128]{2,1,0:T(8,128)(2,1)}, u32[]{:S(2)}, u32[]{:S(2)}) collective-permute-start(bf16[256,8,128]{2,1,0:T(8,128)(2,1)} %broadcast_select_fusion), channel_id=1, source_target_pairs={{0,128},{64,448},{128,256},{192,64},{256,384},{320,192},{384,0},{4... | collective-permute-start | bytes 1572872 | tf_op jit(solution)/shard_map/ppermute | solution.py:446
  53.7 24.7 %collective-permute-start.2 = (bf16[256,8,128]{2,1,0:T(8,128)(2,1)S(1)}, bf16[256,8,128]{2,1,0:T(8,128)(2,1)}, u32[]{:S(2)}, u32[]{:S(2)}) collective-permute-start(bf16[256,8,128]{2,1,0:T(8,128)(2,1)S(1)} %collective-permute-done.1.refs_2_), channel_id=1, source_target_pairs={{0,448},{64,0},{128,64},{192,128},{256,192},{320,256},{384,320},{4... | collective-permute-start | bytes 1572872 | tf_op jit(solution)/shard_map/ppermute | solution.py:403
  83.6 34.1 %copy-start.2 = (bf16[40,2,16,256]{3,2,1,0:T(8,128)(2,1)S(1)}, bf16[40,2,16,256]{3,2,1,0:T(8,128)(2,1)}, u32[]{:S(2)}) copy-start(bf16[40,2,16,256]{3,2,1,0:T(8,128)(2,1)} %ops_hbm.1) | copy-start | bytes 1966084
  83.6 34.0 %all-to-all-start.3 = ((bf16[8,16,8,8,128]{4,3,2,1,0:T(8,128)(2,1)}), bf16[8,16,8,8,128]{4,3,2,1,0:T(8,128)(2,1)S(1)}, u32[]{:S(2)}, u32[]{:S(2)}) async-start(bf16[8,16,8,8,128]{4,3,2,1,0:T(8,128)(2,1)} %get-tuple-element.28), calls=%async_computation.3 | async-start | bytes 4194304 | tf_op jit(solution)/shard_map/all_to_all | solution.py:407
  87.4 58.1 %copy-start = (f32[2,128,256]{2,1,0:T(8,128)S(1)}, f32[2,128,256]{2,1,0:T(8,128)}, u32[]{:S(2)}) copy-start(f32[2,128,256]{2,1,0:T(8,128)} %constant.70.clone.sin_h.sin_t) | copy-start | bytes 786436
  87.4 58.1 %copy-start.1 = (f32[2,128,256]{2,1,0:T(8,128)S(1)}, f32[2,128,256]{2,1,0:T(8,128)}, u32[]{:S(2)}) copy-start(f32[2,128,256]{2,1,0:T(8,128)} %constant.69.clone.cos_h.cos_t) | copy-start | bytes 786436
  87.4 58.1 %copy-start.5 = (bf16[64,128]{1,0:T(8,128)(2,1)S(1)}, bf16[64,128]{1,0:T(8,128)(2,1)}, u32[]{:S(2)}) copy-start(bf16[64,128]{1,0:T(8,128)(2,1)} %constant.75.theta) | copy-start | bytes 49156
  87.4 49.1 %collective-permute-start.7 = (bf16[64,2,8,128]{3,2,1,0:T(8,128)(2,1)}, bf16[64,2,8,128]{3,2,1,0:T(8,128)(2,1)}, u32[]{:S(2)}, u32[]{:S(2)}) collective-permute-start(bf16[64,2,8,128]{3,2,1,0:T(8,128)(2,1)} %get-tuple-element.20), channel_id=1, source_target_pairs={{0,8},{8,16},{16,24},{24,32},{32,40},{40,48},{48,56},{56,0},{64,72... | collective-permute-start | bytes 786440 | tf_op jit(solution)/shard_map/ppermute | solution.py:403
  91.4 50.6 %collective-permute-start.8 = (bf16[64,2,8,128]{3,2,1,0:T(8,128)(2,1)}, bf16[64,2,8,128]{3,2,1,0:T(8,128)(2,1)}, u32[]{:S(2)}, u32[]{:S(2)}) collective-permute-start(bf16[64,2,8,128]{3,2,1,0:T(8,128)(2,1)} %get-tuple-element.21), channel_id=1, source_target_pairs={{0,16},{8,24},{16,32},{24,40},{32,48},{40,56},{48,0},{56,8},{64,80... | collective-permute-start | bytes 786440 | tf_op jit(solution)/shard_map/ppermute | solution.py:403
  117.7 42.2 %copy-start.3 = (bf16[64,2,8,128]{3,2,1,0:T(8,128)(2,1)S(1)}, bf16[64,2,8,128]{3,2,1,0:T(8,128)(2,1)}, u32[]{:S(2)}) copy-start(bf16[64,2,8,128]{3,2,1,0:T(8,128)(2,1)} %get-tuple-element.19.refs_0_) | copy-start | bytes 786436
  120.5 39.4 %copy-start.4 = (bf16[40,2,8,128]{3,2,1,0:T(8,128)(2,1)S(1)}, bf16[40,2,8,128]{3,2,1,0:T(8,128)(2,1)}, u32[]{:S(2)}) copy-start(bf16[40,2,8,128]{3,2,1,0:T(8,128)(2,1)} %refs_8_.1) | copy-start | bytes 491524
  120.5 25.0 %all-to-all-start.4 = ((bf16[16,8,8,128]{3,2,1,0:T(8,128)(2,1)}), bf16[16,8,8,128]{3,2,1,0:T(8,128)(2,1)S(1)}, u32[]{:S(2)}, u32[]{:S(2)}) async-start(bf16[16,8,8,128]{3,2,1,0:T(8,128)(2,1)} %far_parents.1), calls=%async_computation.4 | async-start | bytes 524288 | tf_op jit(solution)/shard_map/all_to_all | solution.py:407
  125.4 29.2 %collective-permute-start.9 = (bf16[64,2,8,128]{3,2,1,0:T(8,128)(2,1)}, bf16[64,2,8,128]{3,2,1,0:T(8,128)(2,1)S(1)}, u32[]{:S(2)}, u32[]{:S(2)}) collective-permute-start(bf16[64,2,8,128]{3,2,1,0:T(8,128)(2,1)} %get-tuple-element.22), channel_id=1, source_target_pairs={{0,24},{8,32},{16,40},{24,48},{32,56},{40,0},{48,8},{56,16},{64,88... | collective-permute-start | bytes 786440 | tf_op jit(solution)/shard_map/ppermute | solution.py:403
  127.3 27.3 %collective-permute-start.10 = (bf16[64,2,8,128]{3,2,1,0:T(8,128)(2,1)}, bf16[64,2,8,128]{3,2,1,0:T(8,128)(2,1)S(1)}, u32[]{:S(2)}, u32[]{:S(2)}) collective-permute-start(bf16[64,2,8,128]{3,2,1,0:T(8,128)(2,1)} %get-tuple-element.23), channel_id=1, source_target_pairs={{0,32},{8,40},{16,48},{24,56},{32,0},{40,8},{48,16},{56,24},{64,96... | collective-permute-start | bytes 786440 | tf_op jit(solution)/shard_map/ppermute | solution.py:403
  130.4 24.3 %collective-permute-start.11 = (bf16[64,2,8,128]{3,2,1,0:T(8,128)(2,1)}, bf16[64,2,8,128]{3,2,1,0:T(8,128)(2,1)S(1)}, u32[]{:S(2)}, u32[]{:S(2)}) collective-permute-start(bf16[64,2,8,128]{3,2,1,0:T(8,128)(2,1)} %get-tuple-element.24), channel_id=1, source_target_pairs={{0,40},{8,48},{16,56},{24,0},{32,8},{40,16},{48,24},{56,32},{64,10... | collective-permute-start | bytes 786440 | tf_op jit(solution)/shard_map/ppermute | solution.py:403
  136.6 20.4 %collective-permute-start.12 = (bf16[64,2,8,128]{3,2,1,0:T(8,128)(2,1)}, bf16[64,2,8,128]{3,2,1,0:T(8,128)(2,1)S(1)}, u32[]{:S(2)}, u32[]{:S(2)}) collective-permute-start(bf16[64,2,8,128]{3,2,1,0:T(8,128)(2,1)} %get-tuple-element.25), channel_id=1, source_target_pairs={{0,48},{8,56},{16,0},{24,8},{32,16},{40,24},{48,32},{56,40},{64,11... | collective-permute-start | bytes 786440 | tf_op jit(solution)/shard_map/ppermute | solution.py:403
  142.0 17.9 %collective-permute-start.13 = (bf16[64,2,8,128]{3,2,1,0:T(8,128)(2,1)}, bf16[64,2,8,128]{3,2,1,0:T(8,128)(2,1)S(1)}, u32[]{:S(2)}, u32[]{:S(2)}) collective-permute-start(bf16[64,2,8,128]{3,2,1,0:T(8,128)(2,1)} %get-tuple-element.26), channel_id=1, source_target_pairs={{0,56},{8,0},{16,8},{24,16},{32,24},{40,32},{48,40},{56,48},{64,12... | collective-permute-start | bytes 786440 | tf_op jit(solution)/shard_map/ppermute | solution.py:403
  149.8 14.3 %all-to-all-start.5 = ((bf16[8,8,2,8,128]{4,3,2,1,0:T(8,128)(2,1)}), bf16[8,8,2,8,128]{4,3,2,1,0:T(8,128)(2,1)S(1)}, u32[]{:S(2)}, u32[]{:S(2)}) async-start(bf16[8,8,2,8,128]{4,3,2,1,0:T(8,128)(2,1)} %lower.1), calls=%async_computation.5 | async-start | bytes 524288 | tf_op jit(solution)/shard_map/all_to_all | solution.py:407

commit v10 on v8

--- a/solution.py
+++ b/solution.py
@@ -135,11 +135,19 @@
     copies = fetch((theta_h, phi_h, cos_h, sin_h), (theta, phi, cos_t, sin_t), sems)
     copies[0].wait()
     copies[1].wait()
-    for r in range(8):
-        for c in range(2):
-            rows = jnp.concatenate([field[s, r, c] for s in range(8)], axis=0)
-            stretched = bmm(theta[...], rows).astype(BF16)
-            wide[r * 2 + c] = bmm(stretched, phi[...])
+    for i in range(4):
+        rows = jnp.concatenate(
+            [
+                jnp.concatenate([field[s, (i * 4 + k) // 2, k % 2] for s in range(8)], axis=0)
+                for k in range(4)
+            ],
+            axis=1,
+        )
+        stretched = bmm(theta[...], rows).astype(BF16)
+        tall = jnp.concatenate([stretched[:, k * 128 : k * 128 + 128] for k in range(4)], axis=0)
+        spread = bmm(tall, phi[...])
+        for k in range(4):
+            wide[i * 4 + k] = spread[k * PT : (k + 1) * PT]
     copies[2].wait()
     copies[3].wait()
     for q in range(2):
@@ -334,7 +342,7 @@
     )(code, *blocks, ops)
 
 
-def down_body(far, theta, phi_h, cos_t, sin_t, out, phi, turned, sem):
+def down_body(far, theta, phi_h, cos_t, sin_t, out, phi, turned, thin, sem):
     copy = pltpu.make_async_copy(phi_h, phi, sem)
     copy.start()
     for q in range(2):
@@ -354,12 +362,17 @@
                 turned[(q * 4 + m) * 2, at, :] = (cr - si).astype(BF16)
                 turned[(q * 4 + m) * 2 + 1, at, :] = (ci + sr).astype(BF16)
     copy.wait()
-    for r in range(8):
-        for c in range(2):
-            narrowed = bmm(turned[r * 2 + c], phi[...]).astype(BF16)
-            term = bmm(theta[...], narrowed).astype(BF16)
+    for i in range(4):
+        tall = jnp.concatenate([turned[i * 4 + k] for k in range(4)], axis=0)
+        narrowed = bmm(tall, phi[...]).astype(BF16)
+        for k in range(4):
+            at = (i * 4 + k) * SUBBOX_HEADINGS
+            thin[:, at : at + SUBBOX_HEADINGS] = narrowed[k * PT : (k + 1) * PT]
+    for i in range(4):
+        term = bmm(theta[...], thin[:, i * 512 : i * 512 + 512]).astype(BF16)
+        for k in range(4):
             for s in range(8):
-                out[s, r, c] = term[s * 8 : s * 8 + 8, :]
+                out[s, (i * 4 + k) // 2, k % 2] = term[s * 8 : s * 8 + 8, k * 128 : k * 128 + 128]
 
 
 def lower(far, tables):
@@ -371,6 +384,7 @@
         scratch_shapes=[
             pltpu.VMEM(tables[1].shape, BF16),
             pltpu.VMEM((16, PT, PP), BF16),
+            pltpu.VMEM((PT, 16 * SUBBOX_HEADINGS), BF16),
             pltpu.SemaphoreType.DMA,
         ],
         compiler_params=pltpu.CompilerParams(vmem_limit_bytes=GRANT),

time: 166 us -> 165 us (level)
  Pallas kernels: 23.7 us -> 20.8 us
  waiting for transfers between devices: 27.2 us -> 29.4 us
    ppermute x13, waiting for transfers between devices: 5.21 us -> 7.33 us  [hop(): return lax.ppermute(x, BOTH, pairs)]
    pallas_call x1, Pallas kernels: 4.35 us -> 2.23 us  [lower(): pl.pallas_call(down_body, out_shape=jax.ShapeDtypeStruct((8, 8, 2, 8, 128...]
  transfers between devices with their start and end apart: 17 -> 17, of which waited for: 3 -> 3; matrix products, arithmetic and copies ran while one was open for 1% -> 1% of each run, Pallas kernels for 10% -> 8%
where the time goes in v10:
time: 165 us; the launch traced here: 164 us
  starting transfers between devices  72.8 us (44%)
  blocking collectives  39 us (24%)
  waiting for transfers between devices  29.4 us (18%)
  Pallas kernels  20.8 us (13%)
  other arithmetic  1.77 us (1%)
    ppermute x13, starting transfers between devices, hop(): return lax.ppermute(x, BOTH, pairs)  52.3 us
    all_to_all x3, blocking collectives, swap(): lax.all_to_all(x, axis, split_axis=0, concat_axis=0, tiled=True, **kw)  39 us
    all_to_all x3, waiting for transfers between devices, swap(): lax.all_to_all(x, axis, split_axis=0, concat_axis=0, tiled=True, **kw)  22 us
    all_to_all x3, starting transfers between devices, swap(): lax.all_to_all(x, axis, split_axis=0, concat_axis=0, tiled=True, **kw)  13.5 us
    ppermute x13, waiting for transfers between devices, hop(): return lax.ppermute(x, BOTH, pairs)  7.33 us
    ppermute x1, starting transfers between devices, local(): up4 = lax.ppermute(onward, BOTH, pairs)  7.03 us
    pallas_call x1, Pallas kernels, select(): pl.pallas_call(select_body, out_shape=(pltpu.HBM((SIDE, 16, 8, 8, 128), B...  5.14 us
    pallas_call x1, Pallas kernels, plan(): pl.pallas_call(plan_body, out_shape=(jax.ShapeDtypeStruct((SIDE, 128), I3...  4.66 us
  transfers between devices with their start and end apart: 17, of which 3 were waited for; matrix products, arithmetic and copies ran while one was open for 1% of the time, Pallas kernels for 8%

profile of v10, /device:TPU:10, one launch (start us, length us, event | category | flops | bytes accessed | tf_op | source)
XLA Modules:
  0.0 164.1 jit_solution(4037567681123387255)
XLA Ops:
  0.0 0.0 copy-start.6
  0.0 11.0 %all_to_all.30 = bf16[64,2,8,128]{3,2,1,0:T(8,128)(2,1)S(1)} all-to-all(bf16[64,2,8,128]{3,2,1,0:T(8,128)(2,1)} %param.15), channel_id=1, replica_groups=mesh['box'=64,'angle'=8] {'angle'}, dimensions={0} | all-to-all | bytes 524288 | tf_op jit(solution)/shard_map/all_to_all | solution.py:413
  11.0 1.8 %lift.1 = bf16[8,2,8,8,128]{4,3,2,1,0:T(8,128)(2,1)S(1)} custom-call(bf16[8,8,2,8,128]{4,3,2,1,0:T(8,128)(2,1)S(1)} %bitcast.23, bf16[128,64]{1,0:T(8,128)(2,1)} %constant.73.theta_h, bf16[128,256]{1,0:T(8,128)(2,1)} %constant.74.phi_h, f32[2,128,256]{2,1,0:T(8,128)} %constant.69.clone.cos_h.cos_t, f32[2,128,256]{2,1,0:T(8,128)} %constant.70.clone.sin_h.sin_t), custom_call_target="tpu_custom_call" | custom-call | tf_op jit(solution)/shard_map/lift/pallas_call | solution.py:177
  12.8 9.9 %all_to_all.31 = bf16[8,2,8,8,128]{4,3,2,1,0:T(8,128)(2,1)S(1)} all-to-all(bf16[8,2,8,8,128]{4,3,2,1,0:T(8,128)(2,1)S(1)} %lift.1), channel_id=1, replica_groups=mesh['box'=64,'angle'=8] {'angle'}, dimensions={0} | all-to-all | bytes 524288 | tf_op jit(solution)/shard_map/all_to_all | solution.py:413
  22.7 0.0 copy-done.6
  22.8 4.5 %collective-permute-start.3 = (bf16[256,8,128]{2,1,0:T(8,128)(2,1)S(1)}, bf16[256,8,128]{2,1,0:T(8,128)(2,1)S(1)}, u32[]{:S(2)}, u32[]{:S(2)}) collective-permute-start(bf16[256,8,128]{2,1,0:T(8,128)(2,1)S(1)} %pad_maximum_fusion.refs_0_), channel_id=1, source_target_pairs={{0,128},{64,192},{128,256},{192,320},{256,384},{320,448},{384,0},{... | collective-permute-start | bytes 1572872 | tf_op jit(solution)/shard_map/ppermute | solution.py:409
  27.3 3.5 %collective-permute-start.1 = (bf16[256,8,128]{2,1,0:T(8,128)(2,1)S(1)}, bf16[256,8,128]{2,1,0:T(8,128)(2,1)S(1)}, u32[]{:S(2)}, u32[]{:S(2)}) collective-permute-start(bf16[256,8,128]{2,1,0:T(8,128)(2,1)S(1)} %pad_maximum_fusion.refs_0_), channel_id=1, source_target_pairs={{0,384},{64,448},{128,0},{192,64},{256,128},{320,192},{384,256},{4... | collective-permute-start | bytes 1572872 | tf_op jit(solution)/shard_map/ppermute | solution.py:409
  30.8 4.1 %collective-permute-start.6 = (bf16[256,8,128]{2,1,0:T(8,128)(2,1)S(1)}, bf16[256,8,128]{2,1,0:T(8,128)(2,1)S(1)}, u32[]{:S(2)}, u32[]{:S(2)}) collective-permute-start(bf16[256,8,128]{2,1,0:T(8,128)(2,1)S(1)} %pad_maximum_fusion.refs_0_), channel_id=1, source_target_pairs={{0,64},{64,128},{128,192},{192,256},{256,320},{320,384},{384,448},... | collective-permute-start | bytes 1572872 | tf_op jit(solution)/shard_map/ppermute | solution.py:409
  34.9 4.6 %collective-permute-start = (bf16[256,8,128]{2,1,0:T(8,128)(2,1)S(1)}, bf16[256,8,128]{2,1,0:T(8,128)(2,1)S(1)}, u32[]{:S(2)}, u32[]{:S(2)}) collective-permute-start(bf16[256,8,128]{2,1,0:T(8,128)(2,1)S(1)} %pad_maximum_fusion.refs_0_), channel_id=1, source_target_pairs={{0,448},{64,0},{128,64},{192,128},{256,192},{320,256},{384,320},{4... | collective-permute-start | bytes 1572872 | tf_op jit(solution)/shard_map/ppermute | solution.py:409
  39.4 0.0 collective-permute-done.3.refs_6_
  39.5 5.6 %collective-permute-start.5 = (bf16[256,8,128]{2,1,0:T(8,128)(2,1)S(1)}, bf16[256,8,128]{2,1,0:T(8,128)(2,1)S(1)}, u32[]{:S(2)}, u32[]{:S(2)}) collective-permute-start(bf16[256,8,128]{2,1,0:T(8,128)(2,1)S(1)} %collective-permute-done.3.refs_6_), channel_id=1, source_target_pairs={{0,64},{64,128},{128,192},{192,256},{256,320},{320,384},{384,448},... | collective-permute-start | bytes 1572872 | tf_op jit(solution)/shard_map/ppermute | solution.py:409
  45.0 0.0 collective-permute-done.1.refs_2_
  45.0 0.9 broadcast_select_fusion
  45.9 7.0 %collective-permute-start.4 = (bf16[256,8,128]{2,1,0:T(8,128)(2,1)}, bf16[256,8,128]{2,1,0:T(8,128)(2,1)}, u32[]{:S(2)}, u32[]{:S(2)}) collective-permute-start(bf16[256,8,128]{2,1,0:T(8,128)(2,1)} %broadcast_select_fusion), channel_id=1, source_target_pairs={{0,128},{64,448},{128,256},{192,64},{256,384},{320,192},{384,0},{4... | collective-permute-start | bytes 1572872 | tf_op jit(solution)/shard_map/ppermute | solution.py:452
  53.0 1.9 %collective-permute-start.2 = (bf16[256,8,128]{2,1,0:T(8,128)(2,1)S(1)}, bf16[256,8,128]{2,1,0:T(8,128)(2,1)}, u32[]{:S(2)}, u32[]{:S(2)}) collective-permute-start(bf16[256,8,128]{2,1,0:T(8,128)(2,1)S(1)} %collective-permute-done.1.refs_2_), channel_id=1, source_target_pairs={{0,448},{64,0},{128,64},{192,128},{256,192},{320,256},{384,320},{4... | collective-permute-start | bytes 1572872 | tf_op jit(solution)/shard_map/ppermute | solution.py:409
  54.9 0.1 pad_add_fusion.where
  55.0 4.7 %plan.1 = (s32[8,128]{1,0:T(8,128)S(1)}, s32[8,64]{1,0:T(8,128)}, s32[8,16]{1,0:T(8,128)}) custom-call(s32[3]{0:T(128)S(1)} %pad_add_fusion.where, s32[8,64]{1,0:T(8,128)} %bitcast.29, s32[8,64]{1,0:T(8,128)} %bitcast.30, s32[32,128]{1,0:T(8,128)} %bitcast.28, s32[8,16]{1,0:T(8,128)} %bitcast.31, s32[8,16]{1,0:T(8,128)} %bitcast.32, s32[8,128]{1,0:T(8,128)} %bitcast.33), custom_call_target="tpu_custom_call" | custom-call | tf_op jit(solution)/shard_map/plan/pallas_call | solution.py:120
  59.6 18.0 %all_to_all.32 = s32[8,1,128]{2,1,0:T(1,128)S(1)} all-to-all(s32[8,1,128]{2,1,0:T(1,128)S(1)} %bitcast.25), channel_id=1, replica_groups={{0,8,16,24,32,40,48,56},{64,72,80,88,96,104,112,120},{128,136,144,152,1..., dimensions={0} | all-to-all | bytes 8192 | tf_op jit(solution)/shard_map/all_to_all | solution.py:413
  77.7 0.0 collective-permute-done.6.refs_7_
  77.7 0.0 collective-permute-done.refs_1_
  77.7 0.0 collective-permute-done.5.refs_5_
  77.7 0.0 collective-permute-done.4.refs_4_
  77.7 0.0 collective-permute-done.2.refs_3_
  77.7 5.1 %select.11 = (bf16[8,16,8,8,128]{4,3,2,1,0:T(8,128)(2,1)}, bf16[64,2,8,128]{3,2,1,0:T(8,128)(2,1)}, bf16[64,2,8,128]{3,2,1,0:T(8,128)(2,1)}, bf16[64,2,8,128]{3,...) custom-call(s32[3]{0:T(128)S(1)} %pad_add_fusion.where, ...), custom_call_target="tpu_custom_call" | custom-call | tf_op jit(solution)/shard_map/select/pallas_call | solution.py:243
  82.9 0.0 copy-start.2
  82.9 3.7 %all-to-all-start.3 = ((bf16[8,16,8,8,128]{4,3,2,1,0:T(8,128)(2,1)}), bf16[8,16,8,8,128]{4,3,2,1,0:T(8,128)(2,1)S(1)}, u32[]{:S(2)}, u32[]{:S(2)}) async-start(bf16[8,16,8,8,128]{4,3,2,1,0:T(8,128)(2,1)} %get-tuple-element.28), calls=%async_computation.3 | async-start | bytes 4194304 | tf_op jit(solution)/shard_map/all_to_all | solution.py:413
  86.6 0.0 copy-start
  86.6 0.0 copy-start.1
  86.6 0.0 copy-start.5
  86.7 3.9 %collective-permute-start.7 = (bf16[64,2,8,128]{3,2,1,0:T(8,128)(2,1)}, bf16[64,2,8,128]{3,2,1,0:T(8,128)(2,1)}, u32[]{:S(2)}, u32[]{:S(2)}) collective-permute-start(bf16[64,2,8,128]{3,2,1,0:T(8,128)(2,1)} %get-tuple-element.20), channel_id=1, source_target_pairs={{0,8},{8,16},{16,24},{24,32},{32,40},{40,48},{48,56},{56,0},{64,72... | collective-permute-start | bytes 786440 | tf_op jit(solution)/shard_map/ppermute | solution.py:409
  90.6 4.3 %collective-permute-start.8 = (bf16[64,2,8,128]{3,2,1,0:T(8,128)(2,1)}, bf16[64,2,8,128]{3,2,1,0:T(8,128)(2,1)}, u32[]{:S(2)}, u32[]{:S(2)}) collective-permute-start(bf16[64,2,8,128]{3,2,1,0:T(8,128)(2,1)} %get-tuple-element.21), channel_id=1, source_target_pairs={{0,16},{8,24},{16,32},{24,40},{32,48},{40,56},{48,0},{56,8},{64,80... | collective-permute-start | bytes 786440 | tf_op jit(solution)/shard_map/ppermute | solution.py:409
  94.9 22.0 %all-to-all-done.3 = bf16[8,16,8,8,128]{4,3,2,1,0:T(8,128)(2,1)S(1)} async-done(((bf16[8,16,8,8,128]{4,3,2,1,0:T(8,128)(2,1)}), bf16[8,16,8,8,128]{4,3,2,1,0:T(8,128)(2,1)S(1)}, u32[]{:S(2)}, u32[]{:S(2)}) %all-to-all-start.3) | async-done | bytes 2097184 | tf_op jit(solution)/shard_map/all_to_all | solution.py:413
  116.9 0.0 copy-done.2
  116.9 0.0 copy-start.3
  116.9 2.8 %far_parents.1 = bf16[16,8,8,128]{3,2,1,0:T(8,128)(2,1)} custom-call(s32[8,16]{1,0:T(8,128)} %get-tuple-element.27.code, bf16[128,8,8,128]{3,2,1,0:T(8,128)(2,1)S(1)} %bitcast.21, bf16[40,2,16,256]{3,2,1,0:T(8,128)(2,1)S(1)} %copy-done.2), custom_call_target="tpu_custom_call" | custom-call | tf_op jit(solution)/shard_map/far_parents/pallas_call | solution.py:290
  119.7 0.0 copy-start.4
  119.7 4.9 %all-to-all-start.4 = ((bf16[16,8,8,128]{3,2,1,0:T(8,128)(2,1)}), bf16[16,8,8,128]{3,2,1,0:T(8,128)(2,1)S(1)}, u32[]{:S(2)}, u32[]{:S(2)}) async-start(bf16[16,8,8,128]{3,2,1,0:T(8,128)(2,1)} %far_parents.1), calls=%async_computation.4 | async-start | bytes 524288 | tf_op jit(solution)/shard_map/all_to_all | solution.py:413
  124.6 1.9 %collective-permute-start.9 = (bf16[64,2,8,128]{3,2,1,0:T(8,128)(2,1)}, bf16[64,2,8,128]{3,2,1,0:T(8,128)(2,1)S(1)}, u32[]{:S(2)}, u32[]{:S(2)}) collective-permute-start(bf16[64,2,8,128]{3,2,1,0:T(8,128)(2,1)} %get-tuple-element.22), channel_id=1, source_target_pairs={{0,24},{8,32},{16,40},{24,48},{32,56},{40,0},{48,8},{56,16},{64,88... | collective-permute-start | bytes 786440 | tf_op jit(solution)/shard_map/ppermute | solution.py:409
  126.6 3.0 %collective-permute-start.10 = (bf16[64,2,8,128]{3,2,1,0:T(8,128)(2,1)}, bf16[64,2,8,128]{3,2,1,0:T(8,128)(2,1)S(1)}, u32[]{:S(2)}, u32[]{:S(2)}) collective-permute-start(bf16[64,2,8,128]{3,2,1,0:T(8,128)(2,1)} %get-tuple-element.23), channel_id=1, source_target_pairs={{0,32},{8,40},{16,48},{24,56},{32,0},{40,8},{48,16},{56,24},{64,96... | collective-permute-start | bytes 786440 | tf_op jit(solution)/shard_map/ppermute | solution.py:409
  129.6 6.2 %collective-permute-start.11 = (bf16[64,2,8,128]{3,2,1,0:T(8,128)(2,1)}, bf16[64,2,8,128]{3,2,1,0:T(8,128)(2,1)S(1)}, u32[]{:S(2)}, u32[]{:S(2)}) collective-permute-start(bf16[64,2,8,128]{3,2,1,0:T(8,128)(2,1)} %get-tuple-element.24), channel_id=1, source_target_pairs={{0,40},{8,48},{16,56},{24,0},{32,8},{40,16},{48,24},{56,32},{64,10... | collective-permute-start | bytes 786440 | tf_op jit(solution)/shard_map/ppermute | solution.py:409
  135.8 0.0 collective-permute-done.7.refs_1_
  135.8 5.4 %collective-permute-start.12 = (bf16[64,2,8,128]{3,2,1,0:T(8,128)(2,1)}, bf16[64,2,8,128]{3,2,1,0:T(8,128)(2,1)S(1)}, u32[]{:S(2)}, u32[]{:S(2)}) collective-permute-start(bf16[64,2,8,128]{3,2,1,0:T(8,128)(2,1)} %get-tuple-element.25), channel_id=1, source_target_pairs={{0,48},{8,56},{16,0},{24,8},{32,16},{40,24},{48,32},{56,40},{64,11... | collective-permute-start | bytes 786440 | tf_op jit(solution)/shard_map/ppermute | solution.py:409
  141.2 0.0 collective-permute-done.8.refs_2_
  141.3 3.4 %collective-permute-start.13 = (bf16[64,2,8,128]{3,2,1,0:T(8,128)(2,1)}, bf16[64,2,8,128]{3,2,1,0:T(8,128)(2,1)S(1)}, u32[]{:S(2)}, u32[]{:S(2)}) collective-permute-start(bf16[64,2,8,128]{3,2,1,0:T(8,128)(2,1)} %get-tuple-element.26), channel_id=1, source_target_pairs={{0,56},{8,0},{16,8},{24,16},{32,24},{40,32},{48,40},{56,48},{64,12... | collective-permute-start | bytes 786440 | tf_op jit(solution)/shard_map/ppermute | solution.py:409
  144.7 0.0 all-to-all-done.4
  144.7 0.0 copy-done
  144.7 0.0 copy-done.1
  144.7 0.0 copy-done.5
  144.7 2.2 %lower.1 = bf16[8,8,2,8,128]{4,3,2,1,0:T(8,128)(2,1)} custom-call(bf16[8,2,8,8,128]{4,3,2,1,0:T(8,128)(2,1)S(1)} %bitcast.22, bf16[64,128]{1,0:T(8,128)(2,1)S(1)} %copy-done.5, bf16[256,128]{1,0:T(8,128)(2,1)} %constant.76.phi_h, f32[2,128,256]{2,1,0:T(8,128)S(1)} %copy-done.1, f32[2,128,256]{2,1,0:T(8,128)S(1)} %copy-done), custom_call_target="tpu_custom_call" | custom-call | tf_op jit(solution)/shard_map/lower/pallas_call | solution.py:379
  147.0 4.8 %all-to-all-start.5 = ((bf16[8,8,2,8,128]{4,3,2,1,0:T(8,128)(2,1)}), bf16[8,8,2,8,128]{4,3,2,1,0:T(8,128)(2,1)S(1)}, u32[]{:S(2)}, u32[]{:S(2)}) async-start(bf16[8,8,2,8,128]{4,3,2,1,0:T(8,128)(2,1)} %lower.1), calls=%async_computation.5 | async-start | bytes 524288 | tf_op jit(solution)/shard_map/all_to_all | solution.py:413
  151.8 0.0 collective-permute-done.9.refs_3_
  151.8 0.0 collective-permute-done.10.refs_4_
  151.8 0.0 collective-permute-done.11.refs_5_
  151.8 4.4 %collective-permute-done.12.refs_6_ = bf16[64,2,8,128]{3,2,1,0:T(8,128)(2,1)S(1)} collective-permute-done((bf16[64,2,8,128]{3,2,1,0:T(8,128)(2,1)}, bf16[64,2,8,128]{3,2,1,0:T(8,128)(2,1)S(1)}, u32[]{:S(2)}, u32[]{:S(2)}) %collective-permute-start.12) | collective-permute-done | bytes 262176 | tf_op jit(solution)/shard_map/ppermute | solution.py:409
  156.2 2.9 %collective-permute-done.13.refs_7_ = bf16[64,2,8,128]{3,2,1,0:T(8,128)(2,1)S(1)} collective-permute-done((bf16[64,2,8,128]{3,2,1,0:T(8,128)(2,1)}, bf16[64,2,8,128]{3,2,1,0:T(8,128)(2,1)S(1)}, u32[]{:S(2)}, u32[]{:S(2)}) %collective-permute-start.13) | collective-permute-done | bytes 262176 | tf_op jit(solution)/shard_map/ppermute | solution.py:409
  159.1 0.0 copy-done.3
  159.1 0.0 copy-done.4
  159.1 4.2 %far_children.1 = f32[64,2,8,128]{3,2,1,0:T(8,128)S(1)} custom-call(s32[8,64]{1,0:T(8,128)} %get-tuple-element.17.code, bf16[64,2,8,128]{3,2,1,0:T(8,128)(2,1)S(1)} %copy-done.3, bf16[64,2,8,128]{3,2,1,0:T(8,128)(2,1)} %collective-permute-done.7.refs_1_, bf16[64,2,8,128]{3,2,1,0:T(8,128)(2,1)} %collective-permute-done.8.refs_2_, ...), custom_call_target="tpu_custom_call" | custom-call | tf_op jit(solution)/shard_map/far_children/pallas_call | solution.py:330
  163.3 0.0 all-to-all-done.5
  163.4 0.8 fusion
  (1 shorter events, 0.0 us)
Async XLA Ops:
  0.0 22.7 %copy-start.6 = (bf16[64,2,8,128]{3,2,1,0:T(8,128)(2,1)S(1)}, bf16[64,2,8,128]{3,2,1,0:T(8,128)(2,1)}, u32[]{:S(2)}) copy-start(bf16[64,2,8,128]{3,2,1,0:T(8,128)(2,1)} %param.15) | copy-start | bytes 786436
  22.8 16.7 %collective-permute-start.3 = (bf16[256,8,128]{2,1,0:T(8,128)(2,1)S(1)}, bf16[256,8,128]{2,1,0:T(8,128)(2,1)S(1)}, u32[]{:S(2)}, u32[]{:S(2)}) collective-permute-start(bf16[256,8,128]{2,1,0:T(8,128)(2,1)S(1)} %pad_maximum_fusion.refs_0_), channel_id=1, source_target_pairs={{0,128},{64,192},{128,256},{192,320},{256,384},{320,448},{384,0},{... | collective-permute-start | bytes 1572872 | tf_op jit(solution)/shard_map/ppermute | solution.py:409
  27.3 17.8 %collective-permute-start.1 = (bf16[256,8,128]{2,1,0:T(8,128)(2,1)S(1)}, bf16[256,8,128]{2,1,0:T(8,128)(2,1)S(1)}, u32[]{:S(2)}, u32[]{:S(2)}) collective-permute-start(bf16[256,8,128]{2,1,0:T(8,128)(2,1)S(1)} %pad_maximum_fusion.refs_0_), channel_id=1, source_target_pairs={{0,384},{64,448},{128,0},{192,64},{256,128},{320,192},{384,256},{4... | collective-permute-start | bytes 1572872 | tf_op jit(solution)/shard_map/ppermute | solution.py:409
  30.8 46.9 %collective-permute-start.6 = (bf16[256,8,128]{2,1,0:T(8,128)(2,1)S(1)}, bf16[256,8,128]{2,1,0:T(8,128)(2,1)S(1)}, u32[]{:S(2)}, u32[]{:S(2)}) collective-permute-start(bf16[256,8,128]{2,1,0:T(8,128)(2,1)S(1)} %pad_maximum_fusion.refs_0_), channel_id=1, source_target_pairs={{0,64},{64,128},{128,192},{192,256},{256,320},{320,384},{384,448},... | collective-permute-start | bytes 1572872 | tf_op jit(solution)/shard_map/ppermute | solution.py:409
  34.9 42.8 %collective-permute-start = (bf16[256,8,128]{2,1,0:T(8,128)(2,1)S(1)}, bf16[256,8,128]{2,1,0:T(8,128)(2,1)S(1)}, u32[]{:S(2)}, u32[]{:S(2)}) collective-permute-start(bf16[256,8,128]{2,1,0:T(8,128)(2,1)S(1)} %pad_maximum_fusion.refs_0_), channel_id=1, source_target_pairs={{0,448},{64,0},{128,64},{192,128},{256,192},{320,256},{384,320},{4... | collective-permute-start | bytes 1572872 | tf_op jit(solution)/shard_map/ppermute | solution.py:409
  39.5 38.2 %collective-permute-start.5 = (bf16[256,8,128]{2,1,0:T(8,128)(2,1)S(1)}, bf16[256,8,128]{2,1,0:T(8,128)(2,1)S(1)}, u32[]{:S(2)}, u32[]{:S(2)}) collective-permute-start(bf16[256,8,128]{2,1,0:T(8,128)(2,1)S(1)} %collective-permute-done.3.refs_6_), channel_id=1, source_target_pairs={{0,64},{64,128},{128,192},{192,256},{256,320},{320,384},{384,448},... | collective-permute-start | bytes 1572872 | tf_op jit(solution)/shard_map/ppermute | solution.py:409
  45.9 31.8 %collective-permute-start.4 = (bf16[256,8,128]{2,1,0:T(8,128)(2,1)}, bf16[256,8,128]{2,1,0:T(8,128)(2,1)}, u32[]{:S(2)}, u32[]{:S(2)}) collective-permute-start(bf16[256,8,128]{2,1,0:T(8,128)(2,1)} %broadcast_select_fusion), channel_id=1, source_target_pairs={{0,128},{64,448},{128,256},{192,64},{256,384},{320,192},{384,0},{4... | collective-permute-start | bytes 1572872 | tf_op jit(solution)/shard_map/ppermute | solution.py:452
  53.0 24.7 %collective-permute-start.2 = (bf16[256,8,128]{2,1,0:T(8,128)(2,1)S(1)}, bf16[256,8,128]{2,1,0:T(8,128)(2,1)}, u32[]{:S(2)}, u32[]{:S(2)}) collective-permute-start(bf16[256,8,128]{2,1,0:T(8,128)(2,1)S(1)} %collective-permute-done.1.refs_2_), channel_id=1, source_target_pairs={{0,448},{64,0},{128,64},{192,128},{256,192},{320,256},{384,320},{4... | collective-permute-start | bytes 1572872 | tf_op jit(solution)/shard_map/ppermute | solution.py:409
  82.9 34.1 %copy-start.2 = (bf16[40,2,16,256]{3,2,1,0:T(8,128)(2,1)S(1)}, bf16[40,2,16,256]{3,2,1,0:T(8,128)(2,1)}, u32[]{:S(2)}) copy-start(bf16[40,2,16,256]{3,2,1,0:T(8,128)(2,1)} %ops_hbm.1) | copy-start | bytes 1966084
  82.9 34.0 %all-to-all-start.3 = ((bf16[8,16,8,8,128]{4,3,2,1,0:T(8,128)(2,1)}), bf16[8,16,8,8,128]{4,3,2,1,0:T(8,128)(2,1)S(1)}, u32[]{:S(2)}, u32[]{:S(2)}) async-start(bf16[8,16,8,8,128]{4,3,2,1,0:T(8,128)(2,1)} %get-tuple-element.28), calls=%async_computation.3 | async-start | bytes 4194304 | tf_op jit(solution)/shard_map/all_to_all | solution.py:413
  86.6 58.1 %copy-start = (f32[2,128,256]{2,1,0:T(8,128)S(1)}, f32[2,128,256]{2,1,0:T(8,128)}, u32[]{:S(2)}) copy-start(f32[2,128,256]{2,1,0:T(8,128)} %constant.70.clone.sin_h.sin_t) | copy-start | bytes 786436
  86.6 58.1 %copy-start.1 = (f32[2,128,256]{2,1,0:T(8,128)S(1)}, f32[2,128,256]{2,1,0:T(8,128)}, u32[]{:S(2)}) copy-start(f32[2,128,256]{2,1,0:T(8,128)} %constant.69.clone.cos_h.cos_t) | copy-start | bytes 786436
  86.6 58.1 %copy-start.5 = (bf16[64,128]{1,0:T(8,128)(2,1)S(1)}, bf16[64,128]{1,0:T(8,128)(2,1)}, u32[]{:S(2)}) copy-start(bf16[64,128]{1,0:T(8,128)(2,1)} %constant.75.theta) | copy-start | bytes 49156
  86.7 49.1 %collective-permute-start.7 = (bf16[64,2,8,128]{3,2,1,0:T(8,128)(2,1)}, bf16[64,2,8,128]{3,2,1,0:T(8,128)(2,1)}, u32[]{:S(2)}, u32[]{:S(2)}) collective-permute-start(bf16[64,2,8,128]{3,2,1,0:T(8,128)(2,1)} %get-tuple-element.20), channel_id=1, source_target_pairs={{0,8},{8,16},{16,24},{24,32},{32,40},{40,48},{48,56},{56,0},{64,72... | collective-permute-start | bytes 786440 | tf_op jit(solution)/shard_map/ppermute | solution.py:409
  90.6 50.6 %collective-permute-start.8 = (bf16[64,2,8,128]{3,2,1,0:T(8,128)(2,1)}, bf16[64,2,8,128]{3,2,1,0:T(8,128)(2,1)}, u32[]{:S(2)}, u32[]{:S(2)}) collective-permute-start(bf16[64,2,8,128]{3,2,1,0:T(8,128)(2,1)} %get-tuple-element.21), channel_id=1, source_target_pairs={{0,16},{8,24},{16,32},{24,40},{32,48},{40,56},{48,0},{56,8},{64,80... | collective-permute-start | bytes 786440 | tf_op jit(solution)/shard_map/ppermute | solution.py:409
  116.9 42.2 %copy-start.3 = (bf16[64,2,8,128]{3,2,1,0:T(8,128)(2,1)S(1)}, bf16[64,2,8,128]{3,2,1,0:T(8,128)(2,1)}, u32[]{:S(2)}) copy-start(bf16[64,2,8,128]{3,2,1,0:T(8,128)(2,1)} %get-tuple-element.19.refs_0_) | copy-start | bytes 786436
  119.7 39.4 %copy-start.4 = (bf16[40,2,8,128]{3,2,1,0:T(8,128)(2,1)S(1)}, bf16[40,2,8,128]{3,2,1,0:T(8,128)(2,1)}, u32[]{:S(2)}) copy-start(bf16[40,2,8,128]{3,2,1,0:T(8,128)(2,1)} %refs_8_.1) | copy-start | bytes 491524
  119.7 25.0 %all-to-all-start.4 = ((bf16[16,8,8,128]{3,2,1,0:T(8,128)(2,1)}), bf16[16,8,8,128]{3,2,1,0:T(8,128)(2,1)S(1)}, u32[]{:S(2)}, u32[]{:S(2)}) async-start(bf16[16,8,8,128]{3,2,1,0:T(8,128)(2,1)} %far_parents.1), calls=%async_computation.4 | async-start | bytes 524288 | tf_op jit(solution)/shard_map/all_to_all | solution.py:413
  124.6 27.1 %collective-permute-start.9 = (bf16[64,2,8,128]{3,2,1,0:T(8,128)(2,1)}, bf16[64,2,8,128]{3,2,1,0:T(8,128)(2,1)S(1)}, u32[]{:S(2)}, u32[]{:S(2)}) collective-permute-start(bf16[64,2,8,128]{3,2,1,0:T(8,128)(2,1)} %get-tuple-element.22), channel_id=1, source_target_pairs={{0,24},{8,32},{16,40},{24,48},{32,56},{40,0},{48,8},{56,16},{64,88... | collective-permute-start | bytes 786440 | tf_op jit(solution)/shard_map/ppermute | solution.py:409
  126.6 25.2 %collective-permute-start.10 = (bf16[64,2,8,128]{3,2,1,0:T(8,128)(2,1)}, bf16[64,2,8,128]{3,2,1,0:T(8,128)(2,1)S(1)}, u32[]{:S(2)}, u32[]{:S(2)}) collective-permute-start(bf16[64,2,8,128]{3,2,1,0:T(8,128)(2,1)} %get-tuple-element.23), channel_id=1, source_target_pairs={{0,32},{8,40},{16,48},{24,56},{32,0},{40,8},{48,16},{56,24},{64,96... | collective-permute-start | bytes 786440 | tf_op jit(solution)/shard_map/ppermute | solution.py:409
  129.6 22.2 %collective-permute-start.11 = (bf16[64,2,8,128]{3,2,1,0:T(8,128)(2,1)}, bf16[64,2,8,128]{3,2,1,0:T(8,128)(2,1)S(1)}, u32[]{:S(2)}, u32[]{:S(2)}) collective-permute-start(bf16[64,2,8,128]{3,2,1,0:T(8,128)(2,1)} %get-tuple-element.24), channel_id=1, source_target_pairs={{0,40},{8,48},{16,56},{24,0},{32,8},{40,16},{48,24},{56,32},{64,10... | collective-permute-start | bytes 786440 | tf_op jit(solution)/shard_map/ppermute | solution.py:409
  135.8 20.4 %collective-permute-start.12 = (bf16[64,2,8,128]{3,2,1,0:T(8,128)(2,1)}, bf16[64,2,8,128]{3,2,1,0:T(8,128)(2,1)S(1)}, u32[]{:S(2)}, u32[]{:S(2)}) collective-permute-start(bf16[64,2,8,128]{3,2,1,0:T(8,128)(2,1)} %get-tuple-element.25), channel_id=1, source_target_pairs={{0,48},{8,56},{16,0},{24,8},{32,16},{40,24},{48,32},{56,40},{64,11... | collective-permute-start | bytes 786440 | tf_op jit(solution)/shard_map/ppermute | solution.py:409
  141.3 17.9 %collective-permute-start.13 = (bf16[64,2,8,128]{3,2,1,0:T(8,128)(2,1)}, bf16[64,2,8,128]{3,2,1,0:T(8,128)(2,1)S(1)}, u32[]{:S(2)}, u32[]{:S(2)}) collective-permute-start(bf16[64,2,8,128]{3,2,1,0:T(8,128)(2,1)} %get-tuple-element.26), channel_id=1, source_target_pairs={{0,56},{8,0},{16,8},{24,16},{32,24},{40,32},{48,40},{56,48},{64,12... | collective-permute-start | bytes 786440 | tf_op jit(solution)/shard_map/ppermute | solution.py:409
  147.0 16.4 %all-to-all-start.5 = ((bf16[8,8,2,8,128]{4,3,2,1,0:T(8,128)(2,1)}), bf16[8,8,2,8,128]{4,3,2,1,0:T(8,128)(2,1)S(1)}, u32[]{:S(2)}, u32[]{:S(2)}) async-start(bf16[8,8,2,8,128]{4,3,2,1,0:T(8,128)(2,1)} %lower.1), calls=%async_computation.5 | async-start | bytes 524288 | tf_op jit(solution)/shard_map/all_to_all | solution.py:413

commit v11 on v10

--- a/solution.py
+++ b/solution.py
@@ -15,6 +15,7 @@
 PP = 256
 WAVE_NUMBER = 6.0
 SIDE = 8
+ORDER = (4, 3, 5, 2, 6, 1, 7)
 BOTH = ("box", "angle")
 F32, BF16, I32 = jnp.float32, jnp.bfloat16, jnp.int32
 VM = pltpu.VMEM
@@ -191,7 +192,7 @@
     pool, parent_buf, child_buf, sems, parent_sems, child_sems = refs[17:]
     copies = [
         pltpu.make_async_copy(
-            b.at[pl.ds(128 * half, 128)], pool.at[half, i], sems.at[half, i]
+            b.at[pl.ds(128 * half, 128)], pool.at[half, pl.ds(128 * i, 128)], sems.at[half, i]
         )
         for half in (1, 0)
         for i, b in enumerate(blocks)
@@ -210,9 +211,8 @@
 
     def peer(h, carry):
         for k in range(16):
-            row = asked[h, 64 + k]
-            at = pl.multiple_of((row & 15) * 8, 8)
-            parent_buf[h, k] = pool[1, row >> 4, pl.ds(at, 8)]
+            at = pl.multiple_of(asked[h, 64 + k] * 8, 8)
+            parent_buf[h, k] = pool[1, pl.ds(at, 8)]
         parent_out(h).start()
         return carry
 
@@ -225,9 +225,8 @@
         def some(i, carry):
             for j in range(16):
                 k = i * 16 + j
-                row = asked[h, k]
-                at = pl.multiple_of((row & 63) * 2, 2)
-                child_buf[d, k] = pool[0, row >> 6, pl.ds(at, 2)]
+                at = pl.multiple_of(asked[h, k] * 2, 2)
+                child_buf[d, k] = pool[0, pl.ds(at, 2)]
             return carry
 
         lax.fori_loop(0, 4, some, 0)
@@ -246,7 +245,7 @@
         in_specs=[pl.BlockSpec(memory_space=pltpu.SMEM)] * 2 + [pl.BlockSpec(memory_space=ANY)] * 8,
         out_specs=(hbm,) * 9,
         scratch_shapes=[
-            pltpu.VMEM((2, 8, 128, 8, 128), BF16),
+            pltpu.VMEM((2, 8 * 128, 8, 128), BF16),
             pltpu.VMEM((SIDE, 16, 8, 8, 128), BF16),
             pltpu.VMEM((SIDE, 64, 2, 8, 128), BF16),
             pltpu.SemaphoreType.DMA((2, 8)),
@@ -303,10 +302,13 @@
 
 
 def child_far_body(code, *refs):
-    blocks, ops_hbm, out, recv, ops, sems = refs[:8], *refs[8:]
-    copies = fetch((ops_hbm, *blocks), (ops.at[pl.ds(0, 40)], *(recv.at[i] for i in range(8))), sems)
-    ops[40] = jnp.zeros(ops.shape[1:], BF16)
-    for copy in copies:
+    blocks, ops_hbm, out, recv, ops, wide, sems = refs[:8], *refs[8:]
+    copies = fetch((ops_hbm, *blocks), (ops, *(recv.at[pl.ds(64 * i, 64)] for i in range(8))), sems)
+    copies[0].wait()
+    for i in range(40):
+        wide[i] = ops[i].astype(F32)
+    wide[40] = jnp.zeros(wide.shape[1:], F32)
+    for copy in copies[1:]:
         copy.wait()
 
     def row(r, carry):
@@ -314,9 +316,9 @@
         imag = jnp.zeros((8, 128), F32)
         for j in range(8):
             both = code[j, r]
-            lane, at, op = both >> 12, (both >> 6) & 63, both & 63
-            a, b = ops[op, 0].astype(F32), ops[op, 1].astype(F32)
-            c, d = recv[lane, at, 0].astype(F32), recv[lane, at, 1].astype(F32)
+            at, op = both >> 6, both & 63
+            a, b = wide[op, 0], wide[op, 1]
+            c, d = recv[at, 0].astype(F32), recv[at, 1].astype(F32)
             real = real + (a * c - b * d)
             imag = imag + (a * d + b * c)
         out[r, 0] = real
@@ -333,8 +335,9 @@
         in_specs=[pl.BlockSpec(memory_space=pltpu.SMEM)] + [pl.BlockSpec(memory_space=ANY)] * 9,
         out_specs=pl.BlockSpec(memory_space=VM),
         scratch_shapes=[
-            pltpu.VMEM((SIDE, 64, 2, 8, 128), BF16),
-            pltpu.VMEM((41, 2, 8, 128), BF16),
+            pltpu.VMEM((SIDE * 64, 2, 8, 128), BF16),
+            pltpu.VMEM((40, 2, 8, 128), BF16),
+            pltpu.VMEM((41, 2, 8, 128), F32),
             pltpu.SemaphoreType.DMA((9,)),
         ],
         compiler_params=pltpu.CompilerParams(vmem_limit_bytes=GRANT),
@@ -456,7 +459,7 @@
     parents_out, *children_out = select(where, asked, blocks)
     parents_in = swap(parents_out, BOTH, axis_index_groups=TRADE)
     children_in = {0: children_out[0]}
-    for d in (4, 3, 5, 2, 6, 1, 7):
+    for d in ORDER:
         children_in[d] = hop(children_out[d], d, TRADE)
     sums = far_parents(hold(parent_code), parents_in.reshape(128, 8, 8, 128), parent_ops)
     turned = swap(sums, "angle").reshape(8, 2, 8, 8, 128)

time: 165 us -> 164 us (level)
  no operation moved by 1% of the time
where the time goes in v11:
time: 164 us; the launch traced here: 163 us
  starting transfers between devices  72.8 us (44%)
  blocking collectives  39 us (24%)
  waiting for transfers between devices  29.4 us (18%)
  Pallas kernels  19.3 us (12%)
  other arithmetic  1.77 us (1%)
    ppermute x13, starting transfers between devices, hop(): return lax.ppermute(x, BOTH, pairs)  52.3 us
    all_to_all x3, blocking collectives, swap(): lax.all_to_all(x, axis, split_axis=0, concat_axis=0, tiled=True, **kw)  39 us
    all_to_all x3, waiting for transfers between devices, swap(): lax.all_to_all(x, axis, split_axis=0, concat_axis=0, tiled=True, **kw)  22 us
    all_to_all x3, starting transfers between devices, swap(): lax.all_to_all(x, axis, split_axis=0, concat_axis=0, tiled=True, **kw)  13.5 us
    ppermute x13, waiting for transfers between devices, hop(): return lax.ppermute(x, BOTH, pairs)  7.33 us
    ppermute x1, starting transfers between devices, local(): up4 = lax.ppermute(onward, BOTH, pairs)  7.03 us
    pallas_call x1, Pallas kernels, plan(): pl.pallas_call(plan_body, out_shape=(jax.ShapeDtypeStruct((SIDE, 128), I3...  4.66 us
    pallas_call x1, Pallas kernels, select(): pl.pallas_call(select_body, out_shape=(pltpu.HBM((SIDE, 16, 8, 8, 128), B...  4.27 us
  transfers between devices with their start and end apart: 17, of which 3 were waited for; matrix products, arithmetic and copies ran while one was open for 1% of the time, Pallas kernels for 8%

profile of v11, /device:TPU:10, one launch (start us, length us, event | category | flops | bytes accessed | tf_op | source)
XLA Modules:
  0.0 162.6 jit_solution(17325472243742931124)
XLA Ops:
  0.0 0.0 copy-start.6
  0.0 11.0 %all_to_all.30 = bf16[64,2,8,128]{3,2,1,0:T(8,128)(2,1)S(1)} all-to-all(bf16[64,2,8,128]{3,2,1,0:T(8,128)(2,1)} %param.15), channel_id=1, replica_groups=mesh['box'=64,'angle'=8] {'angle'}, dimensions={0} | all-to-all | bytes 524288 | tf_op jit(solution)/shard_map/all_to_all | solution.py:416
  11.0 1.8 %lift.1 = bf16[8,2,8,8,128]{4,3,2,1,0:T(8,128)(2,1)S(1)} custom-call(bf16[8,8,2,8,128]{4,3,2,1,0:T(8,128)(2,1)S(1)} %bitcast.23, bf16[128,64]{1,0:T(8,128)(2,1)} %constant.73.theta_h, bf16[128,256]{1,0:T(8,128)(2,1)} %constant.74.phi_h, f32[2,128,256]{2,1,0:T(8,128)} %constant.69.clone.cos_h.cos_t, f32[2,128,256]{2,1,0:T(8,128)} %constant.70.clone.sin_h.sin_t), custom_call_target="tpu_custom_call" | custom-call | tf_op jit(solution)/shard_map/lift/pallas_call | solution.py:178
  12.8 9.9 %all_to_all.31 = bf16[8,2,8,8,128]{4,3,2,1,0:T(8,128)(2,1)S(1)} all-to-all(bf16[8,2,8,8,128]{4,3,2,1,0:T(8,128)(2,1)S(1)} %lift.1), channel_id=1, replica_groups=mesh['box'=64,'angle'=8] {'angle'}, dimensions={0} | all-to-all | bytes 524288 | tf_op jit(solution)/shard_map/all_to_all | solution.py:416
  22.7 0.0 copy-done.6
  22.8 4.5 %collective-permute-start.3 = (bf16[256,8,128]{2,1,0:T(8,128)(2,1)S(1)}, bf16[256,8,128]{2,1,0:T(8,128)(2,1)S(1)}, u32[]{:S(2)}, u32[]{:S(2)}) collective-permute-start(bf16[256,8,128]{2,1,0:T(8,128)(2,1)S(1)} %pad_maximum_fusion.refs_0_), channel_id=1, source_target_pairs={{0,128},{64,192},{128,256},{192,320},{256,384},{320,448},{384,0},{... | collective-permute-start | bytes 1572872 | tf_op jit(solution)/shard_map/ppermute | solution.py:412
  27.3 3.5 %collective-permute-start.1 = (bf16[256,8,128]{2,1,0:T(8,128)(2,1)S(1)}, bf16[256,8,128]{2,1,0:T(8,128)(2,1)S(1)}, u32[]{:S(2)}, u32[]{:S(2)}) collective-permute-start(bf16[256,8,128]{2,1,0:T(8,128)(2,1)S(1)} %pad_maximum_fusion.refs_0_), channel_id=1, source_target_pairs={{0,384},{64,448},{128,0},{192,64},{256,128},{320,192},{384,256},{4... | collective-permute-start | bytes 1572872 | tf_op jit(solution)/shard_map/ppermute | solution.py:412
  30.8 4.1 %collective-permute-start.6 = (bf16[256,8,128]{2,1,0:T(8,128)(2,1)S(1)}, bf16[256,8,128]{2,1,0:T(8,128)(2,1)S(1)}, u32[]{:S(2)}, u32[]{:S(2)}) collective-permute-start(bf16[256,8,128]{2,1,0:T(8,128)(2,1)S(1)} %pad_maximum_fusion.refs_0_), channel_id=1, source_target_pairs={{0,64},{64,128},{128,192},{192,256},{256,320},{320,384},{384,448},... | collective-permute-start | bytes 1572872 | tf_op jit(solution)/shard_map/ppermute | solution.py:412
  34.9 4.6 %collective-permute-start = (bf16[256,8,128]{2,1,0:T(8,128)(2,1)S(1)}, bf16[256,8,128]{2,1,0:T(8,128)(2,1)S(1)}, u32[]{:S(2)}, u32[]{:S(2)}) collective-permute-start(bf16[256,8,128]{2,1,0:T(8,128)(2,1)S(1)} %pad_maximum_fusion.refs_0_), channel_id=1, source_target_pairs={{0,448},{64,0},{128,64},{192,128},{256,192},{320,256},{384,320},{4... | collective-permute-start | bytes 1572872 | tf_op jit(solution)/shard_map/ppermute | solution.py:412
  39.4 0.0 collective-permute-done.3.refs_6_
  39.5 5.6 %collective-permute-start.5 = (bf16[256,8,128]{2,1,0:T(8,128)(2,1)S(1)}, bf16[256,8,128]{2,1,0:T(8,128)(2,1)S(1)}, u32[]{:S(2)}, u32[]{:S(2)}) collective-permute-start(bf16[256,8,128]{2,1,0:T(8,128)(2,1)S(1)} %collective-permute-done.3.refs_6_), channel_id=1, source_target_pairs={{0,64},{64,128},{128,192},{192,256},{256,320},{320,384},{384,448},... | collective-permute-start | bytes 1572872 | tf_op jit(solution)/shard_map/ppermute | solution.py:412
  45.0 0.0 collective-permute-done.1.refs_2_
  45.0 0.9 broadcast_select_fusion
  45.9 7.0 %collective-permute-start.4 = (bf16[256,8,128]{2,1,0:T(8,128)(2,1)}, bf16[256,8,128]{2,1,0:T(8,128)(2,1)}, u32[]{:S(2)}, u32[]{:S(2)}) collective-permute-start(bf16[256,8,128]{2,1,0:T(8,128)(2,1)} %broadcast_select_fusion), channel_id=1, source_target_pairs={{0,128},{64,448},{128,256},{192,64},{256,384},{320,192},{384,0},{4... | collective-permute-start | bytes 1572872 | tf_op jit(solution)/shard_map/ppermute | solution.py:455
  53.0 1.9 %collective-permute-start.2 = (bf16[256,8,128]{2,1,0:T(8,128)(2,1)S(1)}, bf16[256,8,128]{2,1,0:T(8,128)(2,1)}, u32[]{:S(2)}, u32[]{:S(2)}) collective-permute-start(bf16[256,8,128]{2,1,0:T(8,128)(2,1)S(1)} %collective-permute-done.1.refs_2_), channel_id=1, source_target_pairs={{0,448},{64,0},{128,64},{192,128},{256,192},{320,256},{384,320},{4... | collective-permute-start | bytes 1572872 | tf_op jit(solution)/shard_map/ppermute | solution.py:412
  54.9 0.1 pad_add_fusion.where
  55.0 4.7 %plan.1 = (s32[8,128]{1,0:T(8,128)S(1)}, s32[8,64]{1,0:T(8,128)}, s32[8,16]{1,0:T(8,128)}) custom-call(s32[3]{0:T(128)S(1)} %pad_add_fusion.where, s32[8,64]{1,0:T(8,128)} %bitcast.29, s32[8,64]{1,0:T(8,128)} %bitcast.30, s32[32,128]{1,0:T(8,128)} %bitcast.28, s32[8,16]{1,0:T(8,128)} %bitcast.31, s32[8,16]{1,0:T(8,128)} %bitcast.32, s32[8,128]{1,0:T(8,128)} %bitcast.33), custom_call_target="tpu_custom_call" | custom-call | tf_op jit(solution)/shard_map/plan/pallas_call | solution.py:121
  59.6 18.0 %all_to_all.32 = s32[8,1,128]{2,1,0:T(1,128)S(1)} all-to-all(s32[8,1,128]{2,1,0:T(1,128)S(1)} %bitcast.25), channel_id=1, replica_groups={{0,8,16,24,32,40,48,56},{64,72,80,88,96,104,112,120},{128,136,144,152,1..., dimensions={0} | all-to-all | bytes 8192 | tf_op jit(solution)/shard_map/all_to_all | solution.py:416
  77.7 0.0 collective-permute-done.6.refs_7_
  77.7 0.0 collective-permute-done.refs_1_
  77.7 0.0 collective-permute-done.5.refs_5_
  77.7 0.0 collective-permute-done.4.refs_4_
  77.7 0.0 collective-permute-done.2.refs_3_
  77.7 4.3 %select.11 = (bf16[8,16,8,8,128]{4,3,2,1,0:T(8,128)(2,1)}, bf16[64,2,8,128]{3,2,1,0:T(8,128)(2,1)}, bf16[64,2,8,128]{3,2,1,0:T(8,128)(2,1)}, bf16[64,2,8,128]{3,...) custom-call(s32[3]{0:T(128)S(1)} %pad_add_fusion.where, ...), custom_call_target="tpu_custom_call" | custom-call | tf_op jit(solution)/shard_map/select/pallas_call | solution.py:242
  82.0 0.0 copy-start.2
  82.0 3.7 %all-to-all-start.3 = ((bf16[8,16,8,8,128]{4,3,2,1,0:T(8,128)(2,1)}), bf16[8,16,8,8,128]{4,3,2,1,0:T(8,128)(2,1)S(1)}, u32[]{:S(2)}, u32[]{:S(2)}) async-start(bf16[8,16,8,8,128]{4,3,2,1,0:T(8,128)(2,1)} %get-tuple-element.28), calls=%async_computation.3 | async-start | bytes 4194304 | tf_op jit(solution)/shard_map/all_to_all | solution.py:416
  85.8 0.0 copy-start
  85.8 0.0 copy-start.1
  85.8 0.0 copy-start.5
  85.8 3.9 %collective-permute-start.7 = (bf16[64,2,8,128]{3,2,1,0:T(8,128)(2,1)}, bf16[64,2,8,128]{3,2,1,0:T(8,128)(2,1)}, u32[]{:S(2)}, u32[]{:S(2)}) collective-permute-start(bf16[64,2,8,128]{3,2,1,0:T(8,128)(2,1)} %get-tuple-element.20), channel_id=1, source_target_pairs={{0,8},{8,16},{16,24},{24,32},{32,40},{40,48},{48,56},{56,0},{64,72... | collective-permute-start | bytes 786440 | tf_op jit(solution)/shard_map/ppermute | solution.py:412
  89.7 4.3 %collective-permute-start.8 = (bf16[64,2,8,128]{3,2,1,0:T(8,128)(2,1)}, bf16[64,2,8,128]{3,2,1,0:T(8,128)(2,1)}, u32[]{:S(2)}, u32[]{:S(2)}) collective-permute-start(bf16[64,2,8,128]{3,2,1,0:T(8,128)(2,1)} %get-tuple-element.21), channel_id=1, source_target_pairs={{0,16},{8,24},{16,32},{24,40},{32,48},{40,56},{48,0},{56,8},{64,80... | collective-permute-start | bytes 786440 | tf_op jit(solution)/shard_map/ppermute | solution.py:412
  94.0 22.0 %all-to-all-done.3 = bf16[8,16,8,8,128]{4,3,2,1,0:T(8,128)(2,1)S(1)} async-done(((bf16[8,16,8,8,128]{4,3,2,1,0:T(8,128)(2,1)}), bf16[8,16,8,8,128]{4,3,2,1,0:T(8,128)(2,1)S(1)}, u32[]{:S(2)}, u32[]{:S(2)}) %all-to-all-start.3) | async-done | bytes 2097184 | tf_op jit(solution)/shard_map/all_to_all | solution.py:416
  116.0 0.0 copy-done.2
  116.1 0.0 copy-start.3
  116.1 2.8 %far_parents.1 = bf16[16,8,8,128]{3,2,1,0:T(8,128)(2,1)} custom-call(s32[8,16]{1,0:T(8,128)} %get-tuple-element.27.code, bf16[128,8,8,128]{3,2,1,0:T(8,128)(2,1)S(1)} %bitcast.21, bf16[40,2,16,256]{3,2,1,0:T(8,128)(2,1)S(1)} %copy-done.2), custom_call_target="tpu_custom_call" | custom-call | tf_op jit(solution)/shard_map/far_parents/pallas_call | solution.py:289
  118.8 0.0 copy-start.4
  118.9 4.9 %all-to-all-start.4 = ((bf16[16,8,8,128]{3,2,1,0:T(8,128)(2,1)}), bf16[16,8,8,128]{3,2,1,0:T(8,128)(2,1)S(1)}, u32[]{:S(2)}, u32[]{:S(2)}) async-start(bf16[16,8,8,128]{3,2,1,0:T(8,128)(2,1)} %far_parents.1), calls=%async_computation.4 | async-start | bytes 524288 | tf_op jit(solution)/shard_map/all_to_all | solution.py:416
  123.8 1.9 %collective-permute-start.9 = (bf16[64,2,8,128]{3,2,1,0:T(8,128)(2,1)}, bf16[64,2,8,128]{3,2,1,0:T(8,128)(2,1)S(1)}, u32[]{:S(2)}, u32[]{:S(2)}) collective-permute-start(bf16[64,2,8,128]{3,2,1,0:T(8,128)(2,1)} %get-tuple-element.22), channel_id=1, source_target_pairs={{0,24},{8,32},{16,40},{24,48},{32,56},{40,0},{48,8},{56,16},{64,88... | collective-permute-start | bytes 786440 | tf_op jit(solution)/shard_map/ppermute | solution.py:412
  125.7 3.0 %collective-permute-start.10 = (bf16[64,2,8,128]{3,2,1,0:T(8,128)(2,1)}, bf16[64,2,8,128]{3,2,1,0:T(8,128)(2,1)S(1)}, u32[]{:S(2)}, u32[]{:S(2)}) collective-permute-start(bf16[64,2,8,128]{3,2,1,0:T(8,128)(2,1)} %get-tuple-element.23), channel_id=1, source_target_pairs={{0,32},{8,40},{16,48},{24,56},{32,0},{40,8},{48,16},{56,24},{64,96... | collective-permute-start | bytes 786440 | tf_op jit(solution)/shard_map/ppermute | solution.py:412
  128.7 6.2 %collective-permute-start.11 = (bf16[64,2,8,128]{3,2,1,0:T(8,128)(2,1)}, bf16[64,2,8,128]{3,2,1,0:T(8,128)(2,1)S(1)}, u32[]{:S(2)}, u32[]{:S(2)}) collective-permute-start(bf16[64,2,8,128]{3,2,1,0:T(8,128)(2,1)} %get-tuple-element.24), channel_id=1, source_target_pairs={{0,40},{8,48},{16,56},{24,0},{32,8},{40,16},{48,24},{56,32},{64,10... | collective-permute-start | bytes 786440 | tf_op jit(solution)/shard_map/ppermute | solution.py:412
  134.9 0.0 collective-permute-done.7.refs_1_
  134.9 5.4 %collective-permute-start.12 = (bf16[64,2,8,128]{3,2,1,0:T(8,128)(2,1)}, bf16[64,2,8,128]{3,2,1,0:T(8,128)(2,1)S(1)}, u32[]{:S(2)}, u32[]{:S(2)}) collective-permute-start(bf16[64,2,8,128]{3,2,1,0:T(8,128)(2,1)} %get-tuple-element.25), channel_id=1, source_target_pairs={{0,48},{8,56},{16,0},{24,8},{32,16},{40,24},{48,32},{56,40},{64,11... | collective-permute-start | bytes 786440 | tf_op jit(solution)/shard_map/ppermute | solution.py:412
  140.4 0.0 collective-permute-done.8.refs_2_
  140.4 3.4 %collective-permute-start.13 = (bf16[64,2,8,128]{3,2,1,0:T(8,128)(2,1)}, bf16[64,2,8,128]{3,2,1,0:T(8,128)(2,1)S(1)}, u32[]{:S(2)}, u32[]{:S(2)}) collective-permute-start(bf16[64,2,8,128]{3,2,1,0:T(8,128)(2,1)} %get-tuple-element.26), channel_id=1, source_target_pairs={{0,56},{8,0},{16,8},{24,16},{32,24},{40,32},{48,40},{56,48},{64,12... | collective-permute-start | bytes 786440 | tf_op jit(solution)/shard_map/ppermute | solution.py:412
  143.8 0.0 all-to-all-done.4
  143.8 0.0 copy-done
  143.8 0.0 copy-done.1
  143.8 0.0 copy-done.5
  143.8 2.2 %lower.1 = bf16[8,8,2,8,128]{4,3,2,1,0:T(8,128)(2,1)} custom-call(bf16[8,2,8,8,128]{4,3,2,1,0:T(8,128)(2,1)S(1)} %bitcast.22, bf16[64,128]{1,0:T(8,128)(2,1)S(1)} %copy-done.5, bf16[256,128]{1,0:T(8,128)(2,1)} %constant.76.phi_h, f32[2,128,256]{2,1,0:T(8,128)S(1)} %copy-done.1, f32[2,128,256]{2,1,0:T(8,128)S(1)} %copy-done), custom_call_target="tpu_custom_call" | custom-call | tf_op jit(solution)/shard_map/lower/pallas_call | solution.py:382
  146.1 4.8 %all-to-all-start.5 = ((bf16[8,8,2,8,128]{4,3,2,1,0:T(8,128)(2,1)}), bf16[8,8,2,8,128]{4,3,2,1,0:T(8,128)(2,1)S(1)}, u32[]{:S(2)}, u32[]{:S(2)}) async-start(bf16[8,8,2,8,128]{4,3,2,1,0:T(8,128)(2,1)} %lower.1), calls=%async_computation.5 | async-start | bytes 524288 | tf_op jit(solution)/shard_map/all_to_all | solution.py:416
  150.9 0.0 collective-permute-done.9.refs_3_
  150.9 0.0 collective-permute-done.10.refs_4_
  150.9 0.0 collective-permute-done.11.refs_5_
  150.9 4.4 %collective-permute-done.12.refs_6_ = bf16[64,2,8,128]{3,2,1,0:T(8,128)(2,1)S(1)} collective-permute-done((bf16[64,2,8,128]{3,2,1,0:T(8,128)(2,1)}, bf16[64,2,8,128]{3,2,1,0:T(8,128)(2,1)S(1)}, u32[]{:S(2)}, u32[]{:S(2)}) %collective-permute-start.12) | collective-permute-done | bytes 262176 | tf_op jit(solution)/shard_map/ppermute | solution.py:412
  155.3 2.9 %collective-permute-done.13.refs_7_ = bf16[64,2,8,128]{3,2,1,0:T(8,128)(2,1)S(1)} collective-permute-done((bf16[64,2,8,128]{3,2,1,0:T(8,128)(2,1)}, bf16[64,2,8,128]{3,2,1,0:T(8,128)(2,1)S(1)}, u32[]{:S(2)}, u32[]{:S(2)}) %collective-permute-start.13) | collective-permute-done | bytes 262176 | tf_op jit(solution)/shard_map/ppermute | solution.py:412
  158.2 0.0 copy-done.3
  158.2 0.0 copy-done.4
  158.2 3.6 %far_children.1 = f32[64,2,8,128]{3,2,1,0:T(8,128)S(1)} custom-call(s32[8,64]{1,0:T(8,128)} %get-tuple-element.17.code, bf16[64,2,8,128]{3,2,1,0:T(8,128)(2,1)S(1)} %copy-done.3, bf16[64,2,8,128]{3,2,1,0:T(8,128)(2,1)} %collective-permute-done.7.refs_1_, bf16[64,2,8,128]{3,2,1,0:T(8,128)(2,1)} %collective-permute-done.8.refs_2_, ...), custom_call_target="tpu_custom_call" | custom-call | tf_op jit(solution)/shard_map/far_children/pallas_call | solution.py:332
  161.8 0.0 all-to-all-done.5
  161.9 0.8 fusion
  (1 shorter events, 0.0 us)
Async XLA Ops:
  0.0 22.7 %copy-start.6 = (bf16[64,2,8,128]{3,2,1,0:T(8,128)(2,1)S(1)}, bf16[64,2,8,128]{3,2,1,0:T(8,128)(2,1)}, u32[]{:S(2)}) copy-start(bf16[64,2,8,128]{3,2,1,0:T(8,128)(2,1)} %param.15) | copy-start | bytes 786436
  22.8 16.7 %collective-permute-start.3 = (bf16[256,8,128]{2,1,0:T(8,128)(2,1)S(1)}, bf16[256,8,128]{2,1,0:T(8,128)(2,1)S(1)}, u32[]{:S(2)}, u32[]{:S(2)}) collective-permute-start(bf16[256,8,128]{2,1,0:T(8,128)(2,1)S(1)} %pad_maximum_fusion.refs_0_), channel_id=1, source_target_pairs={{0,128},{64,192},{128,256},{192,320},{256,384},{320,448},{384,0},{... | collective-permute-start | bytes 1572872 | tf_op jit(solution)/shard_map/ppermute | solution.py:412
  27.3 17.8 %collective-permute-start.1 = (bf16[256,8,128]{2,1,0:T(8,128)(2,1)S(1)}, bf16[256,8,128]{2,1,0:T(8,128)(2,1)S(1)}, u32[]{:S(2)}, u32[]{:S(2)}) collective-permute-start(bf16[256,8,128]{2,1,0:T(8,128)(2,1)S(1)} %pad_maximum_fusion.refs_0_), channel_id=1, source_target_pairs={{0,384},{64,448},{128,0},{192,64},{256,128},{320,192},{384,256},{4... | collective-permute-start | bytes 1572872 | tf_op jit(solution)/shard_map/ppermute | solution.py:412
  30.8 46.9 %collective-permute-start.6 = (bf16[256,8,128]{2,1,0:T(8,128)(2,1)S(1)}, bf16[256,8,128]{2,1,0:T(8,128)(2,1)S(1)}, u32[]{:S(2)}, u32[]{:S(2)}) collective-permute-start(bf16[256,8,128]{2,1,0:T(8,128)(2,1)S(1)} %pad_maximum_fusion.refs_0_), channel_id=1, source_target_pairs={{0,64},{64,128},{128,192},{192,256},{256,320},{320,384},{384,448},... | collective-permute-start | bytes 1572872 | tf_op jit(solution)/shard_map/ppermute | solution.py:412
  34.9 42.8 %collective-permute-start = (bf16[256,8,128]{2,1,0:T(8,128)(2,1)S(1)}, bf16[256,8,128]{2,1,0:T(8,128)(2,1)S(1)}, u32[]{:S(2)}, u32[]{:S(2)}) collective-permute-start(bf16[256,8,128]{2,1,0:T(8,128)(2,1)S(1)} %pad_maximum_fusion.refs_0_), channel_id=1, source_target_pairs={{0,448},{64,0},{128,64},{192,128},{256,192},{320,256},{384,320},{4... | collective-permute-start | bytes 1572872 | tf_op jit(solution)/shard_map/ppermute | solution.py:412
  39.5 38.2 %collective-permute-start.5 = (bf16[256,8,128]{2,1,0:T(8,128)(2,1)S(1)}, bf16[256,8,128]{2,1,0:T(8,128)(2,1)S(1)}, u32[]{:S(2)}, u32[]{:S(2)}) collective-permute-start(bf16[256,8,128]{2,1,0:T(8,128)(2,1)S(1)} %collective-permute-done.3.refs_6_), channel_id=1, source_target_pairs={{0,64},{64,128},{128,192},{192,256},{256,320},{320,384},{384,448},... | collective-permute-start | bytes 1572872 | tf_op jit(solution)/shard_map/ppermute | solution.py:412
  45.9 31.8 %collective-permute-start.4 = (bf16[256,8,128]{2,1,0:T(8,128)(2,1)}, bf16[256,8,128]{2,1,0:T(8,128)(2,1)}, u32[]{:S(2)}, u32[]{:S(2)}) collective-permute-start(bf16[256,8,128]{2,1,0:T(8,128)(2,1)} %broadcast_select_fusion), channel_id=1, source_target_pairs={{0,128},{64,448},{128,256},{192,64},{256,384},{320,192},{384,0},{4... | collective-permute-start | bytes 1572872 | tf_op jit(solution)/shard_map/ppermute | solution.py:455
  53.0 24.7 %collective-permute-start.2 = (bf16[256,8,128]{2,1,0:T(8,128)(2,1)S(1)}, bf16[256,8,128]{2,1,0:T(8,128)(2,1)}, u32[]{:S(2)}, u32[]{:S(2)}) collective-permute-start(bf16[256,8,128]{2,1,0:T(8,128)(2,1)S(1)} %collective-permute-done.1.refs_2_), channel_id=1, source_target_pairs={{0,448},{64,0},{128,64},{192,128},{256,192},{320,256},{384,320},{4... | collective-permute-start | bytes 1572872 | tf_op jit(solution)/shard_map/ppermute | solution.py:412
  82.0 34.1 %copy-start.2 = (bf16[40,2,16,256]{3,2,1,0:T(8,128)(2,1)S(1)}, bf16[40,2,16,256]{3,2,1,0:T(8,128)(2,1)}, u32[]{:S(2)}) copy-start(bf16[40,2,16,256]{3,2,1,0:T(8,128)(2,1)} %ops_hbm.1) | copy-start | bytes 1966084
  82.0 34.0 %all-to-all-start.3 = ((bf16[8,16,8,8,128]{4,3,2,1,0:T(8,128)(2,1)}), bf16[8,16,8,8,128]{4,3,2,1,0:T(8,128)(2,1)S(1)}, u32[]{:S(2)}, u32[]{:S(2)}) async-start(bf16[8,16,8,8,128]{4,3,2,1,0:T(8,128)(2,1)} %get-tuple-element.28), calls=%async_computation.3 | async-start | bytes 4194304 | tf_op jit(solution)/shard_map/all_to_all | solution.py:416
  85.8 58.1 %copy-start = (f32[2,128,256]{2,1,0:T(8,128)S(1)}, f32[2,128,256]{2,1,0:T(8,128)}, u32[]{:S(2)}) copy-start(f32[2,128,256]{2,1,0:T(8,128)} %constant.70.clone.sin_h.sin_t) | copy-start | bytes 786436
  85.8 58.1 %copy-start.1 = (f32[2,128,256]{2,1,0:T(8,128)S(1)}, f32[2,128,256]{2,1,0:T(8,128)}, u32[]{:S(2)}) copy-start(f32[2,128,256]{2,1,0:T(8,128)} %constant.69.clone.cos_h.cos_t) | copy-start | bytes 786436
  85.8 58.1 %copy-start.5 = (bf16[64,128]{1,0:T(8,128)(2,1)S(1)}, bf16[64,128]{1,0:T(8,128)(2,1)}, u32[]{:S(2)}) copy-start(bf16[64,128]{1,0:T(8,128)(2,1)} %constant.75.theta) | copy-start | bytes 49156
  85.8 49.1 %collective-permute-start.7 = (bf16[64,2,8,128]{3,2,1,0:T(8,128)(2,1)}, bf16[64,2,8,128]{3,2,1,0:T(8,128)(2,1)}, u32[]{:S(2)}, u32[]{:S(2)}) collective-permute-start(bf16[64,2,8,128]{3,2,1,0:T(8,128)(2,1)} %get-tuple-element.20), channel_id=1, source_target_pairs={{0,8},{8,16},{16,24},{24,32},{32,40},{40,48},{48,56},{56,0},{64,72... | collective-permute-start | bytes 786440 | tf_op jit(solution)/shard_map/ppermute | solution.py:412
  89.7 50.6 %collective-permute-start.8 = (bf16[64,2,8,128]{3,2,1,0:T(8,128)(2,1)}, bf16[64,2,8,128]{3,2,1,0:T(8,128)(2,1)}, u32[]{:S(2)}, u32[]{:S(2)}) collective-permute-start(bf16[64,2,8,128]{3,2,1,0:T(8,128)(2,1)} %get-tuple-element.21), channel_id=1, source_target_pairs={{0,16},{8,24},{16,32},{24,40},{32,48},{40,56},{48,0},{56,8},{64,80... | collective-permute-start | bytes 786440 | tf_op jit(solution)/shard_map/ppermute | solution.py:412
  116.1 42.2 %copy-start.3 = (bf16[64,2,8,128]{3,2,1,0:T(8,128)(2,1)S(1)}, bf16[64,2,8,128]{3,2,1,0:T(8,128)(2,1)}, u32[]{:S(2)}) copy-start(bf16[64,2,8,128]{3,2,1,0:T(8,128)(2,1)} %get-tuple-element.19.refs_0_) | copy-start | bytes 786436
  118.8 39.4 %copy-start.4 = (bf16[40,2,8,128]{3,2,1,0:T(8,128)(2,1)S(1)}, bf16[40,2,8,128]{3,2,1,0:T(8,128)(2,1)}, u32[]{:S(2)}) copy-start(bf16[40,2,8,128]{3,2,1,0:T(8,128)(2,1)} %refs_8_.1) | copy-start | bytes 491524
  118.9 25.0 %all-to-all-start.4 = ((bf16[16,8,8,128]{3,2,1,0:T(8,128)(2,1)}), bf16[16,8,8,128]{3,2,1,0:T(8,128)(2,1)S(1)}, u32[]{:S(2)}, u32[]{:S(2)}) async-start(bf16[16,8,8,128]{3,2,1,0:T(8,128)(2,1)} %far_parents.1), calls=%async_computation.4 | async-start | bytes 524288 | tf_op jit(solution)/shard_map/all_to_all | solution.py:416
  123.8 27.1 %collective-permute-start.9 = (bf16[64,2,8,128]{3,2,1,0:T(8,128)(2,1)}, bf16[64,2,8,128]{3,2,1,0:T(8,128)(2,1)S(1)}, u32[]{:S(2)}, u32[]{:S(2)}) collective-permute-start(bf16[64,2,8,128]{3,2,1,0:T(8,128)(2,1)} %get-tuple-element.22), channel_id=1, source_target_pairs={{0,24},{8,32},{16,40},{24,48},{32,56},{40,0},{48,8},{56,16},{64,88... | collective-permute-start | bytes 786440 | tf_op jit(solution)/shard_map/ppermute | solution.py:412
  125.7 25.2 %collective-permute-start.10 = (bf16[64,2,8,128]{3,2,1,0:T(8,128)(2,1)}, bf16[64,2,8,128]{3,2,1,0:T(8,128)(2,1)S(1)}, u32[]{:S(2)}, u32[]{:S(2)}) collective-permute-start(bf16[64,2,8,128]{3,2,1,0:T(8,128)(2,1)} %get-tuple-element.23), channel_id=1, source_target_pairs={{0,32},{8,40},{16,48},{24,56},{32,0},{40,8},{48,16},{56,24},{64,96... | collective-permute-start | bytes 786440 | tf_op jit(solution)/shard_map/ppermute | solution.py:412
  128.7 22.2 %collective-permute-start.11 = (bf16[64,2,8,128]{3,2,1,0:T(8,128)(2,1)}, bf16[64,2,8,128]{3,2,1,0:T(8,128)(2,1)S(1)}, u32[]{:S(2)}, u32[]{:S(2)}) collective-permute-start(bf16[64,2,8,128]{3,2,1,0:T(8,128)(2,1)} %get-tuple-element.24), channel_id=1, source_target_pairs={{0,40},{8,48},{16,56},{24,0},{32,8},{40,16},{48,24},{56,32},{64,10... | collective-permute-start | bytes 786440 | tf_op jit(solution)/shard_map/ppermute | solution.py:412
  134.9 20.4 %collective-permute-start.12 = (bf16[64,2,8,128]{3,2,1,0:T(8,128)(2,1)}, bf16[64,2,8,128]{3,2,1,0:T(8,128)(2,1)S(1)}, u32[]{:S(2)}, u32[]{:S(2)}) collective-permute-start(bf16[64,2,8,128]{3,2,1,0:T(8,128)(2,1)} %get-tuple-element.25), channel_id=1, source_target_pairs={{0,48},{8,56},{16,0},{24,8},{32,16},{40,24},{48,32},{56,40},{64,11... | collective-permute-start | bytes 786440 | tf_op jit(solution)/shard_map/ppermute | solution.py:412
  140.4 17.9 %collective-permute-start.13 = (bf16[64,2,8,128]{3,2,1,0:T(8,128)(2,1)}, bf16[64,2,8,128]{3,2,1,0:T(8,128)(2,1)S(1)}, u32[]{:S(2)}, u32[]{:S(2)}) collective-permute-start(bf16[64,2,8,128]{3,2,1,0:T(8,128)(2,1)} %get-tuple-element.26), channel_id=1, source_target_pairs={{0,56},{8,0},{16,8},{24,16},{32,24},{40,32},{48,40},{56,48},{64,12... | collective-permute-start | bytes 786440 | tf_op jit(solution)/shard_map/ppermute | solution.py:412
  146.1 15.8 %all-to-all-start.5 = ((bf16[8,8,2,8,128]{4,3,2,1,0:T(8,128)(2,1)}), bf16[8,8,2,8,128]{4,3,2,1,0:T(8,128)(2,1)S(1)}, u32[]{:S(2)}, u32[]{:S(2)}) async-start(bf16[8,8,2,8,128]{4,3,2,1,0:T(8,128)(2,1)} %lower.1), calls=%async_computation.5 | async-start | bytes 524288 | tf_op jit(solution)/shard_map/all_to_all | solution.py:416

commit v12 on v11

--- a/solution.py
+++ b/solution.py
@@ -15,7 +15,6 @@
 PP = 256
 WAVE_NUMBER = 6.0
 SIDE = 8
-ORDER = (4, 3, 5, 2, 6, 1, 7)
 BOTH = ("box", "angle")
 F32, BF16, I32 = jnp.float32, jnp.bfloat16, jnp.int32
 VM = pltpu.VMEM
@@ -63,8 +62,9 @@
     table = jnp.concatenate([owner, home - owner * rows_device], axis=0).astype(F32).astype(BF16)
     highs = home.shape[0]
     before = (iota((rows, rows), 0) < iota((rows, rows), 1)).astype(F32).astype(BF16)
-    carry = jnp.zeros((SIDE, 1), F32)
-    wanted = jnp.zeros((2 * SIDE, cap), F32)
+    share = cap // SIDE
+    carry = jnp.zeros((SIDE * SIDE, 1), F32)
+    wanted = jnp.zeros((SIDE, cap), F32)
     for j in range(slots):
         ids = ids_ref[pl.ds(j, 1), :]
         usable = ids >= 0
@@ -79,21 +79,22 @@
         column = jnp.where(core == 0, along_z, along_y)
         place = (jnp.where(core == 0, along_y, along_z) - mine) & 7
         hot = jnp.where((iota((SIDE, rows), 0) == column) & usable, 1.0, 0.0)
-        hot_b = hot.astype(BF16)
-        prefix = bmm(hot_b, before) + carry
-        carry = carry + jnp.sum(hot, axis=1, keepdims=True)
-        rank = jnp.sum(hot * prefix, axis=0, keepdims=True).astype(I32)
+        holder = column * SIDE + place
+        fine = jnp.where((iota((SIDE * SIDE, rows), 0) == holder) & usable, 1.0, 0.0)
+        prefix = bmm(fine.astype(BF16), before) + carry
+        carry = carry + jnp.sum(fine, axis=1, keepdims=True)
+        rank = jnp.sum(fine * prefix, axis=0, keepdims=True).astype(I32)
+        slot = place * share + rank
         lane = column if other is None else (other - column) & 7
-        position = lane * cap + rank
+        position = lane * cap + slot
         code_ref[pl.ds(j, 1), pl.ds(0, rows)] = jnp.where(
             usable, position * 64 + op_ref[pl.ds(j, 1), :], empty_op
         )
-        rank_hot = (iota((cap, rows), 0) == rank).astype(F32).astype(BF16)
-        both = jnp.concatenate([hot * place.astype(F32), hot * loc], axis=0).astype(BF16)
+        slot_hot = (iota((cap, rows), 0) == slot).astype(F32).astype(BF16)
         wanted = wanted + lax.dot_general(
-            both, rank_hot, (((1,), (1,)), ((), ())), preferred_element_type=F32
+            (hot * loc).astype(BF16), slot_hot, (((1,), (1,)), ((), ())), preferred_element_type=F32
         )
-    return (wanted[:SIDE] * rows_device + wanted[SIDE:]).astype(I32)
+    return wanted.astype(I32)
 
 
 def plan_body(where, cl, co, ch, plist, po, ph, want_ref, ccode_ref, pcode_ref):
@@ -189,16 +190,7 @@
 
 def select_body(where, asked, *refs):
     blocks, parents, children = refs[:8], refs[8], refs[9:17]
-    pool, parent_buf, child_buf, sems, parent_sems, child_sems = refs[17:]
-    copies = [
-        pltpu.make_async_copy(
-            b.at[pl.ds(128 * half, 128)], pool.at[half, pl.ds(128 * i, 128)], sems.at[half, i]
-        )
-        for half in (1, 0)
-        for i, b in enumerate(blocks)
-    ]
-    for copy in copies:
-        copy.start()
+    parent_buf, child_buf, parent_sems, child_sems = refs[17:]
 
     def child_out(d):
         return pltpu.make_async_copy(child_buf.at[d], children[d], child_sems.at[d])
@@ -206,30 +198,19 @@
     def parent_out(h):
         return pltpu.make_async_copy(parent_buf.at[h], parents.at[h], parent_sems.at[h])
 
-    for copy in copies[:8]:
-        copy.wait()
-
     def peer(h, carry):
         for k in range(16):
-            at = pl.multiple_of(asked[h, 64 + k] * 8, 8)
-            parent_buf[h, k] = pool[1, pl.ds(at, 8)]
+            at = pl.multiple_of(128 + asked[h, 64 + k] * 8, 8)
+            parent_buf[h, k] = blocks[k // 2][pl.ds(at, 8)]
         parent_out(h).start()
         return carry
 
     lax.fori_loop(0, SIDE, peer, 0)
-    for copy in copies[8:]:
-        copy.wait()
     for d in range(SIDE):
         h = (where[2] + d) & 7
-
-        def some(i, carry):
-            for j in range(16):
-                k = i * 16 + j
-                at = pl.multiple_of(asked[h, k] * 2, 2)
-                child_buf[d, k] = pool[0, pl.ds(at, 2)]
-            return carry
-
-        lax.fori_loop(0, 4, some, 0)
+        for k in range(64):
+            at = pl.multiple_of(asked[h, k] * 2, 2)
+            child_buf[d, k] = blocks[k // 8][pl.ds(at, 2)]
         child_out(d).start()
     for h in range(SIDE):
         parent_out(h).wait()
@@ -242,13 +223,11 @@
     return pl.pallas_call(
         select_body,
         out_shape=(pltpu.HBM((SIDE, 16, 8, 8, 128), BF16),) + (pltpu.HBM((64, 2, 8, 128), BF16),) * SIDE,
-        in_specs=[pl.BlockSpec(memory_space=pltpu.SMEM)] * 2 + [pl.BlockSpec(memory_space=ANY)] * 8,
+        in_specs=[pl.BlockSpec(memory_space=pltpu.SMEM)] * 2 + [pl.BlockSpec(memory_space=VM)] * 8,
         out_specs=(hbm,) * 9,
         scratch_shapes=[
-            pltpu.VMEM((2, 8 * 128, 8, 128), BF16),
             pltpu.VMEM((SIDE, 16, 8, 8, 128), BF16),
             pltpu.VMEM((SIDE, 64, 2, 8, 128), BF16),
-            pltpu.SemaphoreType.DMA((2, 8)),
             pltpu.SemaphoreType.DMA((8,)),
             pltpu.SemaphoreType.DMA((8,)),
         ],
@@ -459,7 +438,7 @@
     parents_out, *children_out = select(where, asked, blocks)
     parents_in = swap(parents_out, BOTH, axis_index_groups=TRADE)
     children_in = {0: children_out[0]}
-    for d in ORDER:
+    for d in (4, 3, 5, 2, 6, 1, 7):
         children_in[d] = hop(children_out[d], d, TRADE)
     sums = far_parents(hold(parent_code), parents_in.reshape(128, 8, 8, 128), parent_ops)
     turned = swap(sums, "angle").reshape(8, 2, 8, 8, 128)

time: 164 us -> 162 us (0.988)
  Pallas kernels: 19.3 us -> 17.3 us
where the time goes in v12:
time: 162 us; the launch traced here: 161 us
  starting transfers between devices  72.8 us (45%)
  blocking collectives  39 us (24%)
  waiting for transfers between devices  29.4 us (18%)
  Pallas kernels  17.3 us (11%)
  other arithmetic  1.77 us (1%)
    ppermute x13, starting transfers between devices, hop(): return lax.ppermute(x, BOTH, pairs)  52.3 us
    all_to_all x3, blocking collectives, swap(): lax.all_to_all(x, axis, split_axis=0, concat_axis=0, tiled=True, **kw)  39 us
    all_to_all x3, waiting for transfers between devices, swap(): lax.all_to_all(x, axis, split_axis=0, concat_axis=0, tiled=True, **kw)  22 us
    all_to_all x3, starting transfers between devices, swap(): lax.all_to_all(x, axis, split_axis=0, concat_axis=0, tiled=True, **kw)  13.5 us
    ppermute x13, waiting for transfers between devices, hop(): return lax.ppermute(x, BOTH, pairs)  7.33 us
    ppermute x1, starting transfers between devices, local(): up4 = lax.ppermute(onward, BOTH, pairs)  7.03 us
    pallas_call x1, Pallas kernels, far_children(): pl.pallas_call(child_far_body, out_shape=jax.ShapeDtypeStruct((64, 2, 8,...  3.59 us
    pallas_call x1, Pallas kernels, plan(): pl.pallas_call(plan_body, out_shape=(jax.ShapeDtypeStruct((SIDE, 128), I3...  3.54 us
  transfers between devices with their start and end apart: 17, of which 3 were waited for; matrix products, arithmetic and copies ran while one was open for 1% of the time, Pallas kernels for 8%

profile of v12, /device:TPU:10, one launch (start us, length us, event | category | flops | bytes accessed | tf_op | source)
XLA Modules:
  0.0 160.6 jit_solution(15894235543251902779)
XLA Ops:
  0.0 0.0 copy-start.6
  0.0 11.0 %all_to_all.30 = bf16[64,2,8,128]{3,2,1,0:T(8,128)(2,1)S(1)} all-to-all(bf16[64,2,8,128]{3,2,1,0:T(8,128)(2,1)} %param.15), channel_id=1, replica_groups=mesh['box'=64,'angle'=8] {'angle'}, dimensions={0} | all-to-all | bytes 524288 | tf_op jit(solution)/shard_map/all_to_all | solution.py:395
  11.0 1.8 %lift.1 = bf16[8,2,8,8,128]{4,3,2,1,0:T(8,128)(2,1)S(1)} custom-call(bf16[8,8,2,8,128]{4,3,2,1,0:T(8,128)(2,1)S(1)} %bitcast.23, bf16[128,64]{1,0:T(8,128)(2,1)} %constant.73.theta_h, bf16[128,256]{1,0:T(8,128)(2,1)} %constant.74.phi_h, f32[2,128,256]{2,1,0:T(8,128)} %constant.69.clone.cos_h.cos_t, f32[2,128,256]{2,1,0:T(8,128)} %constant.70.clone.sin_h.sin_t), custom_call_target="tpu_custom_call" | custom-call | tf_op jit(solution)/shard_map/lift/pallas_call | solution.py:179
  12.8 9.9 %all_to_all.31 = bf16[8,2,8,8,128]{4,3,2,1,0:T(8,128)(2,1)S(1)} all-to-all(bf16[8,2,8,8,128]{4,3,2,1,0:T(8,128)(2,1)S(1)} %lift.1), channel_id=1, replica_groups=mesh['box'=64,'angle'=8] {'angle'}, dimensions={0} | all-to-all | bytes 524288 | tf_op jit(solution)/shard_map/all_to_all | solution.py:395
  22.7 0.0 copy-done.6
  22.8 4.5 %collective-permute-start.3 = (bf16[256,8,128]{2,1,0:T(8,128)(2,1)S(1)}, bf16[256,8,128]{2,1,0:T(8,128)(2,1)S(1)}, u32[]{:S(2)}, u32[]{:S(2)}) collective-permute-start(bf16[256,8,128]{2,1,0:T(8,128)(2,1)S(1)} %pad_maximum_fusion.refs_0_), channel_id=1, source_target_pairs={{0,128},{64,192},{128,256},{192,320},{256,384},{320,448},{384,0},{... | collective-permute-start | bytes 1572872 | tf_op jit(solution)/shard_map/ppermute | solution.py:391
  27.3 3.5 %collective-permute-start.1 = (bf16[256,8,128]{2,1,0:T(8,128)(2,1)S(1)}, bf16[256,8,128]{2,1,0:T(8,128)(2,1)S(1)}, u32[]{:S(2)}, u32[]{:S(2)}) collective-permute-start(bf16[256,8,128]{2,1,0:T(8,128)(2,1)S(1)} %pad_maximum_fusion.refs_0_), channel_id=1, source_target_pairs={{0,384},{64,448},{128,0},{192,64},{256,128},{320,192},{384,256},{4... | collective-permute-start | bytes 1572872 | tf_op jit(solution)/shard_map/ppermute | solution.py:391
  30.8 4.1 %collective-permute-start.6 = (bf16[256,8,128]{2,1,0:T(8,128)(2,1)S(1)}, bf16[256,8,128]{2,1,0:T(8,128)(2,1)S(1)}, u32[]{:S(2)}, u32[]{:S(2)}) collective-permute-start(bf16[256,8,128]{2,1,0:T(8,128)(2,1)S(1)} %pad_maximum_fusion.refs_0_), channel_id=1, source_target_pairs={{0,64},{64,128},{128,192},{192,256},{256,320},{320,384},{384,448},... | collective-permute-start | bytes 1572872 | tf_op jit(solution)/shard_map/ppermute | solution.py:391
  34.9 4.6 %collective-permute-start = (bf16[256,8,128]{2,1,0:T(8,128)(2,1)S(1)}, bf16[256,8,128]{2,1,0:T(8,128)(2,1)S(1)}, u32[]{:S(2)}, u32[]{:S(2)}) collective-permute-start(bf16[256,8,128]{2,1,0:T(8,128)(2,1)S(1)} %pad_maximum_fusion.refs_0_), channel_id=1, source_target_pairs={{0,448},{64,0},{128,64},{192,128},{256,192},{320,256},{384,320},{4... | collective-permute-start | bytes 1572872 | tf_op jit(solution)/shard_map/ppermute | solution.py:391
  39.4 0.0 collective-permute-done.3.refs_6_
  39.5 5.6 %collective-permute-start.5 = (bf16[256,8,128]{2,1,0:T(8,128)(2,1)S(1)}, bf16[256,8,128]{2,1,0:T(8,128)(2,1)S(1)}, u32[]{:S(2)}, u32[]{:S(2)}) collective-permute-start(bf16[256,8,128]{2,1,0:T(8,128)(2,1)S(1)} %collective-permute-done.3.refs_6_), channel_id=1, source_target_pairs={{0,64},{64,128},{128,192},{192,256},{256,320},{320,384},{384,448},... | collective-permute-start | bytes 1572872 | tf_op jit(solution)/shard_map/ppermute | solution.py:391
  45.0 0.0 collective-permute-done.1.refs_2_
  45.0 0.9 broadcast_select_fusion
  45.9 7.0 %collective-permute-start.4 = (bf16[256,8,128]{2,1,0:T(8,128)(2,1)}, bf16[256,8,128]{2,1,0:T(8,128)(2,1)}, u32[]{:S(2)}, u32[]{:S(2)}) collective-permute-start(bf16[256,8,128]{2,1,0:T(8,128)(2,1)} %broadcast_select_fusion), channel_id=1, source_target_pairs={{0,128},{64,448},{128,256},{192,64},{256,384},{320,192},{384,0},{4... | collective-permute-start | bytes 1572872 | tf_op jit(solution)/shard_map/ppermute | solution.py:434
  53.0 1.9 %collective-permute-start.2 = (bf16[256,8,128]{2,1,0:T(8,128)(2,1)S(1)}, bf16[256,8,128]{2,1,0:T(8,128)(2,1)}, u32[]{:S(2)}, u32[]{:S(2)}) collective-permute-start(bf16[256,8,128]{2,1,0:T(8,128)(2,1)S(1)} %collective-permute-done.1.refs_2_), channel_id=1, source_target_pairs={{0,448},{64,0},{128,64},{192,128},{256,192},{320,256},{384,320},{4... | collective-permute-start | bytes 1572872 | tf_op jit(solution)/shard_map/ppermute | solution.py:391
  54.9 0.1 pad_add_fusion.where
  55.0 3.5 %plan.1 = (s32[8,128]{1,0:T(8,128)S(1)}, s32[8,64]{1,0:T(8,128)}, s32[8,16]{1,0:T(8,128)}) custom-call(s32[3]{0:T(128)S(1)} %pad_add_fusion.where, s32[8,64]{1,0:T(8,128)} %bitcast.29, s32[8,64]{1,0:T(8,128)} %bitcast.30, s32[32,128]{1,0:T(8,128)} %bitcast.28, s32[8,16]{1,0:T(8,128)} %bitcast.31, s32[8,16]{1,0:T(8,128)} %bitcast.32, s32[8,128]{1,0:T(8,128)} %bitcast.33), custom_call_target="tpu_custom_call" | custom-call | tf_op jit(solution)/shard_map/plan/pallas_call | solution.py:122
  58.5 18.0 %all_to_all.32 = s32[8,1,128]{2,1,0:T(1,128)S(1)} all-to-all(s32[8,1,128]{2,1,0:T(1,128)S(1)} %bitcast.25), channel_id=1, replica_groups={{0,8,16,24,32,40,48,56},{64,72,80,88,96,104,112,120},{128,136,144,152,1..., dimensions={0} | all-to-all | bytes 8192 | tf_op jit(solution)/shard_map/all_to_all | solution.py:395
  76.6 0.0 collective-permute-done.6.refs_7_
  76.6 0.0 collective-permute-done.refs_1_
  76.6 0.0 collective-permute-done.5.refs_5_
  76.6 0.0 collective-permute-done.4.refs_4_
  76.6 0.0 collective-permute-done.2.refs_3_
  76.6 3.4 %select.11 = (bf16[8,16,8,8,128]{4,3,2,1,0:T(8,128)(2,1)}, bf16[64,2,8,128]{3,2,1,0:T(8,128)(2,1)}, bf16[64,2,8,128]{3,2,1,0:T(8,128)(2,1)}, bf16[64,2,8,128]{3,...) custom-call(s32[3]{0:T(128)S(1)} %pad_add_fusion.where, ...), custom_call_target="tpu_custom_call" | custom-call | tf_op jit(solution)/shard_map/select/pallas_call | solution.py:223
  80.0 0.0 copy-start.2
  80.0 3.7 %all-to-all-start.3 = ((bf16[8,16,8,8,128]{4,3,2,1,0:T(8,128)(2,1)}), bf16[8,16,8,8,128]{4,3,2,1,0:T(8,128)(2,1)S(1)}, u32[]{:S(2)}, u32[]{:S(2)}) async-start(bf16[8,16,8,8,128]{4,3,2,1,0:T(8,128)(2,1)} %get-tuple-element.28), calls=%async_computation.3 | async-start | bytes 4194304 | tf_op jit(solution)/shard_map/all_to_all | solution.py:395
  83.7 0.0 copy-start
  83.8 0.0 copy-start.1
  83.8 0.0 copy-start.5
  83.8 3.9 %collective-permute-start.7 = (bf16[64,2,8,128]{3,2,1,0:T(8,128)(2,1)}, bf16[64,2,8,128]{3,2,1,0:T(8,128)(2,1)}, u32[]{:S(2)}, u32[]{:S(2)}) collective-permute-start(bf16[64,2,8,128]{3,2,1,0:T(8,128)(2,1)} %get-tuple-element.20), channel_id=1, source_target_pairs={{0,8},{8,16},{16,24},{24,32},{32,40},{40,48},{48,56},{56,0},{64,72... | collective-permute-start | bytes 786440 | tf_op jit(solution)/shard_map/ppermute | solution.py:391
  87.7 4.3 %collective-permute-start.8 = (bf16[64,2,8,128]{3,2,1,0:T(8,128)(2,1)}, bf16[64,2,8,128]{3,2,1,0:T(8,128)(2,1)}, u32[]{:S(2)}, u32[]{:S(2)}) collective-permute-start(bf16[64,2,8,128]{3,2,1,0:T(8,128)(2,1)} %get-tuple-element.21), channel_id=1, source_target_pairs={{0,16},{8,24},{16,32},{24,40},{32,48},{40,56},{48,0},{56,8},{64,80... | collective-permute-start | bytes 786440 | tf_op jit(solution)/shard_map/ppermute | solution.py:391
  92.0 22.0 %all-to-all-done.3 = bf16[8,16,8,8,128]{4,3,2,1,0:T(8,128)(2,1)S(1)} async-done(((bf16[8,16,8,8,128]{4,3,2,1,0:T(8,128)(2,1)}), bf16[8,16,8,8,128]{4,3,2,1,0:T(8,128)(2,1)S(1)}, u32[]{:S(2)}, u32[]{:S(2)}) %all-to-all-start.3) | async-done | bytes 2097184 | tf_op jit(solution)/shard_map/all_to_all | solution.py:395
  114.0 0.0 copy-done.2
  114.0 0.0 copy-start.3
  114.0 2.8 %far_parents.1 = bf16[16,8,8,128]{3,2,1,0:T(8,128)(2,1)} custom-call(s32[8,16]{1,0:T(8,128)} %get-tuple-element.27.code, bf16[128,8,8,128]{3,2,1,0:T(8,128)(2,1)S(1)} %bitcast.21, bf16[40,2,16,256]{3,2,1,0:T(8,128)(2,1)S(1)} %copy-done.2), custom_call_target="tpu_custom_call" | custom-call | tf_op jit(solution)/shard_map/far_parents/pallas_call | solution.py:268
  116.8 0.0 copy-start.4
  116.8 4.9 %all-to-all-start.4 = ((bf16[16,8,8,128]{3,2,1,0:T(8,128)(2,1)}), bf16[16,8,8,128]{3,2,1,0:T(8,128)(2,1)S(1)}, u32[]{:S(2)}, u32[]{:S(2)}) async-start(bf16[16,8,8,128]{3,2,1,0:T(8,128)(2,1)} %far_parents.1), calls=%async_computation.4 | async-start | bytes 524288 | tf_op jit(solution)/shard_map/all_to_all | solution.py:395
  121.8 1.9 %collective-permute-start.9 = (bf16[64,2,8,128]{3,2,1,0:T(8,128)(2,1)}, bf16[64,2,8,128]{3,2,1,0:T(8,128)(2,1)S(1)}, u32[]{:S(2)}, u32[]{:S(2)}) collective-permute-start(bf16[64,2,8,128]{3,2,1,0:T(8,128)(2,1)} %get-tuple-element.22), channel_id=1, source_target_pairs={{0,24},{8,32},{16,40},{24,48},{32,56},{40,0},{48,8},{56,16},{64,88... | collective-permute-start | bytes 786440 | tf_op jit(solution)/shard_map/ppermute | solution.py:391
  123.7 3.0 %collective-permute-start.10 = (bf16[64,2,8,128]{3,2,1,0:T(8,128)(2,1)}, bf16[64,2,8,128]{3,2,1,0:T(8,128)(2,1)S(1)}, u32[]{:S(2)}, u32[]{:S(2)}) collective-permute-start(bf16[64,2,8,128]{3,2,1,0:T(8,128)(2,1)} %get-tuple-element.23), channel_id=1, source_target_pairs={{0,32},{8,40},{16,48},{24,56},{32,0},{40,8},{48,16},{56,24},{64,96... | collective-permute-start | bytes 786440 | tf_op jit(solution)/shard_map/ppermute | solution.py:391
  126.7 6.2 %collective-permute-start.11 = (bf16[64,2,8,128]{3,2,1,0:T(8,128)(2,1)}, bf16[64,2,8,128]{3,2,1,0:T(8,128)(2,1)S(1)}, u32[]{:S(2)}, u32[]{:S(2)}) collective-permute-start(bf16[64,2,8,128]{3,2,1,0:T(8,128)(2,1)} %get-tuple-element.24), channel_id=1, source_target_pairs={{0,40},{8,48},{16,56},{24,0},{32,8},{40,16},{48,24},{56,32},{64,10... | collective-permute-start | bytes 786440 | tf_op jit(solution)/shard_map/ppermute | solution.py:391
  132.9 0.0 collective-permute-done.7.refs_1_
  132.9 5.4 %collective-permute-start.12 = (bf16[64,2,8,128]{3,2,1,0:T(8,128)(2,1)}, bf16[64,2,8,128]{3,2,1,0:T(8,128)(2,1)S(1)}, u32[]{:S(2)}, u32[]{:S(2)}) collective-permute-start(bf16[64,2,8,128]{3,2,1,0:T(8,128)(2,1)} %get-tuple-element.25), channel_id=1, source_target_pairs={{0,48},{8,56},{16,0},{24,8},{32,16},{40,24},{48,32},{56,40},{64,11... | collective-permute-start | bytes 786440 | tf_op jit(solution)/shard_map/ppermute | solution.py:391
  138.4 0.0 collective-permute-done.8.refs_2_
  138.4 3.4 %collective-permute-start.13 = (bf16[64,2,8,128]{3,2,1,0:T(8,128)(2,1)}, bf16[64,2,8,128]{3,2,1,0:T(8,128)(2,1)S(1)}, u32[]{:S(2)}, u32[]{:S(2)}) collective-permute-start(bf16[64,2,8,128]{3,2,1,0:T(8,128)(2,1)} %get-tuple-element.26), channel_id=1, source_target_pairs={{0,56},{8,0},{16,8},{24,16},{32,24},{40,32},{48,40},{56,48},{64,12... | collective-permute-start | bytes 786440 | tf_op jit(solution)/shard_map/ppermute | solution.py:391
  141.8 0.0 all-to-all-done.4
  141.8 0.0 copy-done
  141.8 0.0 copy-done.1
  141.8 0.0 copy-done.5
  141.8 2.2 %lower.1 = bf16[8,8,2,8,128]{4,3,2,1,0:T(8,128)(2,1)} custom-call(bf16[8,2,8,8,128]{4,3,2,1,0:T(8,128)(2,1)S(1)} %bitcast.22, bf16[64,128]{1,0:T(8,128)(2,1)S(1)} %copy-done.5, bf16[256,128]{1,0:T(8,128)(2,1)} %constant.76.phi_h, f32[2,128,256]{2,1,0:T(8,128)S(1)} %copy-done.1, f32[2,128,256]{2,1,0:T(8,128)S(1)} %copy-done), custom_call_target="tpu_custom_call" | custom-call | tf_op jit(solution)/shard_map/lower/pallas_call | solution.py:361
  144.1 4.8 %all-to-all-start.5 = ((bf16[8,8,2,8,128]{4,3,2,1,0:T(8,128)(2,1)}), bf16[8,8,2,8,128]{4,3,2,1,0:T(8,128)(2,1)S(1)}, u32[]{:S(2)}, u32[]{:S(2)}) async-start(bf16[8,8,2,8,128]{4,3,2,1,0:T(8,128)(2,1)} %lower.1), calls=%async_computation.5 | async-start | bytes 524288 | tf_op jit(solution)/shard_map/all_to_all | solution.py:395
  148.9 0.0 collective-permute-done.9.refs_3_
  148.9 0.0 collective-permute-done.10.refs_4_
  148.9 0.0 collective-permute-done.11.refs_5_
  148.9 4.4 %collective-permute-done.12.refs_6_ = bf16[64,2,8,128]{3,2,1,0:T(8,128)(2,1)S(1)} collective-permute-done((bf16[64,2,8,128]{3,2,1,0:T(8,128)(2,1)}, bf16[64,2,8,128]{3,2,1,0:T(8,128)(2,1)S(1)}, u32[]{:S(2)}, u32[]{:S(2)}) %collective-permute-start.12) | collective-permute-done | bytes 262176 | tf_op jit(solution)/shard_map/ppermute | solution.py:391
  153.3 2.9 %collective-permute-done.13.refs_7_ = bf16[64,2,8,128]{3,2,1,0:T(8,128)(2,1)S(1)} collective-permute-done((bf16[64,2,8,128]{3,2,1,0:T(8,128)(2,1)}, bf16[64,2,8,128]{3,2,1,0:T(8,128)(2,1)S(1)}, u32[]{:S(2)}, u32[]{:S(2)}) %collective-permute-start.13) | collective-permute-done | bytes 262176 | tf_op jit(solution)/shard_map/ppermute | solution.py:391
  156.2 0.0 copy-done.3
  156.2 0.0 copy-done.4
  156.2 3.6 %far_children.1 = f32[64,2,8,128]{3,2,1,0:T(8,128)S(1)} custom-call(s32[8,64]{1,0:T(8,128)} %get-tuple-element.17.code, bf16[64,2,8,128]{3,2,1,0:T(8,128)(2,1)S(1)} %copy-done.3, bf16[64,2,8,128]{3,2,1,0:T(8,128)(2,1)} %collective-permute-done.7.refs_1_, bf16[64,2,8,128]{3,2,1,0:T(8,128)(2,1)} %collective-permute-done.8.refs_2_, ...), custom_call_target="tpu_custom_call" | custom-call | tf_op jit(solution)/shard_map/far_children/pallas_call | solution.py:311
  159.8 0.0 all-to-all-done.5
  159.8 0.8 fusion
  (1 shorter events, 0.0 us)
Async XLA Ops:
  0.0 22.7 %copy-start.6 = (bf16[64,2,8,128]{3,2,1,0:T(8,128)(2,1)S(1)}, bf16[64,2,8,128]{3,2,1,0:T(8,128)(2,1)}, u32[]{:S(2)}) copy-start(bf16[64,2,8,128]{3,2,1,0:T(8,128)(2,1)} %param.15) | copy-start | bytes 786436
  22.8 16.7 %collective-permute-start.3 = (bf16[256,8,128]{2,1,0:T(8,128)(2,1)S(1)}, bf16[256,8,128]{2,1,0:T(8,128)(2,1)S(1)}, u32[]{:S(2)}, u32[]{:S(2)}) collective-permute-start(bf16[256,8,128]{2,1,0:T(8,128)(2,1)S(1)} %pad_maximum_fusion.refs_0_), channel_id=1, source_target_pairs={{0,128},{64,192},{128,256},{192,320},{256,384},{320,448},{384,0},{... | collective-permute-start | bytes 1572872 | tf_op jit(solution)/shard_map/ppermute | solution.py:391
  27.3 17.8 %collective-permute-start.1 = (bf16[256,8,128]{2,1,0:T(8,128)(2,1)S(1)}, bf16[256,8,128]{2,1,0:T(8,128)(2,1)S(1)}, u32[]{:S(2)}, u32[]{:S(2)}) collective-permute-start(bf16[256,8,128]{2,1,0:T(8,128)(2,1)S(1)} %pad_maximum_fusion.refs_0_), channel_id=1, source_target_pairs={{0,384},{64,448},{128,0},{192,64},{256,128},{320,192},{384,256},{4... | collective-permute-start | bytes 1572872 | tf_op jit(solution)/shard_map/ppermute | solution.py:391
  30.8 45.8 %collective-permute-start.6 = (bf16[256,8,128]{2,1,0:T(8,128)(2,1)S(1)}, bf16[256,8,128]{2,1,0:T(8,128)(2,1)S(1)}, u32[]{:S(2)}, u32[]{:S(2)}) collective-permute-start(bf16[256,8,128]{2,1,0:T(8,128)(2,1)S(1)} %pad_maximum_fusion.refs_0_), channel_id=1, source_target_pairs={{0,64},{64,128},{128,192},{192,256},{256,320},{320,384},{384,448},... | collective-permute-start | bytes 1572872 | tf_op jit(solution)/shard_map/ppermute | solution.py:391
  34.9 41.7 %collective-permute-start = (bf16[256,8,128]{2,1,0:T(8,128)(2,1)S(1)}, bf16[256,8,128]{2,1,0:T(8,128)(2,1)S(1)}, u32[]{:S(2)}, u32[]{:S(2)}) collective-permute-start(bf16[256,8,128]{2,1,0:T(8,128)(2,1)S(1)} %pad_maximum_fusion.refs_0_), channel_id=1, source_target_pairs={{0,448},{64,0},{128,64},{192,128},{256,192},{320,256},{384,320},{4... | collective-permute-start | bytes 1572872 | tf_op jit(solution)/shard_map/ppermute | solution.py:391
  39.5 37.1 %collective-permute-start.5 = (bf16[256,8,128]{2,1,0:T(8,128)(2,1)S(1)}, bf16[256,8,128]{2,1,0:T(8,128)(2,1)S(1)}, u32[]{:S(2)}, u32[]{:S(2)}) collective-permute-start(bf16[256,8,128]{2,1,0:T(8,128)(2,1)S(1)} %collective-permute-done.3.refs_6_), channel_id=1, source_target_pairs={{0,64},{64,128},{128,192},{192,256},{256,320},{320,384},{384,448},... | collective-permute-start | bytes 1572872 | tf_op jit(solution)/shard_map/ppermute | solution.py:391
  45.9 30.7 %collective-permute-start.4 = (bf16[256,8,128]{2,1,0:T(8,128)(2,1)}, bf16[256,8,128]{2,1,0:T(8,128)(2,1)}, u32[]{:S(2)}, u32[]{:S(2)}) collective-permute-start(bf16[256,8,128]{2,1,0:T(8,128)(2,1)} %broadcast_select_fusion), channel_id=1, source_target_pairs={{0,128},{64,448},{128,256},{192,64},{256,384},{320,192},{384,0},{4... | collective-permute-start | bytes 1572872 | tf_op jit(solution)/shard_map/ppermute | solution.py:434
  53.0 23.6 %collective-permute-start.2 = (bf16[256,8,128]{2,1,0:T(8,128)(2,1)S(1)}, bf16[256,8,128]{2,1,0:T(8,128)(2,1)}, u32[]{:S(2)}, u32[]{:S(2)}) collective-permute-start(bf16[256,8,128]{2,1,0:T(8,128)(2,1)S(1)} %collective-permute-done.1.refs_2_), channel_id=1, source_target_pairs={{0,448},{64,0},{128,64},{192,128},{256,192},{320,256},{384,320},{4... | collective-permute-start | bytes 1572872 | tf_op jit(solution)/shard_map/ppermute | solution.py:391
  80.0 34.1 %copy-start.2 = (bf16[40,2,16,256]{3,2,1,0:T(8,128)(2,1)S(1)}, bf16[40,2,16,256]{3,2,1,0:T(8,128)(2,1)}, u32[]{:S(2)}) copy-start(bf16[40,2,16,256]{3,2,1,0:T(8,128)(2,1)} %ops_hbm.1) | copy-start | bytes 1966084
  80.0 34.0 %all-to-all-start.3 = ((bf16[8,16,8,8,128]{4,3,2,1,0:T(8,128)(2,1)}), bf16[8,16,8,8,128]{4,3,2,1,0:T(8,128)(2,1)S(1)}, u32[]{:S(2)}, u32[]{:S(2)}) async-start(bf16[8,16,8,8,128]{4,3,2,1,0:T(8,128)(2,1)} %get-tuple-element.28), calls=%async_computation.3 | async-start | bytes 4194304 | tf_op jit(solution)/shard_map/all_to_all | solution.py:395
  83.7 58.1 %copy-start = (f32[2,128,256]{2,1,0:T(8,128)S(1)}, f32[2,128,256]{2,1,0:T(8,128)}, u32[]{:S(2)}) copy-start(f32[2,128,256]{2,1,0:T(8,128)} %constant.70.clone.sin_h.sin_t) | copy-start | bytes 786436
  83.8 58.1 %copy-start.1 = (f32[2,128,256]{2,1,0:T(8,128)S(1)}, f32[2,128,256]{2,1,0:T(8,128)}, u32[]{:S(2)}) copy-start(f32[2,128,256]{2,1,0:T(8,128)} %constant.69.clone.cos_h.cos_t) | copy-start | bytes 786436
  83.8 58.1 %copy-start.5 = (bf16[64,128]{1,0:T(8,128)(2,1)S(1)}, bf16[64,128]{1,0:T(8,128)(2,1)}, u32[]{:S(2)}) copy-start(bf16[64,128]{1,0:T(8,128)(2,1)} %constant.75.theta) | copy-start | bytes 49156
  83.8 49.1 %collective-permute-start.7 = (bf16[64,2,8,128]{3,2,1,0:T(8,128)(2,1)}, bf16[64,2,8,128]{3,2,1,0:T(8,128)(2,1)}, u32[]{:S(2)}, u32[]{:S(2)}) collective-permute-start(bf16[64,2,8,128]{3,2,1,0:T(8,128)(2,1)} %get-tuple-element.20), channel_id=1, source_target_pairs={{0,8},{8,16},{16,24},{24,32},{32,40},{40,48},{48,56},{56,0},{64,72... | collective-permute-start | bytes 786440 | tf_op jit(solution)/shard_map/ppermute | solution.py:391
  87.7 50.6 %collective-permute-start.8 = (bf16[64,2,8,128]{3,2,1,0:T(8,128)(2,1)}, bf16[64,2,8,128]{3,2,1,0:T(8,128)(2,1)}, u32[]{:S(2)}, u32[]{:S(2)}) collective-permute-start(bf16[64,2,8,128]{3,2,1,0:T(8,128)(2,1)} %get-tuple-element.21), channel_id=1, source_target_pairs={{0,16},{8,24},{16,32},{24,40},{32,48},{40,56},{48,0},{56,8},{64,80... | collective-permute-start | bytes 786440 | tf_op jit(solution)/shard_map/ppermute | solution.py:391
  114.0 42.2 %copy-start.3 = (bf16[64,2,8,128]{3,2,1,0:T(8,128)(2,1)S(1)}, bf16[64,2,8,128]{3,2,1,0:T(8,128)(2,1)}, u32[]{:S(2)}) copy-start(bf16[64,2,8,128]{3,2,1,0:T(8,128)(2,1)} %get-tuple-element.19.refs_0_) | copy-start | bytes 786436
  116.8 39.4 %copy-start.4 = (bf16[40,2,8,128]{3,2,1,0:T(8,128)(2,1)S(1)}, bf16[40,2,8,128]{3,2,1,0:T(8,128)(2,1)}, u32[]{:S(2)}) copy-start(bf16[40,2,8,128]{3,2,1,0:T(8,128)(2,1)} %refs_8_.1) | copy-start | bytes 491524
  116.8 25.0 %all-to-all-start.4 = ((bf16[16,8,8,128]{3,2,1,0:T(8,128)(2,1)}), bf16[16,8,8,128]{3,2,1,0:T(8,128)(2,1)S(1)}, u32[]{:S(2)}, u32[]{:S(2)}) async-start(bf16[16,8,8,128]{3,2,1,0:T(8,128)(2,1)} %far_parents.1), calls=%async_computation.4 | async-start | bytes 524288 | tf_op jit(solution)/shard_map/all_to_all | solution.py:395
  121.8 27.1 %collective-permute-start.9 = (bf16[64,2,8,128]{3,2,1,0:T(8,128)(2,1)}, bf16[64,2,8,128]{3,2,1,0:T(8,128)(2,1)S(1)}, u32[]{:S(2)}, u32[]{:S(2)}) collective-permute-start(bf16[64,2,8,128]{3,2,1,0:T(8,128)(2,1)} %get-tuple-element.22), channel_id=1, source_target_pairs={{0,24},{8,32},{16,40},{24,48},{32,56},{40,0},{48,8},{56,16},{64,88... | collective-permute-start | bytes 786440 | tf_op jit(solution)/shard_map/ppermute | solution.py:391
  123.7 25.2 %collective-permute-start.10 = (bf16[64,2,8,128]{3,2,1,0:T(8,128)(2,1)}, bf16[64,2,8,128]{3,2,1,0:T(8,128)(2,1)S(1)}, u32[]{:S(2)}, u32[]{:S(2)}) collective-permute-start(bf16[64,2,8,128]{3,2,1,0:T(8,128)(2,1)} %get-tuple-element.23), channel_id=1, source_target_pairs={{0,32},{8,40},{16,48},{24,56},{32,0},{40,8},{48,16},{56,24},{64,96... | collective-permute-start | bytes 786440 | tf_op jit(solution)/shard_map/ppermute | solution.py:391
  126.7 22.2 %collective-permute-start.11 = (bf16[64,2,8,128]{3,2,1,0:T(8,128)(2,1)}, bf16[64,2,8,128]{3,2,1,0:T(8,128)(2,1)S(1)}, u32[]{:S(2)}, u32[]{:S(2)}) collective-permute-start(bf16[64,2,8,128]{3,2,1,0:T(8,128)(2,1)} %get-tuple-element.24), channel_id=1, source_target_pairs={{0,40},{8,48},{16,56},{24,0},{32,8},{40,16},{48,24},{56,32},{64,10... | collective-permute-start | bytes 786440 | tf_op jit(solution)/shard_map/ppermute | solution.py:391
  132.9 20.4 %collective-permute-start.12 = (bf16[64,2,8,128]{3,2,1,0:T(8,128)(2,1)}, bf16[64,2,8,128]{3,2,1,0:T(8,128)(2,1)S(1)}, u32[]{:S(2)}, u32[]{:S(2)}) collective-permute-start(bf16[64,2,8,128]{3,2,1,0:T(8,128)(2,1)} %get-tuple-element.25), channel_id=1, source_target_pairs={{0,48},{8,56},{16,0},{24,8},{32,16},{40,24},{48,32},{56,40},{64,11... | collective-permute-start | bytes 786440 | tf_op jit(solution)/shard_map/ppermute | solution.py:391
  138.4 17.9 %collective-permute-start.13 = (bf16[64,2,8,128]{3,2,1,0:T(8,128)(2,1)}, bf16[64,2,8,128]{3,2,1,0:T(8,128)(2,1)S(1)}, u32[]{:S(2)}, u32[]{:S(2)}) collective-permute-start(bf16[64,2,8,128]{3,2,1,0:T(8,128)(2,1)} %get-tuple-element.26), channel_id=1, source_target_pairs={{0,56},{8,0},{16,8},{24,16},{32,24},{40,32},{48,40},{56,48},{64,12... | collective-permute-start | bytes 786440 | tf_op jit(solution)/shard_map/ppermute | solution.py:391
  144.1 15.8 %all-to-all-start.5 = ((bf16[8,8,2,8,128]{4,3,2,1,0:T(8,128)(2,1)}), bf16[8,8,2,8,128]{4,3,2,1,0:T(8,128)(2,1)S(1)}, u32[]{:S(2)}, u32[]{:S(2)}) async-start(bf16[8,8,2,8,128]{4,3,2,1,0:T(8,128)(2,1)} %lower.1), calls=%async_computation.5 | async-start | bytes 524288 | tf_op jit(solution)/shard_map/all_to_all | solution.py:395
